TPU v7x, 32 devices: a whole 2x2x4 slice. The times are simulated.
32 devices in a mesh: grp: 4 (over y, core), row: 4 (over z), col: 2 (over x).
Axes of the slice: x: 2, y: 2, z: 4, core: 2. Of those that a mesh axis runs over, the one named last changes fastest.
Arguments:
- tokens: bfloat16 [16384, 2048], P(('grp', 'row', 'col')), may hold values from -6 to 6
- cotangent: bfloat16 [16384, 2048], P(('grp', 'row', 'col')), may hold values from -15 to 15
- segments: int32 [16384], P(('grp', 'row')), may hold values from 0 to 4, as said below
- positions: int32 [16384], P(('grp', 'row')), may hold values from 0 to 703, as said below
- first_gain: float32 [2048], replicated, may hold values from 0.25 to 1.75
- query_weight: bfloat16 [2048, 2048], P(None, 'col'), may hold values from -0.1875 to 0.1875
- key_matrix: bfloat16 [2048, 1024], replicated, may hold values from -0.1875 to 0.1875
- value_matrix: bfloat16 [2048, 1024], replicated, may hold values from -0.125 to 0.125
- output_weight: bfloat16 [2048, 2048], P('col'), may hold values from -1 to 1
- second_gain: float32 [2048], replicated, may hold values from 0.25 to 1.75
- gate_weight: bfloat16 [2048, 8192], P(None, ('row', 'col')), may hold values from -0.125 to 0.125
- up_weight: bfloat16 [2048, 8192], P(None, ('row', 'col')), may hold values from -0.125 to 0.125
- down_weight: bfloat16 [8192, 2048], P(('row', 'col')), may hold values from -0.09375 to 0.09375
Outputs:
- layer_out: float32 [16384, 2048], P(('grp', 'row', 'col'))
- input_grad: float32 [16384, 2048], P(('grp', 'row', 'col'))
- first_gain_grad: float32 [2048], replicated
- query_grad: float32 [2048, 2048], P(None, 'col')
- key_grad: float32 [2048, 1024], replicated
- value_grad: float32 [2048, 1024], replicated
- output_grad: float32 [2048, 2048], P('col')
- second_gain_grad: float32 [2048], replicated
- gate_grad: float32 [2048, 8192], P(None, ('row', 'col'))
- up_grad: float32 [2048, 8192], P(None, ('row', 'col'))
- down_grad: float32 [8192, 2048], P(('row', 'col'))
Inputs may be any that keep to these rules, and one draw needn't show every extreme that they name: `segments`: tokens come in aligned packs of 1024: the first 512 of a pack are its prompt, segment 0; the other 512 hold its 4 continuations, numbered 1 to 4 in order, each a run of consecutive tokens of 64 to 192 tokens. A prompt's tokens have positions 0 to 511 in order; a continuation's tokens count on from 512.
All inputs are finite; a program needn't handle non-finite values.
Results may differ from a plain program's by a relative error of at most 0.02.
Values may be sent and summed in bfloat16 or wider, within the bound.
No kernel may reach another device: no remote copies, remote signals or barrier semaphores. Data moves between devices by JAX's collectives and lax.ppermute only.
A program may use at most 384 MiB of HBM per device.

v0:
```python
import math

import jax
import jax.numpy as jnp
from jax import lax
from jax.sharding import PartitionSpec as P

QUERY_HEADS = 8
KEY_VALUE_HEADS = 4
HEAD_SIZE = 256
QBLOCK = 512


NORM_EPSILON = 1e-06
ROPE_BASE = 1000042.0
MASKED_SCORE = -1e30


def normalize(values, gain):
    inverse = lax.rsqrt(jnp.mean(values * values, axis=-1, keepdims=True) + NORM_EPSILON)
    return values * inverse * gain


def rope_tables(positions, head_dim):
    half_dim = head_dim // 2
    exponent = jnp.arange(half_dim, dtype=jnp.float32) * (2.0 / head_dim)
    inverse_freq = jnp.exp(-math.log(ROPE_BASE) * exponent)
    angles = positions.astype(jnp.float32)[:, None] * inverse_freq[None, :]
    return (jnp.cos(angles), jnp.sin(angles))


def rotate(values, cosine, sine):
    half_dim = values.shape[-1] // 2
    shape = (values.shape[0],) + (1,) * (values.ndim - 2) + (half_dim,)
    cosine = cosine.reshape(shape)
    sine = sine.reshape(shape)
    first_half = values[..., :half_dim]
    second_half = values[..., half_dim:]
    return jnp.concatenate(
        [first_half * cosine - second_half * sine, second_half * cosine + first_half * sine],
        axis=-1,
    )


def swiglu(gate_val, up_val):
    return jax.nn.silu(gate_val) * up_val


def per_device(
    tokens,
    cotangent,
    segments,
    positions,
    first_gain,
    query_weight,
    key_matrix,
    value_matrix,
    output_weight,
    second_gain,
    gate_weight,
    up_weight,
    down_weight,
):
    head_dim = HEAD_SIZE
    query_heads = query_weight.shape[1] // head_dim
    heads_per_group = QUERY_HEADS // KEY_VALUE_HEADS
    key_heads = max(1, query_heads // heads_per_group)
    head_share = query_heads // key_heads
    head_sharing = max(1, heads_per_group // query_heads)
    key_first = lax.axis_index("col") * query_heads // heads_per_group
    query_cols = query_heads * head_dim
    key_cols = key_heads * head_dim
    width = tokens.shape[1]
    inputs = tokens.astype(jnp.float32)
    key_slice = lax.dynamic_slice_in_dim(key_matrix, key_first * head_dim, key_cols, 1)
    value_slice = lax.dynamic_slice_in_dim(value_matrix, key_first * head_dim, key_cols, 1)
    normalized_input, first_back = jax.vjp(normalize, inputs, first_gain)
    gathered_in = lax.all_gather(normalized_input.astype(jnp.bfloat16), "col", axis=0, tiled=True)
    project_in = jnp.concatenate([query_weight, key_slice, value_slice], axis=1)
    projected = jnp.dot(gathered_in, project_in, preferred_element_type=jnp.float32)
    packed_length = projected.shape[0]
    cosine, sine = rope_tables(positions, head_dim)
    query_low = rotate(
        projected[:, :query_cols].reshape(packed_length, key_heads, head_share, head_dim),
        cosine,
        sine,
    ).astype(jnp.bfloat16)
    key_low = rotate(
        projected[:, query_cols : query_cols + key_cols].reshape(
            packed_length, key_heads, head_dim
        ),
        cosine,
        sine,
    ).astype(jnp.bfloat16)
    value_reduced = (
        projected[:, query_cols + key_cols :]
        .reshape(packed_length, key_heads, head_dim)
        .astype(jnp.bfloat16)
    )
    block_count = packed_length // QBLOCK
    query_blocks = query_low.reshape(block_count, QBLOCK, key_heads, head_share, head_dim)
    seg_blocks = segments.reshape(block_count, QBLOCK)
    pos_blocks = positions.reshape(block_count, QBLOCK)
    score_scale = head_dim ** (-0.5)

    def block_scores(query_block, seg_block, pos_block):
        raw = (
            jnp.einsum("qgrd,kgd->grqk", query_block, key_low, preferred_element_type=jnp.float32)
            * score_scale
        )
        allowed = (positions[None, :] <= pos_block[:, None]) & (
            (segments[None, :] == 0) | (segments[None, :] == seg_block[:, None])
        )
        return jnp.where(allowed[None, None, :, :], raw, MASKED_SCORE)

    def attend(block):
        query_block, seg_block, pos_block = block
        scores = block_scores(query_block, seg_block, pos_block)
        peak = jnp.max(scores, axis=-1, keepdims=True)
        log_total = peak + jnp.log(jnp.sum(jnp.exp(scores - peak), axis=-1, keepdims=True))
        probs_low = jnp.exp(scores - log_total).astype(jnp.bfloat16)
        mixed = jnp.einsum(
            "grqk,kgd->qgrd", probs_low, value_reduced, preferred_element_type=jnp.float32
        )
        return (mixed, log_total[..., 0])

    mixed_all, log_totals = lax.map(attend, (query_blocks, seg_blocks, pos_blocks))
    attn_low = mixed_all.reshape(packed_length, query_cols).astype(jnp.bfloat16)
    rows_now = attn_low
    attn_branch = lax.psum_scatter(
        jnp.dot(rows_now, output_weight, preferred_element_type=jnp.float32),
        "col",
        scatter_dimension=0,
        tiled=True,
    )
    hidden_res = inputs + attn_branch
    normed_mid, second_back = jax.vjp(normalize, hidden_res, second_gain)
    mid_low = normed_mid.astype(jnp.bfloat16)
    gathered_mid = lax.all_gather(mid_low, ("row", "col"), axis=0, tiled=True)
    gate_lin = jnp.dot(gathered_mid, gate_weight, preferred_element_type=jnp.float32)
    up_lin = jnp.dot(gathered_mid, up_weight, preferred_element_type=jnp.float32)
    activated, swiglu_back = jax.vjp(swiglu, gate_lin, up_lin)
    act_low = activated.astype(jnp.bfloat16)
    rows_now = act_low
    mlp_branch = lax.psum_scatter(
        jnp.dot(rows_now, down_weight, preferred_element_type=jnp.float32).astype(jnp.bfloat16),
        ("row", "col"),
        scatter_dimension=0,
        tiled=True,
    ).astype(jnp.float32)
    layer_out = hidden_res + mlp_branch
    shard_rows = lax.all_gather(cotangent, ("row", "col"), axis=0, tiled=True)
    down_total = jnp.einsum("tf,td->fd", act_low, shard_rows, preferred_element_type=jnp.float32)
    grad_rows = jnp.einsum("td,fd->tf", shard_rows, down_weight, preferred_element_type=jnp.float32)
    down_grad = down_total
    act_grad = grad_rows
    gate_grad_f, up_grad_f = swiglu_back(act_grad)
    gate_grad_low = gate_grad_f.astype(jnp.bfloat16)
    up_grad_low = up_grad_f.astype(jnp.bfloat16)
    gate_wgrad = jnp.einsum(
        "td,tf->df", gathered_mid, gate_grad_low, preferred_element_type=jnp.float32
    )
    up_wgrad = jnp.einsum(
        "td,tf->df", gathered_mid, up_grad_low, preferred_element_type=jnp.float32
    )
    mid_grad = lax.psum_scatter(
        jnp.einsum("tf,df->td", gate_grad_low, gate_weight, preferred_element_type=jnp.float32)
        + jnp.einsum("tf,df->td", up_grad_low, up_weight, preferred_element_type=jnp.float32),
        ("row", "col"),
        scatter_dimension=0,
        tiled=True,
    )
    res_from_mid, second_gain_part = second_back(mid_grad)
    res_grad = cotangent.astype(jnp.float32) + res_from_mid
    res_low = res_grad.astype(jnp.bfloat16)
    shard_rows = lax.all_gather(res_low, "col", axis=0, tiled=True)
    out_total = jnp.einsum("tc,td->cd", attn_low, shard_rows, preferred_element_type=jnp.float32)
    grad_rows = jnp.einsum(
        "td,cd->tc", shard_rows, output_weight, preferred_element_type=jnp.float32
    )
    out_wgrad = out_total
    mixed_low = grad_rows.astype(jnp.bfloat16).reshape(
        block_count, QBLOCK, key_heads, head_share, head_dim
    )

    def attend_back(totals, block):
        query_block, seg_block, pos_block, mixed_block, log_block = block
        scores = block_scores(query_block, seg_block, pos_block)
        probs = jnp.exp(scores - log_block[..., None])
        probs_low = probs.astype(jnp.bfloat16)
        value_total = totals[1] + jnp.einsum(
            "grqk,qgrd->kgrd", probs_low, mixed_block, preferred_element_type=jnp.float32
        )
        prob_grad = jnp.einsum(
            "qgrd,kgd->grqk", mixed_block, value_reduced, preferred_element_type=jnp.float32
        )
        row_dot = jnp.sum(probs * prob_grad, axis=-1, keepdims=True)
        score_low = (probs * (prob_grad - row_dot)).astype(jnp.bfloat16)
        query_grad_rows = (
            jnp.einsum("grqk,kgd->qgrd", score_low, key_low, preferred_element_type=jnp.float32)
            * score_scale
        )
        key_total = (
            totals[0]
            + jnp.einsum(
                "grqk,qgrd->kgrd", score_low, query_block, preferred_element_type=jnp.float32
            )
            * score_scale
        )
        return ((key_total, value_total), query_grad_rows)

    zero_heads = jnp.zeros((packed_length, key_heads, head_share, head_dim), jnp.float32)
    (key_grad_rot, value_head_grad), query_grad_blocks = lax.scan(
        attend_back,
        (zero_heads, zero_heads),
        (query_blocks, seg_blocks, pos_blocks, mixed_low, log_totals),
    )
    query_grad_rot = query_grad_blocks.reshape(packed_length, key_heads, head_share, head_dim)
    query_back = (
        rotate(query_grad_rot, cosine, -sine)
        .astype(jnp.bfloat16)
        .reshape(packed_length, query_cols)
    )
    key_back = (
        rotate(key_grad_rot, cosine, -sine).astype(jnp.bfloat16).reshape(packed_length, query_cols)
    )
    value_back = value_head_grad.astype(jnp.bfloat16).reshape(packed_length, query_cols)
    back_all = jnp.concatenate([query_back, key_back, value_back], axis=1)
    key_spread = jnp.repeat(
        key_slice.reshape(width, key_heads, 1, head_dim), head_share, axis=2
    ).reshape(width, query_cols)
    value_spread = jnp.repeat(
        value_slice.reshape(width, key_heads, 1, head_dim), head_share, axis=2
    ).reshape(width, query_cols)
    back_weights = jnp.concatenate([query_weight, key_spread, value_spread], axis=1)
    rows_now = back_all
    in_grad = lax.psum_scatter(
        jnp.einsum("tc,dc->td", rows_now, back_weights, preferred_element_type=jnp.float32).astype(
            jnp.bfloat16
        ),
        "col",
        scatter_dimension=0,
        tiled=True,
    ).astype(jnp.float32)
    res_from_in, first_gain_part = first_back(in_grad)
    input_grad = res_grad + res_from_in
    proj_grad = jnp.einsum("td,tc->dc", gathered_in, back_all, preferred_element_type=jnp.float32)
    query_wgrad = proj_grad[:, :query_cols]
    key_part = jnp.sum(
        proj_grad[:, query_cols : 2 * query_cols].reshape(width, key_heads, head_share, head_dim),
        axis=2,
    ).reshape(width, key_cols)
    value_part = jnp.sum(
        proj_grad[:, 2 * query_cols :].reshape(width, key_heads, head_share, head_dim), axis=2
    ).reshape(width, key_cols)
    query_wgrad, out_wgrad, key_part, value_part, first_sum, second_sum = (
        lax.psum(query_wgrad.astype(jnp.bfloat16), ("grp", "row")).astype(jnp.float32),
        lax.psum(out_wgrad.astype(jnp.bfloat16), ("grp", "row")).astype(jnp.float32),
        lax.psum(key_part.astype(jnp.bfloat16), ("grp", "row")).astype(jnp.float32),
        lax.psum(value_part.astype(jnp.bfloat16), ("grp", "row")).astype(jnp.float32),
        lax.psum(first_gain_part.astype(jnp.bfloat16), ("grp", "row")).astype(jnp.float32),
        lax.psum(second_gain_part.astype(jnp.bfloat16), ("grp", "row")).astype(jnp.float32),
    )
    key_all, value_all, first_rows, second_rows = (
        lax.all_gather(key_part, "col", axis=1, tiled=True),
        lax.all_gather(value_part, "col", axis=1, tiled=True),
        lax.all_gather(first_sum.reshape(1, width), "col", axis=1, tiled=True),
        lax.all_gather(second_sum.reshape(1, width), "col", axis=1, tiled=True),
    )
    col_count = lax.axis_size("col")
    key_full = jnp.sum(
        key_all.reshape(width, col_count // head_sharing, head_sharing, key_cols), axis=2
    ).reshape(width, col_count // head_sharing * key_cols)
    value_full = jnp.sum(
        value_all.reshape(width, col_count // head_sharing, head_sharing, key_cols), axis=2
    ).reshape(width, col_count // head_sharing * key_cols)
    first_gain_grad = jnp.sum(first_rows.reshape(col_count, width), axis=0)
    second_gain_grad = jnp.sum(second_rows.reshape(col_count, width), axis=0)
    gate_wgrad, up_wgrad, down_grad = (
        lax.psum(gate_wgrad.astype(jnp.bfloat16), "grp").astype(jnp.float32),
        lax.psum(up_wgrad.astype(jnp.bfloat16), "grp").astype(jnp.float32),
        lax.psum(down_grad.astype(jnp.bfloat16), "grp").astype(jnp.float32),
    )
    return (
        layer_out,
        input_grad,
        first_gain_grad,
        query_wgrad,
        key_full,
        value_full,
        out_wgrad,
        second_gain_grad,
        gate_wgrad,
        up_wgrad,
        down_grad,
    )


def solution(mesh):
    return jax.shard_map(
        per_device,
        mesh=mesh,
        in_specs=(
            P(("grp", "row", "col"), None),
            P(("grp", "row", "col"), None),
            P(("grp", "row")),
            P(("grp", "row")),
            P(),
            P(None, "col"),
            P(),
            P(),
            P("col", None),
            P(),
            P(None, ("row", "col")),
            P(None, ("row", "col")),
            P(("row", "col"), None),
        ),
        out_specs=(
            P(("grp", "row", "col"), None),
            P(("grp", "row", "col"), None),
            P(),
            P(None, "col"),
            P(),
            P(),
            P("col", None),
            P(),
            P(None, ("row", "col")),
            P(None, ("row", "col")),
            P(("row", "col"), None),
        ),
        check_vma=False,
    )
```

profile of v0, /device:TPU:0, one launch (start us, length us, event | category | flops | bytes accessed | tf_op | source)
XLA Modules:
  0.0 2625.0 jit_solution(5986361226649770376)
XLA Ops:
  21.1 52.5 %all-gather.7.cloned.1.call-done = bf16[1024,2048]{1,0:T(8,128)(2,1)} async-done(((bf16[512,2048]{1,0:T(8,128)(2,1)}), bf16[1024,2048]{1,0:T(8,128)(2,1)}) %all-gather.7.cloned.1.call-update) | async-done | bytes 4194320 | tf_op jit(solution)/shard_map/all_gather | solution.py:78
  73.6 12.8 fusion.56
  110.3 20.1 while.27
  148.1 99.4 %reduce-scatter.5.cloned.1.call-done = f32[512,2048]{1,0:T(8,128)} async-done(((f32[1024,2048]{1,0:T(8,128)}), f32[512,2048]{1,0:T(8,128)}) %reduce-scatter.5.cloned.1.call-update) | async-done | bytes 4194320 | tf_op jit(solution)/shard_map/reduce_scatter | solution.py:130
  254.7 226.8 %all-gather.9.cloned.1.call-done = bf16[4096,2048]{1,0:T(8,128)(2,1)} async-done(((bf16[512,2048]{1,0:T(8,128)(2,1)}), bf16[4096,2048]{1,0:T(8,128)(2,1)}) %all-gather.9.cloned.1.call-update) | async-done | bytes 16777232 | tf_op jit(solution)/shard_map/all_gather | solution.py:139
  481.5 24.7 fusion.85
  506.3 20.8 fusion.86
  527.0 182.0 %all-gather.11.cloned.1.call-done = bf16[4096,2048]{1,0:T(8,128)(2,1)} async-done(((bf16[512,2048]{1,0:T(8,128)(2,1)}), bf16[4096,2048]{1,0:T(8,128)(2,1)}) %all-gather.11.cloned.1.call-update) | async-done | bytes 16777232 | tf_op jit(solution)/shard_map/all_gather | solution.py:152
  709.0 36.2 %multiply_convert_fusion = (bf16[4096,1024]{1,0:T(8,128)(2,1)}, bf16[4096,1024]{1,0:T(8,128)(2,1)}, bf16[4096,1024]{1,0:T(8,128)(2,1)}) fusion(f32[4096,1024]{1,0:T(8,128)} %fusion.85, f32[4096,1024]{1,0:T(8,128)} %fusion.86, bf16[4096,2048]{1,0:T(8,128)(2,1)} %all-gather.11.cloned.1.call-done, bf16[1024,2048]{1,0:T(8,128)(2,1)} %param.29), kind=kOutput, calls=%fused_computation.69 | convolution fusion | flops 17246978048 | bytes 79691776 | tf_op jit(solution)/shard_map/td,fd->tf/dot_general | solution.py:154
  745.2 25.4 fusion.87
  770.5 31.5 %convolution_add_fusion = f32[4096,2048]{1,0:T(8,128)} fusion(f32[4096,2048]{1,0:T(8,128)} %fusion.87, bf16[4096,1024]{1,0:T(8,128)(2,1)} %get-tuple-element.343, bf16[2048,1024]{1,0:T(8,128)(2,1)S(1)} %copy-done.59), kind=kOutput, calls=%fused_computation.65 | convolution fusion | flops 17188257792 | bytes 79691776 | tf_op jit(solution)/shard_map/tf,df->td/dot_general | solution.py:168
  802.1 537.2 %reduce-scatter.9.cloned.1.call-done = f32[512,2048]{1,0:T(8,128)} async-done(((f32[4096,2048]{1,0:T(8,128)}), f32[512,2048]{1,0:T(8,128)}) %reduce-scatter.9.cloned.1.call-update) | async-done | bytes 4194320 | tf_op jit(solution)/shard_map/reduce_scatter | solution.py:166
  1347.9 55.9 %all-gather.13.cloned.1.call-done = bf16[1024,2048]{1,0:T(8,128)(2,1)} async-done(((bf16[512,2048]{1,0:T(8,128)(2,1)}), bf16[1024,2048]{1,0:T(8,128)(2,1)}) %all-gather.13.cloned.1.call-update) | async-done | bytes 4194320 | tf_op jit(solution)/shard_map/all_gather | solution.py:176
  1415.1 56.1 %while.28 = (s32[]{:T(128)}, f32[1024,2,2,256]{0,3,2,1:T(8,128)}, f32[1024,2,2,256]{0,3,2,1:T(8,128)}, f32[2,512,2,2,256]{4,1,0,3,2:T(8,128)}, bf16[2,512,2,2,25...) while((s32[]{:T(128)}, f32[1024,2,2,256]{0,3,2,1:T(8,128)}, ...), condition=%wide.region_12.13_spmd.clone, body=%wide.region_10.12_spmd.clone.sunk | while | flops 5408029696 | bytes 185683760 | solution.py:213
  1491.6 21.6 fusion.73
  1513.2 11.1 fusion.81
  1530.3 11.7 reshape.469
  1542.1 14.3 reduce_sum.116
  1558.1 11.7 reshape.470
  1569.8 14.1 reduce_sum.120
  1594.3 24.3 convolution_convert_fusion.2
  1618.6 24.2 convolution_convert_fusion.1
  1642.9 20.5 convolution_convert_fusion.3
  1694.8 18.9 fusion.70
  1713.8 23.9 convolution_convert_fusion
  1737.8 88.9 %all-reduce.6.cloned.1.call-done = (bf16[2048,1024]{1,0:T(8,128)(2,1)}, bf16[2048,512]{1,0:T(8,128)(2,1)}, bf16[2048,512]{1,0:T(8,128)(2,1)}, bf16[1024,2048]{1,0:T(8,128)(2,1)}) async-done(((bf16[2048,1024]{1,0:T(8,128)(2,1)}, bf16[2048,512]{1,0:T(8,128)(2,1)}, bf16[2048,512]{1,0:T(8,128)(2,1)}, bf16[1024,2048]{1,0:T(8,128)(2,1)}), (bf16[2048,1024]{1,0:T(8,128)(2,1)}, bf16[2048,512]{1,0:T(8,128)(2,1)}, ...) | async-done | bytes 12582928 | tf_op jit(solution)/shard_map/psum | solution.py:257
  1833.8 217.0 %all-reduce.8.cloned.1.call-done = (bf16[2048,1024]{1,0:T(8,128)(2,1)}, bf16[2048,1024]{1,0:T(8,128)(2,1)}, bf16[1024,2048]{1,0:T(8,128)(2,1)}) async-done(((bf16[2048,1024]{1,0:T(8,128)(2,1)}, bf16[2048,1024]{1,0:T(8,128)(2,1)}, bf16[1024,2048]{1,0:T(8,128)(2,1)}), (bf16[2048,1024]{1,0:T(8,128)(2,1)}, bf16[2048,1024]{1,0:T(8,128)(2,1)}, bf16[1024,2048]{1,0:T(8,128)(2,1)})) %all-reduce.8.cloned.1.call-update) | async-done | bytes 12582928 | tf_op jit(solution)/shard_map/psum | solution.py:280
  2075.5 32.8 %reduce-scatter.11.cloned.1.call-done = bf16[512,2048]{1,0:T(8,128)(2,1)} async-done(((bf16[1024,2048]{1,0:T(8,128)(2,1)}), bf16[512,2048]{1,0:T(8,128)(2,1)}) %reduce-scatter.11.cloned.1.call-update) | async-done | bytes 2097168 | tf_op jit(solution)/shard_map/reduce_scatter | solution.py:237
  2111.6 65.9 %all-reduce = (bf16[1,2048]{1,0:T(2,128)(2,1)S(1)}, bf16[1,2048]{1,0:T(2,128)(2,1)S(1)}) all-reduce(bf16[1,2048]{1,0:T(2,128)(2,1)S(1)} %reshape.466, bf16[1,2048]{1,0:T(2,128)(2,1)S(1)} %reshape.471), channel_id=1, replica_groups=mesh['grp'=4,'row'=4,'col'=2] {'grp','row'}, use_global_device_ids=true, to_apply=%region_16.17 | all-reduce | flops 4096 | bytes 16384 | tf_op jit(solution)/shard_map/psum | solution.py:261
  2189.8 204.7 %reduce-scatter.7.cloned.1.call-done = bf16[512,2048]{1,0:T(8,128)(2,1)} async-done(((bf16[4096,2048]{1,0:T(8,128)(2,1)}), bf16[512,2048]{1,0:T(8,128)(2,1)}) %reduce-scatter.7.cloned.1.call-update) | async-done | bytes 2097168 | tf_op jit(solution)/shard_map/reduce_scatter | solution.py:145
  2403.1 96.6 %all-gather.15.cloned.1.call-done = f32[2048,1024]{1,0:T(8,128)} async-done(((f32[2048,512]{1,0:T(8,128)}), f32[2048,1024]{1,0:T(8,128)}) %all-gather.15.cloned.1.call-update) | async-done | bytes 8388624 | tf_op jit(solution)/shard_map/all_gather | solution.py:265
  2499.7 106.0 %all-gather.17.cloned.1.call-done = f32[2048,1024]{1,0:T(8,128)} async-done(((f32[2048,512]{1,0:T(8,128)}), f32[2048,1024]{1,0:T(8,128)}) %all-gather.17.cloned.1.call-update) | async-done | bytes 8388624 | tf_op jit(solution)/shard_map/all_gather | solution.py:266
  (286 shorter events, 296.1 us)
Async XLA Ops:
  7.2 66.4 %all-gather.7.cloned.1.call-start = ((), (), s32[]{:S(2)}) async-start(), calls=%async_computation.4 | async-start | bytes 6291456 | tf_op jit(solution)/shard_map/all_gather | solution.py:78
  14.0 233.5 %reduce-scatter.5.cloned.1.call-start = ((), (), s32[]{:S(2)}) async-start(), calls=%async_computation.5 | async-start | bytes 12582912 | tf_op jit(solution)/shard_map/reduce_scatter | solution.py:130
  17.1 90.9 %copy-start.15 = (f32[1024,128]{1,0:T(8,128)}, f32[1024,128]{1,0:T(8,128)S(1)}, u32[]{:S(2)}) copy-start(f32[1024,128]{1,0:T(8,128)S(1)} %get-tuple-element.366) | copy-start | bytes 1572868
  21.1 52.5 %copy-start.13 = (bf16[2048,512]{1,0:T(8,128)(2,1)}, bf16[2048,512]{1,0:T(8,128)(2,1)S(1)}, u32[]{:S(2)}) copy-start(bf16[2048,512]{1,0:T(8,128)(2,1)S(1)} %get-tuple-element.367) | copy-start | bytes 6291460
  148.0 99.5 %copy-start.5 = (bf16[512,2048]{1,0:T(8,128)(2,1)S(1)}, bf16[512,2048]{1,0:T(8,128)(2,1)}, u32[]{:S(2)}) copy-start(bf16[512,2048]{1,0:T(8,128)(2,1)} %param.17) | copy-start | bytes 6291460
  148.0 104.3 %copy-start.39 = (f32[2048]{0:T(1024)S(1)}, f32[2048]{0:T(1024)}, u32[]{:S(2)}) copy-start(f32[2048]{0:T(1024)} %param.26) | copy-start | bytes 24580
  148.0 333.5 %all-gather.9.cloned.1.call-start = ((), (), s32[]{:S(2)}) async-start(), calls=%async_computation.6 | async-start | bytes 18874368 | tf_op jit(solution)/shard_map/all_gather | solution.py:139
  254.1 454.9 %all-gather.11.cloned.1.call-start = ((), (), s32[]{:S(2)}) async-start(), calls=%async_computation.8 | async-start | bytes 18874368 | tf_op jit(solution)/shard_map/all_gather | solution.py:152
  254.7 1084.6 %reduce-scatter.9.cloned.1.call-start = ((), (), s32[]{:S(2)}) async-start(), calls=%async_computation.9 | async-start | bytes 37748736 | tf_op jit(solution)/shard_map/reduce_scatter | solution.py:166
  481.5 24.7 copy-start.58
  745.2 25.4 copy-start.59
  802.0 537.3 %copy-start.40 = (f32[2048]{0:T(1024)S(1)}, f32[2048]{0:T(1024)}, u32[]{:S(2)}) copy-start(f32[2048]{0:T(1024)} %param.26) | copy-start | bytes 24580
  802.0 537.3 %copy-start.46 = (f32[512]{0:T(512)S(1)}, f32[512]{0:T(512)}, u32[]{:S(2)}) copy-start(f32[512]{0:T(512)} %copy-done.45) | copy-start | bytes 6148
  802.0 543.1 %copy-start.11 = (bf16[512,2048]{1,0:T(8,128)(2,1)S(1)}, bf16[512,2048]{1,0:T(8,128)(2,1)}, u32[]{:S(2)}) copy-start(bf16[512,2048]{1,0:T(8,128)(2,1)} %param.18) | copy-start | bytes 6291460
  802.1 542.5 %copy-start.55 = (f32[512]{0:T(512)S(1)}, f32[512]{0:T(512)}, u32[]{:S(2)}) copy-start(f32[512]{0:T(512)} %copy-done.54) | copy-start | bytes 6148
  802.1 601.7 %all-gather.13.cloned.1.call-start = ((), (), s32[]{:S(2)}) async-start(), calls=%async_computation.10 | async-start | bytes 6291456 | tf_op jit(solution)/shard_map/all_gather | solution.py:176
  1347.8 478.9 %all-reduce.6.cloned.1.call-start = ((), (), s32[]{:S(2)}) async-start(), calls=%async_computation.14 | async-start | bytes 25165824 | tf_op jit(solution)/shard_map/psum | solution.py:257
  1594.2 456.6 %all-reduce.8.cloned.1.call-start = ((), (), s32[]{:S(2)}) async-start(), calls=%async_computation.15 | async-start | bytes 25165824 | tf_op jit(solution)/shard_map/psum | solution.py:280
  1594.3 48.6 %slice-start = ((s8[16777216]{0:T(1024)(128)(4,1)}), s8[4194304]{0:T(1024)(128)(4,1)S(1)}, s32[]{:S(2)}) async-start(s8[16777216]{0:T(1024)(128)(4,1)} %bitcast.226), calls=%async_computation.16 | async-start | bytes 8388608
  1594.3 48.5 %slice-start.1 = ((s8[16777216]{0:T(1024)(128)(4,1)}), s8[4194304]{0:T(1024)(128)(4,1)S(1)}, s32[]{:S(2)}) async-start(s8[16777216]{0:T(1024)(128)(4,1)} %bitcast.226), calls=%async_computation.17 | async-start | bytes 8388608
  1594.3 48.5 %slice-start.4 = ((s8[8388608]{0:T(1024)(128)(4,1)}), s8[4194304]{0:T(1024)(128)(4,1)S(1)}, s32[]{:S(2)}) async-start(s8[8388608]{0:T(1024)(128)(4,1)} %bitcast.228), calls=%async_computation.20 | async-start | bytes 8388608
  1663.4 444.9 %reduce-scatter.11.cloned.1.call-start = ((), (), s32[]{:S(2)}) async-start(), calls=%async_computation.11 | async-start | bytes 6291456 | tf_op jit(solution)/shard_map/reduce_scatter | solution.py:237
  1713.7 680.7 %reduce-scatter.7.cloned.1.call-start = ((), (), s32[]{:S(2)}) async-start(), calls=%async_computation.7 | async-start | bytes 18874368 | tf_op jit(solution)/shard_map/reduce_scatter | solution.py:145
  1737.7 761.9 %all-gather.15.cloned.1.call-start = ((), (), s32[]{:S(2)}) async-start(), calls=%async_computation.12 | async-start | bytes 12582912 | tf_op jit(solution)/shard_map/all_gather | solution.py:265
  1831.1 774.6 %all-gather.17.cloned.1.call-start = ((), (), s32[]{:S(2)}) async-start(), calls=%async_computation.13 | async-start | bytes 12582912 | tf_op jit(solution)/shard_map/all_gather | solution.py:266
  2071.1 37.2 %copy-start.6 = (bf16[512,2048]{1,0:T(8,128)(2,1)S(1)}, bf16[512,2048]{1,0:T(8,128)(2,1)}, u32[]{:S(2)}) copy-start(bf16[512,2048]{1,0:T(8,128)(2,1)} %param.17) | copy-start | bytes 6291460
  2071.1 37.2 %copy-start.44 = (f32[2048]{0:T(1024)S(1)}, f32[2048]{0:T(1024)}, u32[]{:S(2)}) copy-start(f32[2048]{0:T(1024)} %param.21) | copy-start | bytes 24580
  2071.1 37.2 %copy-start.49 = (f32[512]{0:T(512)S(1)}, f32[512]{0:T(512)}, u32[]{:S(2)}) copy-start(f32[512]{0:T(512)} %copy-done.48) | copy-start | bytes 6148
  2075.5 114.2 %copy-start.53 = (f32[512]{0:T(512)S(1)}, f32[512]{0:T(512)}, u32[]{:S(2)}) copy-start(f32[512]{0:T(512)} %copy-done.52) | copy-start | bytes 6148
  2075.5 318.9 %copy-start.41 = (f32[2048]{0:T(1024)S(1)}, f32[2048]{0:T(1024)}, u32[]{:S(2)}) copy-start(f32[2048]{0:T(1024)} %param.26) | copy-start | bytes 24580
  2075.5 318.9 %copy-start.47 = (f32[512]{0:T(512)S(1)}, f32[512]{0:T(512)}, u32[]{:S(2)}) copy-start(f32[512]{0:T(512)} %copy-done.45) | copy-start | bytes 6148
  2075.5 318.9 %copy-start.51 = (f32[512]{0:T(512)S(1)}, f32[512]{0:T(512)}, u32[]{:S(2)}) copy-start(f32[512]{0:T(512)} %copy-done.50) | copy-start | bytes 6148
  (52 other events, 321.5 us)
Sparse Core Ops, SparseCore 0:
  14.1 59.4 all-gather.6
  148.1 99.3 reduce-scatter.4
  254.2 227.2 all-gather.8
  483.5 225.4 all-gather.10
  802.2 537.0 reduce-scatter.8
  1347.9 55.8 all-gather.12
  1594.4 232.3 all-reduce.5
  1830.0 220.7 all-reduce.7
  2053.7 54.5 reduce-scatter.10
  2111.9 282.4 reduce-scatter.6
  2396.6 103.0 all-gather.14
  2501.6 103.9 all-gather.16
where the time goes:
time: 2630 us; the launch traced here: 2620 us
  waiting for transfers between devices  1900 us (72%)
  matrix products  369 us (14%)
  local copies, waits for them, and re-layouts  143 us (5%)
  other arithmetic  122 us (5%)
  blocking collectives  74.9 us (3%)
    reduce_scatter x1, waiting for transfers between devices, per_device(): lax.psum_scatter(jnp.einsum('tf,df->td', gate_grad_low, gate_weight, pref...  537 us
    all_gather x1, waiting for transfers between devices, per_device(): gathered_mid = lax.all_gather(mid_low, ('row', 'col'), axis=0, tiled=True)  227 us
    psum x1, waiting for transfers between devices, per_device(): lax.psum(gate_wgrad.astype(jnp.bfloat16), 'grp').astype(jnp.float32)  217 us
    reduce_scatter x1, waiting for transfers between devices, per_device(): lax.psum_scatter(jnp.dot(rows_now, down_weight, preferred_element_type=jn...  205 us
    all_gather x1, waiting for transfers between devices, per_device(): shard_rows = lax.all_gather(cotangent, ('row', 'col'), axis=0, tiled=True)  182 us
    all_gather x1, waiting for transfers between devices, per_device(): lax.all_gather(value_part, 'col', axis=1, tiled=True)  106 us
    reduce_scatter x1, waiting for transfers between devices, per_device(): lax.psum_scatter(jnp.dot(rows_now, output_weight, preferred_element_type=...  99.4 us
    all_gather x1, waiting for transfers between devices, per_device(): lax.all_gather(key_part, 'col', axis=1, tiled=True)  96.6 us
  transfers between devices with their start and end apart: 12, of which 12 were waited for; matrix products, arithmetic and copies ran while one was open for 9% of the time, Pallas kernels for 0%

commit v1 on v0

v1 whole, which is shorter than its diff:
```python
import math

import jax
import jax.numpy as jnp
from jax import lax
from jax.sharding import PartitionSpec as P

QUERY_HEADS = 8
KEY_VALUE_HEADS = 4
HEAD_SIZE = 256
QBLOCK = 512


NORM_EPSILON = 1e-06
ROPE_BASE = 1000042.0
MASKED_SCORE = -1e30


def normalize(values, gain):
    inverse = lax.rsqrt(jnp.mean(values * values, axis=-1, keepdims=True) + NORM_EPSILON)
    return values * inverse * gain


def rope_tables(positions, head_dim):
    half_dim = head_dim // 2
    exponent = jnp.arange(half_dim, dtype=jnp.float32) * (2.0 / head_dim)
    inverse_freq = jnp.exp(-math.log(ROPE_BASE) * exponent)
    angles = positions.astype(jnp.float32)[:, None] * inverse_freq[None, :]
    return (jnp.cos(angles), jnp.sin(angles))


def rotate(values, cosine, sine):
    half_dim = values.shape[-1] // 2
    shape = (values.shape[0],) + (1,) * (values.ndim - 2) + (half_dim,)
    cosine = cosine.reshape(shape)
    sine = sine.reshape(shape)
    first_half = values[..., :half_dim]
    second_half = values[..., half_dim:]
    return jnp.concatenate(
        [first_half * cosine - second_half * sine, second_half * cosine + first_half * sine],
        axis=-1,
    )


def swap(value, axis, bit):
    count = lax.axis_size(axis)
    return lax.ppermute(value, axis, [(i, i ^ bit) for i in range(count)])


def shift(value, axis, step):
    count = lax.axis_size(axis)
    return lax.ppermute(value, axis, [(i, (i + step) % count) for i in range(count)])


def after(value, *others):
    return lax.optimization_barrier((value, *others))[0]


def ordered(first_when_zero, mine, theirs, dim):
    keep = first_when_zero == 0
    return jnp.concatenate(
        [jnp.where(keep, mine, theirs), jnp.where(keep, theirs, mine)], axis=dim
    )


def dot32(left, right):
    return jnp.dot(left, right, preferred_element_type=jnp.float32)


def dot_nt(left, right):
    return jnp.einsum("td,fd->tf", left, right, preferred_element_type=jnp.float32)


def dot_tn(left, right):
    return jnp.einsum("td,tf->df", left, right, preferred_element_type=jnp.float32)


def low(value):
    return value.astype(jnp.bfloat16)


def wide(value):
    return value.astype(jnp.float32)


def col_gather(mine):
    if lax.axis_size("col") == 2:
        return [mine, swap(mine, "col", 1)]
    return [lax.all_gather(mine, "col", axis=0, tiled=True)]


def col_scatter(product):
    if lax.axis_size("col") == 2:
        theirs = swap(low(product(1)), "col", 1)
        return product(0) + wide(theirs)
    return wide(lax.psum_scatter(low(product(0)), "col", scatter_dimension=0, tiled=True))


def butterfly(value, axes):
    for axis in axes:
        bit = 1
        while bit < lax.axis_size(axis):
            value = value + swap(value, axis, bit)
            bit *= 2
    return value


def half_rows(value, bit):
    size = value.shape[0] // 2
    return lax.dynamic_slice_in_dim(value, bit * size, size, 0)


def sum_copies(value, core, ypos, zpos):
    part = low(wide(half_rows(value, core)) + wide(swap(half_rows(value, 1 - core), "grp", 1)))
    part = low(wide(half_rows(part, ypos)) + wide(swap(half_rows(part, 1 - ypos), "grp", 2)))
    count = lax.axis_size("row")
    size = part.shape[0] // count

    def block(i):
        return lax.dynamic_slice_in_dim(part, lax.rem(zpos + i, count) * size, size, 0)

    total = wide(block(0))
    for k in range(1, count):
        total = total + wide(shift(block(k), "row", k))
    mine = low(total)
    part = jnp.zeros_like(part)
    for k in range(count):
        piece = mine if k == 0 else shift(mine, "row", k)
        part = lax.dynamic_update_slice_in_dim(
            part, piece, lax.rem(zpos - k + count, count) * size, 0
        )
    part = ordered(ypos, part, swap(part, "grp", 2), 0)
    return ordered(core, part, swap(part, "grp", 1), 0)


def pieces_of(weight, dim, core, ypos):
    size = weight.shape[dim] // 4
    mine = lax.dynamic_slice_in_dim(weight, (2 * core + ypos) * size, size, dim)
    other = lax.dynamic_slice_in_dim(weight, (2 * core + 1 - ypos) * size, size, dim)
    return mine, other


def gather_weight(weight, dim, core, ypos):
    mine, other = pieces_of(weight, dim, core, ypos)
    mines, others = [mine], [other]
    for _ in range(lax.axis_size("row") - 1):
        mines.append(shift(mines[-1], "row", 1))
        others.append(swap(mines[-1], "grp", 2))
    return jnp.concatenate(mines + others, axis=dim)


def blocks_of(value, dim, count):
    size = value.shape[dim] // count
    return [lax.slice_in_dim(value, i * size, (i + 1) * size, axis=dim) for i in range(count)]


def ring_sum(blocks):
    total = blocks[-1]
    for block in blocks[-2::-1]:
        total = low(wide(shift(total, "row", -1)) + wide(block))
    return total


def place(mine, other, dim, core, ypos):
    half = ordered(ypos, mine, other, dim)
    return wide(ordered(core, half, swap(half, "grp", 1), dim))


def sum_y_first(grad, dim, core, ypos):
    keep, give = blocks_of(grad, dim, 2)
    part = low(wide(keep) + wide(swap(give, "grp", 2)))
    mine = ring_sum(blocks_of(part, dim, lax.axis_size("row")))
    return place(mine, swap(mine, "grp", 2), dim, core, ypos)


def sum_z_first(grad, dim, core, ypos):
    keep, give = blocks_of(grad, dim, 2)
    count = lax.axis_size("row")
    mine = ring_sum(blocks_of(keep, dim, count))
    other = ring_sum(blocks_of(give, dim, count))
    mine, other = (
        low(wide(mine) + wide(swap(other, "grp", 2))),
        low(wide(other) + wide(swap(mine, "grp", 2))),
    )
    return place(mine, other, dim, core, ypos)


def per_device(
    tokens,
    cotangent,
    segments,
    positions,
    first_gain,
    query_weight,
    key_matrix,
    value_matrix,
    output_weight,
    second_gain,
    gate_weight,
    up_weight,
    down_weight,
):
    head_dim = HEAD_SIZE
    query_heads = query_weight.shape[1] // head_dim
    heads_per_group = QUERY_HEADS // KEY_VALUE_HEADS
    key_heads = max(1, query_heads // heads_per_group)
    head_share = query_heads // key_heads
    head_sharing = max(1, heads_per_group // query_heads)
    col = lax.axis_index("col")
    key_first = col * query_heads // heads_per_group
    query_cols = query_heads * head_dim
    key_cols = key_heads * head_dim
    rows, width = tokens.shape
    grp, zpos = lax.axis_index("grp"), lax.axis_index("row")
    core, ypos = lax.rem(grp, 2), lax.div(grp, 2)
    in_pairs = lax.axis_size("col") == 2

    inputs = wide(tokens)
    normalized_input, first_back = jax.vjp(normalize, inputs, first_gain)
    gathered_in = jnp.concatenate(col_gather(low(normalized_input)), axis=0)
    packed_length = gathered_in.shape[0]
    if in_pairs:
        segments = ordered(col, *blocks_of(segments, 0, 2), 0)
        positions = ordered(col, *blocks_of(positions, 0, 2), 0)

    down_all = gather_weight(down_weight, 0, core, ypos)
    gate_all = gather_weight(gate_weight, 1, core, ypos)
    up_all = gather_weight(up_weight, 1, core, ypos)

    cot_now = after(cotangent, gathered_in)
    cot_pack = jnp.concatenate(col_gather(cot_now), axis=0)
    cot_all = jnp.concatenate([cot_pack, swap(cot_pack, "grp", 1)], axis=0)

    key_slice = lax.dynamic_slice_in_dim(key_matrix, key_first * head_dim, key_cols, 1)
    value_slice = lax.dynamic_slice_in_dim(value_matrix, key_first * head_dim, key_cols, 1)
    project_in = jnp.concatenate([query_weight, key_slice, value_slice], axis=1)
    projected = dot32(gathered_in, project_in)
    cosine, sine = rope_tables(positions, head_dim)
    query_low = low(
        rotate(
            projected[:, :query_cols].reshape(packed_length, key_heads, head_share, head_dim),
            cosine,
            sine,
        )
    )
    key_low = low(
        rotate(
            projected[:, query_cols : query_cols + key_cols].reshape(
                packed_length, key_heads, head_dim
            ),
            cosine,
            sine,
        )
    )
    value_reduced = low(
        projected[:, query_cols + key_cols :].reshape(packed_length, key_heads, head_dim)
    )
    block_count = packed_length // QBLOCK
    query_blocks = query_low.reshape(block_count, QBLOCK, key_heads, head_share, head_dim)
    seg_blocks = segments.reshape(block_count, QBLOCK)
    pos_blocks = positions.reshape(block_count, QBLOCK)
    score_scale = head_dim ** (-0.5)

    def block_scores(query_block, seg_block, pos_block):
        raw = (
            jnp.einsum("qgrd,kgd->grqk", query_block, key_low, preferred_element_type=jnp.float32)
            * score_scale
        )
        allowed = (positions[None, :] <= pos_block[:, None]) & (
            (segments[None, :] == 0) | (segments[None, :] == seg_block[:, None])
        )
        return jnp.where(allowed[None, None, :, :], raw, MASKED_SCORE)

    def attend(block):
        query_block, seg_block, pos_block = block
        scores = block_scores(query_block, seg_block, pos_block)
        peak = jnp.max(scores, axis=-1, keepdims=True)
        log_total = peak + jnp.log(jnp.sum(jnp.exp(scores - peak), axis=-1, keepdims=True))
        probs_low = jnp.exp(scores - log_total).astype(jnp.bfloat16)
        mixed = jnp.einsum(
            "grqk,kgd->qgrd", probs_low, value_reduced, preferred_element_type=jnp.float32
        )
        return (mixed, log_total[..., 0])

    mixed_all, log_totals = lax.map(attend, (query_blocks, seg_blocks, pos_blocks))
    attn_low = low(mixed_all.reshape(packed_length, query_cols))
    attn_parts = blocks_of(attn_low, 0, 2) if in_pairs else [attn_low]
    hidden_res = inputs + col_scatter(lambda i: dot32(attn_parts[i], output_weight))
    normed_mid, second_back = jax.vjp(normalize, hidden_res, second_gain)

    mid_pack = jnp.concatenate(col_gather(low(normed_mid)), axis=0)
    mid_all = jnp.concatenate([mid_pack, swap(mid_pack, "grp", 1)], axis=0)
    act_grad = low(dot_nt(cot_all, down_all))
    gate_lin = low(dot32(mid_all, gate_all))
    up_lin = dot32(mid_all, up_all)
    gate32 = wide(gate_lin)
    sig = jax.nn.sigmoid(gate32)
    act_low = low(gate32 * sig * up_lin)
    gate_grad_low = low(wide(act_grad) * up_lin * sig * (1 + gate32 * (1 - sig)))
    up_grad_low = low(wide(act_grad) * gate32 * sig)
    down_wgrad = low(dot_tn(act_low, cot_all))
    down_grad = sum_z_first(down_wgrad, 0, core, ypos)
    gate_wgrad = low(dot_tn(mid_all, gate_grad_low))
    gate_grad = sum_y_first(gate_wgrad, 1, core, ypos)
    up_wgrad = low(dot_tn(mid_all, up_grad_low))
    up_grad = sum_y_first(up_wgrad, 1, core, ypos)

    def pack_sum(value):
        mine, theirs = blocks_of(value, 0, 2)
        return wide(mine) + wide(swap(low(theirs), "grp", 1))

    mid_part = pack_sum(dot_nt(gate_grad_low, gate_all) + dot_nt(up_grad_low, up_all))
    mid_parts = blocks_of(mid_part, 0, 2) if in_pairs else [mid_part]
    mid_grad = col_scatter(lambda i: mid_parts[i])
    out_part = pack_sum(dot32(act_low, down_all))
    out_parts = blocks_of(out_part, 0, 2) if in_pairs else [out_part]
    layer_out = hidden_res + col_scatter(lambda i: out_parts[i])

    res_from_mid, second_gain_part = second_back(mid_grad)
    res_grad = wide(cotangent) + res_from_mid
    shard_rows = jnp.concatenate(col_gather(low(res_grad)), axis=0)
    out_wgrad = sum_copies(low(dot_tn(attn_low, shard_rows)), core, ypos, zpos)
    mixed_low = low(dot_nt(shard_rows, output_weight)).reshape(
        block_count, QBLOCK, key_heads, head_share, head_dim
    )

    def attend_back(totals, block):
        query_block, seg_block, pos_block, mixed_block, log_block = block
        scores = block_scores(query_block, seg_block, pos_block)
        probs = jnp.exp(scores - log_block[..., None])
        probs_low = probs.astype(jnp.bfloat16)
        value_total = totals[1] + jnp.einsum(
            "grqk,qgrd->kgd", probs_low, mixed_block, preferred_element_type=jnp.float32
        )
        prob_grad = jnp.einsum(
            "qgrd,kgd->grqk", mixed_block, value_reduced, preferred_element_type=jnp.float32
        )
        row_dot = jnp.sum(probs * prob_grad, axis=-1, keepdims=True)
        score_low = (probs * (prob_grad - row_dot)).astype(jnp.bfloat16)
        query_grad_rows = (
            jnp.einsum("grqk,kgd->qgrd", score_low, key_low, preferred_element_type=jnp.float32)
            * score_scale
        )
        key_total = (
            totals[0]
            + jnp.einsum(
                "grqk,qgrd->kgd", score_low, query_block, preferred_element_type=jnp.float32
            )
            * score_scale
        )
        return ((key_total, value_total), query_grad_rows)

    zero_heads = jnp.zeros((packed_length, key_heads, head_dim), jnp.float32)
    (key_grad_rot, value_head_grad), query_grad_blocks = lax.scan(
        attend_back,
        (zero_heads, zero_heads),
        (query_blocks, seg_blocks, pos_blocks, mixed_low, log_totals),
    )
    query_grad_rot = query_grad_blocks.reshape(packed_length, key_heads, head_share, head_dim)
    query_back = low(rotate(query_grad_rot, cosine, -sine)).reshape(packed_length, query_cols)
    key_back = low(rotate(key_grad_rot, cosine, -sine)).reshape(packed_length, key_cols)
    value_back = low(value_head_grad).reshape(packed_length, key_cols)
    back_all = jnp.concatenate([query_back, key_back, value_back], axis=1)
    proj_grad = sum_copies(low(dot_tn(gathered_in, back_all)), core, ypos, zpos)
    back_parts = blocks_of(back_all, 0, 2) if in_pairs else [back_all]
    in_grad = col_scatter(lambda i: dot_nt(back_parts[i], project_in))
    res_from_in, first_gain_part = first_back(in_grad)
    input_grad = res_grad + res_from_in

    query_wgrad = wide(proj_grad[:, :query_cols])
    pair_part = proj_grad[:, query_cols:]
    if in_pairs:
        theirs = swap(pair_part, "col", 1)
        key_full = wide(ordered(col, pair_part[:, :key_cols], theirs[:, :key_cols], 1))
        value_full = wide(ordered(col, pair_part[:, key_cols:], theirs[:, key_cols:], 1))
    else:
        pair_all = wide(lax.all_gather(pair_part, "col", axis=0))
        groups = lax.axis_size("col") // head_sharing

        def spread(piece):
            piece = jnp.sum(piece.reshape(groups, head_sharing, width, key_cols), axis=1)
            return jnp.swapaxes(piece, 0, 1).reshape(width, groups * key_cols)

        key_full = spread(pair_all[..., :key_cols])
        value_full = spread(pair_all[..., key_cols:])
    axes = ("grp", "row", "col")
    first_gain_grad = butterfly(first_gain_part.reshape(8, -1), axes).reshape(-1)
    second_gain_grad = butterfly(second_gain_part.reshape(8, -1), axes).reshape(-1)
    return (
        layer_out,
        input_grad,
        first_gain_grad,
        query_wgrad,
        key_full,
        value_full,
        wide(out_wgrad),
        second_gain_grad,
        gate_grad,
        up_grad,
        down_grad,
    )


def solution(mesh):
    return jax.shard_map(
        per_device,
        mesh=mesh,
        in_specs=(
            P(("grp", "row", "col"), None),
            P(("grp", "row", "col"), None),
            P(("grp", "row")),
            P(("grp", "row")),
            P(),
            P(None, "col"),
            P(),
            P(),
            P("col", None),
            P(),
            P(None, ("row", "col")),
            P(None, ("row", "col")),
            P(("row", "col"), None),
        ),
        out_specs=(
            P(("grp", "row", "col"), None),
            P(("grp", "row", "col"), None),
            P(),
            P(None, "col"),
            P(),
            P(),
            P("col", None),
            P(),
            P(None, ("row", "col")),
            P(None, ("row", "col")),
            P(("row", "col"), None),
        ),
        check_vma=False,
    )
```

time: 2630 us -> 1390 us (0.53)
  waiting for transfers between devices: 1900 us -> 558 us
  starting transfers between devices: 0.5 us -> 107 us
  blocking collectives: 74.9 us -> 0 us
  other arithmetic: 122 us -> 185 us
  local copies, waits for them, and re-layouts: 143 us -> 184 us
    reduce_scatter x4 -> x0, waiting for transfers between devices: 874 us -> none  [the longest x1 537 us: per_device(): lax.psum_scatter(jnp.einsum('tf,df->td', gate_grad_low, gate_weight, pref...]
    all_gather x6 -> x0, waiting for transfers between devices: 720 us -> none  [the longest x1 227 us: per_device(): gathered_mid = lax.all_gather(mid_low, ('row', 'col'), axis=0, tiled=True)]
    ppermute x0 -> x82, waiting for transfers between devices: none -> 558 us  [the longest x49 287 us: swap(): return lax.ppermute(value, axis, [(i, i ^ bit) for i in range(count)])]
    psum x2 -> x0, waiting for transfers between devices: 306 us -> none  [the longest x1 217 us: per_device(): lax.psum(gate_wgrad.astype(jnp.bfloat16), 'grp').astype(jnp.float32)]
    ppermute x0 -> x82, starting transfers between devices: none -> 107 us  [the longest x33 62.6 us: shift(): lax.ppermute(value, axis, [(i, (i + step) % count) for i in range(count)])]
    psum x1 -> x0, blocking collectives: 65.9 us -> none  [per_device(): lax.psum(first_gain_part.astype(jnp.bfloat16), ('grp', 'row'))]
    unnamed x124 -> x181, local copies, waits for them, and re-layouts: 22.2 us -> 84 us
    convert_element_type x11 -> x25, other arithmetic: 41.9 us -> 80.4 us  [the longest x19 53.3 us: low(): return value.astype(jnp.bfloat16)]
  transfers between devices with their start and end apart: 12 -> 82, of which waited for: 12 -> 35; matrix products, arithmetic and copies ran while one was open for 9% -> 40% of each run, Pallas kernels for 0% -> 0%
where the time goes in v1:
time: 1390 us
  waiting for transfers between devices  558 us (40%)
  matrix products  348 us (25%)
  other arithmetic  185 us (13%)
  local copies, waits for them, and re-layouts  184 us (13%)
  starting transfers between devices  107 us (8%)
    ppermute x49, waiting for transfers between devices, swap(): return lax.ppermute(value, axis, [(i, i ^ bit) for i in range(count)])  287 us
    ppermute x33, waiting for transfers between devices, shift(): lax.ppermute(value, axis, [(i, (i + step) % count) for i in range(count)])  271 us
    dot_general x6, matrix products, dot_nt(): jnp.einsum('td,fd->tf', left, right, preferred_element_type=jnp.float32)  100 us
    dot_general x6, matrix products, dot32(): return jnp.dot(left, right, preferred_element_type=jnp.float32)  95.7 us
    dot_general x5, matrix products, dot_tn(): jnp.einsum('td,tf->df', left, right, preferred_element_type=jnp.float32)  95.2 us
    unnamed x181, local copies, waits for them, and re-layouts  84 us
    ppermute x33, starting transfers between devices, shift(): lax.ppermute(value, axis, [(i, (i + step) % count) for i in range(count)])  62.6 us
    convert_element_type x19, other arithmetic, low(): return value.astype(jnp.bfloat16)  53.3 us
  transfers between devices with their start and end apart: 82, of which 35 were waited for; matrix products, arithmetic and copies ran while one was open for 40% of the time, Pallas kernels for 0%

profile of v1, /device:TPU:0, one launch (start us, length us, event | category | flops | bytes accessed | tf_op | source)
XLA Modules:
  0.0 1385.7 jit_solution(1240699055047405822)
XLA Ops:
  43.5 20.2 %collective-permute-done.4 = bf16[2048,256]{1,0:T(8,128)(2,1)} collective-permute-done((bf16[2048,256]{1,0:T(8,128)(2,1)S(1)}, bf16[2048,256]{1,0:T(8,128)(2,1)}, u32[]{:S(2)}, u32[]{:S(2)}) %collective-permute-start.4) | collective-permute-done | bytes 1048608 | tf_op jit(solution)/shard_map/ppermute | solution.py:52
  67.4 18.7 %collective-permute-done.16 = bf16[256,2048]{1,0:T(8,128)(2,1)} collective-permute-done((bf16[256,2048]{1,0:T(8,128)(2,1)}, bf16[256,2048]{1,0:T(8,128)(2,1)}, u32[]{:S(2)}, u32[]{:S(2)}) %collective-permute-start.16) | collective-permute-done | bytes 1048608 | tf_op jit(solution)/shard_map/ppermute | solution.py:52
  128.4 26.1 %while.27 = (s32[]{:T(128)}, bf16[2,512,2,2,256]{1,4,3,2,0:T(8,128)(2,1)}, f32[2,2,2,512]{3,2,1,0:T(2,128)S(1)}, s32[1024]{0:T(1024)S(1)}, s32[2,512]{1,0:T(2,12...) while((s32[]{:T(128)}, ...), condition=%wide.region_4.5_spmd, body=%wide.region_1.4_spmd.sunk | while | flops 2172648448 | bytes 35743876 | solution.py:285
  194.8 14.7 %collective-permute-done.6 = bf16[2048,256]{1,0:T(8,128)(2,1)S(1)} collective-permute-done((bf16[2048,256]{1,0:T(8,128)(2,1)}, bf16[2048,256]{1,0:T(8,128)(2,1)S(1)}, u32[]{:S(2)}, u32[]{:S(2)}) %collective-permute-start.6) | collective-permute-done | bytes 1048608 | tf_op jit(solution)/shard_map/ppermute | solution.py:52
  219.1 17.9 %collective-permute-done.18 = bf16[256,2048]{1,0:T(8,128)(2,1)S(1)} collective-permute-done((bf16[256,2048]{1,0:T(8,128)(2,1)}, bf16[256,2048]{1,0:T(8,128)(2,1)S(1)}, u32[]{:S(2)}, u32[]{:S(2)}) %collective-permute-start.18) | collective-permute-done | bytes 1048608 | tf_op jit(solution)/shard_map/ppermute | solution.py:52
  262.8 17.8 %collective-permute-done.19 = bf16[256,2048]{1,0:T(8,128)(2,1)S(1)} collective-permute-done((bf16[256,2048]{1,0:T(8,128)(2,1)}, bf16[256,2048]{1,0:T(8,128)(2,1)S(1)}, u32[]{:S(2)}, u32[]{:S(2)}) %collective-permute-start.19) | collective-permute-done | bytes 1048608 | tf_op jit(solution)/shard_map/ppermute | solution.py:47
  283.2 19.9 %collective-permute-done.20 = bf16[256,2048]{1,0:T(8,128)(2,1)S(1)} collective-permute-done((bf16[256,2048]{1,0:T(8,128)(2,1)}, bf16[256,2048]{1,0:T(8,128)(2,1)S(1)}, u32[]{:S(2)}, u32[]{:S(2)}) %collective-permute-start.20) | collective-permute-done | bytes 1048608 | tf_op jit(solution)/shard_map/ppermute | solution.py:47
  305.7 19.9 %collective-permute-done.15 = bf16[2048,256]{1,0:T(8,128)(2,1)S(1)} collective-permute-done((bf16[2048,256]{1,0:T(8,128)(2,1)S(1)}, bf16[2048,256]{1,0:T(8,128)(2,1)S(1)}, u32[]{:S(2)}, u32[]{:S(2)}) %collective-permute-start.15) | collective-permute-done | bytes 1048608 | tf_op jit(solution)/shard_map/ppermute | solution.py:47
  327.2 20.8 %collective-permute-done.9 = bf16[2048,256]{1,0:T(8,128)(2,1)S(1)} collective-permute-done((bf16[2048,256]{1,0:T(8,128)(2,1)S(1)}, bf16[2048,256]{1,0:T(8,128)(2,1)S(1)}, u32[]{:S(2)}, u32[]{:S(2)}) %collective-permute-start.9) | collective-permute-done | bytes 1048608 | tf_op jit(solution)/shard_map/ppermute | solution.py:47
  349.1 16.1 %collective-permute-done.21 = bf16[256,2048]{1,0:T(8,128)(2,1)S(1)} collective-permute-done((bf16[256,2048]{1,0:T(8,128)(2,1)S(1)}, bf16[256,2048]{1,0:T(8,128)(2,1)S(1)}, u32[]{:S(2)}, u32[]{:S(2)}) %collective-permute-start.21) | collective-permute-done | bytes 1048608 | tf_op jit(solution)/shard_map/ppermute | solution.py:47
  368.9 23.9 %convolution_convert_fusion.4 = bf16[2048,2048]{1,0:T(8,128)(2,1)} fusion(bf16[2048,2048]{1,0:T(8,128)(2,1)} %constant_dynamic-update-slice_fusion.22, bf16[2048,2048]{1,0:T(8,128)(2,1)} %constant_dynamic-update-slice_fusion.15), kind=kOutput, calls=%fused_computation.107 | convolution fusion | flops 17184063488 | bytes 25165824 | tf_op jit(solution)/shard_map/td,fd->tf/dot_general | solution.py:71
  392.9 22.9 %convolution_convert_fusion.5 = bf16[2048,2048]{1,0:T(8,128)(2,1)} fusion(bf16[2048,2048]{1,0:T(8,128)(2,1)S(1)} %bitcast.232, bf16[1024,2048]{1,0:T(8,128)(2,1)} %collective-permute-done.3, bf16[512,2048]{1,0:T(8,128)(2,1)S(1)} %collective-permute-done.2, bf16[512,2048]{1,0:T(8,128)(2,1)S(1)} %multiply_convert_fusion), kind=kOutput, calls=%fused_computation.108 | convolution fusion | flops 17209229312 | bytes 25165824 | tf_op jit(solution)/shard_map/dot_general | solution.py:67
  415.8 26.4 %fusion.87 = f32[2048,2048]{1,0:T(8,128)} fusion(bf16[2048,2048]{1,0:T(8,128)(2,1)} %constant_dynamic-update-slice_fusion.8, bf16[2048,2048]{1,0:T(8,128)(2,1)} %convolution_convert_fusion.5, bf16[2048,2048]{1,0:T(8,128)(2,1)} %convolution_convert_fusion.4), kind=kOutput, calls=%fused_computation.288 | convolution fusion | flops 17213423616 | bytes 41943040 | tf_op jit(solution)/shard_map/td,fd->tf/dot_general | solution.py:71
  442.2 33.3 %fusion.49 = (bf16[2048,2048]{1,0:T(8,128)(2,1)}, bf16[2048,2048]{1,0:T(8,128)(2,1)}) fusion(bf16[2048,2048]{1,0:T(8,128)(2,1)} %convolution_convert_fusion.4, bf16[2048,2048]{1,0:T(8,128)(2,1)} %convolution_convert_fusion.5, bf16[2048,2048]{1,0:T(8,128)(2,1)} %constant_dynamic-update-slice_fusion.8, bf16[1024,2048]{1,0:T(8,128)(2,1)} %collective-permute-done.3, ...), kind=kOutput, calls=%fused_computation.73 | convolution fusion | flops 17267949568 | bytes 50331648 | tf_op jit(solution)/shard_map/dot_general | solution.py:67
  475.4 26.8 %convolution_add_fusion = f32[2048,2048]{1,0:T(8,128)} fusion(f32[2048,2048]{1,0:T(8,128)} %fusion.87, bf16[2048,2048]{1,0:T(8,128)(2,1)} %get-tuple-element.360, bf16[2048,2048]{1,0:T(8,128)(2,1)} %constant_dynamic-update-slice_fusion.1), kind=kOutput, calls=%fused_computation.88 | convolution fusion | flops 17184063488 | bytes 50331648 | tf_op jit(solution)/shard_map/td,fd->tf/dot_general | solution.py:71
  508.3 21.5 %fusion.94 = f32[2048,2048]{1,0:T(8,128)S(1)} fusion(bf16[2048,2048]{1,0:T(8,128)(2,1)} %get-tuple-element.361, bf16[2048,2048]{1,0:T(8,128)(2,1)} %constant_dynamic-update-slice_fusion.15), kind=kOutput, calls=%fused_computation.293 | convolution fusion | flops 17179869184 | bytes 33554432 | tf_op jit(solution)/shard_map/dot_general | solution.py:67
  533.3 25.9 %convolution_convert_fusion = bf16[2048,2048]{1,0:T(8,128)(2,1)S(1)} fusion(bf16[2048,2048]{1,0:T(8,128)(2,1)} %get-tuple-element.361, bf16[2048,2048]{1,0:T(8,128)(2,1)} %constant_dynamic-update-slice_fusion.22), kind=kOutput, calls=%fused_computation.103 | convolution fusion | flops 17184063488 | bytes 25165824 | tf_op jit(solution)/shard_map/td,tf->df/dot_general | solution.py:75
  568.0 21.6 %collective-permute-done.73 = bf16[256,2048]{1,0:T(8,128)(2,1)} collective-permute-done((bf16[256,2048]{1,0:T(8,128)(2,1)}, bf16[256,2048]{1,0:T(8,128)(2,1)}, u32[]{:S(2)}, u32[]{:S(2)}) %collective-permute-start.73) | collective-permute-done | bytes 1048608 | tf_op jit(solution)/shard_map/ppermute | solution.py:52
  589.6 22.1 %collective-permute-done.76 = bf16[256,2048]{1,0:T(8,128)(2,1)} collective-permute-done((bf16[256,2048]{1,0:T(8,128)(2,1)}, bf16[256,2048]{1,0:T(8,128)(2,1)}, u32[]{:S(2)}, u32[]{:S(2)}) %collective-permute-start.76) | collective-permute-done | bytes 1048608 | tf_op jit(solution)/shard_map/ppermute | solution.py:52
  644.3 23.7 %convolution_convert_fusion.2 = bf16[2048,2048]{0,1:T(8,128)(2,1)} fusion(bf16[2048,2048]{1,0:T(8,128)(2,1)} %get-tuple-element.360, bf16[1024,2048]{1,0:T(8,128)(2,1)} %collective-permute-done.3, bf16[512,2048]{1,0:T(8,128)(2,1)} %copy-done.50, bf16[512,2048]{1,0:T(8,128)(2,1)S(1)} %multiply_convert_fusion), kind=kOutput, calls=%fused_computation.105 | convolution fusion | flops 17209229312 | bytes 25165824 | tf_op jit(solution)/shard_map/td,tf->df/dot_general | solution.py:75
  681.8 38.8 %collective-permute-done.23 = bf16[512,2048]{1,0:T(8,128)(2,1)} collective-permute-done((bf16[512,2048]{1,0:T(8,128)(2,1)}, bf16[512,2048]{1,0:T(8,128)(2,1)}, u32[]{:S(2)}, u32[]{:S(2)}) %collective-permute-start.23) | collective-permute-done | bytes 2097184 | tf_op jit(solution)/shard_map/ppermute | solution.py:47
  728.8 27.8 %convolution_convert_fusion.1 = bf16[2048,2048]{0,1:T(8,128)(2,1)} fusion(bf16[1024,2048]{1,0:T(8,128)(2,1)} %collective-permute-done.3, bf16[512,2048]{1,0:T(8,128)(2,1)} %copy-done.50, bf16[512,2048]{1,0:T(8,128)(2,1)S(1)} %multiply_convert_fusion, bf16[2048,2048]{1,0:T(8,128)(2,1)} %convolution_convert_fusion.5, ...), kind=kOutput, calls=%fused_computation.104 | convolution fusion | flops 17242783744 | bytes 33554432 | tf_op jit(solution)/shard_map/td,tf->df/dot_general | solution.py:75
  787.7 56.5 %while.28 = (s32[]{:T(128)}, f32[1024,2,256]{0,2,1:T(8,128)}, f32[1024,2,256]{0,2,1:T(8,128)}, f32[2,512,2,2,256]{4,1,0,3,2:T(8,128)}, bf16[2,512,2,2,256]{4,1,3...) while((s32[]{:T(128)}, f32[1024,2,256]{0,2,1:T(8,128)}, ...), condition=%wide.region_9.10_spmd.clone, body=%wide.region_7.9_spmd.clone.sunk | while | flops 5405408256 | bytes 210848112 | solution.py:354
  879.0 20.4 %collective-permute-done.80 = bf16[256,2048]{1,0:T(8,128)(2,1)} collective-permute-done((bf16[256,2048]{1,0:T(8,128)(2,1)}, bf16[256,2048]{1,0:T(8,128)(2,1)}, u32[]{:S(2)}, u32[]{:S(2)}) %collective-permute-start.80) | collective-permute-done | bytes 1048608 | tf_op jit(solution)/shard_map/ppermute | solution.py:47
  945.5 14.4 %collective-permute-done.63 = bf16[2048,256]{0,1:T(8,128)(2,1)} collective-permute-done((bf16[2048,256]{0,1:T(8,128)(2,1)}, bf16[2048,256]{0,1:T(8,128)(2,1)}, u32[]{:S(2)}, u32[]{:S(2)}) %collective-permute-start.63) | collective-permute-done | bytes 1048608 | tf_op jit(solution)/shard_map/ppermute | solution.py:52
  963.9 18.5 %collective-permute-done.58 = f32[8,256]{1,0:T(8,128)S(1)} collective-permute-done((f32[8,256]{1,0:T(8,128)S(1)}, f32[8,256]{1,0:T(8,128)S(1)}, u32[]{:S(2)}, u32[]{:S(2)}) %collective-permute-start.58) | collective-permute-done | bytes 8224 | tf_op jit(solution)/shard_map/ppermute | solution.py:47
  1052.6 41.9 %collective-permute-done.38 = bf16[128,2048]{1,0:T(8,128)(2,1)S(1)} collective-permute-done((bf16[128,2048]{1,0:T(8,128)(2,1)S(1)}, bf16[128,2048]{1,0:T(8,128)(2,1)S(1)}, u32[]{:S(2)}, u32[]{:S(2)}) %collective-permute-start.38) | collective-permute-done | bytes 524320 | tf_op jit(solution)/shard_map/ppermute | solution.py:52
  1106.4 15.3 %collective-permute-done.41 = bf16[128,2048]{1,0:T(8,128)(2,1)S(1)} collective-permute-done((bf16[128,2048]{1,0:T(8,128)(2,1)S(1)}, bf16[128,2048]{1,0:T(8,128)(2,1)S(1)}, u32[]{:S(2)}, u32[]{:S(2)}) %collective-permute-start.41) | collective-permute-done | bytes 524320 | tf_op jit(solution)/shard_map/ppermute | solution.py:52
  1135.4 30.6 %collective-permute-done.43 = bf16[512,2048]{1,0:T(8,128)(2,1)} collective-permute-done((bf16[512,2048]{1,0:T(8,128)(2,1)S(1)}, bf16[512,2048]{1,0:T(8,128)(2,1)}, u32[]{:S(2)}, u32[]{:S(2)}) %collective-permute-start.43) | collective-permute-done | bytes 2097184 | tf_op jit(solution)/shard_map/ppermute | solution.py:47
  1177.7 22.5 %collective-permute-start.50 = (bf16[64,2048]{1,0:T(8,128)(2,1)S(1)}, bf16[64,2048]{1,0:T(8,128)(2,1)S(1)}, u32[]{:S(2)}, u32[]{:S(2)}) collective-permute-start(bf16[64,2048]{1,0:T(8,128)(2,1)S(1)} %get-tuple-element.411), channel_id=1, source_target_pairs={{0,6},{2,0},{4,2},{6,4},{1,7},{3,1},{5,3},{7,5},{8,14},{10,8},{12,... | collective-permute-start | bytes 786440 | tf_op jit(solution)/shard_map/ppermute | solution.py:52
  1206.3 14.1 %collective-permute-done.49 = bf16[64,2048]{1,0:T(8,128)(2,1)S(1)} collective-permute-done((bf16[64,2048]{1,0:T(8,128)(2,1)S(1)}, bf16[64,2048]{1,0:T(8,128)(2,1)S(1)}, u32[]{:S(2)}, u32[]{:S(2)}) %collective-permute-start.49) | collective-permute-done | bytes 262176 | tf_op jit(solution)/shard_map/ppermute | solution.py:52
  1319.1 38.7 %collective-permute-done.34 = f32[8,256]{1,0:T(8,128)S(1)} collective-permute-done((f32[8,256]{1,0:T(8,128)S(1)}, f32[8,256]{1,0:T(8,128)S(1)}, u32[]{:S(2)}, u32[]{:S(2)}) %collective-permute-start.34) | collective-permute-done | bytes 8224 | tf_op jit(solution)/shard_map/ppermute | solution.py:47
  (533 shorter events, 685.7 us)
Async XLA Ops:
  7.4 81.1 %collective-permute-start = (bf16[512,2048]{1,0:T(8,128)(2,1)}, bf16[512,2048]{1,0:T(8,128)(2,1)}, u32[]{:S(2)}, u32[]{:S(2)}) collective-permute-start(bf16[512,2048]{1,0:T(8,128)(2,1)} %fusion.60), channel_id=1, source_target_pairs={{0,1},{1,0},{2,3},{3,2},{4,5},{5,4},{6,7},{7,6},{8,9},{9,8},{10,11... | collective-permute-start | bytes 6291464 | tf_op jit(solution)/shard_map/ppermute | solution.py:47
  18.5 148.7 %collective-permute-start.24 = (bf16[512,2048]{1,0:T(8,128)(2,1)}, bf16[512,2048]{1,0:T(8,128)(2,1)}, u32[]{:S(2)}, u32[]{:S(2)}) collective-permute-start(bf16[512,2048]{1,0:T(8,128)(2,1)} %param.18), channel_id=1, source_target_pairs={{0,1},{1,0},{2,3},{3,2},{4,5},{5,4},{6,7},{7,6},{8,9},{9,8},{10,11... | collective-permute-start | bytes 6291464 | tf_op jit(solution)/shard_map/ppermute | solution.py:47
  21.9 64.3 %collective-permute-start.16 = (bf16[256,2048]{1,0:T(8,128)(2,1)}, bf16[256,2048]{1,0:T(8,128)(2,1)}, u32[]{:S(2)}, u32[]{:S(2)}) collective-permute-start(bf16[256,2048]{1,0:T(8,128)(2,1)} %get-tuple-element.345), channel_id=1, source_target_pairs={{0,2},{2,4},{4,6},{6,0},{1,3},{3,5},{5,7},{7,1},{8,10},{10,12},{12... | collective-permute-start | bytes 3145736 | tf_op jit(solution)/shard_map/ppermute | solution.py:52
  41.2 119.4 %collective-permute-start.11 = (bf16[2048,256]{1,0:T(8,128)(2,1)}, bf16[2048,256]{1,0:T(8,128)(2,1)}, u32[]{:S(2)}, u32[]{:S(2)}) collective-permute-start(bf16[2048,256]{1,0:T(8,128)(2,1)} %collective-permute-done.10), channel_id=1, source_target_pairs={{0,2},{2,4},{4,6},{6,0},{1,3},{3,5},{5,7},{7,1},{8,10},{10,12},{12... | collective-permute-start | bytes 3145736 | tf_op jit(solution)/shard_map/ppermute | solution.py:52
  63.6 154.1 %collective-permute-start.13 = (bf16[2048,256]{1,0:T(8,128)(2,1)}, bf16[2048,256]{1,0:T(8,128)(2,1)}, u32[]{:S(2)}, u32[]{:S(2)}) collective-permute-start(bf16[2048,256]{1,0:T(8,128)(2,1)} %collective-permute-done.10), channel_id=1, source_target_pairs={{0,16},{8,24},{16,0},{24,8},{1,17},{9,25},{17,1},{25,9},{2,18},{10... | collective-permute-start | bytes 3145736 | tf_op jit(solution)/shard_map/ppermute | solution.py:47
  86.1 77.3 %collective-permute-start.5 = (bf16[2048,256]{1,0:T(8,128)(2,1)}, bf16[2048,256]{1,0:T(8,128)(2,1)}, u32[]{:S(2)}, u32[]{:S(2)}) collective-permute-start(bf16[2048,256]{1,0:T(8,128)(2,1)} %collective-permute-done.4), channel_id=1, source_target_pairs={{0,2},{2,4},{4,6},{6,0},{1,3},{3,5},{5,7},{7,1},{8,10},{10,12},{12... | collective-permute-start | bytes 3145736 | tf_op jit(solution)/shard_map/ppermute | solution.py:52
  88.4 83.5 %collective-permute-start.17 = (bf16[256,2048]{1,0:T(8,128)(2,1)}, bf16[256,2048]{1,0:T(8,128)(2,1)}, u32[]{:S(2)}, u32[]{:S(2)}) collective-permute-start(bf16[256,2048]{1,0:T(8,128)(2,1)} %collective-permute-done.16), channel_id=1, source_target_pairs={{0,2},{2,4},{4,6},{6,0},{1,3},{3,5},{5,7},{7,1},{8,10},{10,12},{12... | collective-permute-start | bytes 3145736 | tf_op jit(solution)/shard_map/ppermute | solution.py:52
  167.3 72.4 %collective-permute-start.7 = (bf16[2048,256]{1,0:T(8,128)(2,1)}, bf16[2048,256]{1,0:T(8,128)(2,1)S(1)}, u32[]{:S(2)}, u32[]{:S(2)}) collective-permute-start(bf16[2048,256]{1,0:T(8,128)(2,1)} %collective-permute-done.4), channel_id=1, source_target_pairs={{0,16},{8,24},{16,0},{24,8},{1,17},{9,25},{17,1},{25,9},{2,18},{10... | collective-permute-start | bytes 3145736 | tf_op jit(solution)/shard_map/ppermute | solution.py:47
  191.5 174.7 %collective-permute-start.25 = (bf16[1024,2048]{1,0:T(8,128)(2,1)S(1)}, bf16[1024,2048]{1,0:T(8,128)(2,1)S(1)}, u32[]{:S(2)}, u32[]{:S(2)}) collective-permute-start(bf16[1024,2048]{1,0:T(8,128)(2,1)S(1)} %pad_maximum_fusion.4), channel_id=1, source_target_pairs={{0,8},{8,0},{16,24},{24,16},{1,9},{9,1},{17,25},{25,17},{2,10},{10... | collective-permute-start | bytes 12582920 | tf_op jit(solution)/shard_map/ppermute | solution.py:47
  237.1 89.5 %collective-permute-start.2 = (bf16[512,2048]{1,0:T(8,128)(2,1)S(1)}, bf16[512,2048]{1,0:T(8,128)(2,1)S(1)}, u32[]{:S(2)}, u32[]{:S(2)}) collective-permute-start(bf16[512,2048]{1,0:T(8,128)(2,1)S(1)} %multiply_convert_fusion), channel_id=1, source_target_pairs={{0,1},{1,0},{2,3},{3,2},{4,5},{5,4},{6,7},{7,6},{8,9},{9,8},{10,11... | collective-permute-start | bytes 6291464 | tf_op jit(solution)/shard_map/ppermute | solution.py:47
  258.1 67.4 %collective-permute-start.15 = (bf16[2048,256]{1,0:T(8,128)(2,1)S(1)}, bf16[2048,256]{1,0:T(8,128)(2,1)S(1)}, u32[]{:S(2)}, u32[]{:S(2)}) collective-permute-start(bf16[2048,256]{1,0:T(8,128)(2,1)S(1)} %collective-permute-done.12), channel_id=1, source_target_pairs={{0,16},{8,24},{16,0},{24,8},{1,17},{9,25},{17,1},{25,9},{2,18},{10... | collective-permute-start | bytes 3145736 | tf_op jit(solution)/shard_map/ppermute | solution.py:47
  280.6 67.4 %collective-permute-start.9 = (bf16[2048,256]{1,0:T(8,128)(2,1)S(1)}, bf16[2048,256]{1,0:T(8,128)(2,1)S(1)}, u32[]{:S(2)}, u32[]{:S(2)}) collective-permute-start(bf16[2048,256]{1,0:T(8,128)(2,1)S(1)} %collective-permute-done.6), channel_id=1, source_target_pairs={{0,16},{8,24},{16,0},{24,8},{1,17},{9,25},{17,1},{25,9},{2,18},{10... | collective-permute-start | bytes 3145736 | tf_op jit(solution)/shard_map/ppermute | solution.py:47
  327.2 65.7 %collective-permute-start.3 = (bf16[1024,2048]{1,0:T(8,128)(2,1)S(1)}, bf16[1024,2048]{1,0:T(8,128)(2,1)}, u32[]{:S(2)}, u32[]{:S(2)}) collective-permute-start(bf16[1024,2048]{1,0:T(8,128)(2,1)S(1)} %pad_maximum_fusion.3), channel_id=1, source_target_pairs={{0,8},{8,0},{16,24},{24,16},{1,9},{9,1},{17,25},{25,17},{2,10},{10... | collective-permute-start | bytes 12582920 | tf_op jit(solution)/shard_map/ppermute | solution.py:47
  508.3 111.8 %collective-permute-start.26 = (bf16[1024,2048]{1,0:T(8,128)(2,1)}, bf16[1024,2048]{1,0:T(8,128)(2,1)}, u32[]{:S(2)}, u32[]{:S(2)}) collective-permute-start(bf16[1024,2048]{1,0:T(8,128)(2,1)} %slice.375), channel_id=1, source_target_pairs={{0,8},{8,0},{16,24},{24,16},{1,9},{9,1},{17,25},{25,17},{2,10},{10... | collective-permute-start | bytes 12582920 | tf_op jit(solution)/shard_map/ppermute | solution.py:47
  532.8 96.4 %collective-permute-start.22 = (bf16[1024,2048]{1,0:T(8,128)(2,1)}, bf16[1024,2048]{1,0:T(8,128)(2,1)}, u32[]{:S(2)}, u32[]{:S(2)}) collective-permute-start(bf16[1024,2048]{1,0:T(8,128)(2,1)} %slice.376), channel_id=1, source_target_pairs={{0,8},{8,0},{16,24},{24,16},{1,9},{9,1},{17,25},{25,17},{2,10},{10... | collective-permute-start | bytes 12582920 | tf_op jit(solution)/shard_map/ppermute | solution.py:47
  643.1 77.5 %collective-permute-start.23 = (bf16[512,2048]{1,0:T(8,128)(2,1)}, bf16[512,2048]{1,0:T(8,128)(2,1)}, u32[]{:S(2)}, u32[]{:S(2)}) collective-permute-start(bf16[512,2048]{1,0:T(8,128)(2,1)} %slice.378), channel_id=1, source_target_pairs={{0,1},{1,0},{2,3},{3,2},{4,5},{5,4},{6,7},{7,6},{8,9},{9,8},{10,11... | collective-permute-start | bytes 6291464 | tf_op jit(solution)/shard_map/ppermute | solution.py:47
  673.0 96.3 %collective-permute-start.61 = (bf16[2048,1024]{0,1:T(8,128)(2,1)}, bf16[2048,1024]{0,1:T(8,128)(2,1)}, u32[]{:S(2)}, u32[]{:S(2)}) collective-permute-start(bf16[2048,1024]{0,1:T(8,128)(2,1)} %slice.267), channel_id=1, source_target_pairs={{0,16},{8,24},{16,0},{24,8},{1,17},{9,25},{17,1},{25,9},{2,18},{10... | collective-permute-start | bytes 12582920 | tf_op jit(solution)/shard_map/ppermute | solution.py:47
  678.6 84.3 %collective-permute-start.75 = (bf16[256,2048]{1,0:T(8,128)(2,1)}, bf16[256,2048]{1,0:T(8,128)(2,1)}, u32[]{:S(2)}, u32[]{:S(2)}) collective-permute-start(bf16[256,2048]{1,0:T(8,128)(2,1)} %get-tuple-element.366), channel_id=1, source_target_pairs={{0,6},{2,0},{4,2},{6,4},{1,7},{3,1},{5,3},{7,5},{8,14},{10,8},{12,... | collective-permute-start | bytes 3145736 | tf_op jit(solution)/shard_map/ppermute | solution.py:52
  678.6 84.3 %collective-permute-start.78 = (bf16[256,2048]{1,0:T(8,128)(2,1)}, bf16[256,2048]{1,0:T(8,128)(2,1)}, u32[]{:S(2)}, u32[]{:S(2)}) collective-permute-start(bf16[256,2048]{1,0:T(8,128)(2,1)} %get-tuple-element.367), channel_id=1, source_target_pairs={{0,6},{2,0},{4,2},{6,4},{1,7},{3,1},{5,3},{7,5},{8,14},{10,8},{12,... | collective-permute-start | bytes 3145736 | tf_op jit(solution)/shard_map/ppermute | solution.py:52
  761.4 142.6 %collective-permute-start.67 = (bf16[2048,1024]{0,1:T(8,128)(2,1)}, bf16[2048,1024]{0,1:T(8,128)(2,1)}, u32[]{:S(2)}, u32[]{:S(2)}) collective-permute-start(bf16[2048,1024]{0,1:T(8,128)(2,1)} %slice.273), channel_id=1, source_target_pairs={{0,16},{8,24},{16,0},{24,8},{1,17},{9,25},{17,1},{25,9},{2,18},{10... | collective-permute-start | bytes 12582920 | tf_op jit(solution)/shard_map/ppermute | solution.py:47
  767.3 111.8 %collective-permute-start.79 = (bf16[256,2048]{1,0:T(8,128)(2,1)}, bf16[256,2048]{1,0:T(8,128)(2,1)}, u32[]{:S(2)}, u32[]{:S(2)}) collective-permute-start(bf16[256,2048]{1,0:T(8,128)(2,1)} %get-tuple-element.365), channel_id=1, source_target_pairs={{0,16},{8,24},{16,0},{24,8},{1,17},{9,25},{17,1},{25,9},{2,18},{10... | collective-permute-start | bytes 3145736 | tf_op jit(solution)/shard_map/ppermute | solution.py:47
  767.8 131.7 %collective-permute-start.80 = (bf16[256,2048]{1,0:T(8,128)(2,1)}, bf16[256,2048]{1,0:T(8,128)(2,1)}, u32[]{:S(2)}, u32[]{:S(2)}) collective-permute-start(bf16[256,2048]{1,0:T(8,128)(2,1)} %get-tuple-element.364), channel_id=1, source_target_pairs={{0,16},{8,24},{16,0},{24,8},{1,17},{9,25},{17,1},{25,9},{2,18},{10... | collective-permute-start | bytes 3145736 | tf_op jit(solution)/shard_map/ppermute | solution.py:47
  778.1 143.8 %collective-permute-start.62 = (bf16[2048,256]{0,1:T(8,128)(2,1)}, bf16[2048,256]{0,1:T(8,128)(2,1)}, u32[]{:S(2)}, u32[]{:S(2)}) collective-permute-start(bf16[2048,256]{0,1:T(8,128)(2,1)} %slice.268), channel_id=1, source_target_pairs={{0,6},{2,0},{4,2},{6,4},{1,7},{3,1},{5,3},{7,5},{8,14},{10,8},{12,... | collective-permute-start | bytes 3145736 | tf_op jit(solution)/shard_map/ppermute | solution.py:52
  874.4 108.0 %collective-permute-start.35 = (bf16[1024,2048]{1,0:T(8,128)(2,1)}, bf16[1024,2048]{1,0:T(8,128)(2,1)}, u32[]{:S(2)}, u32[]{:S(2)}) collective-permute-start(bf16[1024,2048]{1,0:T(8,128)(2,1)} %constant_dynamic-slice_fusion.14), channel_id=1, source_target_pairs={{0,8},{8,0},{16,24},{24,16},{1,9},{9,1},{17,25},{25,17},{2,10},{10... | collective-permute-start | bytes 12582920 | tf_op jit(solution)/shard_map/ppermute | solution.py:47
  1012.4 120.0 %collective-permute-start.65 = (bf16[2048,256]{0,1:T(8,128)(2,1)S(1)}, bf16[2048,256]{0,1:T(8,128)(2,1)}, u32[]{:S(2)}, u32[]{:S(2)}) collective-permute-start(bf16[2048,256]{0,1:T(8,128)(2,1)S(1)} %add_convert_fusion.16), channel_id=1, source_target_pairs={{0,16},{8,24},{16,0},{24,8},{1,17},{9,25},{17,1},{25,9},{2,18},{10... | collective-permute-start | bytes 3145736 | tf_op jit(solution)/shard_map/ppermute | solution.py:47
  1027.5 143.6 %collective-permute-start.71 = (bf16[2048,256]{0,1:T(8,128)(2,1)S(1)}, bf16[2048,256]{0,1:T(8,128)(2,1)}, u32[]{:S(2)}, u32[]{:S(2)}) collective-permute-start(bf16[2048,256]{0,1:T(8,128)(2,1)S(1)} %add_convert_fusion.13), channel_id=1, source_target_pairs={{0,16},{8,24},{16,0},{24,8},{1,17},{9,25},{17,1},{25,9},{2,18},{10... | collective-permute-start | bytes 3145736 | tf_op jit(solution)/shard_map/ppermute | solution.py:47
  1130.9 91.6 %collective-permute-start.29 = (bf16[512,2048]{1,0:T(8,128)(2,1)}, bf16[512,2048]{1,0:T(8,128)(2,1)}, u32[]{:S(2)}, u32[]{:S(2)}) collective-permute-start(bf16[512,2048]{1,0:T(8,128)(2,1)} %convolution_convert_fusion.8), channel_id=1, source_target_pairs={{0,1},{1,0},{2,3},{3,2},{4,5},{5,4},{6,7},{7,6},{8,9},{9,8},{10,11... | collective-permute-start | bytes 6291464 | tf_op jit(solution)/shard_map/ppermute | solution.py:47
  1171.2 79.5 %collective-permute-start.44 = (bf16[1024,2048]{1,0:T(8,128)(2,1)}, bf16[1024,2048]{1,0:T(8,128)(2,1)}, u32[]{:S(2)}, u32[]{:S(2)}) collective-permute-start(bf16[1024,2048]{1,0:T(8,128)(2,1)} %pad_maximum_fusion.7), channel_id=1, source_target_pairs={{0,8},{8,0},{16,24},{24,16},{1,9},{9,1},{17,25},{25,17},{2,10},{10... | collective-permute-start | bytes 12582920 | tf_op jit(solution)/shard_map/ppermute | solution.py:47
  1206.3 72.3 %collective-permute-start.66 = (bf16[2048,512]{0,1:T(8,128)(2,1)}, bf16[2048,512]{0,1:T(8,128)(2,1)}, u32[]{:S(2)}, u32[]{:S(2)}) collective-permute-start(bf16[2048,512]{0,1:T(8,128)(2,1)} %pad_maximum_fusion.14), channel_id=1, source_target_pairs={{0,8},{8,0},{16,24},{24,16},{1,9},{9,1},{17,25},{25,17},{2,10},{10... | collective-permute-start | bytes 6291464 | tf_op jit(solution)/shard_map/ppermute | solution.py:47
  1220.4 64.7 %collective-permute-start.72 = (bf16[2048,512]{0,1:T(8,128)(2,1)}, bf16[2048,512]{0,1:T(8,128)(2,1)}, u32[]{:S(2)}, u32[]{:S(2)}) collective-permute-start(bf16[2048,512]{0,1:T(8,128)(2,1)} %pad_maximum_fusion.15), channel_id=1, source_target_pairs={{0,8},{8,0},{16,24},{24,16},{1,9},{9,1},{17,25},{25,17},{2,10},{10... | collective-permute-start | bytes 6291464 | tf_op jit(solution)/shard_map/ppermute | solution.py:47
  1264.7 101.7 %collective-permute-start.45 = (bf16[2048,1024]{1,0:T(8,128)(2,1)}, bf16[2048,1024]{1,0:T(8,128)(2,1)}, u32[]{:S(2)}, u32[]{:S(2)}) collective-permute-start(bf16[2048,1024]{1,0:T(8,128)(2,1)} %get-tuple-element.372), channel_id=1, source_target_pairs={{0,1},{1,0},{2,3},{3,2},{4,5},{5,4},{6,7},{7,6},{8,9},{9,8},{10,11... | collective-permute-start | bytes 12582920 | tf_op jit(solution)/shard_map/ppermute | solution.py:47
  1278.5 79.9 %collective-permute-start.55 = (bf16[512,2048]{1,0:T(8,128)(2,1)}, bf16[512,2048]{1,0:T(8,128)(2,1)}, u32[]{:S(2)}, u32[]{:S(2)}) collective-permute-start(bf16[512,2048]{1,0:T(8,128)(2,1)} %pad_maximum_fusion.13), channel_id=1, source_target_pairs={{0,8},{8,0},{16,24},{24,16},{1,9},{9,1},{17,25},{25,17},{2,10},{10... | collective-permute-start | bytes 6291464 | tf_op jit(solution)/shard_map/ppermute | solution.py:47
  (139 other events, 3131.2 us)

commit v2 on v1

v2 whole, which is shorter than its diff:
```python
import math

import jax
import jax.numpy as jnp
from jax import lax
from jax.experimental import pallas as pl
from jax.experimental.pallas import tpu as pltpu
from jax.sharding import PartitionSpec as P

QUERY_HEADS = 8
KEY_VALUE_HEADS = 4
HEAD_SIZE = 256


NORM_EPSILON = 1e-06
ROPE_BASE = 1000042.0
MASKED_SCORE = -1e30


def normalize(values, gain):
    inverse = lax.rsqrt(jnp.mean(values * values, axis=-1, keepdims=True) + NORM_EPSILON)
    return values * inverse * gain


def rope_tables(positions, head_dim):
    half_dim = head_dim // 2
    exponent = jnp.arange(half_dim, dtype=jnp.float32) * (2.0 / head_dim)
    inverse_freq = jnp.exp(-math.log(ROPE_BASE) * exponent)
    angles = positions.astype(jnp.float32)[:, None] * inverse_freq[None, :]
    return (jnp.cos(angles), jnp.sin(angles))


def turn(value, cosine, sine):
    half = value.shape[-1] // 2
    first, second = value[:, :half], value[:, half:]
    return jnp.concatenate(
        [first * cosine - second * sine, second * cosine + first * sine], axis=-1
    )


def kernel_dot(left, right, left_dim, right_dim):
    return lax.dot_general(
        left, right, (((left_dim,), (right_dim,)), ((), ())), preferred_element_type=jnp.float32
    )


def query_spans(length):
    step = length // 4
    return [(i * step, step, (i + 1) * step) for i in range(4)]


def allowed_keys(place, start, size, keys):
    pos_row, pos_col, seg_row, seg_col = place
    key_seg = seg_row[:, :keys]
    return (pos_row[:, :keys] <= pos_col[start : start + size, :]) & (
        (key_seg == 0) | (key_seg == seg_col[start : start + size, :])
    )


def stored_rows(first_ref, length):
    half = length // 2
    offsets = [first_ref[0] * half, (1 - first_ref[0]) * half]

    def rows(start, size):
        offset = pl.multiple_of(offsets[start // half] + start % half, size)
        return pl.ds(offset, size)

    return rows


def attend_kernel(
    first_ref, q_ref, k_ref, v_ref, cos_ref, sin_ref, pr_ref, pc_ref, sr_ref, sc_ref,
    out_ref, q_low_ref, k_low_ref, v_low_ref, key_ref, value_ref,
):
    length, head_dim = k_ref.shape
    rows = stored_rows(first_ref, length)
    place = (pr_ref, pc_ref, sr_ref, sc_ref)
    for start, size, _ in query_spans(length):
        span = slice(start, start + size)
        key = turn(k_ref[rows(start, size), :], cos_ref[span, :], sin_ref[span, :])
        key = key.astype(jnp.bfloat16)
        value = v_ref[rows(start, size), :].astype(jnp.bfloat16)
        key_ref[span, :] = key
        value_ref[span, :] = value
        k_low_ref[rows(start, size), :] = key
        v_low_ref[rows(start, size), :] = value
    for start, size, keys in query_spans(length):
        span = slice(start, start + size)
        allowed = allowed_keys(place, start, size, keys)
        for head in range(q_ref.shape[1] // head_dim):
            cols = slice(head * head_dim, (head + 1) * head_dim)
            query = turn(q_ref[rows(start, size), cols], cos_ref[span, :], sin_ref[span, :])
            query = query.astype(jnp.bfloat16)
            q_low_ref[rows(start, size), cols] = query
            scores = kernel_dot(query, key_ref[:keys, :], 1, 1) * head_dim**-0.5
            scores = jnp.where(allowed, scores, MASKED_SCORE)
            weights = jnp.exp(scores - jnp.max(scores, axis=1, keepdims=True))
            weights = weights * (1 / jnp.sum(weights, axis=1, keepdims=True))
            mixed = kernel_dot(weights.astype(jnp.bfloat16), value_ref[:keys, :], 1, 0)
            out_ref[rows(start, size), cols] = mixed.astype(jnp.bfloat16)


def attend_back_kernel(
    first_ref, q_ref, k_ref, v_ref, m_ref, cos_ref, sin_ref, pr_ref, pc_ref, sr_ref, sc_ref,
    q_back_ref, k_back_ref, v_back_ref, key_ref, value_ref, key_sum, value_sum,
):
    length, head_dim = k_ref.shape
    scale = head_dim**-0.5
    rows = stored_rows(first_ref, length)
    place = (pr_ref, pc_ref, sr_ref, sc_ref)
    for start, size, _ in query_spans(length):
        span = slice(start, start + size)
        key_ref[span, :] = k_ref[rows(start, size), :]
        value_ref[span, :] = v_ref[rows(start, size), :]
    key_sum[...] = jnp.zeros_like(key_sum)
    value_sum[...] = jnp.zeros_like(value_sum)
    for start, size, keys in query_spans(length):
        span = slice(start, start + size)
        allowed = allowed_keys(place, start, size, keys)
        for head in range(q_ref.shape[1] // head_dim):
            cols = slice(head * head_dim, (head + 1) * head_dim)
            query = q_ref[rows(start, size), cols]
            mixed = m_ref[rows(start, size), cols]
            scores = kernel_dot(query, key_ref[:keys, :], 1, 1) * scale
            scores = jnp.where(allowed, scores, MASKED_SCORE)
            probs = jnp.exp(scores - jnp.max(scores, axis=1, keepdims=True))
            probs = probs * (1 / jnp.sum(probs, axis=1, keepdims=True))
            value_sum[:keys, :] += kernel_dot(probs.astype(jnp.bfloat16), mixed, 0, 0)
            prob_grad = kernel_dot(mixed, value_ref[:keys, :], 1, 1)
            row_dot = jnp.sum(probs * prob_grad, axis=1, keepdims=True)
            score_low = (probs * (prob_grad - row_dot)).astype(jnp.bfloat16)
            key_sum[:keys, :] += kernel_dot(score_low, query, 0, 0)
            query_grad = kernel_dot(score_low, key_ref[:keys, :], 1, 0) * scale
            query_grad = turn(query_grad, cos_ref[span, :], -sin_ref[span, :])
            q_back_ref[rows(start, size), cols] = query_grad.astype(jnp.bfloat16)
    for start, size, _ in query_spans(length):
        span = slice(start, start + size)
        key_grad = turn(key_sum[span, :] * scale, cos_ref[span, :], -sin_ref[span, :])
        k_back_ref[rows(start, size), :] = key_grad.astype(jnp.bfloat16)
        v_back_ref[rows(start, size), :] = value_sum[span, :].astype(jnp.bfloat16)


def attention_call(kernel, name, first, heads, tables, outs, scratch, head_dim, flops):
    length = heads[0][0].shape[0]
    key_heads = flops[1]

    def head_spec(width, start):
        return pl.BlockSpec((length, width), lambda g, first_ref: (0, start + g))

    def whole_spec(shape):
        return pl.BlockSpec(shape, lambda g, first_ref: (0, 0))

    return pl.pallas_call(
        kernel,
        grid_spec=pltpu.PrefetchScalarGridSpec(
            num_scalar_prefetch=1,
            grid=(key_heads,),
            in_specs=[head_spec(width, start) for _, width, start in heads]
            + [whole_spec(table.shape) for table in tables],
            out_specs=[head_spec(width, 0) for width in outs],
            scratch_shapes=[pltpu.VMEM((length, head_dim), kind) for kind in scratch],
        ),
        out_shape=[
            jax.ShapeDtypeStruct((length, width * key_heads), jnp.bfloat16) for width in outs
        ],
        cost_estimate=pl.CostEstimate(
            flops=flops[0], bytes_accessed=flops[0] // 200, transcendentals=length * length
        ),
        name=name,
    )(first, *[array for array, _, _ in heads], *tables)


def swap(value, axis, bit):
    count = lax.axis_size(axis)
    return lax.ppermute(value, axis, [(i, i ^ bit) for i in range(count)])


def shift(value, axis, step):
    count = lax.axis_size(axis)
    return lax.ppermute(value, axis, [(i, (i + step) % count) for i in range(count)])


def tie(*values):
    return lax.optimization_barrier(values)


def ordered(first_when_zero, mine, theirs, dim):
    keep = first_when_zero == 0
    return jnp.concatenate(
        [jnp.where(keep, mine, theirs), jnp.where(keep, theirs, mine)], axis=dim
    )


def dot32(left, right):
    return jnp.dot(left, right, preferred_element_type=jnp.float32)


def dot_nt(left, right):
    return jnp.einsum("td,fd->tf", left, right, preferred_element_type=jnp.float32)


def dot_tn(left, right):
    return jnp.einsum("td,tf->df", left, right, preferred_element_type=jnp.float32)


def low(value):
    return value.astype(jnp.bfloat16)


def wide(value):
    return value.astype(jnp.float32)


def col_gather(mine):
    if lax.axis_size("col") == 2:
        return [mine, swap(mine, "col", 1)]
    return [lax.all_gather(mine, "col", axis=0, tiled=True)]


def col_scatter(product):
    if lax.axis_size("col") == 2:
        theirs = swap(low(product(1)), "col", 1)
        return product(0) + wide(theirs)
    return wide(lax.psum_scatter(low(product(0)), "col", scatter_dimension=0, tiled=True))


def blocks_of(value, dim, count):
    size = value.shape[dim] // count
    return [lax.slice_in_dim(value, i * size, (i + 1) * size, axis=dim) for i in range(count)]


def butterfly(value, axes):
    for axis in axes:
        bit = 1
        while bit < lax.axis_size(axis):
            value = value + swap(value, axis, bit)
            bit *= 2
    return value


def half_rows(value, bit):
    size = value.shape[0] // 2
    return lax.dynamic_slice_in_dim(value, bit * size, size, 0)


def row_gather(value):
    return lax.all_gather(value, "row", axis=0, tiled=True)


def row_scatter(value):
    return lax.psum_scatter(value, "row", scatter_dimension=0, tiled=True)


def sum_quarters(value, core, ypos):
    part = low(wide(half_rows(value, core)) + wide(swap(half_rows(value, 1 - core), "grp", 1)))
    part = low(wide(half_rows(part, ypos)) + wide(swap(half_rows(part, 1 - ypos), "grp", 2)))
    return row_gather(row_scatter(part))


def spread_y(part, ypos):
    return ordered(ypos, part, swap(part, "grp", 2), 0)


def spread_core(part, core):
    return ordered(core, part, swap(part, "grp", 1), 0)


def own_quarters(weight, core, ypos):
    size = weight.shape[0] // 4
    mine = lax.dynamic_slice_in_dim(weight, (2 * core + ypos) * size, size, 0)
    other = lax.dynamic_slice_in_dim(weight, (2 * core + 1 - ypos) * size, size, 0)
    return mine, other


def other_quarters(mines, other, zpos):
    count = lax.axis_size("row")
    size = other.shape[0]
    turned = jnp.concatenate(
        [
            lax.dynamic_slice_in_dim(mines, lax.rem(zpos + k, count) * size, size, 0)
            for k in range(1, count)
        ],
        axis=0,
    )
    theirs = swap(turned, "grp", 2)
    others = lax.dynamic_update_slice_in_dim(jnp.zeros_like(mines), other, zpos * size, 0)
    for k in range(1, count):
        others = lax.dynamic_update_slice_in_dim(
            others,
            lax.slice_in_dim(theirs, (k - 1) * size, k * size, axis=0),
            lax.rem(zpos + k, count) * size,
            0,
        )
    return others


def sum_y_first(keep, give, core, ypos):
    part = low(wide(keep) + wide(swap(give, "grp", 2)))
    mine = row_scatter(part)
    return spread_core(spread_y(mine, ypos), core)


def sum_z_first(keep, give, core, ypos):
    mine, other = row_scatter(keep), row_scatter(give)
    mine, other = (
        low(wide(mine) + wide(swap(other, "grp", 2))),
        low(wide(other) + wide(swap(mine, "grp", 2))),
    )
    return spread_core(ordered(ypos, mine, other, 0), core)


def per_device(
    tokens,
    cotangent,
    segments,
    positions,
    first_gain,
    query_weight,
    key_matrix,
    value_matrix,
    output_weight,
    second_gain,
    gate_weight,
    up_weight,
    down_weight,
):
    head_dim = HEAD_SIZE
    query_heads = query_weight.shape[1] // head_dim
    heads_per_group = QUERY_HEADS // KEY_VALUE_HEADS
    key_heads = max(1, query_heads // heads_per_group)
    head_share = query_heads // key_heads
    head_sharing = max(1, heads_per_group // query_heads)
    col = lax.axis_index("col")
    key_first = col * query_heads // heads_per_group
    query_cols = query_heads * head_dim
    key_cols = key_heads * head_dim
    rows, width = tokens.shape
    grp, zpos = lax.axis_index("grp"), lax.axis_index("row")
    core, ypos = lax.rem(grp, 2), lax.div(grp, 2)
    in_pairs = lax.axis_size("col") == 2

    inputs = wide(tokens)
    normalized_input, first_back = jax.vjp(normalize, inputs, first_gain)
    gathered_in = jnp.concatenate(col_gather(low(normalized_input)), axis=0)
    packed_length = gathered_in.shape[0]

    down_mine, down_other = own_quarters(down_weight, core, ypos)
    gate_mine, gate_other = own_quarters(gate_weight.T, core, ypos)
    up_mine, up_other = own_quarters(up_weight.T, core, ypos)
    down_mines, gate_mines, up_mines = [row_gather(m) for m in (down_mine, gate_mine, up_mine)]

    gathered_in, cot_now = tie(gathered_in, cotangent)
    cot_pack = jnp.concatenate(col_gather(cot_now), axis=0)
    cot_all = jnp.concatenate([cot_pack, swap(cot_pack, "grp", 1)], axis=0)

    key_slice = lax.dynamic_slice_in_dim(key_matrix, key_first * head_dim, key_cols, 1)
    value_slice = lax.dynamic_slice_in_dim(value_matrix, key_first * head_dim, key_cols, 1)
    project_in = jnp.concatenate([query_weight, key_slice, value_slice], axis=1)
    projected = dot32(gathered_in, project_in)
    cosine, sine = rope_tables(positions, head_dim)
    tables = (cosine, sine, positions[None], positions[:, None], segments[None], segments[:, None])
    first = (col if in_pairs else jnp.zeros_like(col)).astype(jnp.int32).reshape(1)
    group_cols = head_share * head_dim
    score_flops = query_cols * packed_length * packed_length
    attn_low, query_low, key_low, value_low = attention_call(
        attend_kernel,
        "attend",
        first,
        [
            (projected, group_cols, 0),
            (projected, head_dim, query_heads),
            (projected, head_dim, query_heads + key_heads),
        ],
        tables,
        (group_cols, group_cols, head_dim, head_dim),
        (jnp.bfloat16, jnp.bfloat16),
        head_dim,
        (3 * score_flops, key_heads),
    )
    attn_low, down_mines = tie(attn_low, down_mines)
    down_all = [down_mines, other_quarters(down_mines, down_other, zpos)]
    attn_parts = blocks_of(attn_low, 0, 2) if in_pairs else [attn_low]
    hidden_res = inputs + col_scatter(lambda i: dot32(attn_parts[i], output_weight))
    normed_mid, second_back = jax.vjp(normalize, hidden_res, second_gain)

    mid_pack = jnp.concatenate(col_gather(low(normed_mid)), axis=0)
    mid_pack, gate_mines = tie(mid_pack, gate_mines)
    gate_all = [gate_mines, other_quarters(gate_mines, gate_other, zpos)]
    up_all = [up_mines, other_quarters(up_mines, up_other, zpos)]
    mid_all = jnp.concatenate([mid_pack, swap(mid_pack, "grp", 1)], axis=0)
    acts, gate_backs, up_backs = [], [], []
    for gate_rows, up_rows, down_rows in zip(gate_all, up_all, down_all):
        act_grad = low(dot_nt(cot_all, down_rows))
        gate32 = wide(low(dot_nt(mid_all, gate_rows)))
        up_lin = dot_nt(mid_all, up_rows)
        sig = jax.nn.sigmoid(gate32)
        acts.append(low(gate32 * sig * up_lin))
        gate_backs.append(low(wide(act_grad) * up_lin * sig * (1 + gate32 * (1 - sig))))
        up_backs.append(low(wide(act_grad) * gate32 * sig))
    down_parts = [low(dot_tn(act, cot_all)) for act in acts]
    gate_parts = [low(dot_tn(back, mid_all)) for back in gate_backs]
    up_parts = [low(dot_tn(back, mid_all)) for back in up_backs]

    def token_sum(product):
        both = mid_all.shape[0]
        pack = both // 2
        from_core = wide(swap(low(product(pack, both)), "grp", 1))
        if not in_pairs:
            return col_scatter(lambda i: product(0, pack) + from_core)
        half = pack // 2
        parts = blocks_of(from_core, 0, 2)
        return col_scatter(lambda i: product(i * half, (i + 1) * half) + parts[i])

    def over_hidden(a, b, *pairs):
        return sum(dot32(left[a:b], right) for lefts, rights in pairs for left, right in zip(lefts, rights))

    mid_grad = token_sum(
        lambda a, b: over_hidden(a, b, (gate_backs, gate_all), (up_backs, up_all))
    )
    layer_out = hidden_res + token_sum(lambda a, b: over_hidden(a, b, (acts, down_all)))

    res_from_mid, second_gain_part = second_back(mid_grad)
    res_grad = wide(cotangent) + res_from_mid
    shard_rows = jnp.concatenate(col_gather(low(res_grad)), axis=0)
    shard_rows, *parts = tie(shard_rows, *down_parts, *gate_parts, *up_parts)
    down_grad = sum_z_first(*parts[:2], core, ypos)
    gate_grad = sum_y_first(*parts[2:4], core, ypos)
    up_grad = sum_y_first(*parts[4:], core, ypos)
    out_wgrad = sum_quarters(low(dot_tn(attn_low, shard_rows)), core, ypos)
    out_wgrad = spread_core(spread_y(out_wgrad, ypos), core)
    mixed_low = low(dot_nt(shard_rows, output_weight))
    query_back, key_back, value_back = attention_call(
        attend_back_kernel,
        "attend_back",
        first,
        [
            (query_low, group_cols, 0),
            (key_low, head_dim, 0),
            (value_low, head_dim, 0),
            (mixed_low, group_cols, 0),
        ],
        tables,
        (group_cols, head_dim, head_dim),
        (jnp.bfloat16, jnp.bfloat16, jnp.float32, jnp.float32),
        head_dim,
        (7 * score_flops, key_heads),
    )
    pair_back = jnp.concatenate([key_back, value_back], axis=1)
    back_all = jnp.concatenate([query_back, pair_back], axis=1)
    query_part = sum_quarters(low(dot_tn(gathered_in, query_back)), core, ypos)
    pair_part = sum_quarters(low(dot_tn(gathered_in, pair_back)), core, ypos)
    back_parts = blocks_of(back_all, 0, 2) if in_pairs else [back_all]
    in_grad = col_scatter(lambda i: dot_nt(back_parts[i], project_in))
    res_from_in, _ = first_back(in_grad)
    input_grad = res_grad + res_from_in

    query_wgrad = wide(spread_core(spread_y(query_part, ypos), core))
    pair_part = spread_y(pair_part, ypos)
    if in_pairs:
        theirs = swap(pair_part, "col", 1)
        key_part = ordered(col, pair_part[:, :key_cols], theirs[:, :key_cols], 1)
        value_part = ordered(col, pair_part[:, key_cols:], theirs[:, key_cols:], 1)
        key_full = wide(spread_core(key_part, core))
        value_full = wide(spread_core(value_part, core))
    else:
        pair_part = spread_core(pair_part, core)
        pair_all = wide(lax.all_gather(pair_part, "col", axis=0))
        groups = lax.axis_size("col") // head_sharing

        def spread(piece):
            piece = jnp.sum(piece.reshape(groups, head_sharing, width, key_cols), axis=1)
            return jnp.swapaxes(piece, 0, 1).reshape(width, groups * key_cols)

        key_full = spread(pair_all[..., :key_cols])
        value_full = spread(pair_all[..., key_cols:])
    query_term = jnp.sum(query_wgrad * wide(query_weight), axis=1)
    pair_term = jnp.sum(key_full * wide(key_matrix) + value_full * wide(value_matrix), axis=1)
    query_term = butterfly(query_term.reshape(8, -1), ("col",)).reshape(-1)
    first_gain_grad = (query_term + pair_term) / first_gain
    axes = ("grp", "row", "col")
    second_gain_grad = butterfly(second_gain_part.reshape(8, -1), axes).reshape(-1)
    return (
        layer_out,
        input_grad,
        first_gain_grad,
        query_wgrad,
        key_full,
        value_full,
        wide(out_wgrad),
        second_gain_grad,
        wide(gate_grad).T,
        wide(up_grad).T,
        wide(down_grad),
    )


def solution(mesh):
    return jax.shard_map(
        per_device,
        mesh=mesh,
        in_specs=(
            P(("grp", "row", "col"), None),
            P(("grp", "row", "col"), None),
            P(("grp", "row")),
            P(("grp", "row")),
            P(),
            P(None, "col"),
            P(),
            P(),
            P("col", None),
            P(),
            P(None, ("row", "col")),
            P(None, ("row", "col")),
            P(("row", "col"), None),
        ),
        out_specs=(
            P(("grp", "row", "col"), None),
            P(("grp", "row", "col"), None),
            P(),
            P(None, "col"),
            P(),
            P(),
            P("col", None),
            P(),
            P(None, ("row", "col")),
            P(None, ("row", "col")),
            P(("row", "col"), None),
        ),
        check_vma=False,
    )
```

time: 1390 us -> 1330 us (0.957)
  starting transfers between devices: 107 us -> 37.7 us
  local copies, waits for them, and re-layouts: 184 us -> 115 us
  waiting for transfers between devices: 558 us -> 595 us
  Pallas kernels: 0 us -> 32.2 us
  matrix products: 348 us -> 378 us
  other arithmetic: 185 us -> 155 us
    ppermute x33 -> x0, waiting for transfers between devices: 271 us -> none  [shift(): lax.ppermute(value, axis, [(i, (i + step) % count) for i in range(count)])]
    ppermute x49 -> x44, waiting for transfers between devices: 287 us -> 511 us  [swap(): return lax.ppermute(value, axis, [(i, i ^ bit) for i in range(count)])]
    dot_general x6 -> x21, matrix products: 95.7 us -> 166 us  [dot32(): return jnp.dot(left, right, preferred_element_type=jnp.float32)]
    ppermute x33 -> x0, starting transfers between devices: 62.6 us -> none  [shift(): lax.ppermute(value, axis, [(i, (i + step) % count) for i in range(count)])]
    dot_general x14 -> x0, matrix products: 56.5 us -> none  [the longest x4 12 us: block_scores(): jnp.einsum('qgrd,kgd->grqk', query_block, key_low, preferred_element_type...]
    reduce_scatter x0 -> x7, waiting for transfers between devices: none -> 52.7 us  [row_scatter(): return lax.psum_scatter(value, 'row', scatter_dimension=0, tiled=True)]
    unnamed x181 -> x211, local copies, waits for them, and re-layouts: 84 us -> 46.6 us
    pallas_call x0 -> x2, Pallas kernels: none -> 32.2 us  [attention_call(): pl.pallas_call(kernel, grid_spec=pltpu.PrefetchScalarGridSpec(num_scalar_...]
  transfers between devices with their start and end apart: 82 -> 57, of which waited for: 35 -> 23; matrix products, arithmetic and copies ran while one was open for 40% -> 31% of each run, Pallas kernels for 0% -> 1%
where the time goes in v2:
time: 1330 us
  waiting for transfers between devices  595 us (45%)
  matrix products  378 us (28%)
  other arithmetic  155 us (12%)
  local copies, waits for them, and re-layouts  115 us (9%)
  starting transfers between devices  37.7 us (3%)
  Pallas kernels  32.2 us (2%)
  between operations  15.4 us (1%)
    ppermute x44, waiting for transfers between devices, swap(): return lax.ppermute(value, axis, [(i, i ^ bit) for i in range(count)])  511 us
    dot_general x21, matrix products, dot32(): return jnp.dot(left, right, preferred_element_type=jnp.float32)  166 us
    dot_general x9, matrix products, dot_nt(): jnp.einsum('td,fd->tf', left, right, preferred_element_type=jnp.float32)  115 us
    dot_general x9, matrix products, dot_tn(): jnp.einsum('td,tf->df', left, right, preferred_element_type=jnp.float32)  96.8 us
    reduce_scatter x7, waiting for transfers between devices, row_scatter(): return lax.psum_scatter(value, 'row', scatter_dimension=0, tiled=True)  52.7 us
    unnamed x211, local copies, waits for them, and re-layouts  46.6 us
    ppermute x44, starting transfers between devices, swap(): return lax.ppermute(value, axis, [(i, i ^ bit) for i in range(count)])  36.7 us
    select_n x14, other arithmetic, ordered(): jnp.where(keep, mine, theirs)  35.4 us
  transfers between devices with their start and end apart: 57, of which 23 were waited for; matrix products, arithmetic and copies ran while one was open for 31% of the time, Pallas kernels for 1%

profile of v2, /device:TPU:0, one launch (start us, length us, event | category | flops | bytes accessed | tf_op | source)
XLA Modules:
  0.0 1329.3 jit_solution(6117153506425265079)
XLA Ops:
  27.9 39.3 %collective-permute-done = bf16[512,2048]{1,0:T(8,128)(2,1)} collective-permute-done((bf16[512,2048]{1,0:T(8,128)(2,1)}, bf16[512,2048]{1,0:T(8,128)(2,1)}, u32[]{:S(2)}, u32[]{:S(2)}) %collective-permute-start) | collective-permute-done | bytes 2097184 | tf_op jit(solution)/shard_map/ppermute | solution.py:175
  81.4 14.7 %fusion.81.q_ref.k_ref.v_ref = f32[1024,2048]{1,0:T(8,128)} fusion(bf16[1024,2048]{1,0:T(8,128)(2,1)} %pad_maximum_fusion.1, bf16[2048,512]{1,0:T(8,128)(2,1)} %get-tuple-element.146, bf16[2048,512]{1,0:T(8,128)(2,1)} %get-tuple-element.147, bf16[2048,1024]{1,0:T(8,128)(2,1)} %param.18), kind=kOutput, calls=%fused_computation.244 | convolution fusion | flops 8615100416 | bytes 20971520 | tf_op jit(solution)/shard_map/dot_general | solution.py:195
  148.3 29.0 %all-gather.11.cloned.1.call-done = bf16[1024,2048]{0,1:T(8,128)(2,1)} async-done(((bf16[256,2048]{0,1:T(8,128)(2,1)}), bf16[1024,2048]{0,1:T(8,128)(2,1)}) %all-gather.11.cloned.1.call-update) | async-done | bytes 4194320 | tf_op jit(solution)/shard_map/all_gather | solution.py:247
  204.7 79.9 %collective-permute-done.5 = bf16[768,2048]{0,1:T(8,128)(2,1)S(1)} collective-permute-done((bf16[768,2048]{0,1:T(8,128)(2,1)S(1)}, bf16[768,2048]{0,1:T(8,128)(2,1)S(1)}, u32[]{:S(2)}, u32[]{:S(2)}) %collective-permute-start.5) | collective-permute-done | bytes 3145760 | tf_op jit(solution)/shard_map/ppermute | solution.py:175
  309.7 14.4 %convolution_convert_fusion.6 = bf16[2048,1024]{1,0:T(8,128)(2,1)} fusion(bf16[2048,2048]{1,0:T(8,128)(2,1)} %copy-done.64, bf16[1024,2048]{1,0:T(8,128)(2,1)} %slice_dynamic-update-slice_fusion), kind=kOutput, calls=%fused_computation.86 | convolution fusion | flops 8592031744 | bytes 16777216 | tf_op jit(solution)/shard_map/td,fd->tf/dot_general | solution.py:199
  326.5 46.0 %collective-permute-done.4 = bf16[768,2048]{0,1:T(8,128)(2,1)} collective-permute-done((bf16[768,2048]{0,1:T(8,128)(2,1)}, bf16[768,2048]{0,1:T(8,128)(2,1)}, u32[]{:S(2)}, u32[]{:S(2)}) %collective-permute-start.4) | collective-permute-done | bytes 3145760 | tf_op jit(solution)/shard_map/ppermute | solution.py:175
  386.4 12.6 convolution_convert_fusion.9
  399.1 20.2 %fusion.2 = (bf16[2048,1024]{1,0:T(8,128)(2,1)S(1)}, bf16[2048,1024]{1,0:T(8,128)(2,1)}, bf16[2048,1024]{1,0:T(8,128)(2,1)}) fusion(bf16[2048,1024]{1,0:T(8,128)(2,1)} %convolution_convert_fusion.7, bf16[2048,1024]{1,0:T(8,128)(2,1)} %convolution_convert_fusion.9, bf16[2048,2048]{1,0:T(8,128)(2,1)} %constant_dynamic-update-slice_fusion, ...), kind=kOutput, calls=%fused_computation.12 | convolution fusion | flops 8627683328 | bytes 33554432 | tf_op jit(solution)/shard_map/td,fd->tf/dot_general | solution.py:199
  431.9 12.3 convolution_convert_fusion.8
  444.1 22.4 %fusion.5 = (bf16[2048,1024]{1,0:T(8,128)(2,1)}, bf16[2048,1024]{1,0:T(8,128)(2,1)}, bf16[2048,1024]{1,0:T(8,128)(2,1)}) fusion(bf16[2048,1024]{1,0:T(8,128)(2,1)} %convolution_convert_fusion.6, bf16[2048,1024]{1,0:T(8,128)(2,1)} %convolution_convert_fusion.8, bf16[2048,2048]{1,0:T(8,128)(2,1)} %constant_dynamic-update-slice_fusion, ...), kind=kOutput, calls=%fused_computation.15 | convolution fusion | flops 8627683328 | bytes 33554432 | tf_op jit(solution)/shard_map/td,fd->tf/dot_general | solution.py:199
  520.2 16.7 %add_convert_fusion.2 = bf16[1024,2048]{1,0:T(8,128)(2,1)} fusion(f32[1024,2048]{1,0:T(8,128)} %fusion.37, f32[1024,2048]{1,0:T(8,128)} %fusion.41, f32[1024,2048]{1,0:T(8,128)} %fusion.39, bf16[1024,2048]{1,0:T(8,128)(2,1)} %constant_dynamic-update-slice_fusion.8, bf16[2048,1024]{1,0:T(8,128)(2,1)} %get-tuple-element.85), kind=kOutput, calls=%fused_computation.39 | convolution fusion | flops 4303355904 | bytes 35651584 | tf_op jit(solution)/shard_map/dot_general | solution.py:195
  541.9 14.1 %convolution_convert_fusion.2 = bf16[1024,2048]{1,0:T(8,128)(2,1)} fusion(bf16[2048,1024]{1,0:T(8,128)(2,1)} %get-tuple-element.81, bf16[2048,2048]{1,0:T(8,128)(2,1)} %constant_dynamic-update-slice_fusion), kind=kOutput, calls=%fused_computation.82 | convolution fusion | flops 8592031744 | bytes 16777216 | tf_op jit(solution)/shard_map/td,tf->df/dot_general | solution.py:203
  584.0 13.4 %convolution_convert_fusion = bf16[1024,2048]{1,0:T(8,128)(2,1)} fusion(bf16[2048,1024]{1,0:T(8,128)(2,1)S(1)} %copy-done.65, bf16[2048,2048]{1,0:T(8,128)(2,1)} %constant_dynamic-update-slice_fusion), kind=kOutput, calls=%fused_computation.80 | convolution fusion | flops 8592031744 | bytes 16777216 | tf_op jit(solution)/shard_map/td,tf->df/dot_general | solution.py:203
  597.4 27.2 %collective-permute-done.12 = bf16[512,2048]{1,0:T(8,128)(2,1)} collective-permute-done((bf16[512,2048]{1,0:T(8,128)(2,1)}, bf16[512,2048]{1,0:T(8,128)(2,1)}, u32[]{:S(2)}, u32[]{:S(2)}) %collective-permute-start.12) | collective-permute-done | bytes 2097184 | tf_op jit(solution)/shard_map/ppermute | solution.py:175
  635.4 13.0 convolution_convert_fusion.5
  648.4 14.3 %convolution_convert_fusion.4 = bf16[1024,2048]{1,0:T(8,128)(2,1)} fusion(bf16[2048,1024]{1,0:T(8,128)(2,1)} %get-tuple-element.82, bf16[2048,2048]{1,0:T(8,128)(2,1)} %copy-done.64), kind=kOutput, calls=%fused_computation.84 | convolution fusion | flops 8592031744 | bytes 16777216 | tf_op jit(solution)/shard_map/td,tf->df/dot_general | solution.py:203
  662.7 18.4 %collective-permute-done.13 = bf16[512,2048]{1,0:T(8,128)(2,1)} collective-permute-done((bf16[512,2048]{1,0:T(8,128)(2,1)S(1)}, bf16[512,2048]{1,0:T(8,128)(2,1)}, u32[]{:S(2)}, u32[]{:S(2)}) %collective-permute-start.13) | collective-permute-done | bytes 2097184 | tf_op jit(solution)/shard_map/ppermute | solution.py:175
  689.0 20.2 %attend_back.1 = (bf16[1024,1024]{1,0:T(8,128)(2,1)}, bf16[1024,512]{1,0:T(8,128)(2,1)}, bf16[1024,512]{1,0:T(8,128)(2,1)}) custom-call(s32[1]{0:T(128)} %bitcast.first_ref, bf16[1024,1024]{1,0:T(8,128)(2,1)} %get-tuple-element.38.q_ref, bf16[1024,512]{1,0:T(8,128)(2,1)} %get-tuple-element.39.k_ref, bf16[1024,512]{1,0:T(8,128)(2,1)} %get-tuple-element.40.v_ref, ...), custom_call_target="tpu_custom_call" | custom-call | flops 7516192768 | bytes 37580964 | tf_op jit(solution)/shard_map/attend_back/pallas_call | solution.py:153
  742.9 15.5 %collective-permute-done.16 = bf16[512,1024]{1,0:T(8,128)(2,1)S(1)} collective-permute-done((bf16[512,1024]{1,0:T(8,128)(2,1)S(1)}, bf16[512,1024]{1,0:T(8,128)(2,1)S(1)}, u32[]{:S(2)}, u32[]{:S(2)}) %collective-permute-start.16) | collective-permute-done | bytes 1048608 | tf_op jit(solution)/shard_map/ppermute | solution.py:175
  764.8 24.1 %collective-permute-done.21 = bf16[512,1024]{1,0:T(8,128)(2,1)} collective-permute-done((bf16[512,1024]{1,0:T(8,128)(2,1)S(1)}, bf16[512,1024]{1,0:T(8,128)(2,1)}, u32[]{:S(2)}, u32[]{:S(2)}) %collective-permute-start.21) | collective-permute-done | bytes 1048608 | tf_op jit(solution)/shard_map/ppermute | solution.py:175
  796.3 23.3 %collective-permute-done.27 = bf16[256,2048]{1,0:T(8,128)(2,1)} collective-permute-done((bf16[256,2048]{1,0:T(8,128)(2,1)S(1)}, bf16[256,2048]{1,0:T(8,128)(2,1)}, u32[]{:S(2)}, u32[]{:S(2)}) %collective-permute-start.27) | collective-permute-done | bytes 1048608 | tf_op jit(solution)/shard_map/ppermute | solution.py:175
  823.8 26.2 %reduce-scatter.12.cloned.1.call-done = bf16[64,2048]{1,0:T(8,128)(2,1)} async-done(((bf16[256,2048]{1,0:T(8,128)(2,1)}), bf16[64,2048]{1,0:T(8,128)(2,1)}) %reduce-scatter.12.cloned.1.call-update) | async-done | bytes 262160 | tf_op jit(solution)/shard_map/reduce_scatter | solution.py:251
  863.7 79.9 %collective-permute-done.35 = bf16[1024,2048]{1,0:T(8,128)(2,1)S(1)} collective-permute-done((bf16[1024,2048]{1,0:T(8,128)(2,1)}, bf16[1024,2048]{1,0:T(8,128)(2,1)S(1)}, u32[]{:S(2)}, u32[]{:S(2)}) %collective-permute-start.35) | collective-permute-done | bytes 4194336 | tf_op jit(solution)/shard_map/ppermute | solution.py:175
  1017.7 19.7 %collective-permute-done.34 = f32[8,256]{1,0:T(8,128)S(1)} collective-permute-done((f32[8,256]{1,0:T(8,128)S(1)}, f32[8,256]{1,0:T(8,128)S(1)}, u32[]{:S(2)}, u32[]{:S(2)}) %collective-permute-start.34) | collective-permute-done | bytes 8224 | tf_op jit(solution)/shard_map/ppermute | solution.py:175
  1047.6 21.2 %collective-permute-done.38 = bf16[1024,2048]{1,0:T(8,128)(2,1)S(1)} collective-permute-done((bf16[1024,2048]{1,0:T(8,128)(2,1)}, bf16[1024,2048]{1,0:T(8,128)(2,1)S(1)}, u32[]{:S(2)}, u32[]{:S(2)}) %collective-permute-start.38) | collective-permute-done | bytes 4194336 | tf_op jit(solution)/shard_map/ppermute | solution.py:175
  1081.4 16.3 %fusion.23 = (f32[512,2048]{1,0:T(8,128)}, f32[512,2048]{1,0:T(8,128)}) fusion(bf16[512,2048]{1,0:T(8,128)(2,1)} %param.13, f32[512,2048]{1,0:T(8,128)} %get-tuple-element.145, bf16[512,2048]{1,0:T(8,128)(2,1)} %collective-permute-done.14, f32[512]{0:T(512)S(1)} %multiply_multiply_fusion, f32[2048]{0:T(1024)S(1)} %copy-done.70, f32[512]{0:T(512)S(1)} %copy-done.80, ...), kind=kLoop, calls=%fused_computation.49 | loop fusion | flops 22020096 | bytes 41967616 | tf_op jit(solution)/shard_map/add | solution.py:455
  1104.2 17.6 %collective-permute-done.22 = bf16[512,1024]{1,0:T(8,128)(2,1)} collective-permute-done((bf16[512,1024]{1,0:T(8,128)(2,1)}, bf16[512,1024]{1,0:T(8,128)(2,1)}, u32[]{:S(2)}, u32[]{:S(2)}) %collective-permute-start.22) | collective-permute-done | bytes 1048608 | tf_op jit(solution)/shard_map/ppermute | solution.py:175
  1126.2 18.0 %collective-permute-done.28 = bf16[256,2048]{1,0:T(8,128)(2,1)} collective-permute-done((bf16[256,2048]{1,0:T(8,128)(2,1)}, bf16[256,2048]{1,0:T(8,128)(2,1)}, u32[]{:S(2)}, u32[]{:S(2)}) %collective-permute-start.28) | collective-permute-done | bytes 1048608 | tf_op jit(solution)/shard_map/ppermute | solution.py:175
  1147.3 19.3 %collective-permute-done.41 = bf16[256,2048]{1,0:T(8,128)(2,1)} collective-permute-done((bf16[256,2048]{1,0:T(8,128)(2,1)}, bf16[256,2048]{1,0:T(8,128)(2,1)}, u32[]{:S(2)}, u32[]{:S(2)}) %collective-permute-start.41) | collective-permute-done | bytes 1048608 | tf_op jit(solution)/shard_map/ppermute | solution.py:175
  1166.7 20.5 %collective-permute-done.42 = bf16[256,2048]{1,0:T(8,128)(2,1)S(1)} collective-permute-done((bf16[256,2048]{1,0:T(8,128)(2,1)}, bf16[256,2048]{1,0:T(8,128)(2,1)S(1)}, u32[]{:S(2)}, u32[]{:S(2)}) %collective-permute-start.42) | collective-permute-done | bytes 1048608 | tf_op jit(solution)/shard_map/ppermute | solution.py:175
  1227.6 26.4 %reduce-scatter.16.cloned.1.call-done = bf16[256,2048]{1,0:T(8,128)(2,1)} async-done(((bf16[1024,2048]{1,0:T(8,128)(2,1)}), bf16[256,2048]{1,0:T(8,128)(2,1)}) %reduce-scatter.16.cloned.1.call-update) | async-done | bytes 1048592 | tf_op jit(solution)/shard_map/reduce_scatter | solution.py:251
  1263.3 15.5 %collective-permute-done.39 = bf16[256,2048]{1,0:T(8,128)(2,1)S(1)} collective-permute-done((bf16[256,2048]{1,0:T(8,128)(2,1)}, bf16[256,2048]{1,0:T(8,128)(2,1)S(1)}, u32[]{:S(2)}, u32[]{:S(2)}) %collective-permute-start.39) | collective-permute-done | bytes 1048608 | tf_op jit(solution)/shard_map/ppermute | solution.py:175
  (459 shorter events, 542.1 us)
Async XLA Ops:
  7.2 116.0 %all-gather.7.cloned.1.call-start = ((), (), s32[]{:S(2)}) async-start(), calls=%async_computation.7 | async-start | bytes 5242880 | tf_op jit(solution)/shard_map/all_gather | solution.py:247
  12.4 164.8 %all-gather.11.cloned.1.call-start = ((), (), s32[]{:S(2)}) async-start(), calls=%async_computation.9 | async-start | bytes 5242880 | tf_op jit(solution)/shard_map/all_gather | solution.py:247
  15.3 283.6 %all-gather.9.cloned.1.call-start = ((), (), s32[]{:S(2)}) async-start(), calls=%async_computation.8 | async-start | bytes 5242880 | tf_op jit(solution)/shard_map/all_gather | solution.py:247
  18.3 48.9 %collective-permute-start = (bf16[512,2048]{1,0:T(8,128)(2,1)}, bf16[512,2048]{1,0:T(8,128)(2,1)}, u32[]{:S(2)}, u32[]{:S(2)}) collective-permute-start(bf16[512,2048]{1,0:T(8,128)(2,1)} %fusion.26), channel_id=1, source_target_pairs={{0,1},{1,0},{2,3},{3,2},{4,5},{5,4},{6,7},{7,6},{8,9},{9,8},{10,11... | collective-permute-start | bytes 6291464 | tf_op jit(solution)/shard_map/ppermute | solution.py:175
  22.9 799.4 %reduce-scatter.8.cloned.1.call-start = ((), (), s32[]{:S(2)}) async-start(), calls=%async_computation.10 | async-start | bytes 1310720 | tf_op jit(solution)/shard_map/reduce_scatter | solution.py:251
  123.1 68.5 %collective-permute-start.10 = (bf16[1024,2048]{1,0:T(8,128)(2,1)}, bf16[1024,2048]{1,0:T(8,128)(2,1)}, u32[]{:S(2)}, u32[]{:S(2)}) collective-permute-start(bf16[1024,2048]{1,0:T(8,128)(2,1)} %pad_maximum_fusion.3), channel_id=1, source_target_pairs={{0,8},{8,0},{16,24},{24,16},{1,9},{9,1},{17,25},{25,17},{2,10},{10... | collective-permute-start | bytes 12582920 | tf_op jit(solution)/shard_map/ppermute | solution.py:175
  129.4 52.0 %collective-permute-start.1 = (bf16[512,2048]{1,0:T(8,128)(2,1)}, bf16[512,2048]{1,0:T(8,128)(2,1)}, u32[]{:S(2)}, u32[]{:S(2)}) collective-permute-start(bf16[512,2048]{1,0:T(8,128)(2,1)} %convolution_convert_fusion.13), channel_id=1, source_target_pairs={{0,1},{1,0},{2,3},{3,2},{4,5},{5,4},{6,7},{7,6},{8,9},{9,8},{10,11... | collective-permute-start | bytes 6291464 | tf_op jit(solution)/shard_map/ppermute | solution.py:175
  146.7 141.1 %collective-permute-start.6 = (bf16[768,2048]{1,0:T(8,128)(2,1)}, bf16[768,2048]{1,0:T(8,128)(2,1)}, u32[]{:S(2)}, u32[]{:S(2)}) collective-permute-start(bf16[768,2048]{1,0:T(8,128)(2,1)} %pad_maximum_fusion.7), channel_id=1, source_target_pairs={{0,16},{8,24},{16,0},{24,8},{1,17},{9,25},{17,1},{25,9},{2,18},{10... | collective-permute-start | bytes 9437192 | tf_op jit(solution)/shard_map/ppermute | solution.py:175
  179.8 104.8 %collective-permute-start.5 = (bf16[768,2048]{0,1:T(8,128)(2,1)S(1)}, bf16[768,2048]{0,1:T(8,128)(2,1)S(1)}, u32[]{:S(2)}, u32[]{:S(2)}) collective-permute-start(bf16[768,2048]{0,1:T(8,128)(2,1)S(1)} %pad_maximum_fusion.6), channel_id=1, source_target_pairs={{0,16},{8,24},{16,0},{24,8},{1,17},{9,25},{17,1},{25,9},{2,18},{10... | collective-permute-start | bytes 9437192 | tf_op jit(solution)/shard_map/ppermute | solution.py:175
  190.2 104.6 %collective-permute-start.2 = (bf16[512,2048]{1,0:T(8,128)(2,1)S(1)}, bf16[512,2048]{1,0:T(8,128)(2,1)}, u32[]{:S(2)}, u32[]{:S(2)}) collective-permute-start(bf16[512,2048]{1,0:T(8,128)(2,1)S(1)} %multiply_convert_fusion), channel_id=1, source_target_pairs={{0,1},{1,0},{2,3},{3,2},{4,5},{5,4},{6,7},{7,6},{8,9},{9,8},{10,11... | collective-permute-start | bytes 6291464 | tf_op jit(solution)/shard_map/ppermute | solution.py:175
  302.8 69.7 %collective-permute-start.4 = (bf16[768,2048]{0,1:T(8,128)(2,1)}, bf16[768,2048]{0,1:T(8,128)(2,1)}, u32[]{:S(2)}, u32[]{:S(2)}) collective-permute-start(bf16[768,2048]{0,1:T(8,128)(2,1)} %pad_maximum_fusion.5), channel_id=1, source_target_pairs={{0,16},{8,24},{16,0},{24,8},{1,17},{9,25},{17,1},{25,9},{2,18},{10... | collective-permute-start | bytes 9437192 | tf_op jit(solution)/shard_map/ppermute | solution.py:175
  306.9 74.6 %collective-permute-start.3 = (bf16[1024,2048]{1,0:T(8,128)(2,1)}, bf16[1024,2048]{1,0:T(8,128)(2,1)}, u32[]{:S(2)}, u32[]{:S(2)}) collective-permute-start(bf16[1024,2048]{1,0:T(8,128)(2,1)} %pad_maximum_fusion.2), channel_id=1, source_target_pairs={{0,8},{8,0},{16,24},{24,16},{1,9},{9,1},{17,25},{25,17},{2,10},{10... | collective-permute-start | bytes 12582920 | tf_op jit(solution)/shard_map/ppermute | solution.py:175
  759.8 63.2 %reduce-scatter.10.cloned.1.call-start = ((), (), s32[]{:S(2)}) async-start(), calls=%async_computation.12 | async-start | bytes 1310720 | tf_op jit(solution)/shard_map/reduce_scatter | solution.py:251
  791.6 58.4 %reduce-scatter.12.cloned.1.call-start = ((), (), s32[]{:S(2)}) async-start(), calls=%async_computation.14 | async-start | bytes 1310720 | tf_op jit(solution)/shard_map/reduce_scatter | solution.py:251
  822.2 250.6 %all-gather.13.cloned.1.call-start = ((), (), s32[]{:S(2)}) async-start(), calls=%async_computation.11 | async-start | bytes 1310720 | tf_op jit(solution)/shard_map/all_gather | solution.py:247
  823.0 250.5 %all-gather.15.cloned.1.call-start = ((), (), s32[]{:S(2)}) async-start(), calls=%async_computation.13 | async-start | bytes 1310720 | tf_op jit(solution)/shard_map/all_gather | solution.py:247
  823.7 251.2 %all-gather.17.cloned.1.call-start = ((), (), s32[]{:S(2)}) async-start(), calls=%async_computation.15 | async-start | bytes 1310720 | tf_op jit(solution)/shard_map/all_gather | solution.py:247
  850.0 252.1 %reduce-scatter.20.cloned.1.call-start = ((), (), s32[]{:S(2)}) async-start(), calls=%async_computation.19 | async-start | bytes 5242880 | tf_op jit(solution)/shard_map/reduce_scatter | solution.py:251
  850.6 252.0 %reduce-scatter.18.cloned.1.call-start = ((), (), s32[]{:S(2)}) async-start(), calls=%async_computation.18 | async-start | bytes 5242880 | tf_op jit(solution)/shard_map/reduce_scatter | solution.py:251
  851.4 363.3 %reduce-scatter.14.cloned.1.call-start = ((), (), s32[]{:S(2)}) async-start(), calls=%async_computation.16 | async-start | bytes 5242880 | tf_op jit(solution)/shard_map/reduce_scatter | solution.py:251
  851.4 92.2 %collective-permute-start.35 = (bf16[1024,2048]{1,0:T(8,128)(2,1)}, bf16[1024,2048]{1,0:T(8,128)(2,1)S(1)}, u32[]{:S(2)}, u32[]{:S(2)}) collective-permute-start(bf16[1024,2048]{1,0:T(8,128)(2,1)} %convolution_convert_fusion.2), channel_id=1, source_target_pairs={{0,16},{8,24},{16,0},{24,8},{1,17},{9,25},{17,1},{25,9},{2,18},{10... | collective-permute-start | bytes 12582920 | tf_op jit(solution)/shard_map/ppermute | solution.py:175
  947.7 306.2 %reduce-scatter.16.cloned.1.call-start = ((), (), s32[]{:S(2)}) async-start(), calls=%async_computation.17 | async-start | bytes 5242880 | tf_op jit(solution)/shard_map/reduce_scatter | solution.py:251
  976.1 92.6 %collective-permute-start.38 = (bf16[1024,2048]{1,0:T(8,128)(2,1)}, bf16[1024,2048]{1,0:T(8,128)(2,1)S(1)}, u32[]{:S(2)}, u32[]{:S(2)}) collective-permute-start(bf16[1024,2048]{1,0:T(8,128)(2,1)} %convolution_convert_fusion), channel_id=1, source_target_pairs={{0,16},{8,24},{16,0},{24,8},{1,17},{9,25},{17,1},{25,9},{2,18},{10... | collective-permute-start | bytes 12582920 | tf_op jit(solution)/shard_map/ppermute | solution.py:175
  988.6 49.5 %collective-permute-start.14 = (bf16[512,2048]{1,0:T(8,128)(2,1)}, bf16[512,2048]{1,0:T(8,128)(2,1)}, u32[]{:S(2)}, u32[]{:S(2)}) collective-permute-start(bf16[512,2048]{1,0:T(8,128)(2,1)} %convolution_convert_fusion.14), channel_id=1, source_target_pairs={{0,1},{1,0},{2,3},{3,2},{4,5},{5,4},{6,7},{7,6},{8,9},{9,8},{10,11... | collective-permute-start | bytes 6291464 | tf_op jit(solution)/shard_map/ppermute | solution.py:175
  1017.3 64.1 %collective-permute-start.8 = (bf16[512,2048]{1,0:T(8,128)(2,1)}, bf16[512,2048]{1,0:T(8,128)(2,1)}, u32[]{:S(2)}, u32[]{:S(2)}) collective-permute-start(bf16[512,2048]{1,0:T(8,128)(2,1)} %fusion.30), channel_id=1, source_target_pairs={{0,1},{1,0},{2,3},{3,2},{4,5},{5,4},{6,7},{7,6},{8,9},{9,8},{10,11... | collective-permute-start | bytes 6291464 | tf_op jit(solution)/shard_map/ppermute | solution.py:175
  1074.9 69.3 %collective-permute-start.28 = (bf16[256,2048]{1,0:T(8,128)(2,1)}, bf16[256,2048]{1,0:T(8,128)(2,1)}, u32[]{:S(2)}, u32[]{:S(2)}) collective-permute-start(bf16[256,2048]{1,0:T(8,128)(2,1)} %all-gather.17.cloned.1.call-done), channel_id=1, source_target_pairs={{0,16},{8,24},{16,0},{24,8},{1,17},{9,25},{17,1},{25,9},{2,18},{10... | collective-permute-start | bytes 3145736 | tf_op jit(solution)/shard_map/ppermute | solution.py:175
  1102.1 89.7 %collective-permute-start.18 = (bf16[1024,1024]{1,0:T(8,128)(2,1)}, bf16[1024,1024]{1,0:T(8,128)(2,1)}, u32[]{:S(2)}, u32[]{:S(2)}) collective-permute-start(bf16[1024,1024]{1,0:T(8,128)(2,1)} %pad_maximum_fusion.9), channel_id=1, source_target_pairs={{0,8},{8,0},{16,24},{24,16},{1,9},{9,1},{17,25},{25,17},{2,10},{10... | collective-permute-start | bytes 6291464 | tf_op jit(solution)/shard_map/ppermute | solution.py:175
  1102.1 64.5 %collective-permute-start.41 = (bf16[256,2048]{1,0:T(8,128)(2,1)}, bf16[256,2048]{1,0:T(8,128)(2,1)}, u32[]{:S(2)}, u32[]{:S(2)}) collective-permute-start(bf16[256,2048]{1,0:T(8,128)(2,1)} %reduce-scatter.20.cloned.1.call-done), channel_id=1, source_target_pairs={{0,16},{8,24},{16,0},{24,8},{1,17},{9,25},{17,1},{25,9},{2,18},{10... | collective-permute-start | bytes 3145736 | tf_op jit(solution)/shard_map/ppermute | solution.py:175
  1102.7 84.5 %collective-permute-start.42 = (bf16[256,2048]{1,0:T(8,128)(2,1)}, bf16[256,2048]{1,0:T(8,128)(2,1)S(1)}, u32[]{:S(2)}, u32[]{:S(2)}) collective-permute-start(bf16[256,2048]{1,0:T(8,128)(2,1)} %reduce-scatter.18.cloned.1.call-done), channel_id=1, source_target_pairs={{0,16},{8,24},{16,0},{24,8},{1,17},{9,25},{17,1},{25,9},{2,18},{10... | collective-permute-start | bytes 3145736 | tf_op jit(solution)/shard_map/ppermute | solution.py:175
  1124.7 75.5 %collective-permute-start.23 = (bf16[1024,1024]{1,0:T(8,128)(2,1)}, bf16[1024,1024]{1,0:T(8,128)(2,1)}, u32[]{:S(2)}, u32[]{:S(2)}) collective-permute-start(bf16[1024,1024]{1,0:T(8,128)(2,1)} %pad_maximum_fusion.8), channel_id=1, source_target_pairs={{0,1},{1,0},{2,3},{3,2},{4,5},{5,4},{6,7},{7,6},{8,9},{9,8},{10,11... | collective-permute-start | bytes 6291464 | tf_op jit(solution)/shard_map/ppermute | solution.py:175
  1147.3 60.2 %collective-permute-start.29 = (bf16[512,2048]{1,0:T(8,128)(2,1)}, bf16[512,2048]{1,0:T(8,128)(2,1)}, u32[]{:S(2)}, u32[]{:S(2)}) collective-permute-start(bf16[512,2048]{1,0:T(8,128)(2,1)} %pad_maximum_fusion.12), channel_id=1, source_target_pairs={{0,8},{8,0},{16,24},{24,16},{1,9},{9,1},{17,25},{25,17},{2,10},{10... | collective-permute-start | bytes 6291464 | tf_op jit(solution)/shard_map/ppermute | solution.py:175
  1207.0 51.3 %collective-permute-start.25 = (bf16[1024,1024]{1,0:T(8,128)(2,1)}, bf16[1024,1024]{1,0:T(8,128)(2,1)}, u32[]{:S(2)}, u32[]{:S(2)}) collective-permute-start(bf16[1024,1024]{1,0:T(8,128)(2,1)} %pad_maximum_fusion.11), channel_id=1, source_target_pairs={{0,8},{8,0},{16,24},{24,16},{1,9},{9,1},{17,25},{25,17},{2,10},{10... | collective-permute-start | bytes 6291464 | tf_op jit(solution)/shard_map/ppermute | solution.py:175
  (126 other events, 2068.7 us)
Sparse Core Ops, SparseCore 0:
  12.6 83.4 all-gather.6
  98.2 79.0 all-gather.10
  179.4 78.7 all-gather.8
  759.9 27.6 reduce-scatter.7
  791.7 27.6 reduce-scatter.9
  822.4 27.6 reduce-scatter.11
  851.6 26.4 all-gather.12
  879.7 27.3 all-gather.14
  908.6 27.3 all-gather.16
  938.2 76.5 reduce-scatter.19
  1017.0 77.2 reduce-scatter.17
  1096.4 77.2 reduce-scatter.13
  1176.6 77.2 reduce-scatter.15

commit v3 on v2

--- a/solution.py
+++ b/solution.py
@@ -229,6 +229,35 @@
     return [lax.slice_in_dim(value, i * size, (i + 1) * size, axis=dim) for i in range(count)]
 
 
+def square_gather(for_x, for_y):
+    if lax.axis_size("col") == 2:
+        over_y = swap(for_y, "grp", 2)
+        over_x = swap(for_x, "col", 1)
+        half = for_x.shape[0] // 2
+        across_first = swap(over_x[:half], "grp", 2)
+        across_second = swap(over_y[half:], "col", 1)
+        near = jnp.concatenate([for_x, over_x], axis=0)
+        return near, jnp.concatenate([over_y, across_first, across_second], axis=0)
+    near = lax.all_gather(for_x, "col", axis=0, tiled=True)
+    return near, swap(near, "grp", 2)
+
+
+def square_scatter(near, far):
+    size = far.shape[0]
+    if lax.axis_size("col") == 2:
+        half, part = size // 2, size // 4
+        across_first = swap(far[half : half + part], "grp", 2)
+        across_second = swap(far[half + part :], "col", 1)
+        rest = jnp.zeros_like(across_first)
+        to_y = low(wide(far[:half]) + wide(jnp.concatenate([rest, across_second], axis=0)))
+        to_x = low(near(half, size) + wide(jnp.concatenate([across_first, rest], axis=0)))
+        from_y = swap(to_y, "grp", 2)
+        from_x = swap(to_x, "col", 1)
+        return near(0, half) + wide(from_x) + wide(from_y)
+    total = low(near(0, size) + wide(swap(far, "grp", 2)))
+    return wide(lax.psum_scatter(total, "col", scatter_dimension=0, tiled=True))
+
+
 def butterfly(value, axes):
     for axis in axes:
         bit = 1
@@ -265,48 +294,14 @@
     return ordered(core, part, swap(part, "grp", 1), 0)
 
 
-def own_quarters(weight, core, ypos):
+def own_quarter(weight, core, ypos):
     size = weight.shape[0] // 4
-    mine = lax.dynamic_slice_in_dim(weight, (2 * core + ypos) * size, size, 0)
-    other = lax.dynamic_slice_in_dim(weight, (2 * core + 1 - ypos) * size, size, 0)
-    return mine, other
-
-
-def other_quarters(mines, other, zpos):
-    count = lax.axis_size("row")
-    size = other.shape[0]
-    turned = jnp.concatenate(
-        [
-            lax.dynamic_slice_in_dim(mines, lax.rem(zpos + k, count) * size, size, 0)
-            for k in range(1, count)
-        ],
-        axis=0,
-    )
-    theirs = swap(turned, "grp", 2)
-    others = lax.dynamic_update_slice_in_dim(jnp.zeros_like(mines), other, zpos * size, 0)
-    for k in range(1, count):
-        others = lax.dynamic_update_slice_in_dim(
-            others,
-            lax.slice_in_dim(theirs, (k - 1) * size, k * size, axis=0),
-            lax.rem(zpos + k, count) * size,
-            0,
-        )
-    return others
-
-
-def sum_y_first(keep, give, core, ypos):
-    part = low(wide(keep) + wide(swap(give, "grp", 2)))
-    mine = row_scatter(part)
-    return spread_core(spread_y(mine, ypos), core)
-
-
-def sum_z_first(keep, give, core, ypos):
-    mine, other = row_scatter(keep), row_scatter(give)
-    mine, other = (
-        low(wide(mine) + wide(swap(other, "grp", 2))),
-        low(wide(other) + wide(swap(mine, "grp", 2))),
-    )
-    return spread_core(ordered(ypos, mine, other, 0), core)
+    return lax.dynamic_slice_in_dim(weight, (2 * core + ypos) * size, size, 0)
+
+
+def spread_quarters(part, core, ypos, dim):
+    half = ordered(ypos, part, swap(part, "grp", 2), dim)
+    return wide(ordered(core, half, swap(half, "grp", 1), dim))
 
 
 def per_device(
@@ -344,14 +339,16 @@
     gathered_in = jnp.concatenate(col_gather(low(normalized_input)), axis=0)
     packed_length = gathered_in.shape[0]
 
-    down_mine, down_other = own_quarters(down_weight, core, ypos)
-    gate_mine, gate_other = own_quarters(gate_weight.T, core, ypos)
-    up_mine, up_other = own_quarters(up_weight.T, core, ypos)
-    down_mines, gate_mines, up_mines = [row_gather(m) for m in (down_mine, gate_mine, up_mine)]
+    down_rows, gate_rows, up_rows = [
+        row_gather(own_quarter(weight, core, ypos))
+        for weight in (down_weight, gate_weight.T, up_weight.T)
+    ]
 
     gathered_in, cot_now = tie(gathered_in, cotangent)
-    cot_pack = jnp.concatenate(col_gather(cot_now), axis=0)
-    cot_all = jnp.concatenate([cot_pack, swap(cot_pack, "grp", 1)], axis=0)
+    cot_sets = [
+        jnp.concatenate([pack, swap(pack, "grp", 1)], axis=0)
+        for pack in square_gather(cot_now, cotangent)
+    ]
 
     key_slice = lax.dynamic_slice_in_dim(key_matrix, key_first * head_dim, key_cols, 1)
     value_slice = lax.dynamic_slice_in_dim(value_matrix, key_first * head_dim, key_cols, 1)
@@ -377,57 +374,53 @@
         head_dim,
         (3 * score_flops, key_heads),
     )
-    attn_low, down_mines = tie(attn_low, down_mines)
-    down_all = [down_mines, other_quarters(down_mines, down_other, zpos)]
+    attn_low, down_rows = tie(attn_low, down_rows)
+    act_grads = [low(dot_nt(cot, down_rows)) for cot in cot_sets]
     attn_parts = blocks_of(attn_low, 0, 2) if in_pairs else [attn_low]
     hidden_res = inputs + col_scatter(lambda i: dot32(attn_parts[i], output_weight))
     normed_mid, second_back = jax.vjp(normalize, hidden_res, second_gain)
 
-    mid_pack = jnp.concatenate(col_gather(low(normed_mid)), axis=0)
-    mid_pack, gate_mines = tie(mid_pack, gate_mines)
-    gate_all = [gate_mines, other_quarters(gate_mines, gate_other, zpos)]
-    up_all = [up_mines, other_quarters(up_mines, up_other, zpos)]
-    mid_all = jnp.concatenate([mid_pack, swap(mid_pack, "grp", 1)], axis=0)
+    normed_low = low(normed_mid)
+    mid_sets = [
+        jnp.concatenate([pack, swap(pack, "grp", 1)], axis=0)
+        for pack in square_gather(normed_low, normed_low)
+    ]
     acts, gate_backs, up_backs = [], [], []
-    for gate_rows, up_rows, down_rows in zip(gate_all, up_all, down_all):
-        act_grad = low(dot_nt(cot_all, down_rows))
-        gate32 = wide(low(dot_nt(mid_all, gate_rows)))
-        up_lin = dot_nt(mid_all, up_rows)
+    for mid, act_grad in zip(mid_sets, act_grads):
+        gate32 = wide(low(dot_nt(mid, gate_rows)))
+        up_lin = dot_nt(mid, up_rows)
         sig = jax.nn.sigmoid(gate32)
         acts.append(low(gate32 * sig * up_lin))
         gate_backs.append(low(wide(act_grad) * up_lin * sig * (1 + gate32 * (1 - sig))))
         up_backs.append(low(wide(act_grad) * gate32 * sig))
-    down_parts = [low(dot_tn(act, cot_all)) for act in acts]
-    gate_parts = [low(dot_tn(back, mid_all)) for back in gate_backs]
-    up_parts = [low(dot_tn(back, mid_all)) for back in up_backs]
 
     def token_sum(product):
-        both = mid_all.shape[0]
-        pack = both // 2
-        from_core = wide(swap(low(product(pack, both)), "grp", 1))
-        if not in_pairs:
-            return col_scatter(lambda i: product(0, pack) + from_core)
-        half = pack // 2
-        parts = blocks_of(from_core, 0, 2)
-        return col_scatter(lambda i: product(i * half, (i + 1) * half) + parts[i])
-
-    def over_hidden(a, b, *pairs):
-        return sum(dot32(left[a:b], right) for lefts, rights in pairs for left, right in zip(lefts, rights))
+        pack = packed_length
+        far = low(
+            product(1, 0, pack) + wide(swap(low(product(1, pack, 2 * pack)), "grp", 1))
+        )
+        from_core = wide(swap(low(product(0, pack, 2 * pack)), "grp", 1))
+        return square_scatter(
+            lambda first, last: product(0, first, last) + from_core[first:last], far
+        )
 
     mid_grad = token_sum(
-        lambda a, b: over_hidden(a, b, (gate_backs, gate_all), (up_backs, up_all))
-    )
-    layer_out = hidden_res + token_sum(lambda a, b: over_hidden(a, b, (acts, down_all)))
+        lambda i, a, b: dot32(gate_backs[i][a:b], gate_rows) + dot32(up_backs[i][a:b], up_rows)
+    )
+
+    def weight_part(lefts, rights):
+        return row_scatter(low(sum(dot_tn(left, right) for left, right in zip(lefts, rights))))
+
+    down_part = weight_part(acts, cot_sets)
+    gate_part = weight_part(gate_backs, mid_sets)
+    up_part = weight_part(up_backs, mid_sets)
+    layer_out = hidden_res + token_sum(lambda i, a, b: dot32(acts[i][a:b], down_rows))
 
     res_from_mid, second_gain_part = second_back(mid_grad)
     res_grad = wide(cotangent) + res_from_mid
     shard_rows = jnp.concatenate(col_gather(low(res_grad)), axis=0)
-    shard_rows, *parts = tie(shard_rows, *down_parts, *gate_parts, *up_parts)
-    down_grad = sum_z_first(*parts[:2], core, ypos)
-    gate_grad = sum_y_first(*parts[2:4], core, ypos)
-    up_grad = sum_y_first(*parts[4:], core, ypos)
-    out_wgrad = sum_quarters(low(dot_tn(attn_low, shard_rows)), core, ypos)
-    out_wgrad = spread_core(spread_y(out_wgrad, ypos), core)
+    shard_rows, down_part = tie(shard_rows, down_part)
+    out_part = sum_quarters(low(dot_tn(attn_low, shard_rows)), core, ypos)
     mixed_low = low(dot_nt(shard_rows, output_weight))
     query_back, key_back, value_back = attention_call(
         attend_back_kernel,
@@ -451,19 +444,24 @@
     pair_part = sum_quarters(low(dot_tn(gathered_in, pair_back)), core, ypos)
     back_parts = blocks_of(back_all, 0, 2) if in_pairs else [back_all]
     in_grad = col_scatter(lambda i: dot_nt(back_parts[i], project_in))
+    in_grad, gate_part = tie(in_grad, gate_part)
     res_from_in, _ = first_back(in_grad)
     input_grad = res_grad + res_from_in
 
-    query_wgrad = wide(spread_core(spread_y(query_part, ypos), core))
-    pair_part = spread_y(pair_part, ypos)
+    down_grad = spread_quarters(down_part, core, ypos, 0)
+    gate_grad = spread_quarters(gate_part.T, core, ypos, 1)
+    up_grad = spread_quarters(up_part.T, core, ypos, 1)
+    out_wgrad = spread_quarters(out_part, core, ypos, 0)
+    query_wgrad = spread_quarters(query_part, core, ypos, 0)
+    pair_part = ordered(ypos, pair_part, swap(pair_part, "grp", 2), 0)
     if in_pairs:
         theirs = swap(pair_part, "col", 1)
         key_part = ordered(col, pair_part[:, :key_cols], theirs[:, :key_cols], 1)
         value_part = ordered(col, pair_part[:, key_cols:], theirs[:, key_cols:], 1)
-        key_full = wide(spread_core(key_part, core))
-        value_full = wide(spread_core(value_part, core))
+        key_full = wide(ordered(core, key_part, swap(key_part, "grp", 1), 0))
+        value_full = wide(ordered(core, value_part, swap(value_part, "grp", 1), 0))
     else:
-        pair_part = spread_core(pair_part, core)
+        pair_part = ordered(core, pair_part, swap(pair_part, "grp", 1), 0)
         pair_all = wide(lax.all_gather(pair_part, "col", axis=0))
         groups = lax.axis_size("col") // head_sharing
 
@@ -486,11 +484,11 @@
         query_wgrad,
         key_full,
         value_full,
-        wide(out_wgrad),
+        out_wgrad,
         second_gain_grad,
-        wide(gate_grad).T,
-        wide(up_grad).T,
-        wide(down_grad),
+        gate_grad,
+        up_grad,
+        down_grad,
     )
 
 

time: 1330 us -> 1100 us (0.83)
  waiting for transfers between devices: 595 us -> 401 us
  local copies, waits for them, and re-layouts: 115 us -> 85.8 us
  matrix products: 378 us -> 353 us
  starting transfers between devices: 37.7 us -> 51.7 us
    ppermute x44 -> x54, waiting for transfers between devices: 511 us -> 397 us  [swap(): return lax.ppermute(value, axis, [(i, i ^ bit) for i in range(count)])]
    reduce_scatter x7 -> x6, waiting for transfers between devices: 52.7 us -> 0.05 us  [row_scatter(): return lax.psum_scatter(value, 'row', scatter_dimension=0, tiled=True)]
    dot_general x21 -> x18, matrix products: 166 us -> 130 us  [dot32(): return jnp.dot(left, right, preferred_element_type=jnp.float32)]
    all_gather x6, waiting for transfers between devices: 29 us -> 3.84 us  [row_gather(): return lax.all_gather(value, 'row', axis=0, tiled=True)]
    dynamic_update_slice x12 -> x0, local copies, waits for them, and re-layouts: 16.8 us -> none  [the longest x9 13.3 us: other_quarters(): lax.dynamic_update_slice_in_dim(others, lax.slice_in_dim(theirs, (k - 1)...]
    convert_element_type x4 -> x6, other arithmetic: 13 us -> 29.6 us  [wide(): return value.astype(jnp.float32)]
    ppermute x44 -> x54, starting transfers between devices: 36.7 us -> 50.4 us  [swap(): return lax.ppermute(value, axis, [(i, i ^ bit) for i in range(count)])]
    unnamed x211 -> x192, local copies, waits for them, and re-layouts: 46.6 us -> 48 us
  transfers between devices with their start and end apart: 57 -> 66, of which waited for: 23 -> 20; matrix products, arithmetic and copies ran while one was open for 31% -> 51% of each run, Pallas kernels for 1% -> 3%
where the time goes in v3:
time: 1100 us
  waiting for transfers between devices  401 us (36%)
  matrix products  353 us (32%)
  other arithmetic  156 us (14%)
  local copies, waits for them, and re-layouts  85.8 us (8%)
  starting transfers between devices  51.7 us (5%)
  Pallas kernels  32.5 us (3%)
  between operations  15.7 us (1%)
    ppermute x54, waiting for transfers between devices, swap(): return lax.ppermute(value, axis, [(i, i ^ bit) for i in range(count)])  397 us
    dot_general x18, matrix products, dot32(): return jnp.dot(left, right, preferred_element_type=jnp.float32)  130 us
    dot_general x9, matrix products, dot_nt(): jnp.einsum('td,fd->tf', left, right, preferred_element_type=jnp.float32)  119 us
    dot_general x9, matrix products, dot_tn(): jnp.einsum('td,tf->df', left, right, preferred_element_type=jnp.float32)  104 us
    ppermute x54, starting transfers between devices, swap(): return lax.ppermute(value, axis, [(i, i ^ bit) for i in range(count)])  50.4 us
    unnamed x192, local copies, waits for them, and re-layouts  48 us
    pallas_call x2, Pallas kernels, attention_call(): pl.pallas_call(kernel, grid_spec=pltpu.PrefetchScalarGridSpec(num_scalar_...  32.5 us
    select_n x14, other arithmetic, ordered(): jnp.where(keep, mine, theirs)  32.4 us
  transfers between devices with their start and end apart: 66, of which 20 were waited for; matrix products, arithmetic and copies ran while one was open for 51% of the time, Pallas kernels for 3%

profile of v3, /device:TPU:0, one launch (start us, length us, event | category | flops | bytes accessed | tf_op | source)
XLA Modules:
  0.0 1095.2 jit_solution(13971939945021673098)
XLA Ops:
  27.3 34.4 %collective-permute-done = bf16[512,2048]{1,0:T(8,128)(2,1)} collective-permute-done((bf16[512,2048]{1,0:T(8,128)(2,1)}, bf16[512,2048]{1,0:T(8,128)(2,1)}, u32[]{:S(2)}, u32[]{:S(2)}) %collective-permute-start) | collective-permute-done | bytes 2097184 | tf_op jit(solution)/shard_map/ppermute | solution.py:175
  66.1 11.4 %fusion.86.q_ref.k_ref.v_ref = f32[1024,2048]{1,0:T(8,128)} fusion(bf16[1024,2048]{1,0:T(8,128)(2,1)S(1)} %pad_maximum_fusion.2, bf16[2048,512]{1,0:T(8,128)(2,1)S(1)} %get-tuple-element.117, bf16[2048,512]{1,0:T(8,128)(2,1)S(1)} %get-tuple-element.118, bf16[2048,1024]{1,0:T(8,128)(2,1)S(1)} %copy-done.37), kind=kOutput, calls=%fused_computation.223 | convolution fusion | flops 8615100416 | bytes 20971520 | tf_op jit(solution)/shard_map/dot_general | solution.py:195
  77.4 12.4 %attend.1 = (bf16[1024,1024]{1,0:T(8,128)(2,1)}, bf16[1024,1024]{1,0:T(8,128)(2,1)}, bf16[1024,512]{1,0:T(8,128)(2,1)}, bf16[1024,512]{1,0:T(8,128)(2,1)}) custom-call(s32[1]{0:T(128)} %bitcast.first_ref, f32[1024,2048]{1,0:T(8,128)} %fusion.86.q_ref.k_ref.v_ref, f32[1024,2048]{1,0:T(8,128)} %fusion.86.q_ref.k_ref.v_ref, ...), custom_call_target="tpu_custom_call" | custom-call | flops 3221225472 | bytes 16106127 | tf_op jit(solution)/shard_map/attend/pallas_call | solution.py:153
  100.0 13.1 %collective-permute-done.14 = bf16[512,2048]{1,0:T(8,128)(2,1)} collective-permute-done((bf16[512,2048]{1,0:T(8,128)(2,1)}, bf16[512,2048]{1,0:T(8,128)(2,1)}, u32[]{:S(2)}, u32[]{:S(2)}) %collective-permute-start.14) | collective-permute-done | bytes 2097184 | tf_op jit(solution)/shard_map/ppermute | solution.py:175
  126.2 31.8 %collective-permute-done.1 = bf16[512,2048]{1,0:T(8,128)(2,1)S(1)} collective-permute-done((bf16[512,2048]{1,0:T(8,128)(2,1)S(1)}, bf16[512,2048]{1,0:T(8,128)(2,1)S(1)}, u32[]{:S(2)}, u32[]{:S(2)}) %collective-permute-start.1) | collective-permute-done | bytes 2097184 | tf_op jit(solution)/shard_map/ppermute | solution.py:175
  167.3 13.2 %collective-permute-done.19 = bf16[256,2048]{1,0:T(8,128)(2,1)S(1)} collective-permute-done((bf16[256,2048]{1,0:T(8,128)(2,1)}, bf16[256,2048]{1,0:T(8,128)(2,1)S(1)}, u32[]{:S(2)}, u32[]{:S(2)}) %collective-permute-start.19) | collective-permute-done | bytes 1048608 | tf_op jit(solution)/shard_map/ppermute | solution.py:175
  198.3 25.5 %collective-permute-done.2 = bf16[512,2048]{1,0:T(8,128)(2,1)} collective-permute-done((bf16[512,2048]{1,0:T(8,128)(2,1)S(1)}, bf16[512,2048]{1,0:T(8,128)(2,1)}, u32[]{:S(2)}, u32[]{:S(2)}) %collective-permute-start.2) | collective-permute-done | bytes 2097184 | tf_op jit(solution)/shard_map/ppermute | solution.py:175
  228.0 13.9 %convolution_convert_fusion.1 = bf16[2048,1024]{1,0:T(8,128)(2,1)} fusion(bf16[2048,2048]{1,0:T(8,128)(2,1)} %constant_dynamic-update-slice_fusion.4, bf16[1024,2048]{1,0:T(8,128)(2,1)} %all-gather.7.cloned.1.call-done), kind=kOutput, calls=%fused_computation.93 | convolution fusion | flops 8592031744 | bytes 16777216 | tf_op jit(solution)/shard_map/td,fd->tf/dot_general | solution.py:199
  248.4 10.5 convolution_convert_fusion
  276.8 14.7 %convolution_convert_fusion.3 = bf16[2048,1024]{1,0:T(8,128)(2,1)} fusion(bf16[1024,2048]{0,1:T(8,128)(2,1)} %all-gather.9.cloned.1.call-done, bf16[1024,2048]{1,0:T(8,128)(2,1)} %collective-permute-done.3, bf16[512,2048]{1,0:T(8,128)(2,1)} %collective-permute-done.2, bf16[512,2048]{1,0:T(8,128)(2,1)S(1)} %multiply_convert_fusion), kind=kOutput, calls=%fused_computation.95 | convolution fusion | flops 8617197568 | bytes 16777216 | tf_op jit(solution)/shard_map/td,fd->tf/dot_general | solution.py:199
  291.5 21.0 %fusion.2 = (bf16[2048,1024]{1,0:T(8,128)(2,1)}, bf16[2048,1024]{1,0:T(8,128)(2,1)}, bf16[2048,1024]{1,0:T(8,128)(2,1)}) fusion(bf16[2048,1024]{1,0:T(8,128)(2,1)} %convolution_convert_fusion.1, bf16[2048,1024]{1,0:T(8,128)(2,1)} %convolution_convert_fusion.3, bf16[1024,2048]{0,1:T(8,128)(2,1)} %all-gather.11.cloned.1.call-done, ...), kind=kOutput, calls=%fused_computation.12 | convolution fusion | flops 8652849152 | bytes 33554432 | tf_op jit(solution)/shard_map/td,fd->tf/dot_general | solution.py:199
  312.5 10.9 fusion.49
  337.4 12.6 %convolution_convert_fusion.2 = bf16[2048,1024]{1,0:T(8,128)(2,1)} fusion(bf16[2048,2048]{1,0:T(8,128)(2,1)} %constant_dynamic-update-slice_fusion, bf16[1024,2048]{0,1:T(8,128)(2,1)S(1)} %copy-done.75), kind=kOutput, calls=%fused_computation.94 | convolution fusion | flops 8592031744 | bytes 16777216 | tf_op jit(solution)/shard_map/td,fd->tf/dot_general | solution.py:199
  350.0 20.4 %fusion.5 = (bf16[2048,1024]{1,0:T(8,128)(2,1)S(1)}, bf16[2048,1024]{1,0:T(8,128)(2,1)}, bf16[2048,1024]{1,0:T(8,128)(2,1)}) fusion(bf16[2048,1024]{1,0:T(8,128)(2,1)} %convolution_convert_fusion, bf16[2048,1024]{1,0:T(8,128)(2,1)} %convolution_convert_fusion.2, bf16[2048,2048]{1,0:T(8,128)(2,1)} %constant_dynamic-update-slice_fusion, ...), kind=kOutput, calls=%fused_computation.15 | convolution fusion | flops 8627683328 | bytes 33554432 | tf_op jit(solution)/shard_map/td,fd->tf/dot_general | solution.py:199
  405.1 11.5 %fusion.92 = f32[1024,2048]{1,0:T(8,128)} fusion(bf16[2048,1024]{1,0:T(8,128)(2,1)S(1)} %copy-done.83, bf16[2048,2048]{1,0:T(8,128)(2,1)S(1)} %bitcast.69), kind=kOutput, calls=%fused_computation.228 | convolution fusion | flops 8589934592 | bytes 20971520 | tf_op jit(solution)/shard_map/td,tf->df/dot_general | solution.py:203
  431.2 14.6 %add_convert_fusion.2 = bf16[1024,2048]{1,0:T(8,128)(2,1)} fusion(f32[1024,2048]{1,0:T(8,128)} %fusion.92, bf16[2048,1024]{1,0:T(8,128)(2,1)S(1)} %copy-done.82, bf16[2048,2048]{1,0:T(8,128)(2,1)} %constant_dynamic-update-slice_fusion.4), kind=kOutput, calls=%fused_computation.38 | convolution fusion | flops 8594128896 | bytes 25165824 | tf_op jit(solution)/shard_map/td,tf->df/dot_general | solution.py:203
  466.5 15.3 %fusion.94 = f32[1024,2048]{1,0:T(8,128)} fusion(bf16[2048,1024]{1,0:T(8,128)(2,1)} %get-tuple-element.76, bf16[2048,2048]{1,0:T(8,128)(2,1)} %constant_dynamic-update-slice_fusion), kind=kOutput, calls=%fused_computation.230 | convolution fusion | flops 8589934592 | bytes 20971520 | tf_op jit(solution)/shard_map/td,tf->df/dot_general | solution.py:203
  481.8 20.7 %collective-permute-done.25 = bf16[512,2048]{1,0:T(8,128)(2,1)S(1)} collective-permute-done((bf16[512,2048]{1,0:T(8,128)(2,1)S(1)}, bf16[512,2048]{1,0:T(8,128)(2,1)S(1)}, u32[]{:S(2)}, u32[]{:S(2)}) %collective-permute-start.25) | collective-permute-done | bytes 2097184 | tf_op jit(solution)/shard_map/ppermute | solution.py:175
  518.2 14.1 %add_convert_fusion = bf16[1024,2048]{1,0:T(8,128)(2,1)} fusion(f32[1024,2048]{1,0:T(8,128)} %fusion.94, bf16[2048,1024]{1,0:T(8,128)(2,1)S(1)} %copy-done.81, bf16[1024,2048]{1,0:T(8,128)(2,1)} %collective-permute-done.3, bf16[512,2048]{1,0:T(8,128)(2,1)} %collective-permute-done.2, bf16[512,2048]{1,0:T(8,128)(2,1)S(1)} %copy-done.29), kind=kOutput, calls=%fused_computation.34 | convolution fusion | flops 8619294720 | bytes 25165824 | tf_op jit(solution)/shard_map/td,tf->df/dot_general | solution.py:203
  532.6 30.4 %collective-permute-done.26 = bf16[512,2048]{1,0:T(8,128)(2,1)} collective-permute-done((bf16[512,2048]{1,0:T(8,128)(2,1)}, bf16[512,2048]{1,0:T(8,128)(2,1)}, u32[]{:S(2)}, u32[]{:S(2)}) %collective-permute-start.26) | collective-permute-done | bytes 2097184 | tf_op jit(solution)/shard_map/ppermute | solution.py:175
  577.2 20.1 %attend_back.1 = (bf16[1024,1024]{1,0:T(8,128)(2,1)}, bf16[1024,512]{1,0:T(8,128)(2,1)}, bf16[1024,512]{1,0:T(8,128)(2,1)}) custom-call(s32[1]{0:T(128)} %bitcast.first_ref, bf16[1024,1024]{1,0:T(8,128)(2,1)} %get-tuple-element.31.q_ref, bf16[1024,512]{1,0:T(8,128)(2,1)} %get-tuple-element.32.k_ref, bf16[1024,512]{1,0:T(8,128)(2,1)} %get-tuple-element.33.v_ref, ...), custom_call_target="tpu_custom_call" | custom-call | flops 7516192768 | bytes 37580964 | tf_op jit(solution)/shard_map/attend_back/pallas_call | solution.py:153
  608.2 9.6 convolution_convert_fusion.7
  622.7 14.0 %fusion.93 = f32[1024,2048]{1,0:T(8,128)} fusion(bf16[2048,1024]{1,0:T(8,128)(2,1)S(1)} %copy-done.86, bf16[2048,2048]{1,0:T(8,128)(2,1)} %constant_dynamic-update-slice_fusion), kind=kOutput, calls=%fused_computation.229 | convolution fusion | flops 8589934592 | bytes 20971520 | tf_op jit(solution)/shard_map/td,tf->df/dot_general | solution.py:203
  636.6 9.6 collective-permute-done.34
  647.7 14.9 %add_convert_fusion.1 = bf16[1024,2048]{1,0:T(8,128)(2,1)} fusion(f32[1024,2048]{1,0:T(8,128)} %fusion.93, bf16[2048,1024]{1,0:T(8,128)(2,1)} %get-tuple-element.71, bf16[1024,2048]{1,0:T(8,128)(2,1)} %collective-permute-done.3, bf16[512,2048]{1,0:T(8,128)(2,1)} %collective-permute-done.2, bf16[512,2048]{1,0:T(8,128)(2,1)S(1)} %copy-done.29), kind=kOutput, calls=%fused_computation.37 | convolution fusion | flops 8619294720 | bytes 25165824 | tf_op jit(solution)/shard_map/td,tf->df/dot_general | solution.py:203
  662.7 9.5 convolution_convert_fusion.8
  749.4 91.2 %collective-permute-done.29 = bf16[512,1024]{1,0:T(8,128)(2,1)S(1)} collective-permute-done((bf16[512,1024]{1,0:T(8,128)(2,1)S(1)}, bf16[512,1024]{1,0:T(8,128)(2,1)S(1)}, u32[]{:S(2)}, u32[]{:S(2)}) %collective-permute-start.29) | collective-permute-done | bytes 1048608 | tf_op jit(solution)/shard_map/ppermute | solution.py:175
  855.4 20.5 %collective-permute-done.52 = bf16[256,2048]{1,0:T(8,128)(2,1)S(1)} collective-permute-done((bf16[256,2048]{1,0:T(8,128)(2,1)S(1)}, bf16[256,2048]{1,0:T(8,128)(2,1)S(1)}, u32[]{:S(2)}, u32[]{:S(2)}) %collective-permute-start.52) | collective-permute-done | bytes 1048608 | tf_op jit(solution)/shard_map/ppermute | solution.py:175
  878.9 10.5 collective-permute-done.27
  903.1 29.7 %collective-permute-done.11 = bf16[512,2048]{1,0:T(8,128)(2,1)} collective-permute-done((bf16[512,2048]{1,0:T(8,128)(2,1)}, bf16[512,2048]{1,0:T(8,128)(2,1)}, u32[]{:S(2)}, u32[]{:S(2)}) %collective-permute-start.11) | collective-permute-done | bytes 2097184 | tf_op jit(solution)/shard_map/ppermute | solution.py:175
  932.8 14.5 %fusion.23 = (f32[512,2048]{1,0:T(8,128)}, f32[512,2048]{1,0:T(8,128)}) fusion(bf16[512,2048]{1,0:T(8,128)(2,1)S(1)} %copy-done.4, f32[512,2048]{1,0:T(8,128)} %convert_add_fusion.1, f32[512]{0:T(512)S(1)} %multiply_multiply_fusion, f32[2048]{0:T(1024)S(1)} %copy-done.58, f32[512]{0:T(512)S(1)} %copy-done.66, f32[512,2048]{1,0:T(8,128)} %copy-done, ...), kind=kLoop, calls=%fused_computation.51 | loop fusion | flops 20971520 | bytes 37773312 | tf_op jit(solution)/shard_map/add | solution.py:449
  990.4 37.8 %collective-permute-done.30 = bf16[512,1024]{1,0:T(8,128)(2,1)S(1)} collective-permute-done((bf16[512,1024]{1,0:T(8,128)(2,1)}, bf16[512,1024]{1,0:T(8,128)(2,1)S(1)}, u32[]{:S(2)}, u32[]{:S(2)}) %collective-permute-start.30) | collective-permute-done | bytes 1048608 | tf_op jit(solution)/shard_map/ppermute | solution.py:175
  (432 shorter events, 445.3 us)
Async XLA Ops:
  7.2 86.4 %all-gather.7.cloned.1.call-start = ((), (), s32[]{:S(2)}) async-start(), calls=%async_computation.6 | async-start | bytes 5242880 | tf_op jit(solution)/shard_map/all_gather | solution.py:276
  9.7 267.0 %all-gather.9.cloned.1.call-start = ((), (), s32[]{:S(2)}) async-start(), calls=%async_computation.7 | async-start | bytes 5242880 | tf_op jit(solution)/shard_map/all_gather | solution.py:276
  15.7 102.4 %collective-permute-start.17 = (bf16[512,2048]{1,0:T(8,128)(2,1)}, bf16[512,2048]{1,0:T(8,128)(2,1)}, u32[]{:S(2)}, u32[]{:S(2)}) collective-permute-start(bf16[512,2048]{1,0:T(8,128)(2,1)} %param.14), channel_id=1, source_target_pairs={{0,16},{8,24},{16,0},{24,8},{1,17},{9,25},{17,1},{25,9},{2,18},{10... | collective-permute-start | bytes 6291464 | tf_op jit(solution)/shard_map/ppermute | solution.py:175
  19.5 272.0 %all-gather.11.cloned.1.call-start = ((), (), s32[]{:S(2)}) async-start(), calls=%async_computation.8 | async-start | bytes 5242880 | tf_op jit(solution)/shard_map/all_gather | solution.py:276
  98.5 59.5 %collective-permute-start.1 = (bf16[512,2048]{1,0:T(8,128)(2,1)S(1)}, bf16[512,2048]{1,0:T(8,128)(2,1)S(1)}, u32[]{:S(2)}, u32[]{:S(2)}) collective-permute-start(bf16[512,2048]{1,0:T(8,128)(2,1)S(1)} %convolution_convert_fusion.9), channel_id=1, source_target_pairs={{0,1},{1,0},{2,3},{3,2},{4,5},{5,4},{6,7},{7,6},{8,9},{9,8},{10,11... | collective-permute-start | bytes 6291464 | tf_op jit(solution)/shard_map/ppermute | solution.py:175
  118.1 75.3 %collective-permute-start.15 = (bf16[1024,2048]{1,0:T(8,128)(2,1)}, bf16[1024,2048]{1,0:T(8,128)(2,1)}, u32[]{:S(2)}, u32[]{:S(2)}) collective-permute-start(bf16[1024,2048]{1,0:T(8,128)(2,1)} %pad_maximum_fusion.5), channel_id=1, source_target_pairs={{0,8},{8,0},{16,24},{24,16},{1,9},{9,1},{17,25},{25,17},{2,10},{10... | collective-permute-start | bytes 12582920 | tf_op jit(solution)/shard_map/ppermute | solution.py:175
  120.6 59.9 %collective-permute-start.19 = (bf16[256,2048]{1,0:T(8,128)(2,1)}, bf16[256,2048]{1,0:T(8,128)(2,1)S(1)}, u32[]{:S(2)}, u32[]{:S(2)}) collective-permute-start(bf16[256,2048]{1,0:T(8,128)(2,1)} %slice.169), channel_id=1, source_target_pairs={{0,1},{1,0},{2,3},{3,2},{4,5},{5,4},{6,7},{7,6},{8,9},{9,8},{10,11... | collective-permute-start | bytes 3145736 | tf_op jit(solution)/shard_map/ppermute | solution.py:175
  124.6 55.8 %collective-permute-start.18 = (bf16[256,2048]{1,0:T(8,128)(2,1)}, bf16[256,2048]{1,0:T(8,128)(2,1)}, u32[]{:S(2)}, u32[]{:S(2)}) collective-permute-start(bf16[256,2048]{1,0:T(8,128)(2,1)} %slice.168), channel_id=1, source_target_pairs={{0,16},{8,24},{16,0},{24,8},{1,17},{9,25},{17,1},{25,9},{2,18},{10... | collective-permute-start | bytes 3145736 | tf_op jit(solution)/shard_map/ppermute | solution.py:175
  163.2 60.6 %collective-permute-start.2 = (bf16[512,2048]{1,0:T(8,128)(2,1)S(1)}, bf16[512,2048]{1,0:T(8,128)(2,1)}, u32[]{:S(2)}, u32[]{:S(2)}) collective-permute-start(bf16[512,2048]{1,0:T(8,128)(2,1)S(1)} %multiply_convert_fusion), channel_id=1, source_target_pairs={{0,1},{1,0},{2,3},{3,2},{4,5},{5,4},{6,7},{7,6},{8,9},{9,8},{10,11... | collective-permute-start | bytes 6291464 | tf_op jit(solution)/shard_map/ppermute | solution.py:175
  167.2 400.6 %reduce-scatter.7.cloned.1.call-start = ((), (), s32[]{:S(2)}) async-start(), calls=%async_computation.9 | async-start | bytes 5242880 | tf_op jit(solution)/shard_map/reduce_scatter | solution.py:280
  182.9 59.0 %collective-permute-start.20 = (bf16[1024,2048]{1,0:T(8,128)(2,1)S(1)}, bf16[1024,2048]{1,0:T(8,128)(2,1)S(1)}, u32[]{:S(2)}, u32[]{:S(2)}) collective-permute-start(bf16[1024,2048]{1,0:T(8,128)(2,1)S(1)} %pad_maximum_fusion.6), channel_id=1, source_target_pairs={{0,8},{8,0},{16,24},{24,16},{1,9},{9,1},{17,25},{25,17},{2,10},{10... | collective-permute-start | bytes 12582920 | tf_op jit(solution)/shard_map/ppermute | solution.py:175
  191.7 50.8 %collective-permute-start.5 = (bf16[512,2048]{1,0:T(8,128)(2,1)S(1)}, bf16[512,2048]{1,0:T(8,128)(2,1)S(1)}, u32[]{:S(2)}, u32[]{:S(2)}) collective-permute-start(bf16[512,2048]{1,0:T(8,128)(2,1)S(1)} %multiply_convert_fusion), channel_id=1, source_target_pairs={{0,16},{8,24},{16,0},{24,8},{1,17},{9,25},{17,1},{25,9},{2,18},{10... | collective-permute-start | bytes 6291464 | tf_op jit(solution)/shard_map/ppermute | solution.py:175
  274.7 57.7 %collective-permute-start.8 = (bf16[1024,2048]{1,0:T(8,128)(2,1)}, bf16[1024,2048]{1,0:T(8,128)(2,1)}, u32[]{:S(2)}, u32[]{:S(2)}) collective-permute-start(bf16[1024,2048]{1,0:T(8,128)(2,1)} %pad_maximum_fusion.4), channel_id=1, source_target_pairs={{0,8},{8,0},{16,24},{24,16},{1,9},{9,1},{17,25},{25,17},{2,10},{10... | collective-permute-start | bytes 12582920 | tf_op jit(solution)/shard_map/ppermute | solution.py:175
  331.9 114.0 %collective-permute-start.16 = (bf16[1024,2048]{1,0:T(8,128)(2,1)}, bf16[1024,2048]{1,0:T(8,128)(2,1)}, u32[]{:S(2)}, u32[]{:S(2)}) collective-permute-start(bf16[1024,2048]{1,0:T(8,128)(2,1)} %add_convert_fusion.5), channel_id=1, source_target_pairs={{0,8},{8,0},{16,24},{24,16},{1,9},{9,1},{17,25},{25,17},{2,10},{10... | collective-permute-start | bytes 12582920 | tf_op jit(solution)/shard_map/ppermute | solution.py:175
  445.8 280.3 %reduce-scatter.17.cloned.1.call-start = ((), (), s32[]{:S(2)}) async-start(), calls=%async_computation.17 | async-start | bytes 5242880 | tf_op jit(solution)/shard_map/reduce_scatter | solution.py:280
  532.4 346.4 %reduce-scatter.13.cloned.1.call-start = ((), (), s32[]{:S(2)}) async-start(), calls=%async_computation.13 | async-start | bytes 1310720 | tf_op jit(solution)/shard_map/reduce_scatter | solution.py:280
  617.8 62.7 %collective-permute-start.9 = (bf16[1024,2048]{1,0:T(8,128)(2,1)}, bf16[1024,2048]{1,0:T(8,128)(2,1)}, u32[]{:S(2)}, u32[]{:S(2)}) collective-permute-start(bf16[1024,2048]{1,0:T(8,128)(2,1)} %convolution_convert_fusion.7), channel_id=1, source_target_pairs={{0,8},{8,0},{16,24},{24,16},{1,9},{9,1},{17,25},{25,17},{2,10},{10... | collective-permute-start | bytes 12582920 | tf_op jit(solution)/shard_map/ppermute | solution.py:175
  647.7 251.0 %reduce-scatter.9.cloned.1.call-start = ((), (), s32[]{:S(2)}) async-start(), calls=%async_computation.10 | async-start | bytes 5242880 | tf_op jit(solution)/shard_map/reduce_scatter | solution.py:280
  662.6 239.9 %reduce-scatter.15.cloned.1.call-start = ((), (), s32[]{:S(2)}) async-start(), calls=%async_computation.15 | async-start | bytes 1310720 | tf_op jit(solution)/shard_map/reduce_scatter | solution.py:280
  716.0 127.0 %collective-permute-start.10 = (bf16[256,2048]{1,0:T(8,128)(2,1)}, bf16[256,2048]{1,0:T(8,128)(2,1)}, u32[]{:S(2)}, u32[]{:S(2)}) collective-permute-start(bf16[256,2048]{1,0:T(8,128)(2,1)} %get-tuple-element.99), channel_id=1, source_target_pairs={{0,16},{8,24},{16,0},{24,8},{1,17},{9,25},{17,1},{25,9},{2,18},{10... | collective-permute-start | bytes 3145736 | tf_op jit(solution)/shard_map/ppermute | solution.py:175
  721.3 181.7 %collective-permute-start.13 = (bf16[512,2048]{1,0:T(8,128)(2,1)}, bf16[512,2048]{1,0:T(8,128)(2,1)}, u32[]{:S(2)}, u32[]{:S(2)}) collective-permute-start(bf16[512,2048]{1,0:T(8,128)(2,1)} %add_convert_fusion.11), channel_id=1, source_target_pairs={{0,16},{8,24},{16,0},{24,8},{1,17},{9,25},{17,1},{25,9},{2,18},{10... | collective-permute-start | bytes 6291464 | tf_op jit(solution)/shard_map/ppermute | solution.py:175
  724.6 127.3 %collective-permute-start.47 = (f32[8,256]{1,0:T(8,128)S(1)}, f32[8,256]{1,0:T(8,128)S(1)}, u32[]{:S(2)}, u32[]{:S(2)}) collective-permute-start(f32[8,256]{1,0:T(8,128)S(1)} %add.277), channel_id=1, source_target_pairs={{0,1},{1,0},{2,3},{3,2},{4,5},{5,4},{6,7},{7,6},{8,9},{9,8},{10,11... | collective-permute-start | bytes 24584 | tf_op jit(solution)/shard_map/ppermute | solution.py:175
  728.9 124.5 %collective-permute-start.50 = (bf16[2048,256]{0,1:T(8,128)(2,1)}, bf16[2048,256]{0,1:T(8,128)(2,1)S(1)}, u32[]{:S(2)}, u32[]{:S(2)}) collective-permute-start(bf16[2048,256]{0,1:T(8,128)(2,1)} %bitcast.66), channel_id=1, source_target_pairs={{0,16},{8,24},{16,0},{24,8},{1,17},{9,25},{17,1},{25,9},{2,18},{10... | collective-permute-start | bytes 3145736 | tf_op jit(solution)/shard_map/ppermute | solution.py:175
  732.5 219.0 %reduce-scatter.11.cloned.1.call-start = ((), (), s32[]{:S(2)}) async-start(), calls=%async_computation.11 | async-start | bytes 1310720 | tf_op jit(solution)/shard_map/reduce_scatter | solution.py:280
  740.8 99.8 %collective-permute-start.29 = (bf16[512,1024]{1,0:T(8,128)(2,1)S(1)}, bf16[512,1024]{1,0:T(8,128)(2,1)S(1)}, u32[]{:S(2)}, u32[]{:S(2)}) collective-permute-start(bf16[512,1024]{1,0:T(8,128)(2,1)S(1)} %constant_dynamic-slice_fusion.4), channel_id=1, source_target_pairs={{0,16},{8,24},{16,0},{24,8},{1,17},{9,25},{17,1},{25,9},{2,18},{10... | collective-permute-start | bytes 3145736 | tf_op jit(solution)/shard_map/ppermute | solution.py:175
  842.9 113.4 %all-gather.15.cloned.1.call-start = ((), (), s32[]{:S(2)}) async-start(), calls=%async_computation.14 | async-start | bytes 1310720 | tf_op jit(solution)/shard_map/all_gather | solution.py:276
  850.8 82.1 %collective-permute-start.11 = (bf16[512,2048]{1,0:T(8,128)(2,1)}, bf16[512,2048]{1,0:T(8,128)(2,1)}, u32[]{:S(2)}, u32[]{:S(2)}) collective-permute-start(bf16[512,2048]{1,0:T(8,128)(2,1)} %fusion.33), channel_id=1, source_target_pairs={{0,1},{1,0},{2,3},{3,2},{4,5},{5,4},{6,7},{7,6},{8,9},{9,8},{10,11... | collective-permute-start | bytes 6291464 | tf_op jit(solution)/shard_map/ppermute | solution.py:175
  855.4 96.0 %collective-permute-start.51 = (bf16[2048,512]{0,1:T(8,128)(2,1)}, bf16[2048,512]{0,1:T(8,128)(2,1)}, u32[]{:S(2)}, u32[]{:S(2)}) collective-permute-start(bf16[2048,512]{0,1:T(8,128)(2,1)} %pad_maximum_fusion.14), channel_id=1, source_target_pairs={{0,8},{8,0},{16,24},{24,16},{1,9},{9,1},{17,25},{25,17},{2,10},{10... | collective-permute-start | bytes 6291464 | tf_op jit(solution)/shard_map/ppermute | solution.py:175
  878.8 94.4 %collective-permute-start.53 = (bf16[512,2048]{1,0:T(8,128)(2,1)}, bf16[512,2048]{1,0:T(8,128)(2,1)}, u32[]{:S(2)}, u32[]{:S(2)}) collective-permute-start(bf16[512,2048]{1,0:T(8,128)(2,1)} %pad_maximum_fusion.15), channel_id=1, source_target_pairs={{0,8},{8,0},{16,24},{24,16},{1,9},{9,1},{17,25},{25,17},{2,10},{10... | collective-permute-start | bytes 6291464 | tf_op jit(solution)/shard_map/ppermute | solution.py:175
  878.8 101.5 %all-gather.17.cloned.1.call-start = ((), (), s32[]{:S(2)}) async-start(), calls=%async_computation.16 | async-start | bytes 1310720 | tf_op jit(solution)/shard_map/all_gather | solution.py:276
  902.6 78.8 %all-gather.13.cloned.1.call-start = ((), (), s32[]{:S(2)}) async-start(), calls=%async_computation.12 | async-start | bytes 1310720 | tf_op jit(solution)/shard_map/all_gather | solution.py:276
  986.1 61.9 %collective-permute-start.36 = (bf16[1024,1024]{1,0:T(8,128)(2,1)}, bf16[1024,1024]{1,0:T(8,128)(2,1)}, u32[]{:S(2)}, u32[]{:S(2)}) collective-permute-start(bf16[1024,1024]{1,0:T(8,128)(2,1)} %pad_maximum_fusion.8), channel_id=1, source_target_pairs={{0,1},{1,0},{2,3},{3,2},{4,5},{5,4},{6,7},{7,6},{8,9},{9,8},{10,11... | collective-permute-start | bytes 6291464 | tf_op jit(solution)/shard_map/ppermute | solution.py:175
  (123 other events, 2305.6 us)
Sparse Core Ops, SparseCore 0:
  10.2 83.4 all-gather.6
  95.8 79.0 all-gather.8
  176.4 78.7 all-gather.10
  445.9 76.5 reduce-scatter.6
  532.5 77.0 reduce-scatter.16
  647.8 28.3 reduce-scatter.12
  679.1 75.6 reduce-scatter.8
  757.0 27.7 reduce-scatter.14
  843.0 26.4 reduce-scatter.10
  878.9 27.6 all-gather.14
  908.2 27.3 all-gather.16
  951.6 27.6 all-gather.12

commit v4 on v3

--- a/solution.py
+++ b/solution.py
@@ -217,10 +217,15 @@
     return [lax.all_gather(mine, "col", axis=0, tiled=True)]
 
 
-def col_scatter(product):
+def col_scatter(product, beside=None):
     if lax.axis_size("col") == 2:
         theirs = swap(low(product(1)), "col", 1)
+        if beside is not None:
+            theirs, beside = tie(theirs, beside)
+            return product(0) + wide(theirs), beside
         return product(0) + wide(theirs)
+    if beside is not None:
+        return col_scatter(product), beside
     return wide(lax.psum_scatter(low(product(0)), "col", scatter_dimension=0, tiled=True))
 
 
@@ -229,17 +234,21 @@
     return [lax.slice_in_dim(value, i * size, (i + 1) * size, axis=dim) for i in range(count)]
 
 
-def square_gather(for_x, for_y):
+def square_gather(mine):
     if lax.axis_size("col") == 2:
-        over_y = swap(for_y, "grp", 2)
-        over_x = swap(for_x, "col", 1)
-        half = for_x.shape[0] // 2
+        over_x = swap(mine, "col", 1)
+        over_y = swap(mine, "grp", 2)
+        half = mine.shape[0] // 2
         across_first = swap(over_x[:half], "grp", 2)
         across_second = swap(over_y[half:], "col", 1)
-        near = jnp.concatenate([for_x, over_x], axis=0)
+        near = jnp.concatenate([mine, over_x], axis=0)
         return near, jnp.concatenate([over_y, across_first, across_second], axis=0)
-    near = lax.all_gather(for_x, "col", axis=0, tiled=True)
+    near = lax.all_gather(mine, "col", axis=0, tiled=True)
     return near, swap(near, "grp", 2)
+
+
+def with_core(pack):
+    return jnp.concatenate([pack, swap(pack, "grp", 1)], axis=0)
 
 
 def square_scatter(near, far):
@@ -281,9 +290,16 @@
 
 
 def sum_quarters(value, core, ypos):
-    part = low(wide(half_rows(value, core)) + wide(swap(half_rows(value, 1 - core), "grp", 1)))
+    return sum_y(sum_cores(value, core), ypos)
+
+
+def sum_cores(value, core):
+    return low(wide(half_rows(value, core)) + wide(swap(half_rows(value, 1 - core), "grp", 1)))
+
+
+def sum_y(part, ypos):
     part = low(wide(half_rows(part, ypos)) + wide(swap(half_rows(part, 1 - ypos), "grp", 2)))
-    return row_gather(row_scatter(part))
+    return part
 
 
 def spread_y(part, ypos):
@@ -339,16 +355,19 @@
     gathered_in = jnp.concatenate(col_gather(low(normalized_input)), axis=0)
     packed_length = gathered_in.shape[0]
 
-    down_rows, gate_rows, up_rows = [
-        row_gather(own_quarter(weight, core, ypos))
-        for weight in (down_weight, gate_weight.T, up_weight.T)
+    down_own, gate_own, up_own = [
+        own_quarter(weight, core, ypos) for weight in (down_weight, gate_weight.T, up_weight.T)
     ]
+    down_rows = row_gather(down_own)
+    gate_up = lax.all_gather(jnp.stack([gate_own, up_own]), "row", axis=0)
 
     gathered_in, cot_now = tie(gathered_in, cotangent)
-    cot_sets = [
-        jnp.concatenate([pack, swap(pack, "grp", 1)], axis=0)
-        for pack in square_gather(cot_now, cotangent)
-    ]
+    cot_near = col_gather(cot_now)
+    if in_pairs:
+        cot_far = [swap(cotangent, "grp", 2), swap(cot_near[1], "grp", 2)]
+    else:
+        cot_far = [swap(cot_near[0], "grp", 2)]
+    cot_sets = [with_core(jnp.concatenate(pack, axis=0)) for pack in (cot_near, cot_far)]
 
     key_slice = lax.dynamic_slice_in_dim(key_matrix, key_first * head_dim, key_cols, 1)
     value_slice = lax.dynamic_slice_in_dim(value_matrix, key_first * head_dim, key_cols, 1)
@@ -375,16 +394,20 @@
         (3 * score_flops, key_heads),
     )
     attn_low, down_rows = tie(attn_low, down_rows)
-    act_grads = [low(dot_nt(cot, down_rows)) for cot in cot_sets]
+    act_near = low(dot_nt(cot_sets[0], down_rows))
+    act_far = low(dot_nt(cot_sets[1], down_rows))
     attn_parts = blocks_of(attn_low, 0, 2) if in_pairs else [attn_low]
-    hidden_res = inputs + col_scatter(lambda i: dot32(attn_parts[i], output_weight))
+    from_attention, act_near = col_scatter(
+        lambda i: dot32(attn_parts[i], output_weight), act_near
+    )
+    hidden_res = inputs + from_attention
     normed_mid, second_back = jax.vjp(normalize, hidden_res, second_gain)
 
-    normed_low = low(normed_mid)
-    mid_sets = [
-        jnp.concatenate([pack, swap(pack, "grp", 1)], axis=0)
-        for pack in square_gather(normed_low, normed_low)
-    ]
+    mid_near, mid_far = square_gather(low(normed_mid))
+    mid_near, act_far = tie(mid_near, act_far)
+    mid_sets = [with_core(mid_near), with_core(mid_far)]
+    act_grads = [act_near, act_far]
+    gate_rows, up_rows = [gate_up[:, i].reshape(-1, width) for i in range(2)]
     acts, gate_backs, up_backs = [], [], []
     for mid, act_grad in zip(mid_sets, act_grads):
         gate32 = wide(low(dot_nt(mid, gate_rows)))
@@ -394,34 +417,60 @@
         gate_backs.append(low(wide(act_grad) * up_lin * sig * (1 + gate32 * (1 - sig))))
         up_backs.append(low(wide(act_grad) * gate32 * sig))
 
-    def token_sum(product):
+    def weight_sum(lefts, rights):
+        return low(sum(dot_tn(left, right) for left, right in zip(lefts, rights)))
+
+    def far_sum(product):
         pack = packed_length
-        far = low(
-            product(1, 0, pack) + wide(swap(low(product(1, pack, 2 * pack)), "grp", 1))
-        )
-        from_core = wide(swap(low(product(0, pack, 2 * pack)), "grp", 1))
-        return square_scatter(
-            lambda first, last: product(0, first, last) + from_core[first:last], far
-        )
-
-    mid_grad = token_sum(
-        lambda i, a, b: dot32(gate_backs[i][a:b], gate_rows) + dot32(up_backs[i][a:b], up_rows)
-    )
-
-    def weight_part(lefts, rights):
-        return row_scatter(low(sum(dot_tn(left, right) for left, right in zip(lefts, rights))))
-
-    down_part = weight_part(acts, cot_sets)
-    gate_part = weight_part(gate_backs, mid_sets)
-    up_part = weight_part(up_backs, mid_sets)
-    layer_out = hidden_res + token_sum(lambda i, a, b: dot32(acts[i][a:b], down_rows))
+        theirs = swap(low(product(1, pack, 2 * pack)), "grp", 1)
+        return low(product(1, 0, pack) + wide(theirs))
+
+    def near_sum(product):
+        pack = packed_length
+        return wide(swap(low(product(0, pack, 2 * pack)), "grp", 1))
+
+    def mid_product(i, a, b):
+        return dot32(gate_backs[i][a:b], gate_rows) + dot32(up_backs[i][a:b], up_rows)
+
+    def out_product(i, a, b):
+        return dot32(acts[i][a:b], down_rows)
+
+    down_low = weight_sum(acts, cot_sets)
+    down_low, gate_backs[1], up_backs[1] = tie(down_low, gate_backs[1], up_backs[1])
+    down_part = row_scatter(down_low)
+    mid_far_sum = far_sum(mid_product)
+    mid_from_core = near_sum(mid_product)
+    mid_grad = square_scatter(
+        lambda first, last: mid_product(0, first, last) + mid_from_core[first:last], mid_far_sum
+    )
+    gate_low = weight_sum(gate_backs, mid_sets)
+    up_low = weight_sum(up_backs, mid_sets)
 
     res_from_mid, second_gain_part = second_back(mid_grad)
     res_grad = wide(cotangent) + res_from_mid
-    shard_rows = jnp.concatenate(col_gather(low(res_grad)), axis=0)
-    shard_rows, down_part = tie(shard_rows, down_part)
-    out_part = sum_quarters(low(dot_tn(attn_low, shard_rows)), core, ypos)
+    gate_part = row_scatter(gate_low)
+    up_part = row_scatter(up_low)
+    res_low, down_part = tie(low(res_grad), down_part)
+    shard_rows = jnp.concatenate(col_gather(res_low), axis=0)
+
+    out_far = far_sum(out_product)
+    shard_rows, gate_part, out_far = tie(shard_rows, gate_part, out_far)
+    out_from_core = near_sum(out_product) + wide(swap(out_far, "grp", 2))
+    half_pack = packed_length // 2
+    if in_pairs:
+        layer_rows = col_scatter(
+            lambda i: out_product(0, i * half_pack, (i + 1) * half_pack)
+            + out_from_core[i * half_pack : (i + 1) * half_pack]
+        )
+    else:
+        layer_rows = col_scatter(lambda i: out_product(0, 0, packed_length) + out_from_core)
+    layer_out = hidden_res + layer_rows
+
     mixed_low = low(dot_nt(shard_rows, output_weight))
+    out_low = low(dot_tn(attn_low, shard_rows))
+    mixed_low, out_low = tie(mixed_low, sum_cores(out_low, core))
+    out_part, up_part = tie(sum_y(out_low, ypos), up_part)
+    out_part = row_gather(row_scatter(out_part))
     query_back, key_back, value_back = attention_call(
         attend_back_kernel,
         "attend_back",
@@ -442,9 +491,11 @@
     back_all = jnp.concatenate([query_back, pair_back], axis=1)
     query_part = sum_quarters(low(dot_tn(gathered_in, query_back)), core, ypos)
     pair_part = sum_quarters(low(dot_tn(gathered_in, pair_back)), core, ypos)
+    query_part, pair_part, down_part, gate_part = tie(query_part, pair_part, down_part, gate_part)
+    query_part = row_gather(row_scatter(query_part))
+    pair_part = row_gather(row_scatter(pair_part))
     back_parts = blocks_of(back_all, 0, 2) if in_pairs else [back_all]
     in_grad = col_scatter(lambda i: dot_nt(back_parts[i], project_in))
-    in_grad, gate_part = tie(in_grad, gate_part)
     res_from_in, _ = first_back(in_grad)
     input_grad = res_grad + res_from_in
 
@@ -453,14 +504,20 @@
     up_grad = spread_quarters(up_part.T, core, ypos, 1)
     out_wgrad = spread_quarters(out_part, core, ypos, 0)
     query_wgrad = spread_quarters(query_part, core, ypos, 0)
-    pair_part = ordered(ypos, pair_part, swap(pair_part, "grp", 2), 0)
     if in_pairs:
-        theirs = swap(pair_part, "col", 1)
+        over_x, over_y = swap(pair_part, "col", 1), swap(pair_part, "grp", 2)
+        half = pair_part.shape[0] // 2
+        across = jnp.concatenate(
+            [swap(over_x[:half], "grp", 2), swap(over_y[half:], "col", 1)], axis=0
+        )
+        pair_part = ordered(ypos, pair_part, over_y, 0)
+        theirs = ordered(ypos, over_x, across, 0)
         key_part = ordered(col, pair_part[:, :key_cols], theirs[:, :key_cols], 1)
         value_part = ordered(col, pair_part[:, key_cols:], theirs[:, key_cols:], 1)
         key_full = wide(ordered(core, key_part, swap(key_part, "grp", 1), 0))
         value_full = wide(ordered(core, value_part, swap(value_part, "grp", 1), 0))
     else:
+        pair_part = ordered(ypos, pair_part, swap(pair_part, "grp", 2), 0)
         pair_part = ordered(core, pair_part, swap(pair_part, "grp", 1), 0)
         pair_all = wide(lax.all_gather(pair_part, "col", axis=0))
         groups = lax.axis_size("col") // head_sharing

time: 1100 us -> 1080 us (0.982)
  waiting for transfers between devices: 401 us -> 369 us
  local copies, waits for them, and re-layouts: 85.8 us -> 109 us
  matrix products: 353 us -> 340 us
    ppermute x54 -> x53, waiting for transfers between devices: 397 us -> 347 us  [swap(): return lax.ppermute(value, axis, [(i, i ^ bit) for i in range(count)])]
    all_gather x6 -> x4, waiting for transfers between devices: 3.84 us -> 21 us  [row_gather(): return lax.all_gather(value, 'row', axis=0, tiled=True)]
    unnamed x192 -> x207, local copies, waits for them, and re-layouts: 48 us -> 61.2 us
    concatenate x3 -> x5, local copies, waits for them, and re-layouts: 10.4 us -> 22.1 us  [the longest x4 22.1 us: with_core(): return jnp.concatenate([pack, swap(pack, 'grp', 1)], axis=0)]
    select_n x14 -> x15, other arithmetic: 32.4 us -> 37.4 us  [ordered(): jnp.where(keep, mine, theirs)]
    ppermute x54 -> x53, starting transfers between devices: 50.4 us -> 46.1 us  [swap(): return lax.ppermute(value, axis, [(i, i ^ bit) for i in range(count)])]
    convert_element_type x6 -> x5, other arithmetic: 29.6 us -> 26.8 us  [wide(): return value.astype(jnp.float32)]
    convert_element_type x11 -> x10, other arithmetic: 22.6 us -> 21.3 us  [low(): return value.astype(jnp.bfloat16)]
  transfers between devices with their start and end apart: 66 -> 64, of which waited for: 20 -> 23; matrix products, arithmetic and copies ran while one was open for 51% -> 54% of each run, Pallas kernels for 3% -> 3%
where the time goes in v4:
time: 1080 us
  waiting for transfers between devices  369 us (34%)
  matrix products  340 us (31%)
  other arithmetic  165 us (15%)
  local copies, waits for them, and re-layouts  109 us (10%)
  starting transfers between devices  47.6 us (4%)
  Pallas kernels  32.3 us (3%)
  between operations  15.4 us (1%)
    ppermute x53, waiting for transfers between devices, swap(): return lax.ppermute(value, axis, [(i, i ^ bit) for i in range(count)])  347 us
    dot_general x18, matrix products, dot32(): return jnp.dot(left, right, preferred_element_type=jnp.float32)  125 us
    dot_general x9, matrix products, dot_nt(): jnp.einsum('td,fd->tf', left, right, preferred_element_type=jnp.float32)  115 us
    dot_general x9, matrix products, dot_tn(): jnp.einsum('td,tf->df', left, right, preferred_element_type=jnp.float32)  100 us
    unnamed x207, local copies, waits for them, and re-layouts  61.2 us
    ppermute x53, starting transfers between devices, swap(): return lax.ppermute(value, axis, [(i, i ^ bit) for i in range(count)])  46.1 us
    select_n x15, other arithmetic, ordered(): jnp.where(keep, mine, theirs)  37.4 us
    pallas_call x2, Pallas kernels, attention_call(): pl.pallas_call(kernel, grid_spec=pltpu.PrefetchScalarGridSpec(num_scalar_...  32.3 us
  transfers between devices with their start and end apart: 64, of which 23 were waited for; matrix products, arithmetic and copies ran while one was open for 54% of the time, Pallas kernels for 3%

profile of v4, /device:TPU:0, one launch (start us, length us, event | category | flops | bytes accessed | tf_op | source)
XLA Modules:
  0.0 1077.0 jit_solution(5199427866614558837)
XLA Ops:
  14.5 45.6 %collective-permute-done = bf16[512,2048]{1,0:T(8,128)(2,1)S(1)} collective-permute-done((bf16[512,2048]{1,0:T(8,128)(2,1)S(1)}, bf16[512,2048]{1,0:T(8,128)(2,1)S(1)}, u32[]{:S(2)}, u32[]{:S(2)}) %collective-permute-start) | collective-permute-done | bytes 2097184 | tf_op jit(solution)/shard_map/ppermute | solution.py:175
  84.9 24.8 %collective-permute-done.2 = bf16[512,2048]{1,0:T(8,128)(2,1)} collective-permute-done((bf16[512,2048]{1,0:T(8,128)(2,1)S(1)}, bf16[512,2048]{1,0:T(8,128)(2,1)}, u32[]{:S(2)}, u32[]{:S(2)}) %collective-permute-start.2) | collective-permute-done | bytes 2097184 | tf_op jit(solution)/shard_map/ppermute | solution.py:175
  115.4 11.4 %fusion.80.q_ref.k_ref.v_ref = f32[1024,2048]{1,0:T(8,128)} fusion(bf16[1024,2048]{1,0:T(8,128)(2,1)S(1)} %copy-done.33, bf16[2048,512]{1,0:T(8,128)(2,1)S(1)} %get-tuple-element.175, bf16[2048,512]{1,0:T(8,128)(2,1)S(1)} %get-tuple-element.176, bf16[2048,1024]{1,0:T(8,128)(2,1)S(1)} %copy-done.38), kind=kOutput, calls=%fused_computation.227 | convolution fusion | flops 8615100416 | bytes 20971520 | tf_op jit(solution)/shard_map/dot_general | solution.py:195
  126.7 12.2 %attend.1 = (bf16[1024,1024]{1,0:T(8,128)(2,1)}, bf16[1024,1024]{1,0:T(8,128)(2,1)}, bf16[1024,512]{1,0:T(8,128)(2,1)}, bf16[1024,512]{1,0:T(8,128)(2,1)}) custom-call(s32[1]{0:T(128)} %bitcast.first_ref, f32[1024,2048]{1,0:T(8,128)} %fusion.80.q_ref.k_ref.v_ref, f32[1024,2048]{1,0:T(8,128)} %fusion.80.q_ref.k_ref.v_ref, ...), custom_call_target="tpu_custom_call" | custom-call | flops 3221225472 | bytes 16106127 | tf_op jit(solution)/shard_map/attend/pallas_call | solution.py:153
  145.3 17.0 %collective-permute-done.6 = bf16[512,2048]{1,0:T(8,128)(2,1)} collective-permute-done((bf16[512,2048]{1,0:T(8,128)(2,1)}, bf16[512,2048]{1,0:T(8,128)(2,1)}, u32[]{:S(2)}, u32[]{:S(2)}) %collective-permute-start.6) | collective-permute-done | bytes 2097184 | tf_op jit(solution)/shard_map/ppermute | solution.py:175
  183.9 12.7 %convolution_convert_fusion.3 = bf16[2048,1024]{1,0:T(8,128)(2,1)} fusion(bf16[2048,2048]{1,0:T(8,128)(2,1)} %constant_dynamic-update-slice_fusion, bf16[1024,2048]{1,0:T(8,128)(2,1)S(1)} %copy-done.80), kind=kOutput, calls=%fused_computation.92 | convolution fusion | flops 8592031744 | bytes 16777216 | tf_op jit(solution)/shard_map/td,fd->tf/dot_general | solution.py:199
  196.6 28.9 %collective-permute-done.1 = bf16[512,2048]{1,0:T(8,128)(2,1)S(1)} collective-permute-done((bf16[512,2048]{1,0:T(8,128)(2,1)S(1)}, bf16[512,2048]{1,0:T(8,128)(2,1)S(1)}, u32[]{:S(2)}, u32[]{:S(2)}) %collective-permute-start.1) | collective-permute-done | bytes 2097184 | tf_op jit(solution)/shard_map/ppermute | solution.py:175
  236.9 13.0 %convolution_convert_fusion.2 = bf16[2048,1024]{1,0:T(8,128)(2,1)} fusion(bf16[2048,2048]{1,0:T(8,128)(2,1)} %constant_dynamic-update-slice_fusion.3, bf16[1024,2048]{1,0:T(8,128)(2,1)S(1)} %copy-done.80), kind=kOutput, calls=%fused_computation.91 | convolution fusion | flops 8592031744 | bytes 16777216 | tf_op jit(solution)/shard_map/td,fd->tf/dot_general | solution.py:199
  249.9 26.4 %collective-permute-done.4 = bf16[512,2048]{1,0:T(8,128)(2,1)S(1)} collective-permute-done((bf16[512,2048]{1,0:T(8,128)(2,1)S(1)}, bf16[512,2048]{1,0:T(8,128)(2,1)S(1)}, u32[]{:S(2)}, u32[]{:S(2)}) %collective-permute-start.4) | collective-permute-done | bytes 2097184 | tf_op jit(solution)/shard_map/ppermute | solution.py:175
  290.0 15.5 %collective-permute-done.12 = bf16[256,2048]{1,0:T(8,128)(2,1)S(1)} collective-permute-done((bf16[256,2048]{1,0:T(8,128)(2,1)}, bf16[256,2048]{1,0:T(8,128)(2,1)S(1)}, u32[]{:S(2)}, u32[]{:S(2)}) %collective-permute-start.12) | collective-permute-done | bytes 1048608 | tf_op jit(solution)/shard_map/ppermute | solution.py:175
  326.3 12.6 %convolution_convert_fusion.1 = bf16[2048,1024]{1,0:T(8,128)(2,1)} fusion(bf16[2048,2048]{1,0:T(8,128)(2,1)} %constant_dynamic-update-slice_fusion.6, bf16[1024,2048]{1,0:T(8,128)(2,1)S(1)} %bitcast.85), kind=kOutput, calls=%fused_computation.90 | convolution fusion | flops 8592031744 | bytes 16777216 | tf_op jit(solution)/shard_map/td,fd->tf/dot_general | solution.py:199
  338.9 20.3 %fusion.2 = (bf16[2048,1024]{1,0:T(8,128)(2,1)}, bf16[2048,1024]{1,0:T(8,128)(2,1)}, bf16[2048,1024]{1,0:T(8,128)(2,1)S(1)}) fusion(bf16[2048,1024]{1,0:T(8,128)(2,1)} %convolution_convert_fusion.3, bf16[2048,1024]{1,0:T(8,128)(2,1)} %convolution_convert_fusion.1, bf16[2048,2048]{1,0:T(8,128)(2,1)} %constant_dynamic-update-slice_fusion.6, ...), kind=kOutput, calls=%fused_computation.12 | convolution fusion | flops 8627683328 | bytes 33554432 | tf_op jit(solution)/shard_map/td,fd->tf/dot_general | solution.py:199
  384.2 12.7 %convolution_convert_fusion = bf16[2048,1024]{1,0:T(8,128)(2,1)} fusion(bf16[2048,2048]{1,0:T(8,128)(2,1)} %constant_dynamic-update-slice_fusion.8, bf16[1024,2048]{1,0:T(8,128)(2,1)S(1)} %bitcast.88), kind=kOutput, calls=%fused_computation.89 | convolution fusion | flops 8592031744 | bytes 16777216 | tf_op jit(solution)/shard_map/td,fd->tf/dot_general | solution.py:199
  396.9 20.9 %fusion.5 = (bf16[2048,1024]{1,0:T(8,128)(2,1)}, bf16[2048,1024]{1,0:T(8,128)(2,1)}, bf16[2048,1024]{1,0:T(8,128)(2,1)}) fusion(bf16[2048,1024]{1,0:T(8,128)(2,1)} %convolution_convert_fusion.2, bf16[2048,1024]{1,0:T(8,128)(2,1)} %convolution_convert_fusion, bf16[2048,2048]{1,0:T(8,128)(2,1)} %constant_dynamic-update-slice_fusion.8, ...), kind=kOutput, calls=%fused_computation.15 | convolution fusion | flops 8627683328 | bytes 33554432 | tf_op jit(solution)/shard_map/td,fd->tf/dot_general | solution.py:199
  417.8 12.8 %fusion.85 = f32[1024,2048]{1,0:T(8,128)S(1)} fusion(bf16[2048,1024]{1,0:T(8,128)(2,1)} %get-tuple-element.130, bf16[2048,2048]{1,0:T(8,128)(2,1)} %constant_dynamic-update-slice_fusion.3), kind=kOutput, calls=%fused_computation.231 | convolution fusion | flops 8589934592 | bytes 20971520 | tf_op jit(solution)/shard_map/td,tf->df/dot_general | solution.py:203
  430.6 10.7 add_convert_fusion.5
  474.5 13.8 %fusion.86 = f32[1024,2048]{1,0:T(8,128)} fusion(bf16[2048,1024]{1,0:T(8,128)(2,1)S(1)} %copy-done.88, bf16[2048,2048]{1,0:T(8,128)(2,1)} %constant_dynamic-update-slice_fusion.8), kind=kOutput, calls=%fused_computation.232 | convolution fusion | flops 8589934592 | bytes 20971520 | tf_op jit(solution)/shard_map/td,tf->df/dot_general | solution.py:203
  500.6 12.2 %add_convert_fusion.2 = bf16[1024,2048]{1,0:T(8,128)(2,1)} fusion(f32[1024,2048]{1,0:T(8,128)} %fusion.86, bf16[2048,1024]{1,0:T(8,128)(2,1)S(1)} %copy-done.87, bf16[2048,2048]{1,0:T(8,128)(2,1)S(1)} %bitcast.93), kind=kOutput, calls=%fused_computation.38 | convolution fusion | flops 8594128896 | bytes 25165824 | tf_op jit(solution)/shard_map/td,tf->df/dot_general | solution.py:203
  540.4 15.4 %fusion.87 = f32[1024,2048]{1,0:T(8,128)} fusion(bf16[2048,1024]{1,0:T(8,128)(2,1)} %get-tuple-element.52, bf16[2048,2048]{1,0:T(8,128)(2,1)} %constant_dynamic-update-slice_fusion.8), kind=kOutput, calls=%fused_computation.233 | convolution fusion | flops 8589934592 | bytes 20971520 | tf_op jit(solution)/shard_map/td,tf->df/dot_general | solution.py:203
  555.8 16.2 %collective-permute-done.19 = bf16[512,2048]{1,0:T(8,128)(2,1)S(1)} collective-permute-done((bf16[512,2048]{1,0:T(8,128)(2,1)S(1)}, bf16[512,2048]{1,0:T(8,128)(2,1)S(1)}, u32[]{:S(2)}, u32[]{:S(2)}) %collective-permute-start.19) | collective-permute-done | bytes 2097184 | tf_op jit(solution)/shard_map/ppermute | solution.py:175
  589.0 15.4 %add_convert_fusion = bf16[1024,2048]{1,0:T(8,128)(2,1)} fusion(f32[1024,2048]{1,0:T(8,128)} %fusion.87, bf16[2048,1024]{1,0:T(8,128)(2,1)} %copy-done.85, bf16[2048,2048]{1,0:T(8,128)(2,1)} %constant_dynamic-update-slice_fusion.6), kind=kOutput, calls=%fused_computation.33 | convolution fusion | flops 8594128896 | bytes 25165824 | tf_op jit(solution)/shard_map/td,tf->df/dot_general | solution.py:203
  604.5 10.8 %add_convert_fusion.1 = bf16[1024,2048]{1,0:T(8,128)(2,1)} fusion(bf16[1024,2048]{1,0:T(8,128)(2,1)} %collective-permute-done.21, bf16[1024,2048]{1,0:T(8,128)(2,1)} %all-gather.7.cloned.1.call-done, bf16[2048,1024]{1,0:T(8,128)(2,1)} %get-tuple-element.130), kind=kOutput, calls=%fused_computation.37 | convolution fusion | flops 4301258752 | bytes 14680064 | tf_op jit(solution)/shard_map/dot_general | solution.py:195
  615.3 18.9 %collective-permute-done.20 = bf16[512,2048]{1,0:T(8,128)(2,1)} collective-permute-done((bf16[512,2048]{1,0:T(8,128)(2,1)}, bf16[512,2048]{1,0:T(8,128)(2,1)}, u32[]{:S(2)}, u32[]{:S(2)}) %collective-permute-start.20) | collective-permute-done | bytes 2097184 | tf_op jit(solution)/shard_map/ppermute | solution.py:175
  663.7 9.9 convolution_convert_fusion.8
  686.3 20.2 %attend_back.1 = (bf16[1024,1024]{1,0:T(8,128)(2,1)}, bf16[1024,512]{1,0:T(8,128)(2,1)}, bf16[1024,512]{1,0:T(8,128)(2,1)}) custom-call(s32[1]{0:T(128)} %bitcast.first_ref, bf16[1024,1024]{1,0:T(8,128)(2,1)} %get-tuple-element.56.q_ref, bf16[1024,512]{1,0:T(8,128)(2,1)} %get-tuple-element.57.k_ref, bf16[1024,512]{1,0:T(8,128)(2,1)} %get-tuple-element.58.v_ref, ...), custom_call_target="tpu_custom_call" | custom-call | flops 7516192768 | bytes 37580964 | tf_op jit(solution)/shard_map/attend_back/pallas_call | solution.py:153
  735.4 55.2 %collective-permute-done.39 = bf16[256,2048]{1,0:T(8,128)(2,1)S(1)} collective-permute-done((bf16[256,2048]{1,0:T(8,128)(2,1)S(1)}, bf16[256,2048]{1,0:T(8,128)(2,1)S(1)}, u32[]{:S(2)}, u32[]{:S(2)}) %collective-permute-start.39) | collective-permute-done | bytes 1048608 | tf_op jit(solution)/shard_map/ppermute | solution.py:175
  810.9 12.1 %collective-permute-done.27 = bf16[512,1024]{1,0:T(8,128)(2,1)} collective-permute-done((bf16[512,1024]{1,0:T(8,128)(2,1)}, bf16[512,1024]{1,0:T(8,128)(2,1)}, u32[]{:S(2)}, u32[]{:S(2)}) %collective-permute-start.27) | collective-permute-done | bytes 1048608 | tf_op jit(solution)/shard_map/ppermute | solution.py:175
  827.1 18.3 %collective-permute-done.29 = bf16[512,1024]{1,0:T(8,128)(2,1)} collective-permute-done((bf16[512,1024]{1,0:T(8,128)(2,1)}, bf16[512,1024]{1,0:T(8,128)(2,1)}, u32[]{:S(2)}, u32[]{:S(2)}) %collective-permute-start.29) | collective-permute-done | bytes 1048608 | tf_op jit(solution)/shard_map/ppermute | solution.py:175
  871.8 9.5 fusion.27
  883.8 20.8 %collective-permute-done.23 = bf16[512,2048]{1,0:T(8,128)(2,1)} collective-permute-done((bf16[512,2048]{1,0:T(8,128)(2,1)}, bf16[512,2048]{1,0:T(8,128)(2,1)}, u32[]{:S(2)}, u32[]{:S(2)}) %collective-permute-start.23) | collective-permute-done | bytes 2097184 | tf_op jit(solution)/shard_map/ppermute | solution.py:175
  904.7 14.9 %fusion.23 = (f32[512,2048]{1,0:T(8,128)}, f32[512,2048]{1,0:T(8,128)}) fusion(bf16[512,2048]{1,0:T(8,128)(2,1)} %param.13, f32[512,2048]{1,0:T(8,128)} %get-tuple-element.174, bf16[512,2048]{1,0:T(8,128)(2,1)} %collective-permute-done.25, f32[512]{0:T(512)S(1)} %multiply_multiply_fusion, f32[2048]{0:T(1024)S(1)} %copy-done.67, f32[512]{0:T(512)S(1)} %copy-done.72, ...), kind=kLoop, calls=%fused_computation.51 | loop fusion | flops 20971520 | bytes 37773312 | tf_op jit(solution)/shard_map/add | solution.py:500
  967.0 21.0 %all-gather.9.cloned.1.call-done = bf16[512,1024]{1,0:T(8,128)(2,1)} async-done(((bf16[128,1024]{1,0:T(8,128)(2,1)}), bf16[512,1024]{1,0:T(8,128)(2,1)}) %all-gather.9.cloned.1.call-update) | async-done | bytes 1048592 | tf_op jit(solution)/shard_map/all_gather | solution.py:285
  (444 shorter events, 479.8 us)
Async XLA Ops:
  7.2 163.2 %all-gather.7.cloned.1.call-start = ((), (), s32[]{:S(2)}) async-start(), calls=%async_computation.6 | async-start | bytes 5242880 | tf_op jit(solution)/shard_map/all_gather | solution.py:285
  9.7 304.8 %all-gather.15.cloned.1.call-start = ((), (), s32[]{:S(2)}) async-start(), calls=%async_computation.16 | async-start | bytes 10485760 | tf_op jit(solution)/shard_map/all_gather | solution.py:362
  11.5 48.6 %collective-permute-start = (bf16[512,2048]{1,0:T(8,128)(2,1)S(1)}, bf16[512,2048]{1,0:T(8,128)(2,1)S(1)}, u32[]{:S(2)}, u32[]{:S(2)}) collective-permute-start(bf16[512,2048]{1,0:T(8,128)(2,1)S(1)} %fusion.26), channel_id=1, source_target_pairs={{0,1},{1,0},{2,3},{3,2},{4,5},{5,4},{6,7},{7,6},{8,9},{9,8},{10,11... | collective-permute-start | bytes 6291464 | tf_op jit(solution)/shard_map/ppermute | solution.py:175
  64.5 74.5 %collective-permute-start.5 = (bf16[512,2048]{1,0:T(8,128)(2,1)S(1)}, bf16[512,2048]{1,0:T(8,128)(2,1)}, u32[]{:S(2)}, u32[]{:S(2)}) collective-permute-start(bf16[512,2048]{1,0:T(8,128)(2,1)S(1)} %copy-done.3), channel_id=1, source_target_pairs={{0,16},{8,24},{16,0},{24,8},{1,17},{9,25},{17,1},{25,9},{2,18},{10... | collective-permute-start | bytes 6291464 | tf_op jit(solution)/shard_map/ppermute | solution.py:175
  75.4 512.1 %reduce-scatter.7.cloned.1.call-start = ((), (), s32[]{:S(2)}) async-start(), calls=%async_computation.7 | async-start | bytes 5242880 | tf_op jit(solution)/shard_map/reduce_scatter | solution.py:289
  113.9 65.2 %collective-permute-start.3 = (bf16[1024,2048]{1,0:T(8,128)(2,1)}, bf16[1024,2048]{1,0:T(8,128)(2,1)}, u32[]{:S(2)}, u32[]{:S(2)}) collective-permute-start(bf16[1024,2048]{1,0:T(8,128)(2,1)} %pad_maximum_fusion.2), channel_id=1, source_target_pairs={{0,8},{8,0},{16,24},{24,16},{1,9},{9,1},{17,25},{25,17},{2,10},{10... | collective-permute-start | bytes 12582920 | tf_op jit(solution)/shard_map/ppermute | solution.py:175
  113.9 48.4 %collective-permute-start.6 = (bf16[512,2048]{1,0:T(8,128)(2,1)}, bf16[512,2048]{1,0:T(8,128)(2,1)}, u32[]{:S(2)}, u32[]{:S(2)}) collective-permute-start(bf16[512,2048]{1,0:T(8,128)(2,1)} %collective-permute-done.2), channel_id=1, source_target_pairs={{0,16},{8,24},{16,0},{24,8},{1,17},{9,25},{17,1},{25,9},{2,18},{10... | collective-permute-start | bytes 6291464 | tf_op jit(solution)/shard_map/ppermute | solution.py:175
  167.1 65.1 %collective-permute-start.7 = (bf16[1024,2048]{1,0:T(8,128)(2,1)}, bf16[1024,2048]{1,0:T(8,128)(2,1)}, u32[]{:S(2)}, u32[]{:S(2)}) collective-permute-start(bf16[1024,2048]{1,0:T(8,128)(2,1)} %pad_maximum_fusion.4), channel_id=1, source_target_pairs={{0,8},{8,0},{16,24},{24,16},{1,9},{9,1},{17,25},{25,17},{2,10},{10... | collective-permute-start | bytes 12582920 | tf_op jit(solution)/shard_map/ppermute | solution.py:175
  177.5 47.9 %collective-permute-start.1 = (bf16[512,2048]{1,0:T(8,128)(2,1)S(1)}, bf16[512,2048]{1,0:T(8,128)(2,1)S(1)}, u32[]{:S(2)}, u32[]{:S(2)}) collective-permute-start(bf16[512,2048]{1,0:T(8,128)(2,1)S(1)} %convolution_convert_fusion.9), channel_id=1, source_target_pairs={{0,1},{1,0},{2,3},{3,2},{4,5},{5,4},{6,7},{7,6},{8,9},{9,8},{10,11... | collective-permute-start | bytes 6291464 | tf_op jit(solution)/shard_map/ppermute | solution.py:175
  230.6 50.5 %collective-permute-start.11 = (bf16[512,2048]{1,0:T(8,128)(2,1)S(1)}, bf16[512,2048]{1,0:T(8,128)(2,1)S(1)}, u32[]{:S(2)}, u32[]{:S(2)}) collective-permute-start(bf16[512,2048]{1,0:T(8,128)(2,1)S(1)} %multiply_convert_fusion), channel_id=1, source_target_pairs={{0,16},{8,24},{16,0},{24,8},{1,17},{9,25},{17,1},{25,9},{2,18},{10... | collective-permute-start | bytes 6291464 | tf_op jit(solution)/shard_map/ppermute | solution.py:175
  311.1 68.2 %collective-permute-start.14 = (bf16[1024,2048]{1,0:T(8,128)(2,1)}, bf16[1024,2048]{1,0:T(8,128)(2,1)}, u32[]{:S(2)}, u32[]{:S(2)}) collective-permute-start(bf16[1024,2048]{1,0:T(8,128)(2,1)} %pad_maximum_fusion.5), channel_id=1, source_target_pairs={{0,8},{8,0},{16,24},{24,16},{1,9},{9,1},{17,25},{25,17},{2,10},{10... | collective-permute-start | bytes 12582920 | tf_op jit(solution)/shard_map/ppermute | solution.py:175
  373.2 140.2 %collective-permute-start.10 = (bf16[1024,2048]{1,0:T(8,128)(2,1)}, bf16[1024,2048]{1,0:T(8,128)(2,1)}, u32[]{:S(2)}, u32[]{:S(2)}) collective-permute-start(bf16[1024,2048]{1,0:T(8,128)(2,1)} %add_convert_fusion.6), channel_id=1, source_target_pairs={{0,8},{8,0},{16,24},{24,16},{1,9},{9,1},{17,25},{25,17},{2,10},{10... | collective-permute-start | bytes 12582920 | tf_op jit(solution)/shard_map/ppermute | solution.py:175
  454.5 183.8 %reduce-scatter.9.cloned.1.call-start = ((), (), s32[]{:S(2)}) async-start(), calls=%async_computation.8 | async-start | bytes 5242880 | tf_op jit(solution)/shard_map/reduce_scatter | solution.py:289
  512.8 279.1 %reduce-scatter.15.cloned.1.call-start = ((), (), s32[]{:S(2)}) async-start(), calls=%async_computation.13 | async-start | bytes 5242880 | tf_op jit(solution)/shard_map/reduce_scatter | solution.py:289
  540.3 64.1 %collective-permute-start.21 = (bf16[1024,2048]{1,0:T(8,128)(2,1)}, bf16[1024,2048]{1,0:T(8,128)(2,1)}, u32[]{:S(2)}, u32[]{:S(2)}) collective-permute-start(bf16[1024,2048]{1,0:T(8,128)(2,1)} %convolution_convert_fusion.7), channel_id=1, source_target_pairs={{0,8},{8,0},{16,24},{24,16},{1,9},{9,1},{17,25},{25,17},{2,10},{10... | collective-permute-start | bytes 12582920 | tf_op jit(solution)/shard_map/ppermute | solution.py:175
  604.4 264.4 %reduce-scatter.17.cloned.1.call-start = ((), (), s32[]{:S(2)}) async-start(), calls=%async_computation.14 | async-start | bytes 1310720 | tf_op jit(solution)/shard_map/reduce_scatter | solution.py:289
  673.7 174.9 %collective-permute-start.9 = (bf16[1024,2048]{1,0:T(8,128)(2,1)}, bf16[1024,2048]{1,0:T(8,128)(2,1)}, u32[]{:S(2)}, u32[]{:S(2)}) collective-permute-start(bf16[1024,2048]{1,0:T(8,128)(2,1)} %convolution_convert_fusion.8), channel_id=1, source_target_pairs={{0,8},{8,0},{16,24},{24,16},{1,9},{9,1},{17,25},{25,17},{2,10},{10... | collective-permute-start | bytes 12582920 | tf_op jit(solution)/shard_map/ppermute | solution.py:175
  673.7 53.1 %collective-permute-start.46 = (f32[8,256]{1,0:T(8,128)S(1)}, f32[8,256]{1,0:T(8,128)S(1)}, u32[]{:S(2)}, u32[]{:S(2)}) collective-permute-start(f32[8,256]{1,0:T(8,128)S(1)} %add.266), channel_id=1, source_target_pairs={{0,1},{1,0},{2,3},{3,2},{4,5},{5,4},{6,7},{7,6},{8,9},{9,8},{10,11... | collective-permute-start | bytes 24584 | tf_op jit(solution)/shard_map/ppermute | solution.py:175
  675.2 173.3 %collective-permute-start.22 = (bf16[1024,2048]{1,0:T(8,128)(2,1)}, bf16[1024,2048]{1,0:T(8,128)(2,1)}, u32[]{:S(2)}, u32[]{:S(2)}) collective-permute-start(bf16[1024,2048]{1,0:T(8,128)(2,1)} %add_convert_fusion.1), channel_id=1, source_target_pairs={{0,16},{8,24},{16,0},{24,8},{1,17},{9,25},{17,1},{25,9},{2,18},{10... | collective-permute-start | bytes 12582920 | tf_op jit(solution)/shard_map/ppermute | solution.py:175
  715.6 76.6 %collective-permute-start.26 = (bf16[1024,1024]{1,0:T(8,128)(2,1)}, bf16[1024,1024]{1,0:T(8,128)(2,1)}, u32[]{:S(2)}, u32[]{:S(2)}) collective-permute-start(bf16[1024,1024]{1,0:T(8,128)(2,1)} %constant_dynamic-slice_fusion.4), channel_id=1, source_target_pairs={{0,8},{8,0},{16,24},{24,16},{1,9},{9,1},{17,25},{25,17},{2,10},{10... | collective-permute-start | bytes 6291464 | tf_op jit(solution)/shard_map/ppermute | solution.py:175
  725.2 72.9 %collective-permute-start.28 = (bf16[1024,1024]{1,0:T(8,128)(2,1)}, bf16[1024,1024]{1,0:T(8,128)(2,1)}, u32[]{:S(2)}, u32[]{:S(2)}) collective-permute-start(bf16[1024,1024]{1,0:T(8,128)(2,1)} %constant_dynamic-slice_fusion.2), channel_id=1, source_target_pairs={{0,8},{8,0},{16,24},{24,16},{1,9},{9,1},{17,25},{25,17},{2,10},{10... | collective-permute-start | bytes 6291464 | tf_op jit(solution)/shard_map/ppermute | solution.py:175
  726.8 63.8 %collective-permute-start.39 = (bf16[256,2048]{1,0:T(8,128)(2,1)S(1)}, bf16[256,2048]{1,0:T(8,128)(2,1)S(1)}, u32[]{:S(2)}, u32[]{:S(2)}) collective-permute-start(bf16[256,2048]{1,0:T(8,128)(2,1)S(1)} %constant_dynamic-slice_fusion), channel_id=1, source_target_pairs={{0,16},{8,24},{16,0},{24,8},{1,17},{9,25},{17,1},{25,9},{2,18},{10... | collective-permute-start | bytes 3145736 | tf_op jit(solution)/shard_map/ppermute | solution.py:175
  792.0 127.7 %reduce-scatter.13.cloned.1.call-start = ((), (), s32[]{:S(2)}) async-start(), calls=%async_computation.11 | async-start | bytes 1310720 | tf_op jit(solution)/shard_map/reduce_scatter | solution.py:289
  810.2 61.6 %collective-permute-start.25 = (bf16[512,2048]{1,0:T(8,128)(2,1)}, bf16[512,2048]{1,0:T(8,128)(2,1)}, u32[]{:S(2)}, u32[]{:S(2)}) collective-permute-start(bf16[512,2048]{1,0:T(8,128)(2,1)} %convolution_convert_fusion.10), channel_id=1, source_target_pairs={{0,1},{1,0},{2,3},{3,2},{4,5},{5,4},{6,7},{7,6},{8,9},{9,8},{10,11... | collective-permute-start | bytes 6291464 | tf_op jit(solution)/shard_map/ppermute | solution.py:175
  848.5 84.0 %all-gather.13.cloned.1.call-start = ((), (), s32[]{:S(2)}) async-start(), calls=%async_computation.15 | async-start | bytes 1310720 | tf_op jit(solution)/shard_map/all_gather | solution.py:285
  868.8 72.7 %reduce-scatter.11.cloned.1.call-start = ((), (), s32[]{:S(2)}) async-start(), calls=%async_computation.9 | async-start | bytes 1310720 | tf_op jit(solution)/shard_map/reduce_scatter | solution.py:289
  881.4 84.4 %all-gather.11.cloned.1.call-start = ((), (), s32[]{:S(2)}) async-start(), calls=%async_computation.12 | async-start | bytes 1310720 | tf_op jit(solution)/shard_map/all_gather | solution.py:285
  881.7 55.0 %collective-permute-start.50 = (bf16[2048,512]{0,1:T(8,128)(2,1)}, bf16[2048,512]{0,1:T(8,128)(2,1)}, u32[]{:S(2)}, u32[]{:S(2)}) collective-permute-start(bf16[2048,512]{0,1:T(8,128)(2,1)} %pad_maximum_fusion.13), channel_id=1, source_target_pairs={{0,8},{8,0},{16,24},{24,16},{1,9},{9,1},{17,25},{25,17},{2,10},{10... | collective-permute-start | bytes 6291464 | tf_op jit(solution)/shard_map/ppermute | solution.py:175
  919.8 68.3 %all-gather.9.cloned.1.call-start = ((), (), s32[]{:S(2)}) async-start(), calls=%async_computation.10 | async-start | bytes 1310720 | tf_op jit(solution)/shard_map/all_gather | solution.py:285
  936.7 68.7 %collective-permute-start.52 = (bf16[512,2048]{1,0:T(8,128)(2,1)}, bf16[512,2048]{1,0:T(8,128)(2,1)}, u32[]{:S(2)}, u32[]{:S(2)}) collective-permute-start(bf16[512,2048]{1,0:T(8,128)(2,1)} %pad_maximum_fusion.14), channel_id=1, source_target_pairs={{0,8},{8,0},{16,24},{24,16},{1,9},{9,1},{17,25},{25,17},{2,10},{10... | collective-permute-start | bytes 6291464 | tf_op jit(solution)/shard_map/ppermute | solution.py:175
  960.4 74.7 %collective-permute-start.41 = (bf16[512,2048]{1,0:T(8,128)(2,1)}, bf16[512,2048]{1,0:T(8,128)(2,1)}, u32[]{:S(2)}, u32[]{:S(2)}) collective-permute-start(bf16[512,2048]{1,0:T(8,128)(2,1)} %pad_maximum_fusion.11), channel_id=1, source_target_pairs={{0,8},{8,0},{16,24},{24,16},{1,9},{9,1},{17,25},{25,17},{2,10},{10... | collective-permute-start | bytes 6291464 | tf_op jit(solution)/shard_map/ppermute | solution.py:175
  965.7 48.8 %collective-permute-start.33 = (bf16[512,1024]{1,0:T(8,128)(2,1)}, bf16[512,1024]{1,0:T(8,128)(2,1)}, u32[]{:S(2)}, u32[]{:S(2)}) collective-permute-start(bf16[512,1024]{1,0:T(8,128)(2,1)} %all-gather.11.cloned.1.call-done), channel_id=1, source_target_pairs={{0,16},{8,24},{16,0},{24,8},{1,17},{9,25},{17,1},{25,9},{2,18},{10... | collective-permute-start | bytes 3145736 | tf_op jit(solution)/shard_map/ppermute | solution.py:175
  (127 other events, 2261.1 us)
Sparse Core Ops, SparseCore 0:
  10.2 83.4 all-gather.6
  95.8 148.0 all-gather.14
  454.6 77.3 reduce-scatter.6
  534.7 77.2 reduce-scatter.8
  614.2 77.6 reduce-scatter.14
  792.1 25.4 reduce-scatter.16
  848.6 25.4 reduce-scatter.12
  875.6 26.4 all-gather.12
  904.5 26.6 reduce-scatter.10
  932.6 26.4 all-gather.10
  960.7 27.3 all-gather.8

commit v5 on v4

--- a/solution.py
+++ b/solution.py
@@ -361,13 +361,15 @@
     down_rows = row_gather(down_own)
     gate_up = lax.all_gather(jnp.stack([gate_own, up_own]), "row", axis=0)
 
-    gathered_in, cot_now = tie(gathered_in, cotangent)
+    cot_far = []
+    if in_pairs:
+        gathered_in, cot_now, cot_over_y = tie(
+            gathered_in, cotangent, swap(cotangent, "grp", 2)
+        )
+        cot_far.append(cot_over_y)
+    else:
+        gathered_in, cot_now = tie(gathered_in, cotangent)
     cot_near = col_gather(cot_now)
-    if in_pairs:
-        cot_far = [swap(cotangent, "grp", 2), swap(cot_near[1], "grp", 2)]
-    else:
-        cot_far = [swap(cot_near[0], "grp", 2)]
-    cot_sets = [with_core(jnp.concatenate(pack, axis=0)) for pack in (cot_near, cot_far)]
 
     key_slice = lax.dynamic_slice_in_dim(key_matrix, key_first * head_dim, key_cols, 1)
     value_slice = lax.dynamic_slice_in_dim(value_matrix, key_first * head_dim, key_cols, 1)
@@ -393,7 +395,9 @@
         head_dim,
         (3 * score_flops, key_heads),
     )
-    attn_low, down_rows = tie(attn_low, down_rows)
+    attn_low, down_rows, cot_near[-1] = tie(attn_low, down_rows, cot_near[-1])
+    cot_far.append(swap(cot_near[-1], "grp", 2))
+    cot_sets = [with_core(jnp.concatenate(pack, axis=0)) for pack in (cot_near, cot_far)]
     act_near = low(dot_nt(cot_sets[0], down_rows))
     act_far = low(dot_nt(cot_sets[1], down_rows))
     attn_parts = blocks_of(attn_low, 0, 2) if in_pairs else [attn_low]
@@ -405,12 +409,15 @@
 
     mid_near, mid_far = square_gather(low(normed_mid))
     mid_near, act_far = tie(mid_near, act_far)
-    mid_sets = [with_core(mid_near), with_core(mid_far)]
+    gate_rows, up_rows = [gate_up[:, i].reshape(-1, width) for i in range(2)]
+    mid_near = with_core(mid_near)
+    gate_near, mid_far = tie(low(dot_nt(mid_near, gate_rows)), mid_far)
+    mid_sets = [mid_near, with_core(mid_far)]
+    gate_lins = [gate_near, low(dot_nt(mid_sets[1], gate_rows))]
     act_grads = [act_near, act_far]
-    gate_rows, up_rows = [gate_up[:, i].reshape(-1, width) for i in range(2)]
     acts, gate_backs, up_backs = [], [], []
-    for mid, act_grad in zip(mid_sets, act_grads):
-        gate32 = wide(low(dot_nt(mid, gate_rows)))
+    for mid, act_grad, gate_lin in zip(mid_sets, act_grads, gate_lins):
+        gate32 = wide(gate_lin)
         up_lin = dot_nt(mid, up_rows)
         sig = jax.nn.sigmoid(gate32)
         acts.append(low(gate32 * sig * up_lin))
@@ -427,7 +434,7 @@
 
     def near_sum(product):
         pack = packed_length
-        return wide(swap(low(product(0, pack, 2 * pack)), "grp", 1))
+        return swap(low(product(0, pack, 2 * pack)), "grp", 1)
 
     def mid_product(i, a, b):
         return dot32(gate_backs[i][a:b], gate_rows) + dot32(up_backs[i][a:b], up_rows)
@@ -438,39 +445,33 @@
     down_low = weight_sum(acts, cot_sets)
     down_low, gate_backs[1], up_backs[1] = tie(down_low, gate_backs[1], up_backs[1])
     down_part = row_scatter(down_low)
+    mid_from_core = near_sum(mid_product)
     mid_far_sum = far_sum(mid_product)
-    mid_from_core = near_sum(mid_product)
+    mid_far_sum, gate_backs[0], up_backs[0], gate_backs[1] = tie(
+        mid_far_sum, gate_backs[0], up_backs[0], gate_backs[1]
+    )
     mid_grad = square_scatter(
-        lambda first, last: mid_product(0, first, last) + mid_from_core[first:last], mid_far_sum
+        lambda first, last: mid_product(0, first, last) + wide(mid_from_core[first:last]),
+        mid_far_sum,
     )
     gate_low = weight_sum(gate_backs, mid_sets)
-    up_low = weight_sum(up_backs, mid_sets)
+    gate_part = row_scatter(gate_low)
+    out_far = far_sum(out_product)
+    out_far, up_backs[1] = tie(out_far, up_backs[1])
+    out_over_y = swap(out_far, "grp", 2)
+    up_part = row_scatter(weight_sum(up_backs, mid_sets))
 
     res_from_mid, second_gain_part = second_back(mid_grad)
     res_grad = wide(cotangent) + res_from_mid
-    gate_part = row_scatter(gate_low)
-    up_part = row_scatter(up_low)
     res_low, down_part = tie(low(res_grad), down_part)
     shard_rows = jnp.concatenate(col_gather(res_low), axis=0)
-
-    out_far = far_sum(out_product)
-    shard_rows, gate_part, out_far = tie(shard_rows, gate_part, out_far)
-    out_from_core = near_sum(out_product) + wide(swap(out_far, "grp", 2))
-    half_pack = packed_length // 2
-    if in_pairs:
-        layer_rows = col_scatter(
-            lambda i: out_product(0, i * half_pack, (i + 1) * half_pack)
-            + out_from_core[i * half_pack : (i + 1) * half_pack]
-        )
-    else:
-        layer_rows = col_scatter(lambda i: out_product(0, 0, packed_length) + out_from_core)
-    layer_out = hidden_res + layer_rows
+    shard_rows, gate_part = tie(shard_rows, gate_part)
 
     mixed_low = low(dot_nt(shard_rows, output_weight))
     out_low = low(dot_tn(attn_low, shard_rows))
     mixed_low, out_low = tie(mixed_low, sum_cores(out_low, core))
     out_part, up_part = tie(sum_y(out_low, ypos), up_part)
-    out_part = row_gather(row_scatter(out_part))
+    out_part = row_scatter(out_part)
     query_back, key_back, value_back = attention_call(
         attend_back_kernel,
         "attend_back",
@@ -487,15 +488,29 @@
         head_dim,
         (7 * score_flops, key_heads),
     )
+    query_back, out_over_y, acts[0] = tie(query_back, out_over_y, acts[0])
     pair_back = jnp.concatenate([key_back, value_back], axis=1)
     back_all = jnp.concatenate([query_back, pair_back], axis=1)
     query_part = sum_quarters(low(dot_tn(gathered_in, query_back)), core, ypos)
     pair_part = sum_quarters(low(dot_tn(gathered_in, pair_back)), core, ypos)
-    query_part, pair_part, down_part, gate_part = tie(query_part, pair_part, down_part, gate_part)
-    query_part = row_gather(row_scatter(query_part))
-    pair_part = row_gather(row_scatter(pair_part))
+    query_part, pair_part, down_part, gate_part, second_gain_part, acts[0] = tie(
+        query_part, pair_part, down_part, gate_part, second_gain_part, acts[0]
+    )
+    out_part, query_part, pair_part = tie(
+        out_part, row_scatter(query_part), row_scatter(pair_part)
+    )
+    pair_part, query_part, out_part = [row_gather(p) for p in (pair_part, query_part, out_part)]
     back_parts = blocks_of(back_all, 0, 2) if in_pairs else [back_all]
     in_grad = col_scatter(lambda i: dot_nt(back_parts[i], project_in))
+
+    out_from_core = near_sum(out_product)
+    piece = packed_length // 2 if in_pairs else packed_length
+
+    def out_rows(i):
+        part = slice(i * piece, (i + 1) * piece)
+        return out_product(0, part.start, part.stop) + wide(out_from_core[part]) + wide(out_over_y[part])
+
+    layer_out = hidden_res + col_scatter(out_rows)
     res_from_in, _ = first_back(in_grad)
     input_grad = res_grad + res_from_in
 

time: 1080 us -> 1100 us (1.019)
  waiting for transfers between devices: 369 us -> 416 us
  other arithmetic: 165 us -> 145 us
    ppermute x53, waiting for transfers between devices: 347 us -> 416 us  [swap(): return lax.ppermute(value, axis, [(i, i ^ bit) for i in range(count)])]
    all_gather x4, waiting for transfers between devices: 21 us -> 0.01 us  [row_gather(): return lax.all_gather(value, 'row', axis=0, tiled=True)]
    concatenate x4, local copies, waits for them, and re-layouts: 22.1 us -> 10.8 us  [with_core(): return jnp.concatenate([pack, swap(pack, 'grp', 1)], axis=0)]
    convert_element_type x5 -> x4, other arithmetic: 26.8 us -> 19.4 us  [wide(): return value.astype(jnp.float32)]
    unnamed x207 -> x225, local copies, waits for them, and re-layouts: 61.2 us -> 66.3 us
  transfers between devices with their start and end apart: 64 -> 64, of which waited for: 23 -> 24; matrix products, arithmetic and copies ran while one was open for 54% -> 42% of each run, Pallas kernels for 3% -> 3%
where the time goes in v5:
time: 1100 us; the launch traced here: 1090 us
  waiting for transfers between devices  416 us (38%)
  matrix products  332 us (30%)
  other arithmetic  145 us (13%)
  local copies, waits for them, and re-layouts  103 us (9%)
  starting transfers between devices  45.4 us (4%)
  Pallas kernels  31.9 us (3%)
  between operations  15.7 us (1%)
    ppermute x53, waiting for transfers between devices, swap(): return lax.ppermute(value, axis, [(i, i ^ bit) for i in range(count)])  416 us
    dot_general x18, matrix products, dot32(): return jnp.dot(left, right, preferred_element_type=jnp.float32)  120 us
    dot_general x9, matrix products, dot_nt(): jnp.einsum('td,fd->tf', left, right, preferred_element_type=jnp.float32)  112 us
    dot_general x9, matrix products, dot_tn(): jnp.einsum('td,tf->df', left, right, preferred_element_type=jnp.float32)  100 us
    unnamed x225, local copies, waits for them, and re-layouts  66.3 us
    ppermute x53, starting transfers between devices, swap(): return lax.ppermute(value, axis, [(i, i ^ bit) for i in range(count)])  44.4 us
    select_n x15, other arithmetic, ordered(): jnp.where(keep, mine, theirs)  32.9 us
    pallas_call x2, Pallas kernels, attention_call(): pl.pallas_call(kernel, grid_spec=pltpu.PrefetchScalarGridSpec(num_scalar_...  31.9 us
  transfers between devices with their start and end apart: 64, of which 24 were waited for; matrix products, arithmetic and copies ran while one was open for 42% of the time, Pallas kernels for 3%

profile of v5, /device:TPU:0, one launch (start us, length us, event | category | flops | bytes accessed | tf_op | source)
XLA Modules:
  0.0 1089.1 jit_solution(10838740138552016101)
XLA Ops:
  25.2 39.6 %collective-permute-done = bf16[512,2048]{1,0:T(8,128)(2,1)} collective-permute-done((bf16[512,2048]{1,0:T(8,128)(2,1)}, bf16[512,2048]{1,0:T(8,128)(2,1)}, u32[]{:S(2)}, u32[]{:S(2)}) %collective-permute-start) | collective-permute-done | bytes 2097184 | tf_op jit(solution)/shard_map/ppermute | solution.py:175
  76.5 14.7 %fusion.69.q_ref.k_ref.v_ref = f32[1024,2048]{1,0:T(8,128)} fusion(bf16[1024,2048]{1,0:T(8,128)(2,1)} %pad_maximum_fusion.1, bf16[2048,512]{1,0:T(8,128)(2,1)} %get-tuple-element.211, bf16[2048,512]{1,0:T(8,128)(2,1)} %get-tuple-element.212, bf16[2048,1024]{1,0:T(8,128)(2,1)} %param.18), kind=kOutput, calls=%fused_computation.215 | convolution fusion | flops 8615100416 | bytes 20971520 | tf_op jit(solution)/shard_map/dot_general | solution.py:195
  91.3 11.9 %attend.1 = (bf16[1024,1024]{1,0:T(8,128)(2,1)}, bf16[1024,1024]{1,0:T(8,128)(2,1)}, bf16[1024,512]{1,0:T(8,128)(2,1)}, bf16[1024,512]{1,0:T(8,128)(2,1)}) custom-call(s32[1]{0:T(128)} %bitcast.first_ref, f32[1024,2048]{1,0:T(8,128)} %fusion.69.q_ref.k_ref.v_ref, f32[1024,2048]{1,0:T(8,128)} %fusion.69.q_ref.k_ref.v_ref, ...), custom_call_target="tpu_custom_call" | custom-call | flops 3221225472 | bytes 16106127 | tf_op jit(solution)/shard_map/attend/pallas_call | solution.py:153
  103.2 13.4 %collective-permute-done.2 = bf16[512,2048]{1,0:T(8,128)(2,1)} collective-permute-done((bf16[512,2048]{1,0:T(8,128)(2,1)S(1)}, bf16[512,2048]{1,0:T(8,128)(2,1)}, u32[]{:S(2)}, u32[]{:S(2)}) %collective-permute-start.2) | collective-permute-done | bytes 2097184 | tf_op jit(solution)/shard_map/ppermute | solution.py:175
  146.0 23.0 %collective-permute-done.6 = bf16[512,2048]{1,0:T(8,128)(2,1)} collective-permute-done((bf16[512,2048]{1,0:T(8,128)(2,1)}, bf16[512,2048]{1,0:T(8,128)(2,1)}, u32[]{:S(2)}, u32[]{:S(2)}) %collective-permute-start.6) | collective-permute-done | bytes 2097184 | tf_op jit(solution)/shard_map/ppermute | solution.py:175
  178.3 14.0 %convolution_convert_fusion.3 = bf16[2048,1024]{1,0:T(8,128)(2,1)} fusion(bf16[2048,2048]{1,0:T(8,128)(2,1)} %constant_dynamic-update-slice_fusion, bf16[1024,2048]{1,0:T(8,128)(2,1)} %all-gather.7.cloned.1.call-done), kind=kOutput, calls=%fused_computation.84 | convolution fusion | flops 8592031744 | bytes 16777216 | tf_op jit(solution)/shard_map/td,fd->tf/dot_general | solution.py:199
  201.6 10.8 convolution_convert_fusion.2
  212.5 35.1 %collective-permute-done.5 = bf16[512,2048]{1,0:T(8,128)(2,1)S(1)} collective-permute-done((bf16[512,2048]{1,0:T(8,128)(2,1)S(1)}, bf16[512,2048]{1,0:T(8,128)(2,1)S(1)}, u32[]{:S(2)}, u32[]{:S(2)}) %collective-permute-start.5) | collective-permute-done | bytes 2097184 | tf_op jit(solution)/shard_map/ppermute | solution.py:175
  251.3 46.6 %collective-permute-done.9 = bf16[512,2048]{1,0:T(8,128)(2,1)S(1)} collective-permute-done((bf16[512,2048]{1,0:T(8,128)(2,1)S(1)}, bf16[512,2048]{1,0:T(8,128)(2,1)S(1)}, u32[]{:S(2)}, u32[]{:S(2)}) %collective-permute-start.9) | collective-permute-done | bytes 2097184 | tf_op jit(solution)/shard_map/ppermute | solution.py:175
  333.5 10.5 convolution_convert_fusion.1
  347.5 21.1 %fusion.5 = (bf16[2048,1024]{1,0:T(8,128)(2,1)}, bf16[2048,1024]{1,0:T(8,128)(2,1)}, bf16[2048,1024]{1,0:T(8,128)(2,1)}) fusion(bf16[2048,1024]{1,0:T(8,128)(2,1)} %convolution_convert_fusion.3, bf16[2048,1024]{1,0:T(8,128)(2,1)} %convolution_convert_fusion.1, bf16[2048,2048]{1,0:T(8,128)(2,1)} %copy-done.50, bf16[1024,2048]{1,0:T(8,128)(2,1)S(1)} %bitcast.79), kind=kOutput, calls=%fused_computation.15 | convolution fusion | flops 8627683328 | bytes 33554432 | tf_op jit(solution)/shard_map/td,fd->tf/dot_general | solution.py:199
  372.1 10.6 convolution_convert_fusion
  382.6 16.8 %fusion.2 = (bf16[2048,1024]{1,0:T(8,128)(2,1)}, bf16[2048,1024]{1,0:T(8,128)(2,1)}, bf16[2048,1024]{1,0:T(8,128)(2,1)}) fusion(bf16[2048,1024]{1,0:T(8,128)(2,1)} %convolution_convert_fusion.2, bf16[2048,1024]{1,0:T(8,128)(2,1)} %convolution_convert_fusion, bf16[2048,2048]{1,0:T(8,128)(2,1)S(1)} %constant_dynamic-update-slice_fusion.8, ...), kind=kOutput, calls=%fused_computation.12 | convolution fusion | flops 8627683328 | bytes 33554432 | tf_op jit(solution)/shard_map/td,fd->tf/dot_general | solution.py:199
  399.4 12.8 %fusion.73 = f32[1024,2048]{1,0:T(8,128)S(1)} fusion(bf16[2048,1024]{1,0:T(8,128)(2,1)} %get-tuple-element.162, bf16[2048,2048]{1,0:T(8,128)(2,1)} %copy-done.63), kind=kOutput, calls=%fused_computation.219 | convolution fusion | flops 8589934592 | bytes 20971520 | tf_op jit(solution)/shard_map/td,tf->df/dot_general | solution.py:203
  412.2 13.2 %add_convert_fusion.6 = bf16[1024,2048]{1,0:T(8,128)(2,1)} fusion(f32[1024,2048]{1,0:T(8,128)S(1)} %fusion.73, bf16[2048,1024]{1,0:T(8,128)(2,1)S(1)} %copy-done.90, bf16[2048,2048]{1,0:T(8,128)(2,1)} %constant_dynamic-update-slice_fusion), kind=kOutput, calls=%fused_computation.41 | convolution fusion | flops 8594128896 | bytes 25165824 | tf_op jit(solution)/shard_map/td,tf->df/dot_general | solution.py:203
  445.8 12.0 %add_convert_fusion.3 = bf16[1024,2048]{1,0:T(8,128)(2,1)} fusion(f32[1024,2048]{1,0:T(8,128)} %fusion.34, bf16[1024,2048]{1,0:T(8,128)(2,1)} %bitcast.78, bf16[2048,1024]{1,0:T(8,128)(2,1)} %get-tuple-element.78), kind=kOutput, calls=%fused_computation.38 | convolution fusion | flops 4299161600 | bytes 18874368 | tf_op jit(solution)/shard_map/dot_general | solution.py:195
  484.2 11.6 %fusion.74 = f32[1024,2048]{1,0:T(8,128)} fusion(bf16[2048,1024]{1,0:T(8,128)(2,1)S(1)} %copy-done.94, bf16[2048,2048]{1,0:T(8,128)(2,1)S(1)} %bitcast.97), kind=kOutput, calls=%fused_computation.220 | convolution fusion | flops 8589934592 | bytes 20971520 | tf_op jit(solution)/shard_map/td,tf->df/dot_general | solution.py:203
  495.8 13.5 %add_convert_fusion.2 = bf16[1024,2048]{1,0:T(8,128)(2,1)} fusion(f32[1024,2048]{1,0:T(8,128)} %fusion.74, bf16[2048,1024]{1,0:T(8,128)(2,1)} %get-tuple-element.77, bf16[2048,2048]{1,0:T(8,128)(2,1)S(1)} %bitcast.95), kind=kOutput, calls=%fused_computation.37 | convolution fusion | flops 8594128896 | bytes 25165824 | tf_op jit(solution)/shard_map/td,tf->df/dot_general | solution.py:203
  509.6 10.8 add_convert_fusion.1
  537.0 13.2 %fusion.75 = f32[1024,2048]{1,0:T(8,128)} fusion(bf16[2048,1024]{1,0:T(8,128)(2,1)} %get-tuple-element.96, bf16[2048,2048]{1,0:T(8,128)(2,1)S(1)} %bitcast.99), kind=kOutput, calls=%fused_computation.221 | convolution fusion | flops 8589934592 | bytes 20971520 | tf_op jit(solution)/shard_map/td,tf->df/dot_general | solution.py:203
  550.1 24.1 %collective-permute-done.18 = bf16[512,2048]{1,0:T(8,128)(2,1)S(1)} collective-permute-done((bf16[512,2048]{1,0:T(8,128)(2,1)S(1)}, bf16[512,2048]{1,0:T(8,128)(2,1)S(1)}, u32[]{:S(2)}, u32[]{:S(2)}) %collective-permute-start.18) | collective-permute-done | bytes 2097184 | tf_op jit(solution)/shard_map/ppermute | solution.py:175
  588.7 15.3 %add_convert_fusion = bf16[1024,2048]{1,0:T(8,128)(2,1)} fusion(f32[1024,2048]{1,0:T(8,128)} %fusion.75, bf16[2048,1024]{1,0:T(8,128)(2,1)} %get-tuple-element.78, bf16[2048,2048]{1,0:T(8,128)(2,1)} %copy-done.50), kind=kOutput, calls=%fused_computation.35 | convolution fusion | flops 8594128896 | bytes 25165824 | tf_op jit(solution)/shard_map/td,tf->df/dot_general | solution.py:203
  604.3 30.7 %collective-permute-done.19 = bf16[512,2048]{1,0:T(8,128)(2,1)} collective-permute-done((bf16[512,2048]{1,0:T(8,128)(2,1)S(1)}, bf16[512,2048]{1,0:T(8,128)(2,1)}, u32[]{:S(2)}, u32[]{:S(2)}) %collective-permute-start.19) | collective-permute-done | bytes 2097184 | tf_op jit(solution)/shard_map/ppermute | solution.py:175
  660.9 20.0 %attend_back.1 = (bf16[1024,1024]{1,0:T(8,128)(2,1)}, bf16[1024,512]{1,0:T(8,128)(2,1)}, bf16[1024,512]{1,0:T(8,128)(2,1)}) custom-call(s32[1]{0:T(128)} %bitcast.first_ref, bf16[1024,1024]{1,0:T(8,128)(2,1)} %get-tuple-element.66.q_ref, bf16[1024,512]{1,0:T(8,128)(2,1)} %get-tuple-element.67.k_ref, bf16[1024,512]{1,0:T(8,128)(2,1)} %get-tuple-element.68.v_ref, ...), custom_call_target="tpu_custom_call" | custom-call | flops 7516192768 | bytes 37580964 | tf_op jit(solution)/shard_map/attend_back/pallas_call | solution.py:153
  704.1 23.7 %collective-permute-done.30 = bf16[256,2048]{1,0:T(8,128)(2,1)} collective-permute-done((bf16[256,2048]{1,0:T(8,128)(2,1)S(1)}, bf16[256,2048]{1,0:T(8,128)(2,1)}, u32[]{:S(2)}, u32[]{:S(2)}) %collective-permute-start.30) | collective-permute-done | bytes 1048608 | tf_op jit(solution)/shard_map/ppermute | solution.py:175
  743.4 16.8 %collective-permute-done.24 = bf16[512,1024]{1,0:T(8,128)(2,1)} collective-permute-done((bf16[512,1024]{1,0:T(8,128)(2,1)S(1)}, bf16[512,1024]{1,0:T(8,128)(2,1)}, u32[]{:S(2)}, u32[]{:S(2)}) %collective-permute-start.24) | collective-permute-done | bytes 1048608 | tf_op jit(solution)/shard_map/ppermute | solution.py:175
  762.8 18.1 %collective-permute-done.26 = bf16[512,1024]{1,0:T(8,128)(2,1)} collective-permute-done((bf16[512,1024]{1,0:T(8,128)(2,1)}, bf16[512,1024]{1,0:T(8,128)(2,1)}, u32[]{:S(2)}, u32[]{:S(2)}) %collective-permute-start.26) | collective-permute-done | bytes 1048608 | tf_op jit(solution)/shard_map/ppermute | solution.py:175
  794.6 21.6 %collective-permute-done.49 = bf16[2048,256]{0,1:T(8,128)(2,1)} collective-permute-done((bf16[2048,256]{0,1:T(8,128)(2,1)S(1)}, bf16[2048,256]{0,1:T(8,128)(2,1)}, u32[]{:S(2)}, u32[]{:S(2)}) %collective-permute-start.49) | collective-permute-done | bytes 1048608 | tf_op jit(solution)/shard_map/ppermute | solution.py:175
  818.9 19.9 %collective-permute-done.29 = bf16[512,2048]{1,0:T(8,128)(2,1)} collective-permute-done((bf16[512,2048]{1,0:T(8,128)(2,1)}, bf16[512,2048]{1,0:T(8,128)(2,1)}, u32[]{:S(2)}, u32[]{:S(2)}) %collective-permute-start.29) | collective-permute-done | bytes 2097184 | tf_op jit(solution)/shard_map/ppermute | solution.py:175
  883.6 17.5 %collective-permute-done.51 = bf16[256,2048]{1,0:T(8,128)(2,1)} collective-permute-done((bf16[256,2048]{1,0:T(8,128)(2,1)}, bf16[256,2048]{1,0:T(8,128)(2,1)}, u32[]{:S(2)}, u32[]{:S(2)}) %collective-permute-start.51) | collective-permute-done | bytes 1048608 | tf_op jit(solution)/shard_map/ppermute | solution.py:175
  980.2 13.3 %collective-permute-done.34 = bf16[512,1024]{1,0:T(8,128)(2,1)} collective-permute-done((bf16[512,1024]{1,0:T(8,128)(2,1)}, bf16[512,1024]{1,0:T(8,128)(2,1)}, u32[]{:S(2)}, u32[]{:S(2)}) %collective-permute-start.34) | collective-permute-done | bytes 1048608 | tf_op jit(solution)/shard_map/ppermute | solution.py:175
  995.2 20.7 %collective-permute-done.40 = bf16[256,2048]{1,0:T(8,128)(2,1)S(1)} collective-permute-done((bf16[256,2048]{1,0:T(8,128)(2,1)}, bf16[256,2048]{1,0:T(8,128)(2,1)S(1)}, u32[]{:S(2)}, u32[]{:S(2)}) %collective-permute-start.40) | collective-permute-done | bytes 1048608 | tf_op jit(solution)/shard_map/ppermute | solution.py:175
  (461 shorter events, 476.6 us)
Async XLA Ops:
  7.2 109.4 %all-gather.7.cloned.1.call-start = ((), (), s32[]{:S(2)}) async-start(), calls=%async_computation.6 | async-start | bytes 5242880 | tf_op jit(solution)/shard_map/all_gather | solution.py:285
  9.6 297.4 %all-gather.15.cloned.1.call-start = ((), (), s32[]{:S(2)}) async-start(), calls=%async_computation.16 | async-start | bytes 10485760 | tf_op jit(solution)/shard_map/all_gather | solution.py:362
  15.9 48.9 %collective-permute-start = (bf16[512,2048]{1,0:T(8,128)(2,1)}, bf16[512,2048]{1,0:T(8,128)(2,1)}, u32[]{:S(2)}, u32[]{:S(2)}) collective-permute-start(bf16[512,2048]{1,0:T(8,128)(2,1)} %fusion.26), channel_id=1, source_target_pairs={{0,1},{1,0},{2,3},{3,2},{4,5},{5,4},{6,7},{7,6},{8,9},{9,8},{10,11... | collective-permute-start | bytes 6291464 | tf_op jit(solution)/shard_map/ppermute | solution.py:175
  18.9 50.8 %collective-permute-start.1 = (bf16[512,2048]{1,0:T(8,128)(2,1)S(1)}, bf16[512,2048]{1,0:T(8,128)(2,1)}, u32[]{:S(2)}, u32[]{:S(2)}) collective-permute-start(bf16[512,2048]{1,0:T(8,128)(2,1)S(1)} %copy-done.5), channel_id=1, source_target_pairs={{0,16},{8,24},{16,0},{24,8},{1,17},{9,25},{17,1},{25,9},{2,18},{10... | collective-permute-start | bytes 6291464 | tf_op jit(solution)/shard_map/ppermute | solution.py:175
  69.6 46.9 %collective-permute-start.2 = (bf16[512,2048]{1,0:T(8,128)(2,1)S(1)}, bf16[512,2048]{1,0:T(8,128)(2,1)}, u32[]{:S(2)}, u32[]{:S(2)}) collective-permute-start(bf16[512,2048]{1,0:T(8,128)(2,1)S(1)} %copy-done.5), channel_id=1, source_target_pairs={{0,1},{1,0},{2,3},{3,2},{4,5},{5,4},{6,7},{7,6},{8,9},{9,8},{10,11... | collective-permute-start | bytes 6291464 | tf_op jit(solution)/shard_map/ppermute | solution.py:175
  120.7 52.8 %collective-permute-start.4 = (bf16[1024,2048]{1,0:T(8,128)(2,1)}, bf16[1024,2048]{1,0:T(8,128)(2,1)}, u32[]{:S(2)}, u32[]{:S(2)}) collective-permute-start(bf16[1024,2048]{1,0:T(8,128)(2,1)} %pad_maximum_fusion.2), channel_id=1, source_target_pairs={{0,8},{8,0},{16,24},{24,16},{1,9},{9,1},{17,25},{25,17},{2,10},{10... | collective-permute-start | bytes 12582920 | tf_op jit(solution)/shard_map/ppermute | solution.py:175
  120.7 48.4 %collective-permute-start.6 = (bf16[512,2048]{1,0:T(8,128)(2,1)}, bf16[512,2048]{1,0:T(8,128)(2,1)}, u32[]{:S(2)}, u32[]{:S(2)}) collective-permute-start(bf16[512,2048]{1,0:T(8,128)(2,1)} %collective-permute-done.2), channel_id=1, source_target_pairs={{0,16},{8,24},{16,0},{24,8},{1,17},{9,25},{17,1},{25,9},{2,18},{10... | collective-permute-start | bytes 6291464 | tf_op jit(solution)/shard_map/ppermute | solution.py:175
  131.6 456.5 %reduce-scatter.7.cloned.1.call-start = ((), (), s32[]{:S(2)}) async-start(), calls=%async_computation.7 | async-start | bytes 5242880 | tf_op jit(solution)/shard_map/reduce_scatter | solution.py:289
  139.1 53.2 %collective-permute-start.3 = (bf16[512,2048]{1,0:T(8,128)(2,1)}, bf16[512,2048]{1,0:T(8,128)(2,1)}, u32[]{:S(2)}, u32[]{:S(2)}) collective-permute-start(bf16[512,2048]{1,0:T(8,128)(2,1)} %convolution_convert_fusion.9), channel_id=1, source_target_pairs={{0,1},{1,0},{2,3},{3,2},{4,5},{5,4},{6,7},{7,6},{8,9},{9,8},{10,11... | collective-permute-start | bytes 6291464 | tf_op jit(solution)/shard_map/ppermute | solution.py:175
  199.4 48.1 %collective-permute-start.5 = (bf16[512,2048]{1,0:T(8,128)(2,1)S(1)}, bf16[512,2048]{1,0:T(8,128)(2,1)S(1)}, u32[]{:S(2)}, u32[]{:S(2)}) collective-permute-start(bf16[512,2048]{1,0:T(8,128)(2,1)S(1)} %multiply_convert_fusion), channel_id=1, source_target_pairs={{0,1},{1,0},{2,3},{3,2},{4,5},{5,4},{6,7},{7,6},{8,9},{9,8},{10,11... | collective-permute-start | bytes 6291464 | tf_op jit(solution)/shard_map/ppermute | solution.py:175
  249.8 81.2 %collective-permute-start.8 = (bf16[1024,2048]{1,0:T(8,128)(2,1)}, bf16[1024,2048]{1,0:T(8,128)(2,1)}, u32[]{:S(2)}, u32[]{:S(2)}) collective-permute-start(bf16[1024,2048]{1,0:T(8,128)(2,1)} %pad_maximum_fusion.3), channel_id=1, source_target_pairs={{0,8},{8,0},{16,24},{24,16},{1,9},{9,1},{17,25},{25,17},{2,10},{10... | collective-permute-start | bytes 12582920 | tf_op jit(solution)/shard_map/ppermute | solution.py:175
  249.8 48.0 %collective-permute-start.9 = (bf16[512,2048]{1,0:T(8,128)(2,1)S(1)}, bf16[512,2048]{1,0:T(8,128)(2,1)S(1)}, u32[]{:S(2)}, u32[]{:S(2)}) collective-permute-start(bf16[512,2048]{1,0:T(8,128)(2,1)S(1)} %multiply_convert_fusion), channel_id=1, source_target_pairs={{0,16},{8,24},{16,0},{24,8},{1,17},{9,25},{17,1},{25,9},{2,18},{10... | collective-permute-start | bytes 6291464 | tf_op jit(solution)/shard_map/ppermute | solution.py:175
  445.7 193.4 %reduce-scatter.9.cloned.1.call-start = ((), (), s32[]{:S(2)}) async-start(), calls=%async_computation.8 | async-start | bytes 5242880 | tf_op jit(solution)/shard_map/reduce_scatter | solution.py:289
  457.8 69.5 %collective-permute-start.14 = (bf16[1024,2048]{1,0:T(8,128)(2,1)}, bf16[1024,2048]{1,0:T(8,128)(2,1)}, u32[]{:S(2)}, u32[]{:S(2)}) collective-permute-start(bf16[1024,2048]{1,0:T(8,128)(2,1)} %add_convert_fusion.3), channel_id=1, source_target_pairs={{0,8},{8,0},{16,24},{24,16},{1,9},{9,1},{17,25},{25,17},{2,10},{10... | collective-permute-start | bytes 12582920 | tf_op jit(solution)/shard_map/ppermute | solution.py:175
  509.4 221.1 %reduce-scatter.11.cloned.1.call-start = ((), (), s32[]{:S(2)}) async-start(), calls=%async_computation.9 | async-start | bytes 5242880 | tf_op jit(solution)/shard_map/reduce_scatter | solution.py:289
  525.7 48.6 %collective-permute-start.18 = (bf16[512,2048]{1,0:T(8,128)(2,1)S(1)}, bf16[512,2048]{1,0:T(8,128)(2,1)S(1)}, u32[]{:S(2)}, u32[]{:S(2)}) collective-permute-start(bf16[512,2048]{1,0:T(8,128)(2,1)S(1)} %add_convert_fusion.11), channel_id=1, source_target_pairs={{0,16},{8,24},{16,0},{24,8},{1,17},{9,25},{17,1},{25,9},{2,18},{10... | collective-permute-start | bytes 6291464 | tf_op jit(solution)/shard_map/ppermute | solution.py:175
  532.3 47.8 %collective-permute-start.16 = (bf16[512,2048]{1,0:T(8,128)(2,1)S(1)}, bf16[512,2048]{1,0:T(8,128)(2,1)}, u32[]{:S(2)}, u32[]{:S(2)}) collective-permute-start(bf16[512,2048]{1,0:T(8,128)(2,1)S(1)} %add_convert_fusion.12), channel_id=1, source_target_pairs={{0,1},{1,0},{2,3},{3,2},{4,5},{5,4},{6,7},{7,6},{8,9},{9,8},{10,11... | collective-permute-start | bytes 6291464 | tf_op jit(solution)/shard_map/ppermute | solution.py:175
  535.5 145.4 %collective-permute-start.22 = (bf16[1024,2048]{1,0:T(8,128)(2,1)}, bf16[1024,2048]{1,0:T(8,128)(2,1)}, u32[]{:S(2)}, u32[]{:S(2)}) collective-permute-start(bf16[1024,2048]{1,0:T(8,128)(2,1)} %add_convert_fusion.1), channel_id=1, source_target_pairs={{0,16},{8,24},{16,0},{24,8},{1,17},{9,25},{17,1},{25,9},{2,18},{10... | collective-permute-start | bytes 12582920 | tf_op jit(solution)/shard_map/ppermute | solution.py:175
  588.1 46.9 %collective-permute-start.19 = (bf16[512,2048]{1,0:T(8,128)(2,1)S(1)}, bf16[512,2048]{1,0:T(8,128)(2,1)}, u32[]{:S(2)}, u32[]{:S(2)}) collective-permute-start(bf16[512,2048]{1,0:T(8,128)(2,1)S(1)} %fusion.70), channel_id=1, source_target_pairs={{0,1},{1,0},{2,3},{3,2},{4,5},{5,4},{6,7},{7,6},{8,9},{9,8},{10,11... | collective-permute-start | bytes 6291464 | tf_op jit(solution)/shard_map/ppermute | solution.py:175
  604.1 252.3 %reduce-scatter.13.cloned.1.call-start = ((), (), s32[]{:S(2)}) async-start(), calls=%async_computation.10 | async-start | bytes 1310720 | tf_op jit(solution)/shard_map/reduce_scatter | solution.py:289
  730.5 125.9 %reduce-scatter.15.cloned.1.call-start = ((), (), s32[]{:S(2)}) async-start(), calls=%async_computation.11 | async-start | bytes 1310720 | tf_op jit(solution)/shard_map/reduce_scatter | solution.py:289
  783.8 72.6 %reduce-scatter.17.cloned.1.call-start = ((), (), s32[]{:S(2)}) async-start(), calls=%async_computation.12 | async-start | bytes 1310720 | tf_op jit(solution)/shard_map/reduce_scatter | solution.py:289
  792.6 46.2 %collective-permute-start.29 = (bf16[512,2048]{1,0:T(8,128)(2,1)}, bf16[512,2048]{1,0:T(8,128)(2,1)}, u32[]{:S(2)}, u32[]{:S(2)}) collective-permute-start(bf16[512,2048]{1,0:T(8,128)(2,1)} %convolution_convert_fusion.10), channel_id=1, source_target_pairs={{0,1},{1,0},{2,3},{3,2},{4,5},{5,4},{6,7},{7,6},{8,9},{9,8},{10,11... | collective-permute-start | bytes 6291464 | tf_op jit(solution)/shard_map/ppermute | solution.py:175
  794.5 150.2 %all-gather.9.cloned.1.call-start = ((), (), s32[]{:S(2)}) async-start(), calls=%async_computation.13 | async-start | bytes 1310720 | tf_op jit(solution)/shard_map/all_gather | solution.py:285
  852.7 53.3 %collective-permute-start.50 = (bf16[2048,512]{0,1:T(8,128)(2,1)}, bf16[2048,512]{0,1:T(8,128)(2,1)}, u32[]{:S(2)}, u32[]{:S(2)}) collective-permute-start(bf16[2048,512]{0,1:T(8,128)(2,1)} %pad_maximum_fusion.13), channel_id=1, source_target_pairs={{0,8},{8,0},{16,24},{24,16},{1,9},{9,1},{17,25},{25,17},{2,10},{10... | collective-permute-start | bytes 6291464 | tf_op jit(solution)/shard_map/ppermute | solution.py:175
  856.4 95.4 %all-gather.11.cloned.1.call-start = ((), (), s32[]{:S(2)}) async-start(), calls=%async_computation.14 | async-start | bytes 1310720 | tf_op jit(solution)/shard_map/all_gather | solution.py:285
  875.5 78.7 %collective-permute-start.27 = (bf16[1024,2048]{1,0:T(8,128)(2,1)}, bf16[1024,2048]{1,0:T(8,128)(2,1)}, u32[]{:S(2)}, u32[]{:S(2)}) collective-permute-start(bf16[1024,2048]{1,0:T(8,128)(2,1)} %convolution_convert_fusion.4), channel_id=1, source_target_pairs={{0,8},{8,0},{16,24},{24,16},{1,9},{9,1},{17,25},{25,17},{2,10},{10... | collective-permute-start | bytes 12582920 | tf_op jit(solution)/shard_map/ppermute | solution.py:175
  883.6 70.2 %all-gather.13.cloned.1.call-start = ((), (), s32[]{:S(2)}) async-start(), calls=%async_computation.15 | async-start | bytes 1310720 | tf_op jit(solution)/shard_map/all_gather | solution.py:285
  953.8 62.1 %collective-permute-start.40 = (bf16[256,2048]{1,0:T(8,128)(2,1)}, bf16[256,2048]{1,0:T(8,128)(2,1)S(1)}, u32[]{:S(2)}, u32[]{:S(2)}) collective-permute-start(bf16[256,2048]{1,0:T(8,128)(2,1)} %all-gather.13.cloned.1.call-done), channel_id=1, source_target_pairs={{0,16},{8,24},{16,0},{24,8},{1,17},{9,25},{17,1},{25,9},{2,18},{10... | collective-permute-start | bytes 3145736 | tf_op jit(solution)/shard_map/ppermute | solution.py:175
  960.5 79.9 %collective-permute-start.28 = (bf16[512,2048]{1,0:T(8,128)(2,1)S(1)}, bf16[512,2048]{1,0:T(8,128)(2,1)}, u32[]{:S(2)}, u32[]{:S(2)}) collective-permute-start(bf16[512,2048]{1,0:T(8,128)(2,1)S(1)} %add_convert_fusion.7), channel_id=1, source_target_pairs={{0,1},{1,0},{2,3},{3,2},{4,5},{5,4},{6,7},{7,6},{8,9},{9,8},{10,11... | collective-permute-start | bytes 6291464 | tf_op jit(solution)/shard_map/ppermute | solution.py:175
  973.9 79.2 %collective-permute-start.32 = (bf16[1024,1024]{1,0:T(8,128)(2,1)}, bf16[1024,1024]{1,0:T(8,128)(2,1)}, u32[]{:S(2)}, u32[]{:S(2)}) collective-permute-start(bf16[1024,1024]{1,0:T(8,128)(2,1)} %pad_maximum_fusion.8), channel_id=1, source_target_pairs={{0,8},{8,0},{16,24},{24,16},{1,9},{9,1},{17,25},{25,17},{2,10},{10... | collective-permute-start | bytes 6291464 | tf_op jit(solution)/shard_map/ppermute | solution.py:175
  979.5 47.1 %collective-permute-start.36 = (bf16[256,1024]{1,0:T(8,128)(2,1)S(1)}, bf16[256,1024]{1,0:T(8,128)(2,1)S(1)}, u32[]{:S(2)}, u32[]{:S(2)}) collective-permute-start(bf16[256,1024]{1,0:T(8,128)(2,1)S(1)} %slice.168), channel_id=1, source_target_pairs={{0,16},{8,24},{16,0},{24,8},{1,17},{9,25},{17,1},{25,9},{2,18},{10... | collective-permute-start | bytes 1572872 | tf_op jit(solution)/shard_map/ppermute | solution.py:175
  (137 other events, 2050.1 us)
Sparse Core Ops, SparseCore 0:
  10.1 83.4 all-gather.6
  131.7 149.9 all-gather.14
  445.9 77.0 reduce-scatter.6
  525.1 77.3 reduce-scatter.8
  605.2 77.2 reduce-scatter.10
  730.6 27.4 reduce-scatter.12
  783.9 27.3 reduce-scatter.14
  814.2 25.7 reduce-scatter.16
  856.5 27.6 all-gather.8
  885.6 27.0 all-gather.10
  922.7 27.3 all-gather.12

commit v6 on v5

--- a/solution.py
+++ b/solution.py
@@ -217,15 +217,10 @@
     return [lax.all_gather(mine, "col", axis=0, tiled=True)]
 
 
-def col_scatter(product, beside=None):
+def col_scatter(product):
     if lax.axis_size("col") == 2:
         theirs = swap(low(product(1)), "col", 1)
-        if beside is not None:
-            theirs, beside = tie(theirs, beside)
-            return product(0) + wide(theirs), beside
         return product(0) + wide(theirs)
-    if beside is not None:
-        return col_scatter(product), beside
     return wide(lax.psum_scatter(low(product(0)), "col", scatter_dimension=0, tiled=True))
 
 
@@ -234,24 +229,27 @@
     return [lax.slice_in_dim(value, i * size, (i + 1) * size, axis=dim) for i in range(count)]
 
 
-def square_gather(mine):
+def square_gather(mine, beside_first, beside_second):
     if lax.axis_size("col") == 2:
-        over_x = swap(mine, "col", 1)
-        over_y = swap(mine, "grp", 2)
+        over_x, over_y, beside_first = tie(
+            swap(mine, "col", 1), swap(mine, "grp", 2), beside_first
+        )
         half = mine.shape[0] // 2
-        across_first = swap(over_x[:half], "grp", 2)
-        across_second = swap(over_y[half:], "col", 1)
+        across_first, across_second, beside_second = tie(
+            swap(over_x[:half], "grp", 2), swap(over_y[half:], "col", 1), beside_second
+        )
         near = jnp.concatenate([mine, over_x], axis=0)
-        return near, jnp.concatenate([over_y, across_first, across_second], axis=0)
+        far = jnp.concatenate([over_y, across_first, across_second], axis=0)
+        return near, far, beside_first, beside_second
     near = lax.all_gather(mine, "col", axis=0, tiled=True)
-    return near, swap(near, "grp", 2)
+    return near, swap(near, "grp", 2), beside_first, beside_second
 
 
 def with_core(pack):
     return jnp.concatenate([pack, swap(pack, "grp", 1)], axis=0)
 
 
-def square_scatter(near, far):
+def square_scatter(near, far, later):
     size = far.shape[0]
     if lax.axis_size("col") == 2:
         half, part = size // 2, size // 4
@@ -260,11 +258,12 @@
         rest = jnp.zeros_like(across_first)
         to_y = low(wide(far[:half]) + wide(jnp.concatenate([rest, across_second], axis=0)))
         to_x = low(near(half, size) + wide(jnp.concatenate([across_first, rest], axis=0)))
+        to_y, to_x, *later = tie(to_y, to_x, *later)
         from_y = swap(to_y, "grp", 2)
         from_x = swap(to_x, "col", 1)
-        return near(0, half) + wide(from_x) + wide(from_y)
+        return near(0, half) + wide(from_x) + wide(from_y), later
     total = low(near(0, size) + wide(swap(far, "grp", 2)))
-    return wide(lax.psum_scatter(total, "col", scatter_dimension=0, tiled=True))
+    return wide(lax.psum_scatter(total, "col", scatter_dimension=0, tiled=True)), later
 
 
 def butterfly(value, axes):
@@ -355,21 +354,16 @@
     gathered_in = jnp.concatenate(col_gather(low(normalized_input)), axis=0)
     packed_length = gathered_in.shape[0]
 
-    down_own, gate_own, up_own = [
-        own_quarter(weight, core, ypos) for weight in (down_weight, gate_weight.T, up_weight.T)
+    down_rows, gate_rows, up_rows = [
+        row_gather(own_quarter(weight, core, ypos))
+        for weight in (down_weight, gate_weight.T, up_weight.T)
     ]
-    down_rows = row_gather(down_own)
-    gate_up = lax.all_gather(jnp.stack([gate_own, up_own]), "row", axis=0)
-
-    cot_far = []
-    if in_pairs:
-        gathered_in, cot_now, cot_over_y = tie(
-            gathered_in, cotangent, swap(cotangent, "grp", 2)
-        )
-        cot_far.append(cot_over_y)
-    else:
-        gathered_in, cot_now = tie(gathered_in, cotangent)
+
+    gathered_in, cot_now = tie(gathered_in, cotangent)
     cot_near = col_gather(cot_now)
+    cot_far = [swap(cotangent, "grp", 2)] if in_pairs else []
+    cot_far.append(swap(cot_near[-1], "grp", 2))
+    cot_sets = [with_core(jnp.concatenate(pack, axis=0)) for pack in (cot_near, cot_far)]
 
     key_slice = lax.dynamic_slice_in_dim(key_matrix, key_first * head_dim, key_cols, 1)
     value_slice = lax.dynamic_slice_in_dim(value_matrix, key_first * head_dim, key_cols, 1)
@@ -395,25 +389,16 @@
         head_dim,
         (3 * score_flops, key_heads),
     )
-    attn_low, down_rows, cot_near[-1] = tie(attn_low, down_rows, cot_near[-1])
-    cot_far.append(swap(cot_near[-1], "grp", 2))
-    cot_sets = [with_core(jnp.concatenate(pack, axis=0)) for pack in (cot_near, cot_far)]
+    attn_low, down_rows = tie(attn_low, down_rows)
     act_near = low(dot_nt(cot_sets[0], down_rows))
     act_far = low(dot_nt(cot_sets[1], down_rows))
     attn_parts = blocks_of(attn_low, 0, 2) if in_pairs else [attn_low]
-    from_attention, act_near = col_scatter(
-        lambda i: dot32(attn_parts[i], output_weight), act_near
-    )
-    hidden_res = inputs + from_attention
+    hidden_res = inputs + col_scatter(lambda i: dot32(attn_parts[i], output_weight))
     normed_mid, second_back = jax.vjp(normalize, hidden_res, second_gain)
 
-    mid_near, mid_far = square_gather(low(normed_mid))
-    mid_near, act_far = tie(mid_near, act_far)
-    gate_rows, up_rows = [gate_up[:, i].reshape(-1, width) for i in range(2)]
-    mid_near = with_core(mid_near)
-    gate_near, mid_far = tie(low(dot_nt(mid_near, gate_rows)), mid_far)
-    mid_sets = [mid_near, with_core(mid_far)]
-    gate_lins = [gate_near, low(dot_nt(mid_sets[1], gate_rows))]
+    mid_near, mid_far, act_near, act_far = square_gather(low(normed_mid), act_near, act_far)
+    mid_sets = [with_core(mid_near), with_core(mid_far)]
+    gate_lins = [low(dot_nt(mid, gate_rows)) for mid in mid_sets]
     act_grads = [act_near, act_far]
     acts, gate_backs, up_backs = [], [], []
     for mid, act_grad, gate_lin in zip(mid_sets, act_grads, gate_lins):
@@ -447,18 +432,17 @@
     down_part = row_scatter(down_low)
     mid_from_core = near_sum(mid_product)
     mid_far_sum = far_sum(mid_product)
-    mid_far_sum, gate_backs[0], up_backs[0], gate_backs[1] = tie(
-        mid_far_sum, gate_backs[0], up_backs[0], gate_backs[1]
-    )
-    mid_grad = square_scatter(
+    mid_far_sum, gate_backs[0], up_backs[0] = tie(mid_far_sum, gate_backs[0], up_backs[0])
+    mid_grad, (gate_backs[1], acts[1]) = square_scatter(
         lambda first, last: mid_product(0, first, last) + wide(mid_from_core[first:last]),
         mid_far_sum,
-    )
-    gate_low = weight_sum(gate_backs, mid_sets)
-    gate_part = row_scatter(gate_low)
+        [gate_backs[1], acts[1]],
+    )
+    gate_part = row_scatter(weight_sum(gate_backs, mid_sets))
     out_far = far_sum(out_product)
     out_far, up_backs[1] = tie(out_far, up_backs[1])
-    out_over_y = swap(out_far, "grp", 2)
+    out_first, out_second = blocks_of(out_far, 0, 2)
+    out_first = swap(out_first, "grp", 2)
     up_part = row_scatter(weight_sum(up_backs, mid_sets))
 
     res_from_mid, second_gain_part = second_back(mid_grad)
@@ -469,9 +453,8 @@
 
     mixed_low = low(dot_nt(shard_rows, output_weight))
     out_low = low(dot_tn(attn_low, shard_rows))
-    mixed_low, out_low = tie(mixed_low, sum_cores(out_low, core))
-    out_part, up_part = tie(sum_y(out_low, ypos), up_part)
-    out_part = row_scatter(out_part)
+    mixed_low, out_low, out_first = tie(mixed_low, sum_cores(out_low, core), out_first)
+    out_low = sum_y(out_low, ypos)
     query_back, key_back, value_back = attention_call(
         attend_back_kernel,
         "attend_back",
@@ -488,21 +471,25 @@
         head_dim,
         (7 * score_flops, key_heads),
     )
-    query_back, out_over_y, acts[0] = tie(query_back, out_over_y, acts[0])
+    query_back, out_low = tie(query_back, out_low)
+    out_part, up_part = tie(out_low, up_part)
+    out_part = row_gather(row_scatter(out_part))
     pair_back = jnp.concatenate([key_back, value_back], axis=1)
     back_all = jnp.concatenate([query_back, pair_back], axis=1)
-    query_part = sum_quarters(low(dot_tn(gathered_in, query_back)), core, ypos)
-    pair_part = sum_quarters(low(dot_tn(gathered_in, pair_back)), core, ypos)
-    query_part, pair_part, down_part, gate_part, second_gain_part, acts[0] = tie(
-        query_part, pair_part, down_part, gate_part, second_gain_part, acts[0]
-    )
-    out_part, query_part, pair_part = tie(
-        out_part, row_scatter(query_part), row_scatter(pair_part)
-    )
-    pair_part, query_part, out_part = [row_gather(p) for p in (pair_part, query_part, out_part)]
+    query_low_grad = low(dot_tn(gathered_in, query_back))
+    pair_low_grad = low(dot_tn(gathered_in, pair_back))
+    query_low_grad, pair_low_grad, acts[0] = tie(query_low_grad, pair_low_grad, acts[0])
+    query_part = sum_quarters(query_low_grad, core, ypos)
+    pair_part = sum_quarters(pair_low_grad, core, ypos)
+    query_part, pair_part, down_part, gate_part, second_gain_part, out_second = tie(
+        query_part, pair_part, down_part, gate_part, second_gain_part, out_second
+    )
+    both_part = row_gather(row_scatter(jnp.concatenate([query_part, pair_part], axis=1)))
+    query_part, pair_part = both_part[:, :query_cols], both_part[:, query_cols:]
     back_parts = blocks_of(back_all, 0, 2) if in_pairs else [back_all]
     in_grad = col_scatter(lambda i: dot_nt(back_parts[i], project_in))
 
+    out_over_y = jnp.concatenate([out_first, swap(out_second, "grp", 2)], axis=0)
     out_from_core = near_sum(out_product)
     piece = packed_length // 2 if in_pairs else packed_length
 

time: 1100 us -> 1090 us (level)
  matrix products: 332 us -> 360 us
  waiting for transfers between devices: 416 us -> 393 us
  local copies, waits for them, and re-layouts: 103 us -> 91.9 us
    ppermute x53 -> x54, waiting for transfers between devices: 416 us -> 388 us  [swap(): return lax.ppermute(value, axis, [(i, i ^ bit) for i in range(count)])]
    dot_general x9, matrix products: 112 us -> 124 us  [dot_nt(): jnp.einsum('td,fd->tf', left, right, preferred_element_type=jnp.float32)]
    dot_general x18, matrix products: 120 us -> 131 us  [dot32(): return jnp.dot(left, right, preferred_element_type=jnp.float32)]
    unnamed x225 -> x220, local copies, waits for them, and re-layouts: 66.3 us -> 57 us
    convert_element_type x10 -> x11, other arithmetic: 22 us -> 27.5 us  [low(): return value.astype(jnp.bfloat16)]
    ppermute x53 -> x54, starting transfers between devices: 44.4 us -> 41.3 us  [swap(): return lax.ppermute(value, axis, [(i, i ^ bit) for i in range(count)])]
  transfers between devices with their start and end apart: 64 -> 64, of which waited for: 24 -> 26; matrix products, arithmetic and copies ran while one was open for 42% -> 44% of each run, Pallas kernels for 3% -> 3%
where the time goes in v6:
time: 1090 us; the launch traced here: 1080 us
  waiting for transfers between devices  393 us (36%)
  matrix products  360 us (33%)
  other arithmetic  143 us (13%)
  local copies, waits for them, and re-layouts  91.9 us (8%)
  starting transfers between devices  42.3 us (4%)
  Pallas kernels  32.2 us (3%)
  between operations  15.6 us (1%)
    ppermute x54, waiting for transfers between devices, swap(): return lax.ppermute(value, axis, [(i, i ^ bit) for i in range(count)])  388 us
    dot_general x18, matrix products, dot32(): return jnp.dot(left, right, preferred_element_type=jnp.float32)  131 us
    dot_general x9, matrix products, dot_nt(): jnp.einsum('td,fd->tf', left, right, preferred_element_type=jnp.float32)  124 us
    dot_general x9, matrix products, dot_tn(): jnp.einsum('td,tf->df', left, right, preferred_element_type=jnp.float32)  104 us
    unnamed x220, local copies, waits for them, and re-layouts  57 us
    ppermute x54, starting transfers between devices, swap(): return lax.ppermute(value, axis, [(i, i ^ bit) for i in range(count)])  41.3 us
    pallas_call x2, Pallas kernels, attention_call(): pl.pallas_call(kernel, grid_spec=pltpu.PrefetchScalarGridSpec(num_scalar_...  32.2 us
    select_n x15, other arithmetic, ordered(): jnp.where(keep, mine, theirs)  31.5 us
  transfers between devices with their start and end apart: 64, of which 26 were waited for; matrix products, arithmetic and copies ran while one was open for 44% of the time, Pallas kernels for 3%

profile of v6, /device:TPU:0, one launch (start us, length us, event | category | flops | bytes accessed | tf_op | source)
XLA Modules:
  0.0 1077.3 jit_solution(9322985761967032319)
XLA Ops:
  26.3 37.1 %collective-permute-done = bf16[512,2048]{1,0:T(8,128)(2,1)} collective-permute-done((bf16[512,2048]{1,0:T(8,128)(2,1)}, bf16[512,2048]{1,0:T(8,128)(2,1)}, u32[]{:S(2)}, u32[]{:S(2)}) %collective-permute-start) | collective-permute-done | bytes 2097184 | tf_op jit(solution)/shard_map/ppermute | solution.py:175
  75.2 14.7 %fusion.73.q_ref.k_ref.v_ref = f32[1024,2048]{1,0:T(8,128)} fusion(bf16[1024,2048]{1,0:T(8,128)(2,1)} %pad_maximum_fusion.2, bf16[2048,512]{1,0:T(8,128)(2,1)} %get-tuple-element.190, bf16[2048,512]{1,0:T(8,128)(2,1)} %get-tuple-element.191, bf16[2048,1024]{1,0:T(8,128)(2,1)} %param.18), kind=kOutput, calls=%fused_computation.218 | convolution fusion | flops 8615100416 | bytes 20971520 | tf_op jit(solution)/shard_map/dot_general | solution.py:195
  89.9 12.0 %attend.1 = (bf16[1024,1024]{1,0:T(8,128)(2,1)}, bf16[1024,1024]{1,0:T(8,128)(2,1)}, bf16[1024,512]{1,0:T(8,128)(2,1)}, bf16[1024,512]{1,0:T(8,128)(2,1)}) custom-call(s32[1]{0:T(128)} %bitcast.first_ref, f32[1024,2048]{1,0:T(8,128)} %fusion.73.q_ref.k_ref.v_ref, f32[1024,2048]{1,0:T(8,128)} %fusion.73.q_ref.k_ref.v_ref, ...), custom_call_target="tpu_custom_call" | custom-call | flops 3221225472 | bytes 16106127 | tf_op jit(solution)/shard_map/attend/pallas_call | solution.py:153
  101.9 13.3 %collective-permute-done.4 = bf16[512,2048]{1,0:T(8,128)(2,1)} collective-permute-done((bf16[512,2048]{1,0:T(8,128)(2,1)S(1)}, bf16[512,2048]{1,0:T(8,128)(2,1)}, u32[]{:S(2)}, u32[]{:S(2)}) %collective-permute-start.4) | collective-permute-done | bytes 2097184 | tf_op jit(solution)/shard_map/ppermute | solution.py:175
  133.3 34.4 %collective-permute-done.10 = bf16[512,2048]{1,0:T(8,128)(2,1)} collective-permute-done((bf16[512,2048]{1,0:T(8,128)(2,1)}, bf16[512,2048]{1,0:T(8,128)(2,1)}, u32[]{:S(2)}, u32[]{:S(2)}) %collective-permute-start.10) | collective-permute-done | bytes 2097184 | tf_op jit(solution)/shard_map/ppermute | solution.py:175
  186.6 13.7 %convolution_convert_fusion.3 = bf16[2048,1024]{1,0:T(8,128)(2,1)} fusion(bf16[2048,2048]{1,0:T(8,128)(2,1)S(1)} %constant_dynamic-update-slice_fusion, bf16[1024,2048]{1,0:T(8,128)(2,1)} %all-gather.6.cloned.1.call-done), kind=kOutput, calls=%fused_computation.85 | convolution fusion | flops 8592031744 | bytes 16777216 | tf_op jit(solution)/shard_map/td,fd->tf/dot_general | solution.py:199
  200.4 28.6 %collective-permute-done.2 = bf16[512,2048]{1,0:T(8,128)(2,1)S(1)} collective-permute-done((bf16[512,2048]{1,0:T(8,128)(2,1)S(1)}, bf16[512,2048]{1,0:T(8,128)(2,1)S(1)}, u32[]{:S(2)}, u32[]{:S(2)}) %collective-permute-start.2) | collective-permute-done | bytes 2097184 | tf_op jit(solution)/shard_map/ppermute | solution.py:175
  242.7 12.6 %convolution_convert_fusion.1 = bf16[2048,1024]{1,0:T(8,128)(2,1)} fusion(bf16[2048,2048]{1,0:T(8,128)(2,1)} %constant_dynamic-update-slice_fusion.3, bf16[1024,2048]{1,0:T(8,128)(2,1)S(1)} %copy-done.78), kind=kOutput, calls=%fused_computation.83 | convolution fusion | flops 8592031744 | bytes 16777216 | tf_op jit(solution)/shard_map/td,fd->tf/dot_general | solution.py:199
  269.3 14.7 %convolution_convert_fusion.2 = bf16[2048,1024]{1,0:T(8,128)(2,1)} fusion(bf16[1024,2048]{0,1:T(8,128)(2,1)} %all-gather.8.cloned.1.call-done, bf16[1024,2048]{1,0:T(8,128)(2,1)} %collective-permute-done.6, bf16[512,2048]{1,0:T(8,128)(2,1)} %copy-done.35, bf16[512,2048]{1,0:T(8,128)(2,1)S(1)} %multiply_convert_fusion), kind=kOutput, calls=%fused_computation.84 | convolution fusion | flops 8617197568 | bytes 16777216 | tf_op jit(solution)/shard_map/td,fd->tf/dot_general | solution.py:199
  284.0 20.8 %fusion.5 = (bf16[2048,1024]{1,0:T(8,128)(2,1)}, bf16[2048,1024]{1,0:T(8,128)(2,1)}, bf16[2048,1024]{1,0:T(8,128)(2,1)}) fusion(bf16[2048,1024]{1,0:T(8,128)(2,1)} %convolution_convert_fusion.3, bf16[2048,1024]{1,0:T(8,128)(2,1)} %convolution_convert_fusion.2, bf16[1024,2048]{0,1:T(8,128)(2,1)} %all-gather.10.cloned.1.call-done, ...), kind=kOutput, calls=%fused_computation.15 | convolution fusion | flops 8652849152 | bytes 33554432 | tf_op jit(solution)/shard_map/td,fd->tf/dot_general | solution.py:199
  309.8 13.0 %convolution_convert_fusion = bf16[2048,1024]{1,0:T(8,128)(2,1)} fusion(bf16[2048,2048]{1,0:T(8,128)(2,1)} %constant_dynamic-update-slice_fusion.6, bf16[1024,2048]{0,1:T(8,128)(2,1)S(1)} %copy-done.82), kind=kOutput, calls=%fused_computation.82 | convolution fusion | flops 8592031744 | bytes 16777216 | tf_op jit(solution)/shard_map/td,fd->tf/dot_general | solution.py:199
  322.8 20.8 %fusion.2 = (bf16[2048,1024]{1,0:T(8,128)(2,1)}, bf16[2048,1024]{1,0:T(8,128)(2,1)}, bf16[2048,1024]{1,0:T(8,128)(2,1)}) fusion(bf16[2048,1024]{1,0:T(8,128)(2,1)} %convolution_convert_fusion.1, bf16[2048,1024]{1,0:T(8,128)(2,1)} %convolution_convert_fusion, bf16[2048,2048]{1,0:T(8,128)(2,1)} %constant_dynamic-update-slice_fusion.6, ...), kind=kOutput, calls=%fused_computation.12 | convolution fusion | flops 8627683328 | bytes 33554432 | tf_op jit(solution)/shard_map/td,fd->tf/dot_general | solution.py:199
  343.6 13.2 %fusion.78 = f32[1024,2048]{1,0:T(8,128)S(1)} fusion(bf16[2048,1024]{1,0:T(8,128)(2,1)} %get-tuple-element.85, bf16[2048,2048]{1,0:T(8,128)(2,1)} %constant_dynamic-update-slice_fusion.3), kind=kOutput, calls=%fused_computation.223 | convolution fusion | flops 8589934592 | bytes 20971520 | tf_op jit(solution)/shard_map/td,tf->df/dot_general | solution.py:203
  356.9 11.1 %add_convert_fusion.6 = bf16[1024,2048]{1,0:T(8,128)(2,1)} fusion(f32[1024,2048]{1,0:T(8,128)S(1)} %fusion.78, bf16[2048,1024]{1,0:T(8,128)(2,1)S(1)} %copy-done.94, bf16[2048,2048]{1,0:T(8,128)(2,1)S(1)} %bitcast.68), kind=kOutput, calls=%fused_computation.42 | convolution fusion | flops 8594128896 | bytes 25165824 | tf_op jit(solution)/shard_map/td,tf->df/dot_general | solution.py:203
  368.0 10.9 %fusion.44 = f32[1024,2048]{1,0:T(8,128)} fusion(bf16[1024,2048]{0,1:T(8,128)(2,1)} %all-gather.8.cloned.1.call-done, bf16[2048,1024]{1,0:T(8,128)(2,1)} %get-tuple-element.83), kind=kOutput, calls=%fused_computation.122 | convolution fusion | flops 4294967296 | bytes 14680064 | tf_op jit(solution)/shard_map/dot_general | solution.py:195
  403.4 10.9 %fusion.47 = f32[1024,2048]{1,0:T(8,128)} fusion(bf16[1024,2048]{0,1:T(8,128)(2,1)} %all-gather.8.cloned.1.call-done, bf16[2048,1024]{1,0:T(8,128)(2,1)} %get-tuple-element.83), kind=kOutput, calls=%fused_computation.125 | convolution fusion | flops 4294967296 | bytes 14680064 | tf_op jit(solution)/shard_map/dot_general | solution.py:195
  431.5 18.5 %collective-permute-done.15 = bf16[256,2048]{1,0:T(8,128)(2,1)S(1)} collective-permute-done((bf16[256,2048]{1,0:T(8,128)(2,1)S(1)}, bf16[256,2048]{1,0:T(8,128)(2,1)S(1)}, u32[]{:S(2)}, u32[]{:S(2)}) %collective-permute-start.15) | collective-permute-done | bytes 1048608 | tf_op jit(solution)/shard_map/ppermute | solution.py:175
  466.2 14.2 %fusion.79 = f32[1024,2048]{1,0:T(8,128)} fusion(bf16[2048,1024]{1,0:T(8,128)(2,1)S(1)} %copy-done.100, bf16[2048,2048]{1,0:T(8,128)(2,1)} %constant_dynamic-update-slice_fusion.6), kind=kOutput, calls=%fused_computation.224 | convolution fusion | flops 8589934592 | bytes 20971520 | tf_op jit(solution)/shard_map/td,tf->df/dot_general | solution.py:203
  480.5 13.8 %add_convert_fusion.2 = bf16[1024,2048]{1,0:T(8,128)(2,1)} fusion(f32[1024,2048]{1,0:T(8,128)} %fusion.79, bf16[2048,1024]{1,0:T(8,128)(2,1)S(1)} %copy-done.93, bf16[1024,2048]{1,0:T(8,128)(2,1)} %collective-permute-done.6, bf16[512,2048]{1,0:T(8,128)(2,1)S(1)} %copy-done.36, bf16[512,2048]{1,0:T(8,128)(2,1)S(1)} %copy-done.33), kind=kOutput, calls=%fused_computation.38 | convolution fusion | flops 8619294720 | bytes 25165824 | tf_op jit(solution)/shard_map/td,tf->df/dot_general | solution.py:203
  517.3 10.9 %add_convert_fusion.1 = bf16[1024,2048]{1,0:T(8,128)(2,1)} fusion(bf16[1024,2048]{1,0:T(8,128)(2,1)} %collective-permute-done.21, bf16[1024,2048]{1,0:T(8,128)(2,1)} %all-gather.6.cloned.1.call-done, bf16[2048,1024]{1,0:T(8,128)(2,1)} %get-tuple-element.85), kind=kOutput, calls=%fused_computation.37 | convolution fusion | flops 4301258752 | bytes 14680064 | tf_op jit(solution)/shard_map/dot_general | solution.py:195
  528.2 13.8 %fusion.80 = f32[1024,2048]{1,0:T(8,128)} fusion(bf16[2048,1024]{1,0:T(8,128)(2,1)S(1)} %copy-done.98, bf16[2048,2048]{1,0:T(8,128)(2,1)} %constant_dynamic-update-slice_fusion.6), kind=kOutput, calls=%fused_computation.225 | convolution fusion | flops 8589934592 | bytes 20971520 | tf_op jit(solution)/shard_map/td,tf->df/dot_general | solution.py:203
  542.0 14.0 %add_convert_fusion = bf16[1024,2048]{1,0:T(8,128)(2,1)} fusion(f32[1024,2048]{1,0:T(8,128)} %fusion.80, bf16[2048,1024]{1,0:T(8,128)(2,1)S(1)} %copy-done.91, bf16[1024,2048]{1,0:T(8,128)(2,1)} %collective-permute-done.6, bf16[512,2048]{1,0:T(8,128)(2,1)S(1)} %copy-done.37, bf16[512,2048]{1,0:T(8,128)(2,1)S(1)} %copy-done.33), kind=kOutput, calls=%fused_computation.34 | convolution fusion | flops 8619294720 | bytes 25165824 | tf_op jit(solution)/shard_map/td,tf->df/dot_general | solution.py:203
  599.8 34.2 %collective-permute-done.22 = bf16[512,2048]{1,0:T(8,128)(2,1)} collective-permute-done((bf16[512,2048]{1,0:T(8,128)(2,1)}, bf16[512,2048]{1,0:T(8,128)(2,1)}, u32[]{:S(2)}, u32[]{:S(2)}) %collective-permute-start.22) | collective-permute-done | bytes 2097184 | tf_op jit(solution)/shard_map/ppermute | solution.py:175
  635.8 20.3 %attend_back.1 = (bf16[1024,1024]{1,0:T(8,128)(2,1)}, bf16[1024,512]{1,0:T(8,128)(2,1)}, bf16[1024,512]{1,0:T(8,128)(2,1)}) custom-call(s32[1]{0:T(128)} %bitcast.first_ref, bf16[1024,1024]{1,0:T(8,128)(2,1)} %get-tuple-element.63.q_ref, bf16[1024,512]{1,0:T(8,128)(2,1)} %get-tuple-element.64.k_ref, bf16[1024,512]{1,0:T(8,128)(2,1)} %get-tuple-element.65.v_ref, ...), custom_call_target="tpu_custom_call" | custom-call | flops 7516192768 | bytes 37580964 | tf_op jit(solution)/shard_map/attend_back/pallas_call | solution.py:153
  695.7 15.0 %collective-permute-done.26 = bf16[512,1024]{1,0:T(8,128)(2,1)} collective-permute-done((bf16[512,1024]{1,0:T(8,128)(2,1)S(1)}, bf16[512,1024]{1,0:T(8,128)(2,1)}, u32[]{:S(2)}, u32[]{:S(2)}) %collective-permute-start.26) | collective-permute-done | bytes 1048608 | tf_op jit(solution)/shard_map/ppermute | solution.py:175
  712.3 20.4 %collective-permute-done.28 = bf16[512,1024]{1,0:T(8,128)(2,1)} collective-permute-done((bf16[512,1024]{1,0:T(8,128)(2,1)}, bf16[512,1024]{1,0:T(8,128)(2,1)}, u32[]{:S(2)}, u32[]{:S(2)}) %collective-permute-start.28) | collective-permute-done | bytes 1048608 | tf_op jit(solution)/shard_map/ppermute | solution.py:175
  758.0 13.4 %collective-permute-done.50 = bf16[2048,256]{0,1:T(8,128)(2,1)S(1)} collective-permute-done((bf16[2048,256]{0,1:T(8,128)(2,1)S(1)}, bf16[2048,256]{0,1:T(8,128)(2,1)S(1)}, u32[]{:S(2)}, u32[]{:S(2)}) %collective-permute-start.50) | collective-permute-done | bytes 1048608 | tf_op jit(solution)/shard_map/ppermute | solution.py:175
  824.2 51.8 %collective-permute-done.48 = bf16[2048,256]{0,1:T(8,128)(2,1)} collective-permute-done((bf16[2048,256]{0,1:T(8,128)(2,1)}, bf16[2048,256]{0,1:T(8,128)(2,1)}, u32[]{:S(2)}, u32[]{:S(2)}) %collective-permute-start.48) | collective-permute-done | bytes 1048608 | tf_op jit(solution)/shard_map/ppermute | solution.py:175
  880.8 17.6 %collective-permute-done.52 = bf16[256,2048]{1,0:T(8,128)(2,1)} collective-permute-done((bf16[256,2048]{1,0:T(8,128)(2,1)}, bf16[256,2048]{1,0:T(8,128)(2,1)}, u32[]{:S(2)}, u32[]{:S(2)}) %collective-permute-start.52) | collective-permute-done | bytes 1048608 | tf_op jit(solution)/shard_map/ppermute | solution.py:175
  934.4 43.9 %collective-permute-done.36 = bf16[512,1024]{1,0:T(8,128)(2,1)S(1)} collective-permute-done((bf16[512,1024]{1,0:T(8,128)(2,1)S(1)}, bf16[512,1024]{1,0:T(8,128)(2,1)S(1)}, u32[]{:S(2)}, u32[]{:S(2)}) %collective-permute-start.36) | collective-permute-done | bytes 1048608 | tf_op jit(solution)/shard_map/ppermute | solution.py:175
  1008.0 14.7 %collective-permute-done.32 = bf16[512,1024]{1,0:T(8,128)(2,1)S(1)} collective-permute-done((bf16[512,1024]{1,0:T(8,128)(2,1)S(1)}, bf16[512,1024]{1,0:T(8,128)(2,1)S(1)}, u32[]{:S(2)}, u32[]{:S(2)}) %collective-permute-start.32) | collective-permute-done | bytes 1048608 | tf_op jit(solution)/shard_map/ppermute | solution.py:175
  1024.9 10.2 fusion.23
  (454 shorter events, 453.2 us)
Async XLA Ops:
  7.2 113.6 %all-gather.6.cloned.1.call-start = ((), (), s32[]{:S(2)}) async-start(), calls=%async_computation.5 | async-start | bytes 5242880 | tf_op jit(solution)/shard_map/all_gather | solution.py:284
  9.7 259.6 %all-gather.8.cloned.1.call-start = ((), (), s32[]{:S(2)}) async-start(), calls=%async_computation.6 | async-start | bytes 5242880 | tf_op jit(solution)/shard_map/all_gather | solution.py:284
  14.5 48.9 %collective-permute-start = (bf16[512,2048]{1,0:T(8,128)(2,1)}, bf16[512,2048]{1,0:T(8,128)(2,1)}, u32[]{:S(2)}, u32[]{:S(2)}) collective-permute-start(bf16[512,2048]{1,0:T(8,128)(2,1)} %fusion.26), channel_id=1, source_target_pairs={{0,1},{1,0},{2,3},{3,2},{4,5},{5,4},{6,7},{7,6},{8,9},{9,8},{10,11... | collective-permute-start | bytes 6291464 | tf_op jit(solution)/shard_map/ppermute | solution.py:175
  19.7 264.3 %all-gather.10.cloned.1.call-start = ((), (), s32[]{:S(2)}) async-start(), calls=%async_computation.7 | async-start | bytes 5242880 | tf_op jit(solution)/shard_map/all_gather | solution.py:284
  19.8 113.4 %collective-permute-start.9 = (bf16[512,2048]{1,0:T(8,128)(2,1)S(1)}, bf16[512,2048]{1,0:T(8,128)(2,1)}, u32[]{:S(2)}, u32[]{:S(2)}) collective-permute-start(bf16[512,2048]{1,0:T(8,128)(2,1)S(1)} %copy-done.5), channel_id=1, source_target_pairs={{0,16},{8,24},{16,0},{24,8},{1,17},{9,25},{17,1},{25,9},{2,18},{10... | collective-permute-start | bytes 6291464 | tf_op jit(solution)/shard_map/ppermute | solution.py:175
  68.2 46.9 %collective-permute-start.4 = (bf16[512,2048]{1,0:T(8,128)(2,1)S(1)}, bf16[512,2048]{1,0:T(8,128)(2,1)}, u32[]{:S(2)}, u32[]{:S(2)}) collective-permute-start(bf16[512,2048]{1,0:T(8,128)(2,1)S(1)} %copy-done.5), channel_id=1, source_target_pairs={{0,1},{1,0},{2,3},{3,2},{4,5},{5,4},{6,7},{7,6},{8,9},{9,8},{10,11... | collective-permute-start | bytes 6291464 | tf_op jit(solution)/shard_map/ppermute | solution.py:175
  119.3 64.7 %collective-permute-start.5 = (bf16[1024,2048]{1,0:T(8,128)(2,1)}, bf16[1024,2048]{1,0:T(8,128)(2,1)}, u32[]{:S(2)}, u32[]{:S(2)}) collective-permute-start(bf16[1024,2048]{1,0:T(8,128)(2,1)} %pad_maximum_fusion.3), channel_id=1, source_target_pairs={{0,8},{8,0},{16,24},{24,16},{1,9},{9,1},{17,25},{25,17},{2,10},{10... | collective-permute-start | bytes 12582920 | tf_op jit(solution)/shard_map/ppermute | solution.py:175
  119.3 48.4 %collective-permute-start.10 = (bf16[512,2048]{1,0:T(8,128)(2,1)}, bf16[512,2048]{1,0:T(8,128)(2,1)}, u32[]{:S(2)}, u32[]{:S(2)}) collective-permute-start(bf16[512,2048]{1,0:T(8,128)(2,1)} %collective-permute-done.4), channel_id=1, source_target_pairs={{0,16},{8,24},{16,0},{24,8},{1,17},{9,25},{17,1},{25,9},{2,18},{10... | collective-permute-start | bytes 6291464 | tf_op jit(solution)/shard_map/ppermute | solution.py:175
  127.0 48.1 %collective-permute-start.1 = (bf16[512,2048]{1,0:T(8,128)(2,1)}, bf16[512,2048]{1,0:T(8,128)(2,1)}, u32[]{:S(2)}, u32[]{:S(2)}) collective-permute-start(bf16[512,2048]{1,0:T(8,128)(2,1)} %convolution_convert_fusion.9), channel_id=1, source_target_pairs={{0,1},{1,0},{2,3},{3,2},{4,5},{5,4},{6,7},{7,6},{8,9},{9,8},{10,11... | collective-permute-start | bytes 6291464 | tf_op jit(solution)/shard_map/ppermute | solution.py:175
  130.8 385.8 %reduce-scatter.6.cloned.1.call-start = ((), (), s32[]{:S(2)}) async-start(), calls=%async_computation.8 | async-start | bytes 5242880 | tf_op jit(solution)/shard_map/reduce_scatter | solution.py:288
  170.2 70.1 %collective-permute-start.11 = (bf16[1024,2048]{1,0:T(8,128)(2,1)S(1)}, bf16[1024,2048]{1,0:T(8,128)(2,1)S(1)}, u32[]{:S(2)}, u32[]{:S(2)}) collective-permute-start(bf16[1024,2048]{1,0:T(8,128)(2,1)S(1)} %pad_maximum_fusion.5), channel_id=1, source_target_pairs={{0,8},{8,0},{16,24},{24,16},{1,9},{9,1},{17,25},{25,17},{2,10},{10... | collective-permute-start | bytes 12582920 | tf_op jit(solution)/shard_map/ppermute | solution.py:175
  181.9 47.0 %collective-permute-start.2 = (bf16[512,2048]{1,0:T(8,128)(2,1)S(1)}, bf16[512,2048]{1,0:T(8,128)(2,1)S(1)}, u32[]{:S(2)}, u32[]{:S(2)}) collective-permute-start(bf16[512,2048]{1,0:T(8,128)(2,1)S(1)} %multiply_convert_fusion), channel_id=1, source_target_pairs={{0,1},{1,0},{2,3},{3,2},{4,5},{5,4},{6,7},{7,6},{8,9},{9,8},{10,11... | collective-permute-start | bytes 6291464 | tf_op jit(solution)/shard_map/ppermute | solution.py:175
  403.3 48.7 %collective-permute-start.14 = (bf16[1024,2048]{1,0:T(8,128)(2,1)}, bf16[1024,2048]{1,0:T(8,128)(2,1)}, u32[]{:S(2)}, u32[]{:S(2)}) collective-permute-start(bf16[1024,2048]{1,0:T(8,128)(2,1)} %add_convert_fusion.3), channel_id=1, source_target_pairs={{0,8},{8,0},{16,24},{24,16},{1,9},{9,1},{17,25},{25,17},{2,10},{10... | collective-permute-start | bytes 12582920 | tf_op jit(solution)/shard_map/ppermute | solution.py:175
  403.3 168.9 %reduce-scatter.8.cloned.1.call-start = ((), (), s32[]{:S(2)}) async-start(), calls=%async_computation.9 | async-start | bytes 5242880 | tf_op jit(solution)/shard_map/reduce_scatter | solution.py:288
  458.0 47.6 %collective-permute-start.18 = (bf16[512,2048]{1,0:T(8,128)(2,1)}, bf16[512,2048]{1,0:T(8,128)(2,1)}, u32[]{:S(2)}, u32[]{:S(2)}) collective-permute-start(bf16[512,2048]{1,0:T(8,128)(2,1)} %add_convert_fusion.12), channel_id=1, source_target_pairs={{0,16},{8,24},{16,0},{24,8},{1,17},{9,25},{17,1},{25,9},{2,18},{10... | collective-permute-start | bytes 6291464 | tf_op jit(solution)/shard_map/ppermute | solution.py:175
  459.5 47.3 %collective-permute-start.17 = (bf16[512,2048]{1,0:T(8,128)(2,1)}, bf16[512,2048]{1,0:T(8,128)(2,1)}, u32[]{:S(2)}, u32[]{:S(2)}) collective-permute-start(bf16[512,2048]{1,0:T(8,128)(2,1)} %add_convert_fusion.11), channel_id=1, source_target_pairs={{0,1},{1,0},{2,3},{3,2},{4,5},{5,4},{6,7},{7,6},{8,9},{9,8},{10,11... | collective-permute-start | bytes 6291464 | tf_op jit(solution)/shard_map/ppermute | solution.py:175
  466.2 51.0 %collective-permute-start.21 = (bf16[1024,2048]{1,0:T(8,128)(2,1)}, bf16[1024,2048]{1,0:T(8,128)(2,1)}, u32[]{:S(2)}, u32[]{:S(2)}) collective-permute-start(bf16[1024,2048]{1,0:T(8,128)(2,1)} %convolution_convert_fusion.7), channel_id=1, source_target_pairs={{0,8},{8,0},{16,24},{24,16},{1,9},{9,1},{17,25},{25,17},{2,10},{10... | collective-permute-start | bytes 12582920 | tf_op jit(solution)/shard_map/ppermute | solution.py:175
  494.3 186.5 %reduce-scatter.12.cloned.1.call-start = ((), (), s32[]{:S(2)}) async-start(), calls=%async_computation.12 | async-start | bytes 5242880 | tf_op jit(solution)/shard_map/reduce_scatter | solution.py:288
  556.0 226.6 %reduce-scatter.14.cloned.1.call-start = ((), (), s32[]{:S(2)}) async-start(), calls=%async_computation.13 | async-start | bytes 1310720 | tf_op jit(solution)/shard_map/reduce_scatter | solution.py:288
  586.3 47.8 %collective-permute-start.22 = (bf16[512,2048]{1,0:T(8,128)(2,1)}, bf16[512,2048]{1,0:T(8,128)(2,1)}, u32[]{:S(2)}, u32[]{:S(2)}) collective-permute-start(bf16[512,2048]{1,0:T(8,128)(2,1)} %get-tuple-element.166), channel_id=1, source_target_pairs={{0,16},{8,24},{16,0},{24,8},{1,17},{9,25},{17,1},{25,9},{2,18},{10... | collective-permute-start | bytes 6291464 | tf_op jit(solution)/shard_map/ppermute | solution.py:175
  680.8 143.4 %reduce-scatter.10.cloned.1.call-start = ((), (), s32[]{:S(2)}) async-start(), calls=%async_computation.10 | async-start | bytes 2621440 | tf_op jit(solution)/shard_map/reduce_scatter | solution.py:288
  735.9 144.3 %all-gather.14.cloned.1.call-start = ((), (), s32[]{:S(2)}) async-start(), calls=%async_computation.14 | async-start | bytes 1310720 | tf_op jit(solution)/shard_map/all_gather | solution.py:284
  745.5 47.5 %collective-permute-start.31 = (bf16[512,2048]{1,0:T(8,128)(2,1)}, bf16[512,2048]{1,0:T(8,128)(2,1)}, u32[]{:S(2)}, u32[]{:S(2)}) collective-permute-start(bf16[512,2048]{1,0:T(8,128)(2,1)} %convolution_convert_fusion.10), channel_id=1, source_target_pairs={{0,1},{1,0},{2,3},{3,2},{4,5},{5,4},{6,7},{7,6},{8,9},{9,8},{10,11... | collective-permute-start | bytes 6291464 | tf_op jit(solution)/shard_map/ppermute | solution.py:175
  782.6 120.3 %collective-permute-start.24 = (bf16[1024,2048]{1,0:T(8,128)(2,1)}, bf16[1024,2048]{1,0:T(8,128)(2,1)}, u32[]{:S(2)}, u32[]{:S(2)}) collective-permute-start(bf16[1024,2048]{1,0:T(8,128)(2,1)} %convolution_convert_fusion.4), channel_id=1, source_target_pairs={{0,8},{8,0},{16,24},{24,16},{1,9},{9,1},{17,25},{25,17},{2,10},{10... | collective-permute-start | bytes 12582920 | tf_op jit(solution)/shard_map/ppermute | solution.py:175
  782.6 138.4 %all-gather.12.cloned.1.call-start = ((), (), s32[]{:S(2)}) async-start(), calls=%async_computation.11 | async-start | bytes 2621440 | tf_op jit(solution)/shard_map/all_gather | solution.py:284
  804.6 98.2 %collective-permute-start.29 = (bf16[512,2048]{1,0:T(8,128)(2,1)}, bf16[512,2048]{1,0:T(8,128)(2,1)}, u32[]{:S(2)}, u32[]{:S(2)}) collective-permute-start(bf16[512,2048]{1,0:T(8,128)(2,1)} %get-tuple-element.99), channel_id=1, source_target_pairs={{0,16},{8,24},{16,0},{24,8},{1,17},{9,25},{17,1},{25,9},{2,18},{10... | collective-permute-start | bytes 6291464 | tf_op jit(solution)/shard_map/ppermute | solution.py:175
  805.3 70.7 %collective-permute-start.48 = (bf16[2048,256]{0,1:T(8,128)(2,1)}, bf16[2048,256]{0,1:T(8,128)(2,1)}, u32[]{:S(2)}, u32[]{:S(2)}) collective-permute-start(bf16[2048,256]{0,1:T(8,128)(2,1)} %bitcast.7), channel_id=1, source_target_pairs={{0,16},{8,24},{16,0},{24,8},{1,17},{9,25},{17,1},{25,9},{2,18},{10... | collective-permute-start | bytes 3145736 | tf_op jit(solution)/shard_map/ppermute | solution.py:175
  806.8 91.6 %collective-permute-start.52 = (bf16[256,2048]{1,0:T(8,128)(2,1)}, bf16[256,2048]{1,0:T(8,128)(2,1)}, u32[]{:S(2)}, u32[]{:S(2)}) collective-permute-start(bf16[256,2048]{1,0:T(8,128)(2,1)} %reduce-scatter.6.cloned.1.call-done), channel_id=1, source_target_pairs={{0,16},{8,24},{16,0},{24,8},{1,17},{9,25},{17,1},{25,9},{2,18},{10... | collective-permute-start | bytes 3145736 | tf_op jit(solution)/shard_map/ppermute | solution.py:175
  907.7 116.9 %collective-permute-start.30 = (bf16[512,2048]{1,0:T(8,128)(2,1)}, bf16[512,2048]{1,0:T(8,128)(2,1)}, u32[]{:S(2)}, u32[]{:S(2)}) collective-permute-start(bf16[512,2048]{1,0:T(8,128)(2,1)} %add_convert_fusion.7), channel_id=1, source_target_pairs={{0,1},{1,0},{2,3},{3,2},{4,5},{5,4},{6,7},{7,6},{8,9},{9,8},{10,11... | collective-permute-start | bytes 6291464 | tf_op jit(solution)/shard_map/ppermute | solution.py:175
  921.0 114.1 %collective-permute-start.42 = (bf16[512,2048]{1,0:T(8,128)(2,1)}, bf16[512,2048]{1,0:T(8,128)(2,1)}, u32[]{:S(2)}, u32[]{:S(2)}) collective-permute-start(bf16[512,2048]{1,0:T(8,128)(2,1)} %pad_maximum_fusion.12), channel_id=1, source_target_pairs={{0,8},{8,0},{16,24},{24,16},{1,9},{9,1},{17,25},{25,17},{2,10},{10... | collective-permute-start | bytes 6291464 | tf_op jit(solution)/shard_map/ppermute | solution.py:175
  922.3 58.3 %collective-permute-start.35 = (bf16[512,1024]{1,0:T(8,128)(2,1)S(1)}, bf16[512,1024]{1,0:T(8,128)(2,1)S(1)}, u32[]{:S(2)}, u32[]{:S(2)}) collective-permute-start(bf16[512,1024]{1,0:T(8,128)(2,1)S(1)} %slice.161), channel_id=1, source_target_pairs={{0,16},{8,24},{16,0},{24,8},{1,17},{9,25},{17,1},{25,9},{2,18},{10... | collective-permute-start | bytes 3145736 | tf_op jit(solution)/shard_map/ppermute | solution.py:175
  923.0 55.3 %collective-permute-start.36 = (bf16[512,1024]{1,0:T(8,128)(2,1)S(1)}, bf16[512,1024]{1,0:T(8,128)(2,1)S(1)}, u32[]{:S(2)}, u32[]{:S(2)}) collective-permute-start(bf16[512,1024]{1,0:T(8,128)(2,1)S(1)} %slice.161), channel_id=1, source_target_pairs={{0,1},{1,0},{2,3},{3,2},{4,5},{5,4},{6,7},{7,6},{8,9},{9,8},{10,11... | collective-permute-start | bytes 3145736 | tf_op jit(solution)/shard_map/ppermute | solution.py:175
  (135 other events, 2076.4 us)
Sparse Core Ops, SparseCore 0:
  10.2 83.4 all-gather.5
  95.2 79.0 all-gather.7
  175.8 78.7 all-gather.9
  403.4 77.3 reduce-scatter.5
  494.4 77.7 reduce-scatter.7
  574.9 77.2 reduce-scatter.11
  680.9 27.2 reduce-scatter.13
  736.0 43.3 reduce-scatter.9
  782.7 26.5 all-gather.13
  824.3 46.4 all-gather.11

commit v7 on v6

--- a/solution.py
+++ b/solution.py
@@ -288,10 +288,6 @@
     return lax.psum_scatter(value, "row", scatter_dimension=0, tiled=True)
 
 
-def sum_quarters(value, core, ypos):
-    return sum_y(sum_cores(value, core), ypos)
-
-
 def sum_cores(value, core):
     return low(wide(half_rows(value, core)) + wide(swap(half_rows(value, 1 - core), "grp", 1)))
 
@@ -314,8 +310,8 @@
     return lax.dynamic_slice_in_dim(weight, (2 * core + ypos) * size, size, 0)
 
 
-def spread_quarters(part, core, ypos, dim):
-    half = ordered(ypos, part, swap(part, "grp", 2), dim)
+def spread_quarters(part, over_y, core, ypos, dim):
+    half = ordered(ypos, part, over_y, dim)
     return wide(ordered(core, half, swap(half, "grp", 1), dim))
 
 
@@ -433,27 +429,26 @@
     mid_from_core = near_sum(mid_product)
     mid_far_sum = far_sum(mid_product)
     mid_far_sum, gate_backs[0], up_backs[0] = tie(mid_far_sum, gate_backs[0], up_backs[0])
-    mid_grad, (gate_backs[1], acts[1]) = square_scatter(
+    mid_grad, (gate_backs[1],) = square_scatter(
         lambda first, last: mid_product(0, first, last) + wide(mid_from_core[first:last]),
         mid_far_sum,
-        [gate_backs[1], acts[1]],
+        [gate_backs[1]],
     )
     gate_part = row_scatter(weight_sum(gate_backs, mid_sets))
-    out_far = far_sum(out_product)
-    out_far, up_backs[1] = tie(out_far, up_backs[1])
-    out_first, out_second = blocks_of(out_far, 0, 2)
-    out_first = swap(out_first, "grp", 2)
     up_part = row_scatter(weight_sum(up_backs, mid_sets))
 
     res_from_mid, second_gain_part = second_back(mid_grad)
     res_grad = wide(cotangent) + res_from_mid
     res_low, down_part = tie(low(res_grad), down_part)
     shard_rows = jnp.concatenate(col_gather(res_low), axis=0)
-    shard_rows, gate_part = tie(shard_rows, gate_part)
+    down_over_y = swap(down_part, "grp", 2)
+    shard_rows, gate_part, down_over_y = tie(shard_rows, gate_part, down_over_y)
+    gate_part = gate_part.T
+    gate_over_y = swap(gate_part, "grp", 2)
 
     mixed_low = low(dot_nt(shard_rows, output_weight))
     out_low = low(dot_tn(attn_low, shard_rows))
-    mixed_low, out_low, out_first = tie(mixed_low, sum_cores(out_low, core), out_first)
+    mixed_low, out_low = tie(mixed_low, sum_cores(out_low, core))
     out_low = sum_y(out_low, ypos)
     query_back, key_back, value_back = attention_call(
         attend_back_kernel,
@@ -478,34 +473,49 @@
     back_all = jnp.concatenate([query_back, pair_back], axis=1)
     query_low_grad = low(dot_tn(gathered_in, query_back))
     pair_low_grad = low(dot_tn(gathered_in, pair_back))
-    query_low_grad, pair_low_grad, acts[0] = tie(query_low_grad, pair_low_grad, acts[0])
-    query_part = sum_quarters(query_low_grad, core, ypos)
-    pair_part = sum_quarters(pair_low_grad, core, ypos)
-    query_part, pair_part, down_part, gate_part, second_gain_part, out_second = tie(
-        query_part, pair_part, down_part, gate_part, second_gain_part, out_second
-    )
-    both_part = row_gather(row_scatter(jnp.concatenate([query_part, pair_part], axis=1)))
-    query_part, pair_part = both_part[:, :query_cols], both_part[:, query_cols:]
+    query_low_grad, pair_low_grad, *acts = tie(query_low_grad, pair_low_grad, *acts)
+    query_part, pair_part, gate_over_y = tie(
+        sum_cores(query_low_grad, core), sum_cores(pair_low_grad, core), gate_over_y
+    )
     back_parts = blocks_of(back_all, 0, 2) if in_pairs else [back_all]
     in_grad = col_scatter(lambda i: dot_nt(back_parts[i], project_in))
-
-    out_over_y = jnp.concatenate([out_first, swap(out_second, "grp", 2)], axis=0)
+    query_part, pair_part, out_part, up_part, second_gain_part, in_grad = tie(
+        sum_y(query_part, ypos),
+        sum_y(pair_part, ypos),
+        out_part,
+        up_part,
+        second_gain_part,
+        in_grad,
+    )
+    both_part = row_scatter(jnp.concatenate([query_part, pair_part], axis=1))
+    up_part = up_part.T
+    up_over_y = swap(up_part, "grp", 2)
+    out_over_y = swap(out_part, "grp", 2)
     out_from_core = near_sum(out_product)
-    piece = packed_length // 2 if in_pairs else packed_length
-
-    def out_rows(i):
-        part = slice(i * piece, (i + 1) * piece)
-        return out_product(0, part.start, part.stop) + wide(out_from_core[part]) + wide(out_over_y[part])
-
-    layer_out = hidden_res + col_scatter(out_rows)
+    layer_rows, (both_part, up_over_y) = square_scatter(
+        lambda first, last: out_product(0, first, last) + wide(out_from_core[first:last]),
+        far_sum(out_product),
+        [both_part, up_over_y],
+    )
+    layer_out = hidden_res + layer_rows
     res_from_in, _ = first_back(in_grad)
     input_grad = res_grad + res_from_in
 
-    down_grad = spread_quarters(down_part, core, ypos, 0)
-    gate_grad = spread_quarters(gate_part.T, core, ypos, 1)
-    up_grad = spread_quarters(up_part.T, core, ypos, 1)
-    out_wgrad = spread_quarters(out_part, core, ypos, 0)
-    query_wgrad = spread_quarters(query_part, core, ypos, 0)
+    both_part, layer_out, input_grad, out_over_y = tie(
+        row_gather(both_part), layer_out, input_grad, out_over_y
+    )
+    size = both_part.shape[0]
+    project_rows = lax.dynamic_slice_in_dim(project_in, (2 * core + ypos) * size, size, 0)
+    term = jnp.sum(wide(both_part) * wide(project_rows), axis=1)
+    term = butterfly(term.reshape(8, -1), ("col",)).reshape(-1)
+    term = ordered(ypos, term, swap(term, "grp", 2), 0)
+    first_gain_grad = ordered(core, term, swap(term, "grp", 1), 0) / first_gain
+    query_part, pair_part = both_part[:, :query_cols], both_part[:, query_cols:]
+    down_grad = spread_quarters(down_part, down_over_y, core, ypos, 0)
+    gate_grad = spread_quarters(gate_part, gate_over_y, core, ypos, 1)
+    up_grad = spread_quarters(up_part, up_over_y, core, ypos, 1)
+    out_wgrad = spread_quarters(out_part, out_over_y, core, ypos, 0)
+    query_wgrad = spread_quarters(query_part, swap(query_part, "grp", 2), core, ypos, 0)
     if in_pairs:
         over_x, over_y = swap(pair_part, "col", 1), swap(pair_part, "grp", 2)
         half = pair_part.shape[0] // 2
@@ -530,10 +540,6 @@
 
         key_full = spread(pair_all[..., :key_cols])
         value_full = spread(pair_all[..., key_cols:])
-    query_term = jnp.sum(query_wgrad * wide(query_weight), axis=1)
-    pair_term = jnp.sum(key_full * wide(key_matrix) + value_full * wide(value_matrix), axis=1)
-    query_term = butterfly(query_term.reshape(8, -1), ("col",)).reshape(-1)
-    first_gain_grad = (query_term + pair_term) / first_gain
     axes = ("grp", "row", "col")
     second_gain_grad = butterfly(second_gain_part.reshape(8, -1), axes).reshape(-1)
     return (

time: 1090 us -> 1030 us (0.945)
  waiting for transfers between devices: 393 us -> 342 us
    ppermute x54 -> x57, waiting for transfers between devices: 388 us -> 342 us  [swap(): return lax.ppermute(value, axis, [(i, i ^ bit) for i in range(count)])]
    convert_element_type x4 -> x7, other arithmetic: 17.1 us -> 30.6 us  [wide(): return value.astype(jnp.float32)]
    reduce_sum x2 -> x1, other arithmetic: 14.1 us -> 2.84 us  [per_device(): term = jnp.sum(wide(both_part) * wide(project_rows), axis=1)]
    unnamed x220 -> x191, local copies, waits for them, and re-layouts: 57 us -> 52.3 us
    select_n x15 -> x17, other arithmetic: 31.5 us -> 27.2 us  [ordered(): jnp.where(keep, mine, theirs)]
    ppermute x54 -> x57, starting transfers between devices: 41.3 us -> 45 us  [swap(): return lax.ppermute(value, axis, [(i, i ^ bit) for i in range(count)])]
  transfers between devices with their start and end apart: 64 -> 67, of which waited for: 26 -> 24; matrix products, arithmetic and copies ran while one was open for 44% -> 47% of each run, Pallas kernels for 3% -> 3%
where the time goes in v7:
time: 1030 us; the launch traced here: 1020 us
  matrix products  352 us (34%)
  waiting for transfers between devices  342 us (33%)
  other arithmetic  145 us (14%)
  local copies, waits for them, and re-layouts  90.9 us (9%)
  starting transfers between devices  46.1 us (4%)
  Pallas kernels  32.2 us (3%)
  between operations  15.5 us (2%)
    ppermute x57, waiting for transfers between devices, swap(): return lax.ppermute(value, axis, [(i, i ^ bit) for i in range(count)])  342 us
    dot_general x18, matrix products, dot32(): return jnp.dot(left, right, preferred_element_type=jnp.float32)  129 us
    dot_general x9, matrix products, dot_nt(): jnp.einsum('td,fd->tf', left, right, preferred_element_type=jnp.float32)  116 us
    dot_general x9, matrix products, dot_tn(): jnp.einsum('td,tf->df', left, right, preferred_element_type=jnp.float32)  107 us
    unnamed x191, local copies, waits for them, and re-layouts  52.3 us
    ppermute x57, starting transfers between devices, swap(): return lax.ppermute(value, axis, [(i, i ^ bit) for i in range(count)])  45 us
    pallas_call x2, Pallas kernels, attention_call(): pl.pallas_call(kernel, grid_spec=pltpu.PrefetchScalarGridSpec(num_scalar_...  32.2 us
    convert_element_type x7, other arithmetic, wide(): return value.astype(jnp.float32)  30.6 us
  transfers between devices with their start and end apart: 67, of which 24 were waited for; matrix products, arithmetic and copies ran while one was open for 47% of the time, Pallas kernels for 3%

profile of v7, /device:TPU:0, one launch (start us, length us, event | category | flops | bytes accessed | tf_op | source)
XLA Modules:
  0.0 1023.7 jit_solution(9144012019479323872)
XLA Ops:
  24.7 37.0 %collective-permute-done = bf16[512,2048]{1,0:T(8,128)(2,1)} collective-permute-done((bf16[512,2048]{1,0:T(8,128)(2,1)}, bf16[512,2048]{1,0:T(8,128)(2,1)}, u32[]{:S(2)}, u32[]{:S(2)}) %collective-permute-start) | collective-permute-done | bytes 2097184 | tf_op jit(solution)/shard_map/ppermute | solution.py:175
  73.4 14.7 %fusion.79.q_ref.k_ref.v_ref = f32[1024,2048]{1,0:T(8,128)} fusion(bf16[1024,2048]{1,0:T(8,128)(2,1)} %pad_maximum_fusion.2, bf16[2048,512]{1,0:T(8,128)(2,1)} %get-tuple-element.205, bf16[2048,512]{1,0:T(8,128)(2,1)} %get-tuple-element.206, bf16[2048,1024]{1,0:T(8,128)(2,1)} %param.18), kind=kOutput, calls=%fused_computation.224 | convolution fusion | flops 8615100416 | bytes 20971520 | tf_op jit(solution)/shard_map/dot_general | solution.py:195
  88.1 12.0 %attend.1 = (bf16[1024,1024]{1,0:T(8,128)(2,1)}, bf16[1024,1024]{1,0:T(8,128)(2,1)}, bf16[1024,512]{1,0:T(8,128)(2,1)}, bf16[1024,512]{1,0:T(8,128)(2,1)}) custom-call(s32[1]{0:T(128)} %bitcast.first_ref, f32[1024,2048]{1,0:T(8,128)} %fusion.79.q_ref.k_ref.v_ref, f32[1024,2048]{1,0:T(8,128)} %fusion.79.q_ref.k_ref.v_ref, ...), custom_call_target="tpu_custom_call" | custom-call | flops 3221225472 | bytes 16106127 | tf_op jit(solution)/shard_map/attend/pallas_call | solution.py:153
  100.1 13.5 %collective-permute-done.4 = bf16[512,2048]{1,0:T(8,128)(2,1)} collective-permute-done((bf16[512,2048]{1,0:T(8,128)(2,1)}, bf16[512,2048]{1,0:T(8,128)(2,1)}, u32[]{:S(2)}, u32[]{:S(2)}) %collective-permute-start.4) | collective-permute-done | bytes 2097184 | tf_op jit(solution)/shard_map/ppermute | solution.py:175
  133.9 32.9 %collective-permute-done.10 = bf16[512,2048]{1,0:T(8,128)(2,1)} collective-permute-done((bf16[512,2048]{1,0:T(8,128)(2,1)}, bf16[512,2048]{1,0:T(8,128)(2,1)}, u32[]{:S(2)}, u32[]{:S(2)}) %collective-permute-start.10) | collective-permute-done | bytes 2097184 | tf_op jit(solution)/shard_map/ppermute | solution.py:175
  186.0 13.7 %convolution_convert_fusion.3 = bf16[2048,1024]{1,0:T(8,128)(2,1)} fusion(bf16[2048,2048]{1,0:T(8,128)(2,1)S(1)} %constant_dynamic-update-slice_fusion, bf16[1024,2048]{1,0:T(8,128)(2,1)} %all-gather.6.cloned.1.call-done), kind=kOutput, calls=%fused_computation.85 | convolution fusion | flops 8592031744 | bytes 16777216 | tf_op jit(solution)/shard_map/td,fd->tf/dot_general | solution.py:199
  199.7 28.6 %collective-permute-done.2 = bf16[512,2048]{1,0:T(8,128)(2,1)S(1)} collective-permute-done((bf16[512,2048]{1,0:T(8,128)(2,1)S(1)}, bf16[512,2048]{1,0:T(8,128)(2,1)S(1)}, u32[]{:S(2)}, u32[]{:S(2)}) %collective-permute-start.2) | collective-permute-done | bytes 2097184 | tf_op jit(solution)/shard_map/ppermute | solution.py:175
  242.0 12.6 %convolution_convert_fusion.1 = bf16[2048,1024]{1,0:T(8,128)(2,1)} fusion(bf16[2048,2048]{1,0:T(8,128)(2,1)} %constant_dynamic-update-slice_fusion.3, bf16[1024,2048]{1,0:T(8,128)(2,1)S(1)} %copy-done.65), kind=kOutput, calls=%fused_computation.83 | convolution fusion | flops 8592031744 | bytes 16777216 | tf_op jit(solution)/shard_map/td,fd->tf/dot_general | solution.py:199
  268.7 14.7 %convolution_convert_fusion.2 = bf16[2048,1024]{1,0:T(8,128)(2,1)} fusion(bf16[1024,2048]{0,1:T(8,128)(2,1)} %all-gather.8.cloned.1.call-done, bf16[1024,2048]{1,0:T(8,128)(2,1)} %collective-permute-done.6, bf16[512,2048]{1,0:T(8,128)(2,1)} %copy-done.25, bf16[512,2048]{1,0:T(8,128)(2,1)S(1)} %multiply_convert_fusion), kind=kOutput, calls=%fused_computation.84 | convolution fusion | flops 8617197568 | bytes 16777216 | tf_op jit(solution)/shard_map/td,fd->tf/dot_general | solution.py:199
  283.4 20.8 %fusion.5 = (bf16[2048,1024]{1,0:T(8,128)(2,1)}, bf16[2048,1024]{1,0:T(8,128)(2,1)}, bf16[2048,1024]{1,0:T(8,128)(2,1)}) fusion(bf16[2048,1024]{1,0:T(8,128)(2,1)} %convolution_convert_fusion.3, bf16[2048,1024]{1,0:T(8,128)(2,1)} %convolution_convert_fusion.2, bf16[1024,2048]{0,1:T(8,128)(2,1)} %all-gather.10.cloned.1.call-done, ...), kind=kOutput, calls=%fused_computation.15 | convolution fusion | flops 8652849152 | bytes 33554432 | tf_op jit(solution)/shard_map/td,fd->tf/dot_general | solution.py:199
  309.2 13.0 %convolution_convert_fusion = bf16[2048,1024]{1,0:T(8,128)(2,1)} fusion(bf16[2048,2048]{1,0:T(8,128)(2,1)} %constant_dynamic-update-slice_fusion.6, bf16[1024,2048]{0,1:T(8,128)(2,1)S(1)} %copy-done.70), kind=kOutput, calls=%fused_computation.82 | convolution fusion | flops 8592031744 | bytes 16777216 | tf_op jit(solution)/shard_map/td,fd->tf/dot_general | solution.py:199
  322.2 20.8 %fusion.2 = (bf16[2048,1024]{1,0:T(8,128)(2,1)}, bf16[2048,1024]{1,0:T(8,128)(2,1)}, bf16[2048,1024]{1,0:T(8,128)(2,1)}) fusion(bf16[2048,1024]{1,0:T(8,128)(2,1)} %convolution_convert_fusion.1, bf16[2048,1024]{1,0:T(8,128)(2,1)} %convolution_convert_fusion, bf16[2048,2048]{1,0:T(8,128)(2,1)} %constant_dynamic-update-slice_fusion.6, ...), kind=kOutput, calls=%fused_computation.12 | convolution fusion | flops 8627683328 | bytes 33554432 | tf_op jit(solution)/shard_map/td,fd->tf/dot_general | solution.py:199
  343.0 13.2 %fusion.82 = f32[1024,2048]{1,0:T(8,128)S(1)} fusion(bf16[2048,1024]{1,0:T(8,128)(2,1)} %get-tuple-element.101, bf16[2048,2048]{1,0:T(8,128)(2,1)} %constant_dynamic-update-slice_fusion.3), kind=kOutput, calls=%fused_computation.227 | convolution fusion | flops 8589934592 | bytes 20971520 | tf_op jit(solution)/shard_map/td,tf->df/dot_general | solution.py:203
  356.3 11.1 %add_convert_fusion.6 = bf16[1024,2048]{1,0:T(8,128)(2,1)} fusion(f32[1024,2048]{1,0:T(8,128)S(1)} %fusion.82, bf16[2048,1024]{1,0:T(8,128)(2,1)S(1)} %copy-done.81, bf16[2048,2048]{1,0:T(8,128)(2,1)S(1)} %bitcast.66), kind=kOutput, calls=%fused_computation.40 | convolution fusion | flops 8594128896 | bytes 25165824 | tf_op jit(solution)/shard_map/td,tf->df/dot_general | solution.py:203
  367.4 10.9 %fusion.46 = f32[1024,2048]{1,0:T(8,128)} fusion(bf16[1024,2048]{0,1:T(8,128)(2,1)} %all-gather.8.cloned.1.call-done, bf16[2048,1024]{1,0:T(8,128)(2,1)} %get-tuple-element.92), kind=kOutput, calls=%fused_computation.122 | convolution fusion | flops 4294967296 | bytes 14680064 | tf_op jit(solution)/shard_map/dot_general | solution.py:195
  402.8 10.9 %fusion.49 = f32[1024,2048]{1,0:T(8,128)} fusion(bf16[1024,2048]{0,1:T(8,128)(2,1)} %all-gather.8.cloned.1.call-done, bf16[2048,1024]{1,0:T(8,128)(2,1)} %get-tuple-element.92), kind=kOutput, calls=%fused_computation.125 | convolution fusion | flops 4294967296 | bytes 14680064 | tf_op jit(solution)/shard_map/dot_general | solution.py:195
  427.6 19.7 %collective-permute-done.15 = bf16[256,2048]{1,0:T(8,128)(2,1)S(1)} collective-permute-done((bf16[256,2048]{1,0:T(8,128)(2,1)S(1)}, bf16[256,2048]{1,0:T(8,128)(2,1)S(1)}, u32[]{:S(2)}, u32[]{:S(2)}) %collective-permute-start.15) | collective-permute-done | bytes 1048608 | tf_op jit(solution)/shard_map/ppermute | solution.py:175
  455.3 13.8 %fusion.83 = f32[1024,2048]{1,0:T(8,128)} fusion(bf16[2048,1024]{1,0:T(8,128)(2,1)S(1)} %copy-done.86, bf16[2048,2048]{1,0:T(8,128)(2,1)} %constant_dynamic-update-slice_fusion.6), kind=kOutput, calls=%fused_computation.228 | convolution fusion | flops 8589934592 | bytes 20971520 | tf_op jit(solution)/shard_map/td,tf->df/dot_general | solution.py:203
  469.1 13.8 %add_convert_fusion.2 = bf16[1024,2048]{1,0:T(8,128)(2,1)} fusion(f32[1024,2048]{1,0:T(8,128)} %fusion.83, bf16[2048,1024]{1,0:T(8,128)(2,1)S(1)} %copy-done.80, bf16[1024,2048]{1,0:T(8,128)(2,1)} %collective-permute-done.6, bf16[512,2048]{1,0:T(8,128)(2,1)S(1)} %copy-done.26, bf16[512,2048]{1,0:T(8,128)(2,1)S(1)} %copy-done.17), kind=kOutput, calls=%fused_computation.36 | convolution fusion | flops 8619294720 | bytes 25165824 | tf_op jit(solution)/shard_map/td,tf->df/dot_general | solution.py:203
  485.4 15.0 %fusion.84 = f32[1024,2048]{1,0:T(8,128)} fusion(bf16[2048,1024]{1,0:T(8,128)(2,1)} %get-tuple-element.83, bf16[2048,2048]{1,0:T(8,128)(2,1)} %constant_dynamic-update-slice_fusion.6), kind=kOutput, calls=%fused_computation.229 | convolution fusion | flops 8589934592 | bytes 20971520 | tf_op jit(solution)/shard_map/td,tf->df/dot_general | solution.py:203
  508.0 22.6 %collective-permute-done.18 = bf16[512,2048]{1,0:T(8,128)(2,1)S(1)} collective-permute-done((bf16[512,2048]{1,0:T(8,128)(2,1)}, bf16[512,2048]{1,0:T(8,128)(2,1)S(1)}, u32[]{:S(2)}, u32[]{:S(2)}) %collective-permute-start.18) | collective-permute-done | bytes 2097184 | tf_op jit(solution)/shard_map/ppermute | solution.py:175
  544.0 15.1 %add_convert_fusion = bf16[1024,2048]{1,0:T(8,128)(2,1)} fusion(f32[1024,2048]{1,0:T(8,128)} %fusion.84, bf16[2048,1024]{1,0:T(8,128)(2,1)} %get-tuple-element.86, bf16[1024,2048]{1,0:T(8,128)(2,1)} %collective-permute-done.6, bf16[512,2048]{1,0:T(8,128)(2,1)} %copy-done.25, bf16[512,2048]{1,0:T(8,128)(2,1)S(1)} %copy-done.17), kind=kOutput, calls=%fused_computation.34 | convolution fusion | flops 8619294720 | bytes 25165824 | tf_op jit(solution)/shard_map/td,tf->df/dot_general | solution.py:203
  559.2 30.1 %collective-permute-done.19 = bf16[512,2048]{1,0:T(8,128)(2,1)} collective-permute-done((bf16[512,2048]{1,0:T(8,128)(2,1)}, bf16[512,2048]{1,0:T(8,128)(2,1)}, u32[]{:S(2)}, u32[]{:S(2)}) %collective-permute-start.19) | collective-permute-done | bytes 2097184 | tf_op jit(solution)/shard_map/ppermute | solution.py:175
  626.8 20.2 %attend_back.1 = (bf16[1024,1024]{1,0:T(8,128)(2,1)}, bf16[1024,512]{1,0:T(8,128)(2,1)}, bf16[1024,512]{1,0:T(8,128)(2,1)}) custom-call(s32[1]{0:T(128)} %bitcast.first_ref, bf16[1024,1024]{1,0:T(8,128)(2,1)} %get-tuple-element.70.q_ref, bf16[1024,512]{1,0:T(8,128)(2,1)} %get-tuple-element.71.k_ref, bf16[1024,512]{1,0:T(8,128)(2,1)} %get-tuple-element.72.v_ref, ...), custom_call_target="tpu_custom_call" | custom-call | flops 7516192768 | bytes 37580964 | tf_op jit(solution)/shard_map/attend_back/pallas_call | solution.py:153
  647.1 9.5 convolution_convert_fusion.6
  711.1 26.8 %collective-permute-done.32 = bf16[512,2048]{1,0:T(8,128)(2,1)} collective-permute-done((bf16[512,2048]{1,0:T(8,128)(2,1)}, bf16[512,2048]{1,0:T(8,128)(2,1)}, u32[]{:S(2)}, u32[]{:S(2)}) %collective-permute-start.32) | collective-permute-done | bytes 2097184 | tf_op jit(solution)/shard_map/ppermute | solution.py:175
  785.1 20.6 %collective-permute-done.50 = f32[8,256]{1,0:T(8,128)S(1)} collective-permute-done((f32[8,256]{1,0:T(8,128)S(1)}, f32[8,256]{1,0:T(8,128)S(1)}, u32[]{:S(2)}, u32[]{:S(2)}) %collective-permute-start.50) | collective-permute-done | bytes 8224 | tf_op jit(solution)/shard_map/ppermute | solution.py:175
  816.5 13.8 %collective-permute-done.33 = bf16[2048,256]{0,1:T(8,128)(2,1)S(1)} collective-permute-done((bf16[2048,256]{0,1:T(8,128)(2,1)S(1)}, bf16[2048,256]{0,1:T(8,128)(2,1)S(1)}, u32[]{:S(2)}, u32[]{:S(2)}) %collective-permute-start.33) | collective-permute-done | bytes 1048608 | tf_op jit(solution)/shard_map/ppermute | solution.py:175
  884.4 29.8 %collective-permute-done.35 = bf16[512,2048]{1,0:T(8,128)(2,1)} collective-permute-done((bf16[512,2048]{1,0:T(8,128)(2,1)}, bf16[512,2048]{1,0:T(8,128)(2,1)}, u32[]{:S(2)}, u32[]{:S(2)}) %collective-permute-start.35) | collective-permute-done | bytes 2097184 | tf_op jit(solution)/shard_map/ppermute | solution.py:175
  914.3 13.6 %fusion.23 = (f32[512,2048]{1,0:T(8,128)}, f32[512,2048]{1,0:T(8,128)}) fusion(bf16[512,2048]{1,0:T(8,128)(2,1)S(1)} %copy-done.4, f32[512,2048]{1,0:T(8,128)} %convert_add_fusion.1, f32[512]{0:T(512)S(1)} %multiply_multiply_fusion, f32[2048]{0:T(1024)S(1)} %copy-done.48, f32[512]{0:T(512)S(1)} %copy-done.57, f32[512,2048]{1,0:T(8,128)} %copy-done, ...), kind=kLoop, calls=%fused_computation.49 | loop fusion | flops 22020096 | bytes 35676160 | tf_op jit(solution)/shard_map/add | solution.py:502
  938.5 14.6 %collective-permute-done.37 = f32[8,64]{1,0:T(8,128)S(1)} collective-permute-done((f32[8,64]{1,0:T(8,128)S(1)}, f32[8,64]{1,0:T(8,128)S(1)}, u32[]{:S(2)}, u32[]{:S(2)}) %collective-permute-start.37) | collective-permute-done | bytes 2080 | tf_op jit(solution)/shard_map/ppermute | solution.py:175
  977.9 15.9 %collective-permute-done.40 = bf16[512,1024]{1,0:T(8,128)(2,1)S(1)} collective-permute-done((bf16[512,1024]{1,0:T(8,128)(2,1)S(1)}, bf16[512,1024]{1,0:T(8,128)(2,1)S(1)}, u32[]{:S(2)}, u32[]{:S(2)}) %collective-permute-start.40) | collective-permute-done | bytes 1048608 | tf_op jit(solution)/shard_map/ppermute | solution.py:175
  (439 shorter events, 432.7 us)
Async XLA Ops:
  7.2 112.8 %all-gather.6.cloned.1.call-start = ((), (), s32[]{:S(2)}) async-start(), calls=%async_computation.5 | async-start | bytes 5242880 | tf_op jit(solution)/shard_map/all_gather | solution.py:284
  9.7 258.9 %all-gather.8.cloned.1.call-start = ((), (), s32[]{:S(2)}) async-start(), calls=%async_computation.6 | async-start | bytes 5242880 | tf_op jit(solution)/shard_map/all_gather | solution.py:284
  12.8 48.9 %collective-permute-start = (bf16[512,2048]{1,0:T(8,128)(2,1)}, bf16[512,2048]{1,0:T(8,128)(2,1)}, u32[]{:S(2)}, u32[]{:S(2)}) collective-permute-start(bf16[512,2048]{1,0:T(8,128)(2,1)} %fusion.26), channel_id=1, source_target_pairs={{0,1},{1,0},{2,3},{3,2},{4,5},{5,4},{6,7},{7,6},{8,9},{9,8},{10,11... | collective-permute-start | bytes 6291464 | tf_op jit(solution)/shard_map/ppermute | solution.py:175
  18.0 265.4 %all-gather.10.cloned.1.call-start = ((), (), s32[]{:S(2)}) async-start(), calls=%async_computation.7 | async-start | bytes 5242880 | tf_op jit(solution)/shard_map/all_gather | solution.py:284
  18.1 115.8 %collective-permute-start.9 = (bf16[512,2048]{1,0:T(8,128)(2,1)}, bf16[512,2048]{1,0:T(8,128)(2,1)}, u32[]{:S(2)}, u32[]{:S(2)}) collective-permute-start(bf16[512,2048]{1,0:T(8,128)(2,1)} %param.14), channel_id=1, source_target_pairs={{0,16},{8,24},{16,0},{24,8},{1,17},{9,25},{17,1},{25,9},{2,18},{10... | collective-permute-start | bytes 6291464 | tf_op jit(solution)/shard_map/ppermute | solution.py:175
  66.5 47.1 %collective-permute-start.4 = (bf16[512,2048]{1,0:T(8,128)(2,1)}, bf16[512,2048]{1,0:T(8,128)(2,1)}, u32[]{:S(2)}, u32[]{:S(2)}) collective-permute-start(bf16[512,2048]{1,0:T(8,128)(2,1)} %param.14), channel_id=1, source_target_pairs={{0,1},{1,0},{2,3},{3,2},{4,5},{5,4},{6,7},{7,6},{8,9},{9,8},{10,11... | collective-permute-start | bytes 6291464 | tf_op jit(solution)/shard_map/ppermute | solution.py:175
  118.5 64.9 %collective-permute-start.5 = (bf16[1024,2048]{1,0:T(8,128)(2,1)}, bf16[1024,2048]{1,0:T(8,128)(2,1)}, u32[]{:S(2)}, u32[]{:S(2)}) collective-permute-start(bf16[1024,2048]{1,0:T(8,128)(2,1)} %pad_maximum_fusion.3), channel_id=1, source_target_pairs={{0,8},{8,0},{16,24},{24,16},{1,9},{9,1},{17,25},{25,17},{2,10},{10... | collective-permute-start | bytes 12582920 | tf_op jit(solution)/shard_map/ppermute | solution.py:175
  118.5 48.4 %collective-permute-start.10 = (bf16[512,2048]{1,0:T(8,128)(2,1)}, bf16[512,2048]{1,0:T(8,128)(2,1)}, u32[]{:S(2)}, u32[]{:S(2)}) collective-permute-start(bf16[512,2048]{1,0:T(8,128)(2,1)} %collective-permute-done.4), channel_id=1, source_target_pairs={{0,16},{8,24},{16,0},{24,8},{1,17},{9,25},{17,1},{25,9},{2,18},{10... | collective-permute-start | bytes 6291464 | tf_op jit(solution)/shard_map/ppermute | solution.py:175
  126.2 48.1 %collective-permute-start.1 = (bf16[512,2048]{1,0:T(8,128)(2,1)}, bf16[512,2048]{1,0:T(8,128)(2,1)}, u32[]{:S(2)}, u32[]{:S(2)}) collective-permute-start(bf16[512,2048]{1,0:T(8,128)(2,1)} %convolution_convert_fusion.9), channel_id=1, source_target_pairs={{0,1},{1,0},{2,3},{3,2},{4,5},{5,4},{6,7},{7,6},{8,9},{9,8},{10,11... | collective-permute-start | bytes 6291464 | tf_op jit(solution)/shard_map/ppermute | solution.py:175
  130.0 412.8 %reduce-scatter.6.cloned.1.call-start = ((), (), s32[]{:S(2)}) async-start(), calls=%async_computation.8 | async-start | bytes 5242880 | tf_op jit(solution)/shard_map/reduce_scatter | solution.py:288
  169.4 70.3 %collective-permute-start.11 = (bf16[1024,2048]{1,0:T(8,128)(2,1)S(1)}, bf16[1024,2048]{1,0:T(8,128)(2,1)S(1)}, u32[]{:S(2)}, u32[]{:S(2)}) collective-permute-start(bf16[1024,2048]{1,0:T(8,128)(2,1)S(1)} %pad_maximum_fusion.5), channel_id=1, source_target_pairs={{0,8},{8,0},{16,24},{24,16},{1,9},{9,1},{17,25},{25,17},{2,10},{10... | collective-permute-start | bytes 12582920 | tf_op jit(solution)/shard_map/ppermute | solution.py:175
  181.3 47.0 %collective-permute-start.2 = (bf16[512,2048]{1,0:T(8,128)(2,1)S(1)}, bf16[512,2048]{1,0:T(8,128)(2,1)S(1)}, u32[]{:S(2)}, u32[]{:S(2)}) collective-permute-start(bf16[512,2048]{1,0:T(8,128)(2,1)S(1)} %multiply_convert_fusion), channel_id=1, source_target_pairs={{0,1},{1,0},{2,3},{3,2},{4,5},{5,4},{6,7},{7,6},{8,9},{9,8},{10,11... | collective-permute-start | bytes 6291464 | tf_op jit(solution)/shard_map/ppermute | solution.py:175
  182.9 46.6 %collective-permute-start.3 = (bf16[512,2048]{1,0:T(8,128)(2,1)S(1)}, bf16[512,2048]{1,0:T(8,128)(2,1)S(1)}, u32[]{:S(2)}, u32[]{:S(2)}) collective-permute-start(bf16[512,2048]{1,0:T(8,128)(2,1)S(1)} %multiply_convert_fusion), channel_id=1, source_target_pairs={{0,16},{8,24},{16,0},{24,8},{1,17},{9,25},{17,1},{25,9},{2,18},{10... | collective-permute-start | bytes 6291464 | tf_op jit(solution)/shard_map/ppermute | solution.py:175
  402.8 190.8 %reduce-scatter.8.cloned.1.call-start = ((), (), s32[]{:S(2)}) async-start(), calls=%async_computation.9 | async-start | bytes 5242880 | tf_op jit(solution)/shard_map/reduce_scatter | solution.py:288
  482.9 195.0 %reduce-scatter.10.cloned.1.call-start = ((), (), s32[]{:S(2)}) async-start(), calls=%async_computation.10 | async-start | bytes 5242880 | tf_op jit(solution)/shard_map/reduce_scatter | solution.py:288
  483.0 47.6 %collective-permute-start.18 = (bf16[512,2048]{1,0:T(8,128)(2,1)}, bf16[512,2048]{1,0:T(8,128)(2,1)S(1)}, u32[]{:S(2)}, u32[]{:S(2)}) collective-permute-start(bf16[512,2048]{1,0:T(8,128)(2,1)} %add_convert_fusion.13), channel_id=1, source_target_pairs={{0,16},{8,24},{16,0},{24,8},{1,17},{9,25},{17,1},{25,9},{2,18},{10... | collective-permute-start | bytes 6291464 | tf_op jit(solution)/shard_map/ppermute | solution.py:175
  484.7 47.2 %collective-permute-start.17 = (bf16[512,2048]{1,0:T(8,128)(2,1)}, bf16[512,2048]{1,0:T(8,128)(2,1)S(1)}, u32[]{:S(2)}, u32[]{:S(2)}) collective-permute-start(bf16[512,2048]{1,0:T(8,128)(2,1)} %add_convert_fusion.12), channel_id=1, source_target_pairs={{0,1},{1,0},{2,3},{3,2},{4,5},{5,4},{6,7},{7,6},{8,9},{9,8},{10,11... | collective-permute-start | bytes 6291464 | tf_op jit(solution)/shard_map/ppermute | solution.py:175
  543.5 50.0 %collective-permute-start.20 = (bf16[256,2048]{1,0:T(8,128)(2,1)}, bf16[256,2048]{1,0:T(8,128)(2,1)S(1)}, u32[]{:S(2)}, u32[]{:S(2)}) collective-permute-start(bf16[256,2048]{1,0:T(8,128)(2,1)} %reduce-scatter.6.cloned.1.call-done), channel_id=1, source_target_pairs={{0,16},{8,24},{16,0},{24,8},{1,17},{9,25},{17,1},{25,9},{2,18},{10... | collective-permute-start | bytes 3145736 | tf_op jit(solution)/shard_map/ppermute | solution.py:175
  559.1 151.9 %reduce-scatter.12.cloned.1.call-start = ((), (), s32[]{:S(2)}) async-start(), calls=%async_computation.11 | async-start | bytes 1310720 | tf_op jit(solution)/shard_map/reduce_scatter | solution.py:288
  610.4 97.3 %collective-permute-start.29 = (bf16[2048,256]{0,1:T(8,128)(2,1)S(1)}, bf16[2048,256]{0,1:T(8,128)(2,1)}, u32[]{:S(2)}, u32[]{:S(2)}) collective-permute-start(bf16[2048,256]{0,1:T(8,128)(2,1)S(1)} %bitcast.63), channel_id=1, source_target_pairs={{0,16},{8,24},{16,0},{24,8},{1,17},{9,25},{17,1},{25,9},{2,18},{10... | collective-permute-start | bytes 3145736 | tf_op jit(solution)/shard_map/ppermute | solution.py:175
  614.5 74.9 %collective-permute-start.56 = (bf16[512,2048]{1,0:T(8,128)(2,1)}, bf16[512,2048]{1,0:T(8,128)(2,1)}, u32[]{:S(2)}, u32[]{:S(2)}) collective-permute-start(bf16[512,2048]{1,0:T(8,128)(2,1)} %pad_maximum_fusion.15), channel_id=1, source_target_pairs={{0,8},{8,0},{16,24},{24,16},{1,9},{9,1},{17,25},{25,17},{2,10},{10... | collective-permute-start | bytes 6291464 | tf_op jit(solution)/shard_map/ppermute | solution.py:175
  673.5 88.2 %collective-permute-start.23 = (bf16[1024,2048]{1,0:T(8,128)(2,1)}, bf16[1024,2048]{1,0:T(8,128)(2,1)}, u32[]{:S(2)}, u32[]{:S(2)}) collective-permute-start(bf16[1024,2048]{1,0:T(8,128)(2,1)} %convolution_convert_fusion.5), channel_id=1, source_target_pairs={{0,8},{8,0},{16,24},{24,16},{1,9},{9,1},{17,25},{25,17},{2,10},{10... | collective-permute-start | bytes 12582920 | tf_op jit(solution)/shard_map/ppermute | solution.py:175
  677.9 80.7 %all-gather.12.cloned.1.call-start = ((), (), s32[]{:S(2)}) async-start(), calls=%async_computation.12 | async-start | bytes 1310720 | tf_op jit(solution)/shard_map/all_gather | solution.py:284
  689.5 48.4 %collective-permute-start.32 = (bf16[512,2048]{1,0:T(8,128)(2,1)}, bf16[512,2048]{1,0:T(8,128)(2,1)}, u32[]{:S(2)}, u32[]{:S(2)}) collective-permute-start(bf16[512,2048]{1,0:T(8,128)(2,1)} %convolution_convert_fusion.10), channel_id=1, source_target_pairs={{0,1},{1,0},{2,3},{3,2},{4,5},{5,4},{6,7},{7,6},{8,9},{9,8},{10,11... | collective-permute-start | bytes 6291464 | tf_op jit(solution)/shard_map/ppermute | solution.py:175
  701.6 109.2 %collective-permute-start.25 = (bf16[1024,2048]{1,0:T(8,128)(2,1)}, bf16[1024,2048]{1,0:T(8,128)(2,1)}, u32[]{:S(2)}, u32[]{:S(2)}) collective-permute-start(bf16[1024,2048]{1,0:T(8,128)(2,1)} %convolution_convert_fusion.4), channel_id=1, source_target_pairs={{0,8},{8,0},{16,24},{24,16},{1,9},{9,1},{17,25},{25,17},{2,10},{10... | collective-permute-start | bytes 12582920 | tf_op jit(solution)/shard_map/ppermute | solution.py:175
  709.5 46.6 %collective-permute-start.31 = (bf16[512,1024]{1,0:T(8,128)(2,1)}, bf16[512,1024]{1,0:T(8,128)(2,1)}, u32[]{:S(2)}, u32[]{:S(2)}) collective-permute-start(bf16[512,1024]{1,0:T(8,128)(2,1)} %constant_dynamic-slice_fusion), channel_id=1, source_target_pairs={{0,16},{8,24},{16,0},{24,8},{1,17},{9,25},{17,1},{25,9},{2,18},{10... | collective-permute-start | bytes 3145736 | tf_op jit(solution)/shard_map/ppermute | solution.py:175
  711.0 119.3 %reduce-scatter.14.cloned.1.call-start = ((), (), s32[]{:S(2)}) async-start(), calls=%async_computation.13 | async-start | bytes 2621440 | tf_op jit(solution)/shard_map/reduce_scatter | solution.py:288
  761.5 166.4 %all-gather.14.cloned.1.call-start = ((), (), s32[]{:S(2)}) async-start(), calls=%async_computation.14 | async-start | bytes 2621440 | tf_op jit(solution)/shard_map/all_gather | solution.py:284
  785.0 65.5 %collective-permute-start.54 = (bf16[2048,512]{0,1:T(8,128)(2,1)}, bf16[2048,512]{0,1:T(8,128)(2,1)}, u32[]{:S(2)}, u32[]{:S(2)}) collective-permute-start(bf16[2048,512]{0,1:T(8,128)(2,1)} %pad_maximum_fusion.13), channel_id=1, source_target_pairs={{0,8},{8,0},{16,24},{24,16},{1,9},{9,1},{17,25},{25,17},{2,10},{10... | collective-permute-start | bytes 6291464 | tf_op jit(solution)/shard_map/ppermute | solution.py:175
  846.1 81.8 %collective-permute-start.36 = (bf16[256,2048]{1,0:T(8,128)(2,1)}, bf16[256,2048]{1,0:T(8,128)(2,1)}, u32[]{:S(2)}, u32[]{:S(2)}) collective-permute-start(bf16[256,2048]{1,0:T(8,128)(2,1)} %all-gather.12.cloned.1.call-done), channel_id=1, source_target_pairs={{0,16},{8,24},{16,0},{24,8},{1,17},{9,25},{17,1},{25,9},{2,18},{10... | collective-permute-start | bytes 3145736 | tf_op jit(solution)/shard_map/ppermute | solution.py:175
  846.8 67.4 %collective-permute-start.35 = (bf16[512,2048]{1,0:T(8,128)(2,1)}, bf16[512,2048]{1,0:T(8,128)(2,1)}, u32[]{:S(2)}, u32[]{:S(2)}) collective-permute-start(bf16[512,2048]{1,0:T(8,128)(2,1)} %add_convert_fusion.10), channel_id=1, source_target_pairs={{0,16},{8,24},{16,0},{24,8},{1,17},{9,25},{17,1},{25,9},{2,18},{10... | collective-permute-start | bytes 6291464 | tf_op jit(solution)/shard_map/ppermute | solution.py:175
  848.4 65.8 %collective-permute-start.34 = (bf16[512,2048]{1,0:T(8,128)(2,1)}, bf16[512,2048]{1,0:T(8,128)(2,1)}, u32[]{:S(2)}, u32[]{:S(2)}) collective-permute-start(bf16[512,2048]{1,0:T(8,128)(2,1)} %add_convert_fusion.9), channel_id=1, source_target_pairs={{0,1},{1,0},{2,3},{3,2},{4,5},{5,4},{6,7},{7,6},{8,9},{9,8},{10,11... | collective-permute-start | bytes 6291464 | tf_op jit(solution)/shard_map/ppermute | solution.py:175
  (124 other events, 2064.4 us)
Sparse Core Ops, SparseCore 0:
  10.2 83.4 all-gather.5
  95.2 79.0 all-gather.7
  175.8 78.7 all-gather.9
  402.9 77.2 reduce-scatter.5
  483.0 77.1 reduce-scatter.7
  562.4 77.2 reduce-scatter.9
  678.0 26.9 reduce-scatter.11
  711.1 28.2 all-gather.11
  761.6 43.8 reduce-scatter.13
  850.5 44.9 all-gather.13

commit v8 on v7

--- a/solution.py
+++ b/solution.py
@@ -435,14 +435,18 @@
         [gate_backs[1]],
     )
     gate_part = row_scatter(weight_sum(gate_backs, mid_sets))
-    up_part = row_scatter(weight_sum(up_backs, mid_sets))
-
     res_from_mid, second_gain_part = second_back(mid_grad)
     res_grad = wide(cotangent) + res_from_mid
-    res_low, down_part = tie(low(res_grad), down_part)
+    res_low, down_part, second_gain_part, *up_backs = tie(
+        low(res_grad), down_part, second_gain_part, *up_backs
+    )
+    up_part = row_scatter(weight_sum(up_backs, mid_sets))
+    second_gain_part = butterfly(second_gain_part.reshape(8, -1), ("grp", "row"))
     shard_rows = jnp.concatenate(col_gather(res_low), axis=0)
     down_over_y = swap(down_part, "grp", 2)
-    shard_rows, gate_part, down_over_y = tie(shard_rows, gate_part, down_over_y)
+    shard_rows, gate_part, down_over_y, second_gain_part = tie(
+        shard_rows, gate_part, down_over_y, second_gain_part
+    )
     gate_part = gate_part.T
     gate_over_y = swap(gate_part, "grp", 2)
 
@@ -473,37 +477,40 @@
     back_all = jnp.concatenate([query_back, pair_back], axis=1)
     query_low_grad = low(dot_tn(gathered_in, query_back))
     pair_low_grad = low(dot_tn(gathered_in, pair_back))
-    query_low_grad, pair_low_grad, *acts = tie(query_low_grad, pair_low_grad, *acts)
-    query_part, pair_part, gate_over_y = tie(
-        sum_cores(query_low_grad, core), sum_cores(pair_low_grad, core), gate_over_y
+    query_part, pair_part, gate_over_y, *acts = tie(
+        sum_cores(query_low_grad, core), sum_cores(pair_low_grad, core), gate_over_y, *acts
     )
     back_parts = blocks_of(back_all, 0, 2) if in_pairs else [back_all]
     in_grad = col_scatter(lambda i: dot_nt(back_parts[i], project_in))
-    query_part, pair_part, out_part, up_part, second_gain_part, in_grad = tie(
-        sum_y(query_part, ypos),
-        sum_y(pair_part, ypos),
-        out_part,
-        up_part,
-        second_gain_part,
-        in_grad,
+    query_part, pair_part, out_part, up_part, in_grad = tie(
+        sum_y(query_part, ypos), sum_y(pair_part, ypos), out_part, up_part, in_grad
     )
     both_part = row_scatter(jnp.concatenate([query_part, pair_part], axis=1))
     up_part = up_part.T
     up_over_y = swap(up_part, "grp", 2)
     out_over_y = swap(out_part, "grp", 2)
     out_from_core = near_sum(out_product)
-    layer_rows, (both_part, up_over_y) = square_scatter(
-        lambda first, last: out_product(0, first, last) + wide(out_from_core[first:last]),
-        far_sum(out_product),
-        [both_part, up_over_y],
-    )
+    out_far = far_sum(out_product)
+
+    def out_near(first, last):
+        return out_product(0, first, last) + wide(out_from_core[first:last])
+
+    if in_pairs:
+        mid_row = packed_length // 2
+        across = swap(out_far[mid_row:], "col", 1)
+        out_far = low(wide(out_far[:mid_row]) + wide(across))
+    both_part, up_over_y, out_over_y, out_far = tie(both_part, up_over_y, out_over_y, out_far)
+    from_y = wide(swap(out_far, "grp", 2))
+    if in_pairs:
+        from_x = wide(swap(low(out_near(mid_row, packed_length)), "col", 1))
+        layer_rows = out_near(0, mid_row) + from_x + from_y
+    else:
+        layer_rows = col_scatter(lambda i: out_near(0, packed_length) + from_y)
     layer_out = hidden_res + layer_rows
     res_from_in, _ = first_back(in_grad)
     input_grad = res_grad + res_from_in
 
-    both_part, layer_out, input_grad, out_over_y = tie(
-        row_gather(both_part), layer_out, input_grad, out_over_y
-    )
+    both_part, layer_out, input_grad = tie(row_gather(both_part), layer_out, input_grad)
     size = both_part.shape[0]
     project_rows = lax.dynamic_slice_in_dim(project_in, (2 * core + ypos) * size, size, 0)
     term = jnp.sum(wide(both_part) * wide(project_rows), axis=1)
@@ -540,8 +547,7 @@
 
         key_full = spread(pair_all[..., :key_cols])
         value_full = spread(pair_all[..., key_cols:])
-    axes = ("grp", "row", "col")
-    second_gain_grad = butterfly(second_gain_part.reshape(8, -1), axes).reshape(-1)
+    second_gain_grad = butterfly(second_gain_part, ("col",)).reshape(-1)
     return (
         layer_out,
         input_grad,

time: 1030 us -> 971 us (0.943)
  waiting for transfers between devices: 342 us -> 265 us
  other arithmetic: 145 us -> 160 us
    ppermute x57 -> x56, waiting for transfers between devices: 342 us -> 264 us  [swap(): return lax.ppermute(value, axis, [(i, i ^ bit) for i in range(count)])]
    unnamed x191 -> x223, local copies, waits for them, and re-layouts: 52.3 us -> 56.8 us
    ppermute x57 -> x56, starting transfers between devices: 45 us -> 46.2 us  [swap(): return lax.ppermute(value, axis, [(i, i ^ bit) for i in range(count)])]
  transfers between devices with their start and end apart: 67 -> 66, of which waited for: 24 -> 22; matrix products, arithmetic and copies ran while one was open for 47% -> 51% of each run, Pallas kernels for 3% -> 3%
where the time goes in v8:
time: 971 us; the launch traced here: 960 us
  matrix products  347 us (36%)
  waiting for transfers between devices  265 us (27%)
  other arithmetic  160 us (16%)
  local copies, waits for them, and re-layouts  93.2 us (10%)
  starting transfers between devices  47.6 us (5%)
  Pallas kernels  32 us (3%)
  between operations  15.7 us (2%)
    ppermute x56, waiting for transfers between devices, swap(): return lax.ppermute(value, axis, [(i, i ^ bit) for i in range(count)])  264 us
    dot_general x18, matrix products, dot32(): return jnp.dot(left, right, preferred_element_type=jnp.float32)  128 us
    dot_general x9, matrix products, dot_nt(): jnp.einsum('td,fd->tf', left, right, preferred_element_type=jnp.float32)  116 us
    dot_general x9, matrix products, dot_tn(): jnp.einsum('td,tf->df', left, right, preferred_element_type=jnp.float32)  103 us
    unnamed x223, local copies, waits for them, and re-layouts  56.8 us
    ppermute x56, starting transfers between devices, swap(): return lax.ppermute(value, axis, [(i, i ^ bit) for i in range(count)])  46.2 us
    select_n x17, other arithmetic, ordered(): jnp.where(keep, mine, theirs)  36.3 us
    pallas_call x2, Pallas kernels, attention_call(): pl.pallas_call(kernel, grid_spec=pltpu.PrefetchScalarGridSpec(num_scalar_...  32 us
  transfers between devices with their start and end apart: 66, of which 22 were waited for; matrix products, arithmetic and copies ran while one was open for 51% of the time, Pallas kernels for 3%

profile of v8, /device:TPU:0, one launch (start us, length us, event | category | flops | bytes accessed | tf_op | source)
XLA Modules:
  0.0 960.0 jit_solution(10313164685469279138)
XLA Ops:
  24.6 37.0 %collective-permute-done = bf16[512,2048]{1,0:T(8,128)(2,1)} collective-permute-done((bf16[512,2048]{1,0:T(8,128)(2,1)}, bf16[512,2048]{1,0:T(8,128)(2,1)}, u32[]{:S(2)}, u32[]{:S(2)}) %collective-permute-start) | collective-permute-done | bytes 2097184 | tf_op jit(solution)/shard_map/ppermute | solution.py:175
  73.4 14.7 %fusion.73.q_ref.k_ref.v_ref = f32[1024,2048]{1,0:T(8,128)} fusion(bf16[1024,2048]{1,0:T(8,128)(2,1)} %pad_maximum_fusion.2, bf16[2048,512]{1,0:T(8,128)(2,1)} %get-tuple-element.203, bf16[2048,512]{1,0:T(8,128)(2,1)} %get-tuple-element.204, bf16[2048,1024]{1,0:T(8,128)(2,1)} %param.18), kind=kOutput, calls=%fused_computation.222 | convolution fusion | flops 8615100416 | bytes 20971520 | tf_op jit(solution)/shard_map/dot_general | solution.py:195
  88.1 12.1 %attend.1 = (bf16[1024,1024]{1,0:T(8,128)(2,1)}, bf16[1024,1024]{1,0:T(8,128)(2,1)}, bf16[1024,512]{1,0:T(8,128)(2,1)}, bf16[1024,512]{1,0:T(8,128)(2,1)}) custom-call(s32[1]{0:T(128)} %bitcast.first_ref, f32[1024,2048]{1,0:T(8,128)} %fusion.73.q_ref.k_ref.v_ref, f32[1024,2048]{1,0:T(8,128)} %fusion.73.q_ref.k_ref.v_ref, ...), custom_call_target="tpu_custom_call" | custom-call | flops 3221225472 | bytes 16106127 | tf_op jit(solution)/shard_map/attend/pallas_call | solution.py:153
  100.2 13.5 %collective-permute-done.4 = bf16[512,2048]{1,0:T(8,128)(2,1)} collective-permute-done((bf16[512,2048]{1,0:T(8,128)(2,1)}, bf16[512,2048]{1,0:T(8,128)(2,1)}, u32[]{:S(2)}, u32[]{:S(2)}) %collective-permute-start.4) | collective-permute-done | bytes 2097184 | tf_op jit(solution)/shard_map/ppermute | solution.py:175
  133.7 33.1 %collective-permute-done.10 = bf16[512,2048]{1,0:T(8,128)(2,1)} collective-permute-done((bf16[512,2048]{1,0:T(8,128)(2,1)}, bf16[512,2048]{1,0:T(8,128)(2,1)}, u32[]{:S(2)}, u32[]{:S(2)}) %collective-permute-start.10) | collective-permute-done | bytes 2097184 | tf_op jit(solution)/shard_map/ppermute | solution.py:175
  186.0 13.7 %convolution_convert_fusion.3 = bf16[2048,1024]{1,0:T(8,128)(2,1)} fusion(bf16[2048,2048]{1,0:T(8,128)(2,1)S(1)} %constant_dynamic-update-slice_fusion, bf16[1024,2048]{1,0:T(8,128)(2,1)} %all-gather.6.cloned.1.call-done), kind=kOutput, calls=%fused_computation.85 | convolution fusion | flops 8592031744 | bytes 16777216 | tf_op jit(solution)/shard_map/td,fd->tf/dot_general | solution.py:199
  199.7 28.6 %collective-permute-done.2 = bf16[512,2048]{1,0:T(8,128)(2,1)S(1)} collective-permute-done((bf16[512,2048]{1,0:T(8,128)(2,1)S(1)}, bf16[512,2048]{1,0:T(8,128)(2,1)S(1)}, u32[]{:S(2)}, u32[]{:S(2)}) %collective-permute-start.2) | collective-permute-done | bytes 2097184 | tf_op jit(solution)/shard_map/ppermute | solution.py:175
  242.0 12.6 %convolution_convert_fusion.1 = bf16[2048,1024]{1,0:T(8,128)(2,1)} fusion(bf16[2048,2048]{1,0:T(8,128)(2,1)} %constant_dynamic-update-slice_fusion.3, bf16[1024,2048]{1,0:T(8,128)(2,1)S(1)} %copy-done.82), kind=kOutput, calls=%fused_computation.83 | convolution fusion | flops 8592031744 | bytes 16777216 | tf_op jit(solution)/shard_map/td,fd->tf/dot_general | solution.py:199
  268.7 14.8 %convolution_convert_fusion.2 = bf16[2048,1024]{1,0:T(8,128)(2,1)} fusion(bf16[1024,2048]{0,1:T(8,128)(2,1)} %all-gather.8.cloned.1.call-done, bf16[1024,2048]{1,0:T(8,128)(2,1)} %collective-permute-done.6, bf16[512,2048]{1,0:T(8,128)(2,1)} %copy-done.38, bf16[512,2048]{1,0:T(8,128)(2,1)S(1)} %multiply_convert_fusion), kind=kOutput, calls=%fused_computation.84 | convolution fusion | flops 8617197568 | bytes 16777216 | tf_op jit(solution)/shard_map/td,fd->tf/dot_general | solution.py:199
  283.4 20.8 %fusion.5 = (bf16[2048,1024]{1,0:T(8,128)(2,1)}, bf16[2048,1024]{1,0:T(8,128)(2,1)}, bf16[2048,1024]{1,0:T(8,128)(2,1)}) fusion(bf16[2048,1024]{1,0:T(8,128)(2,1)} %convolution_convert_fusion.3, bf16[2048,1024]{1,0:T(8,128)(2,1)} %convolution_convert_fusion.2, bf16[1024,2048]{0,1:T(8,128)(2,1)} %all-gather.10.cloned.1.call-done, ...), kind=kOutput, calls=%fused_computation.15 | convolution fusion | flops 8652849152 | bytes 33554432 | tf_op jit(solution)/shard_map/td,fd->tf/dot_general | solution.py:199
  309.2 13.2 %convolution_convert_fusion = bf16[2048,1024]{1,0:T(8,128)(2,1)} fusion(bf16[2048,2048]{1,0:T(8,128)(2,1)} %constant_dynamic-update-slice_fusion.6, bf16[1024,2048]{0,1:T(8,128)(2,1)S(1)} %copy-done.85), kind=kOutput, calls=%fused_computation.82 | convolution fusion | flops 8592031744 | bytes 16777216 | tf_op jit(solution)/shard_map/td,fd->tf/dot_general | solution.py:199
  322.4 20.8 %fusion.2 = (bf16[2048,1024]{1,0:T(8,128)(2,1)}, bf16[2048,1024]{1,0:T(8,128)(2,1)}, bf16[2048,1024]{1,0:T(8,128)(2,1)}) fusion(bf16[2048,1024]{1,0:T(8,128)(2,1)} %convolution_convert_fusion.1, bf16[2048,1024]{1,0:T(8,128)(2,1)} %convolution_convert_fusion, bf16[2048,2048]{1,0:T(8,128)(2,1)} %constant_dynamic-update-slice_fusion.6, ...), kind=kOutput, calls=%fused_computation.12 | convolution fusion | flops 8627683328 | bytes 33554432 | tf_op jit(solution)/shard_map/td,fd->tf/dot_general | solution.py:199
  343.3 12.9 %fusion.75 = f32[1024,2048]{1,0:T(8,128)S(1)} fusion(bf16[2048,1024]{1,0:T(8,128)(2,1)} %get-tuple-element.114, bf16[2048,2048]{1,0:T(8,128)(2,1)} %constant_dynamic-update-slice_fusion.3), kind=kOutput, calls=%fused_computation.224 | convolution fusion | flops 8589934592 | bytes 20971520 | tf_op jit(solution)/shard_map/td,tf->df/dot_general | solution.py:203
  356.3 11.1 %add_convert_fusion.6 = bf16[1024,2048]{1,0:T(8,128)(2,1)} fusion(f32[1024,2048]{1,0:T(8,128)S(1)} %fusion.75, bf16[2048,1024]{1,0:T(8,128)(2,1)S(1)} %copy-done.96, bf16[2048,2048]{1,0:T(8,128)(2,1)S(1)} %bitcast.66), kind=kOutput, calls=%fused_computation.40 | convolution fusion | flops 8594128896 | bytes 25165824 | tf_op jit(solution)/shard_map/td,tf->df/dot_general | solution.py:203
  367.3 10.9 %fusion.43 = f32[1024,2048]{1,0:T(8,128)} fusion(bf16[1024,2048]{0,1:T(8,128)(2,1)} %all-gather.8.cloned.1.call-done, bf16[2048,1024]{1,0:T(8,128)(2,1)} %get-tuple-element.92), kind=kOutput, calls=%fused_computation.121 | convolution fusion | flops 4294967296 | bytes 14680064 | tf_op jit(solution)/shard_map/dot_general | solution.py:195
  378.3 8.7 add_convert_fusion.5
  402.8 10.9 %fusion.46 = f32[1024,2048]{1,0:T(8,128)} fusion(bf16[1024,2048]{0,1:T(8,128)(2,1)} %all-gather.8.cloned.1.call-done, bf16[2048,1024]{1,0:T(8,128)(2,1)} %get-tuple-element.92), kind=kOutput, calls=%fused_computation.124 | convolution fusion | flops 4294967296 | bytes 14680064 | tf_op jit(solution)/shard_map/dot_general | solution.py:195
  427.8 19.7 %collective-permute-done.15 = bf16[256,2048]{1,0:T(8,128)(2,1)S(1)} collective-permute-done((bf16[256,2048]{1,0:T(8,128)(2,1)S(1)}, bf16[256,2048]{1,0:T(8,128)(2,1)S(1)}, u32[]{:S(2)}, u32[]{:S(2)}) %collective-permute-start.15) | collective-permute-done | bytes 1048608 | tf_op jit(solution)/shard_map/ppermute | solution.py:175
  457.6 13.9 %fusion.76 = f32[1024,2048]{1,0:T(8,128)} fusion(bf16[2048,1024]{1,0:T(8,128)(2,1)S(1)} %copy-done.102, bf16[2048,2048]{1,0:T(8,128)(2,1)} %constant_dynamic-update-slice_fusion.6), kind=kOutput, calls=%fused_computation.225 | convolution fusion | flops 8589934592 | bytes 20971520 | tf_op jit(solution)/shard_map/td,tf->df/dot_general | solution.py:203
  471.5 13.9 %add_convert_fusion.2 = bf16[1024,2048]{1,0:T(8,128)(2,1)} fusion(f32[1024,2048]{1,0:T(8,128)} %fusion.76, bf16[2048,1024]{1,0:T(8,128)(2,1)S(1)} %copy-done.95, bf16[1024,2048]{1,0:T(8,128)(2,1)} %collective-permute-done.6, bf16[512,2048]{1,0:T(8,128)(2,1)S(1)} %copy-done.39, bf16[512,2048]{1,0:T(8,128)(2,1)S(1)} %copy-done.24), kind=kOutput, calls=%fused_computation.36 | convolution fusion | flops 8619294720 | bytes 25165824 | tf_op jit(solution)/shard_map/td,tf->df/dot_general | solution.py:203
  528.3 14.9 %fusion.77 = f32[1024,2048]{1,0:T(8,128)} fusion(bf16[2048,1024]{1,0:T(8,128)(2,1)} %get-tuple-element.107, bf16[2048,2048]{1,0:T(8,128)(2,1)} %constant_dynamic-update-slice_fusion.6), kind=kOutput, calls=%fused_computation.226 | convolution fusion | flops 8589934592 | bytes 20971520 | tf_op jit(solution)/shard_map/td,tf->df/dot_general | solution.py:203
  545.8 13.8 %add_convert_fusion.1 = bf16[1024,2048]{1,0:T(8,128)(2,1)} fusion(f32[1024,2048]{1,0:T(8,128)} %fusion.77, bf16[2048,1024]{1,0:T(8,128)(2,1)S(1)} %copy-done.93, bf16[1024,2048]{1,0:T(8,128)(2,1)} %collective-permute-done.6, bf16[512,2048]{1,0:T(8,128)(2,1)S(1)} %copy-done.40, bf16[512,2048]{1,0:T(8,128)(2,1)S(1)} %copy-done.24), kind=kOutput, calls=%fused_computation.35 | convolution fusion | flops 8619294720 | bytes 25165824 | tf_op jit(solution)/shard_map/td,tf->df/dot_general | solution.py:203
  560.1 12.2 %collective-permute-done.19 = bf16[512,2048]{1,0:T(8,128)(2,1)} collective-permute-done((bf16[512,2048]{1,0:T(8,128)(2,1)}, bf16[512,2048]{1,0:T(8,128)(2,1)}, u32[]{:S(2)}, u32[]{:S(2)}) %collective-permute-start.19) | collective-permute-done | bytes 2097184 | tf_op jit(solution)/shard_map/ppermute | solution.py:175
  600.8 20.0 %attend_back.1 = (bf16[1024,1024]{1,0:T(8,128)(2,1)}, bf16[1024,512]{1,0:T(8,128)(2,1)}, bf16[1024,512]{1,0:T(8,128)(2,1)}) custom-call(s32[1]{0:T(128)} %bitcast.first_ref, bf16[1024,1024]{1,0:T(8,128)(2,1)} %get-tuple-element.70.q_ref, bf16[1024,512]{1,0:T(8,128)(2,1)} %get-tuple-element.71.k_ref, bf16[1024,512]{1,0:T(8,128)(2,1)} %get-tuple-element.72.v_ref, ...), custom_call_target="tpu_custom_call" | custom-call | flops 7516192768 | bytes 37580964 | tf_op jit(solution)/shard_map/attend_back/pallas_call | solution.py:153
  694.7 16.5 %collective-permute-done.32 = bf16[512,2048]{1,0:T(8,128)(2,1)} collective-permute-done((bf16[512,2048]{1,0:T(8,128)(2,1)}, bf16[512,2048]{1,0:T(8,128)(2,1)}, u32[]{:S(2)}, u32[]{:S(2)}) %collective-permute-start.32) | collective-permute-done | bytes 2097184 | tf_op jit(solution)/shard_map/ppermute | solution.py:175
  735.5 8.7 add_convert_fusion
  764.7 28.4 %collective-permute-done.36 = bf16[512,2048]{1,0:T(8,128)(2,1)S(1)} collective-permute-done((bf16[512,2048]{1,0:T(8,128)(2,1)S(1)}, bf16[512,2048]{1,0:T(8,128)(2,1)S(1)}, u32[]{:S(2)}, u32[]{:S(2)}) %collective-permute-start.36) | collective-permute-done | bytes 2097184 | tf_op jit(solution)/shard_map/ppermute | solution.py:175
  810.8 9.4 copy.30
  820.2 16.4 %collective-permute-done.38 = bf16[512,2048]{1,0:T(8,128)(2,1)} collective-permute-done((bf16[512,2048]{1,0:T(8,128)(2,1)}, bf16[512,2048]{1,0:T(8,128)(2,1)}, u32[]{:S(2)}, u32[]{:S(2)}) %collective-permute-start.38) | collective-permute-done | bytes 2097184 | tf_op jit(solution)/shard_map/ppermute | solution.py:175
  844.5 13.6 %fusion.23 = (f32[512,2048]{1,0:T(8,128)}, f32[512,2048]{1,0:T(8,128)}) fusion(bf16[512,2048]{1,0:T(8,128)(2,1)S(1)} %copy-done.4, f32[512,2048]{1,0:T(8,128)} %convert_add_fusion.1, f32[512]{0:T(512)S(1)} %multiply_multiply_fusion, f32[2048]{0:T(1024)S(1)} %copy-done.66, f32[512]{0:T(512)S(1)} %copy-done.74, f32[512,2048]{1,0:T(8,128)} %copy-done, ...), kind=kLoop, calls=%fused_computation.49 | loop fusion | flops 22020096 | bytes 35676160 | tf_op jit(solution)/shard_map/add | solution.py:511
  872.2 10.8 %collective-permute-done.46 = bf16[512,1024]{1,0:T(8,128)(2,1)S(1)} collective-permute-done((bf16[512,1024]{1,0:T(8,128)(2,1)S(1)}, bf16[512,1024]{1,0:T(8,128)(2,1)S(1)}, u32[]{:S(2)}, u32[]{:S(2)}) %collective-permute-start.46) | collective-permute-done | bytes 1048608 | tf_op jit(solution)/shard_map/ppermute | solution.py:175
  920.2 9.4 copy.31
  (469 shorter events, 433.0 us)
Async XLA Ops:
  7.2 112.7 %all-gather.6.cloned.1.call-start = ((), (), s32[]{:S(2)}) async-start(), calls=%async_computation.5 | async-start | bytes 5242880 | tf_op jit(solution)/shard_map/all_gather | solution.py:284
  9.7 258.9 %all-gather.8.cloned.1.call-start = ((), (), s32[]{:S(2)}) async-start(), calls=%async_computation.6 | async-start | bytes 5242880 | tf_op jit(solution)/shard_map/all_gather | solution.py:284
  12.7 48.9 %collective-permute-start = (bf16[512,2048]{1,0:T(8,128)(2,1)}, bf16[512,2048]{1,0:T(8,128)(2,1)}, u32[]{:S(2)}, u32[]{:S(2)}) collective-permute-start(bf16[512,2048]{1,0:T(8,128)(2,1)} %fusion.26), channel_id=1, source_target_pairs={{0,1},{1,0},{2,3},{3,2},{4,5},{5,4},{6,7},{7,6},{8,9},{9,8},{10,11... | collective-permute-start | bytes 6291464 | tf_op jit(solution)/shard_map/ppermute | solution.py:175
  18.0 265.4 %all-gather.10.cloned.1.call-start = ((), (), s32[]{:S(2)}) async-start(), calls=%async_computation.7 | async-start | bytes 5242880 | tf_op jit(solution)/shard_map/all_gather | solution.py:284
  18.1 115.6 %collective-permute-start.9 = (bf16[512,2048]{1,0:T(8,128)(2,1)}, bf16[512,2048]{1,0:T(8,128)(2,1)}, u32[]{:S(2)}, u32[]{:S(2)}) collective-permute-start(bf16[512,2048]{1,0:T(8,128)(2,1)} %param.14), channel_id=1, source_target_pairs={{0,16},{8,24},{16,0},{24,8},{1,17},{9,25},{17,1},{25,9},{2,18},{10... | collective-permute-start | bytes 6291464 | tf_op jit(solution)/shard_map/ppermute | solution.py:175
  66.5 47.1 %collective-permute-start.4 = (bf16[512,2048]{1,0:T(8,128)(2,1)}, bf16[512,2048]{1,0:T(8,128)(2,1)}, u32[]{:S(2)}, u32[]{:S(2)}) collective-permute-start(bf16[512,2048]{1,0:T(8,128)(2,1)} %param.14), channel_id=1, source_target_pairs={{0,1},{1,0},{2,3},{3,2},{4,5},{5,4},{6,7},{7,6},{8,9},{9,8},{10,11... | collective-permute-start | bytes 6291464 | tf_op jit(solution)/shard_map/ppermute | solution.py:175
  118.4 64.9 %collective-permute-start.5 = (bf16[1024,2048]{1,0:T(8,128)(2,1)}, bf16[1024,2048]{1,0:T(8,128)(2,1)}, u32[]{:S(2)}, u32[]{:S(2)}) collective-permute-start(bf16[1024,2048]{1,0:T(8,128)(2,1)} %pad_maximum_fusion.3), channel_id=1, source_target_pairs={{0,8},{8,0},{16,24},{24,16},{1,9},{9,1},{17,25},{25,17},{2,10},{10... | collective-permute-start | bytes 12582920 | tf_op jit(solution)/shard_map/ppermute | solution.py:175
  118.5 48.4 %collective-permute-start.10 = (bf16[512,2048]{1,0:T(8,128)(2,1)}, bf16[512,2048]{1,0:T(8,128)(2,1)}, u32[]{:S(2)}, u32[]{:S(2)}) collective-permute-start(bf16[512,2048]{1,0:T(8,128)(2,1)} %collective-permute-done.4), channel_id=1, source_target_pairs={{0,16},{8,24},{16,0},{24,8},{1,17},{9,25},{17,1},{25,9},{2,18},{10... | collective-permute-start | bytes 6291464 | tf_op jit(solution)/shard_map/ppermute | solution.py:175
  126.2 48.1 %collective-permute-start.1 = (bf16[512,2048]{1,0:T(8,128)(2,1)}, bf16[512,2048]{1,0:T(8,128)(2,1)}, u32[]{:S(2)}, u32[]{:S(2)}) collective-permute-start(bf16[512,2048]{1,0:T(8,128)(2,1)} %convolution_convert_fusion.9), channel_id=1, source_target_pairs={{0,1},{1,0},{2,3},{3,2},{4,5},{5,4},{6,7},{7,6},{8,9},{9,8},{10,11... | collective-permute-start | bytes 6291464 | tf_op jit(solution)/shard_map/ppermute | solution.py:175
  129.9 385.8 %reduce-scatter.6.cloned.1.call-start = ((), (), s32[]{:S(2)}) async-start(), calls=%async_computation.8 | async-start | bytes 5242880 | tf_op jit(solution)/shard_map/reduce_scatter | solution.py:288
  169.4 70.3 %collective-permute-start.11 = (bf16[1024,2048]{1,0:T(8,128)(2,1)S(1)}, bf16[1024,2048]{1,0:T(8,128)(2,1)S(1)}, u32[]{:S(2)}, u32[]{:S(2)}) collective-permute-start(bf16[1024,2048]{1,0:T(8,128)(2,1)S(1)} %pad_maximum_fusion.5), channel_id=1, source_target_pairs={{0,8},{8,0},{16,24},{24,16},{1,9},{9,1},{17,25},{25,17},{2,10},{10... | collective-permute-start | bytes 12582920 | tf_op jit(solution)/shard_map/ppermute | solution.py:175
  181.3 47.0 %collective-permute-start.2 = (bf16[512,2048]{1,0:T(8,128)(2,1)S(1)}, bf16[512,2048]{1,0:T(8,128)(2,1)S(1)}, u32[]{:S(2)}, u32[]{:S(2)}) collective-permute-start(bf16[512,2048]{1,0:T(8,128)(2,1)S(1)} %multiply_convert_fusion), channel_id=1, source_target_pairs={{0,1},{1,0},{2,3},{3,2},{4,5},{5,4},{6,7},{7,6},{8,9},{9,8},{10,11... | collective-permute-start | bytes 6291464 | tf_op jit(solution)/shard_map/ppermute | solution.py:175
  402.7 46.6 %collective-permute-start.14 = (bf16[1024,2048]{1,0:T(8,128)(2,1)}, bf16[1024,2048]{1,0:T(8,128)(2,1)}, u32[]{:S(2)}, u32[]{:S(2)}) collective-permute-start(bf16[1024,2048]{1,0:T(8,128)(2,1)} %add_convert_fusion.3), channel_id=1, source_target_pairs={{0,8},{8,0},{16,24},{24,16},{1,9},{9,1},{17,25},{25,17},{2,10},{10... | collective-permute-start | bytes 12582920 | tf_op jit(solution)/shard_map/ppermute | solution.py:175
  402.7 174.1 %reduce-scatter.8.cloned.1.call-start = ((), (), s32[]{:S(2)}) async-start(), calls=%async_computation.9 | async-start | bytes 5242880 | tf_op jit(solution)/shard_map/reduce_scatter | solution.py:288
  455.4 47.6 %collective-permute-start.18 = (bf16[512,2048]{1,0:T(8,128)(2,1)}, bf16[512,2048]{1,0:T(8,128)(2,1)}, u32[]{:S(2)}, u32[]{:S(2)}) collective-permute-start(bf16[512,2048]{1,0:T(8,128)(2,1)} %add_convert_fusion.13), channel_id=1, source_target_pairs={{0,16},{8,24},{16,0},{24,8},{1,17},{9,25},{17,1},{25,9},{2,18},{10... | collective-permute-start | bytes 6291464 | tf_op jit(solution)/shard_map/ppermute | solution.py:175
  457.0 47.3 %collective-permute-start.17 = (bf16[512,2048]{1,0:T(8,128)(2,1)}, bf16[512,2048]{1,0:T(8,128)(2,1)}, u32[]{:S(2)}, u32[]{:S(2)}) collective-permute-start(bf16[512,2048]{1,0:T(8,128)(2,1)} %add_convert_fusion.12), channel_id=1, source_target_pairs={{0,1},{1,0},{2,3},{3,2},{4,5},{5,4},{6,7},{7,6},{8,9},{9,8},{10,11... | collective-permute-start | bytes 6291464 | tf_op jit(solution)/shard_map/ppermute | solution.py:175
  485.5 165.8 %reduce-scatter.10.cloned.1.call-start = ((), (), s32[]{:S(2)}) async-start(), calls=%async_computation.10 | async-start | bytes 5242880 | tf_op jit(solution)/shard_map/reduce_scatter | solution.py:288
  524.5 47.8 %collective-permute-start.19 = (bf16[512,2048]{1,0:T(8,128)(2,1)}, bf16[512,2048]{1,0:T(8,128)(2,1)}, u32[]{:S(2)}, u32[]{:S(2)}) collective-permute-start(bf16[512,2048]{1,0:T(8,128)(2,1)} %fusion.71), channel_id=1, source_target_pairs={{0,1},{1,0},{2,3},{3,2},{4,5},{5,4},{6,7},{7,6},{8,9},{9,8},{10,11... | collective-permute-start | bytes 6291464 | tf_op jit(solution)/shard_map/ppermute | solution.py:175
  525.2 51.6 %collective-permute-start.20 = (bf16[256,2048]{1,0:T(8,128)(2,1)S(1)}, bf16[256,2048]{1,0:T(8,128)(2,1)}, u32[]{:S(2)}, u32[]{:S(2)}) collective-permute-start(bf16[256,2048]{1,0:T(8,128)(2,1)S(1)} %copy-done.55), channel_id=1, source_target_pairs={{0,16},{8,24},{16,0},{24,8},{1,17},{9,25},{17,1},{25,9},{2,18},{10... | collective-permute-start | bytes 3145736 | tf_op jit(solution)/shard_map/ppermute | solution.py:175
  559.6 130.6 %reduce-scatter.12.cloned.1.call-start = ((), (), s32[]{:S(2)}) async-start(), calls=%async_computation.11 | async-start | bytes 1310720 | tf_op jit(solution)/shard_map/reduce_scatter | solution.py:288
  584.8 84.5 %collective-permute-start.29 = (bf16[2048,256]{0,1:T(8,128)(2,1)S(1)}, bf16[2048,256]{0,1:T(8,128)(2,1)}, u32[]{:S(2)}, u32[]{:S(2)}) collective-permute-start(bf16[2048,256]{0,1:T(8,128)(2,1)S(1)} %bitcast.63), channel_id=1, source_target_pairs={{0,16},{8,24},{16,0},{24,8},{1,17},{9,25},{17,1},{25,9},{2,18},{10... | collective-permute-start | bytes 3145736 | tf_op jit(solution)/shard_map/ppermute | solution.py:175
  595.7 50.9 %collective-permute-start.55 = (bf16[512,2048]{1,0:T(8,128)(2,1)}, bf16[512,2048]{1,0:T(8,128)(2,1)}, u32[]{:S(2)}, u32[]{:S(2)}) collective-permute-start(bf16[512,2048]{1,0:T(8,128)(2,1)} %pad_maximum_fusion.15), channel_id=1, source_target_pairs={{0,8},{8,0},{16,24},{24,16},{1,9},{9,1},{17,25},{25,17},{2,10},{10... | collective-permute-start | bytes 6291464 | tf_op jit(solution)/shard_map/ppermute | solution.py:175
  651.3 80.6 %all-gather.12.cloned.1.call-start = ((), (), s32[]{:S(2)}) async-start(), calls=%async_computation.12 | async-start | bytes 1310720 | tf_op jit(solution)/shard_map/all_gather | solution.py:284
  662.8 48.4 %collective-permute-start.32 = (bf16[512,2048]{1,0:T(8,128)(2,1)}, bf16[512,2048]{1,0:T(8,128)(2,1)}, u32[]{:S(2)}, u32[]{:S(2)}) collective-permute-start(bf16[512,2048]{1,0:T(8,128)(2,1)} %convolution_convert_fusion.10), channel_id=1, source_target_pairs={{0,1},{1,0},{2,3},{3,2},{4,5},{5,4},{6,7},{7,6},{8,9},{9,8},{10,11... | collective-permute-start | bytes 6291464 | tf_op jit(solution)/shard_map/ppermute | solution.py:175
  675.5 59.9 %collective-permute-start.35 = (bf16[1024,2048]{1,0:T(8,128)(2,1)}, bf16[1024,2048]{1,0:T(8,128)(2,1)}, u32[]{:S(2)}, u32[]{:S(2)}) collective-permute-start(bf16[1024,2048]{1,0:T(8,128)(2,1)} %convolution_convert_fusion.5), channel_id=1, source_target_pairs={{0,8},{8,0},{16,24},{24,16},{1,9},{9,1},{17,25},{25,17},{2,10},{10... | collective-permute-start | bytes 12582920 | tf_op jit(solution)/shard_map/ppermute | solution.py:175
  690.1 68.1 %collective-permute-start.37 = (bf16[1024,2048]{1,0:T(8,128)(2,1)}, bf16[1024,2048]{1,0:T(8,128)(2,1)}, u32[]{:S(2)}, u32[]{:S(2)}) collective-permute-start(bf16[1024,2048]{1,0:T(8,128)(2,1)} %convolution_convert_fusion.4), channel_id=1, source_target_pairs={{0,8},{8,0},{16,24},{24,16},{1,9},{9,1},{17,25},{25,17},{2,10},{10... | collective-permute-start | bytes 12582920 | tf_op jit(solution)/shard_map/ppermute | solution.py:175
  690.2 107.7 %reduce-scatter.14.cloned.1.call-start = ((), (), s32[]{:S(2)}) async-start(), calls=%async_computation.13 | async-start | bytes 2621440 | tf_op jit(solution)/shard_map/reduce_scatter | solution.py:288
  735.0 123.1 %all-gather.14.cloned.1.call-start = ((), (), s32[]{:S(2)}) async-start(), calls=%async_computation.14 | async-start | bytes 2621440 | tf_op jit(solution)/shard_map/all_gather | solution.py:284
  744.5 48.6 %collective-permute-start.36 = (bf16[512,2048]{1,0:T(8,128)(2,1)S(1)}, bf16[512,2048]{1,0:T(8,128)(2,1)S(1)}, u32[]{:S(2)}, u32[]{:S(2)}) collective-permute-start(bf16[512,2048]{1,0:T(8,128)(2,1)S(1)} %slice.159), channel_id=1, source_target_pairs={{0,1},{1,0},{2,3},{3,2},{4,5},{5,4},{6,7},{7,6},{8,9},{9,8},{10,11... | collective-permute-start | bytes 6291464 | tf_op jit(solution)/shard_map/ppermute | solution.py:175
  763.6 73.0 %collective-permute-start.38 = (bf16[512,2048]{1,0:T(8,128)(2,1)}, bf16[512,2048]{1,0:T(8,128)(2,1)}, u32[]{:S(2)}, u32[]{:S(2)}) collective-permute-start(bf16[512,2048]{1,0:T(8,128)(2,1)} %add_convert_fusion.7), channel_id=1, source_target_pairs={{0,1},{1,0},{2,3},{3,2},{4,5},{5,4},{6,7},{7,6},{8,9},{9,8},{10,11... | collective-permute-start | bytes 6291464 | tf_op jit(solution)/shard_map/ppermute | solution.py:175
  802.7 59.4 %collective-permute-start.51 = (bf16[512,2048]{1,0:T(8,128)(2,1)}, bf16[512,2048]{1,0:T(8,128)(2,1)}, u32[]{:S(2)}, u32[]{:S(2)}) collective-permute-start(bf16[512,2048]{1,0:T(8,128)(2,1)} %pad_maximum_fusion.12), channel_id=1, source_target_pairs={{0,8},{8,0},{16,24},{24,16},{1,9},{9,1},{17,25},{25,17},{2,10},{10... | collective-permute-start | bytes 6291464 | tf_op jit(solution)/shard_map/ppermute | solution.py:175
  805.4 61.9 %collective-permute-start.54 = (bf16[2048,512]{0,1:T(8,128)(2,1)}, bf16[2048,512]{0,1:T(8,128)(2,1)}, u32[]{:S(2)}, u32[]{:S(2)}) collective-permute-start(bf16[2048,512]{0,1:T(8,128)(2,1)} %pad_maximum_fusion.14), channel_id=1, source_target_pairs={{0,8},{8,0},{16,24},{24,16},{1,9},{9,1},{17,25},{25,17},{2,10},{10... | collective-permute-start | bytes 6291464 | tf_op jit(solution)/shard_map/ppermute | solution.py:175
  (139 other events, 1993.7 us)
Sparse Core Ops, SparseCore 0:
  10.2 83.4 all-gather.5
  95.2 79.0 all-gather.7
  175.8 78.7 all-gather.9
  402.9 77.2 reduce-scatter.5
  485.6 77.5 reduce-scatter.7
  565.9 77.2 reduce-scatter.9
  651.4 28.0 reduce-scatter.11
  690.3 29.2 all-gather.11
  735.1 44.4 reduce-scatter.13
  798.0 46.2 all-gather.13

commit v9 on v8

--- a/solution.py
+++ b/solution.py
@@ -500,17 +500,26 @@
         across = swap(out_far[mid_row:], "col", 1)
         out_far = low(wide(out_far[:mid_row]) + wide(across))
     both_part, up_over_y, out_over_y, out_far = tie(both_part, up_over_y, out_over_y, out_far)
-    from_y = wide(swap(out_far, "grp", 2))
+    from_y = swap(out_far, "grp", 2)
+    gate_grad = spread_quarters(gate_part, gate_over_y, core, ypos, 1)
+    up_grad = spread_quarters(up_part, up_over_y, core, ypos, 1)
+    out_wgrad = spread_quarters(out_part, out_over_y, core, ypos, 0)
+    both_part = row_gather(both_part)
     if in_pairs:
-        from_x = wide(swap(low(out_near(mid_row, packed_length)), "col", 1))
-        layer_rows = out_near(0, mid_row) + from_x + from_y
+        both_part, from_x = tie(
+            both_part, swap(low(out_near(mid_row, packed_length)), "col", 1)
+        )
+    both_part, from_y, gate_grad, up_grad, out_wgrad = tie(
+        both_part, from_y, gate_grad, up_grad, out_wgrad
+    )
+    if in_pairs:
+        layer_rows = out_near(0, mid_row) + wide(from_x) + wide(from_y)
     else:
-        layer_rows = col_scatter(lambda i: out_near(0, packed_length) + from_y)
+        layer_rows = col_scatter(lambda i: out_near(0, packed_length) + wide(from_y))
     layer_out = hidden_res + layer_rows
     res_from_in, _ = first_back(in_grad)
     input_grad = res_grad + res_from_in
 
-    both_part, layer_out, input_grad = tie(row_gather(both_part), layer_out, input_grad)
     size = both_part.shape[0]
     project_rows = lax.dynamic_slice_in_dim(project_in, (2 * core + ypos) * size, size, 0)
     term = jnp.sum(wide(both_part) * wide(project_rows), axis=1)
@@ -519,16 +528,10 @@
     first_gain_grad = ordered(core, term, swap(term, "grp", 1), 0) / first_gain
     query_part, pair_part = both_part[:, :query_cols], both_part[:, query_cols:]
     down_grad = spread_quarters(down_part, down_over_y, core, ypos, 0)
-    gate_grad = spread_quarters(gate_part, gate_over_y, core, ypos, 1)
-    up_grad = spread_quarters(up_part, up_over_y, core, ypos, 1)
-    out_wgrad = spread_quarters(out_part, out_over_y, core, ypos, 0)
     query_wgrad = spread_quarters(query_part, swap(query_part, "grp", 2), core, ypos, 0)
     if in_pairs:
-        over_x, over_y = swap(pair_part, "col", 1), swap(pair_part, "grp", 2)
-        half = pair_part.shape[0] // 2
-        across = jnp.concatenate(
-            [swap(over_x[:half], "grp", 2), swap(over_y[half:], "col", 1)], axis=0
-        )
+        over_x, over_y = tie(swap(pair_part, "col", 1), swap(pair_part, "grp", 2))
+        across = swap(over_y, "col", 1)
         pair_part = ordered(ypos, pair_part, over_y, 0)
         theirs = ordered(ypos, over_x, across, 0)
         key_part = ordered(col, pair_part[:, :key_cols], theirs[:, :key_cols], 1)

time: 971 us -> 1020 us (1.050)
  waiting for transfers between devices: 265 us -> 324 us
  local copies, waits for them, and re-layouts: 93.2 us -> 82.8 us
    ppermute x56 -> x55, waiting for transfers between devices: 264 us -> 319 us  [swap(): return lax.ppermute(value, axis, [(i, i ^ bit) for i in range(count)])]
    unnamed x223 -> x218, local copies, waits for them, and re-layouts: 56.8 us -> 52.4 us
    ppermute x56 -> x55, starting transfers between devices: 46.2 us -> 43.1 us  [swap(): return lax.ppermute(value, axis, [(i, i ^ bit) for i in range(count)])]
  transfers between devices with their start and end apart: 66 -> 65, of which waited for: 22 -> 25; matrix products, arithmetic and copies ran while one was open for 51% -> 47% of each run, Pallas kernels for 3% -> 3%
where the time goes in v9:
time: 1020 us; the launch traced here: 1010 us
  matrix products  353 us (35%)
  waiting for transfers between devices  324 us (32%)
  other arithmetic  153 us (15%)
  local copies, waits for them, and re-layouts  82.8 us (8%)
  starting transfers between devices  44.4 us (4%)
  Pallas kernels  32.4 us (3%)
  between operations  16 us (2%)
    ppermute x55, waiting for transfers between devices, swap(): return lax.ppermute(value, axis, [(i, i ^ bit) for i in range(count)])  319 us
    dot_general x18, matrix products, dot32(): return jnp.dot(left, right, preferred_element_type=jnp.float32)  129 us
    dot_general x9, matrix products, dot_nt(): jnp.einsum('td,fd->tf', left, right, preferred_element_type=jnp.float32)  120 us
    dot_general x9, matrix products, dot_tn(): jnp.einsum('td,tf->df', left, right, preferred_element_type=jnp.float32)  104 us
    unnamed x218, local copies, waits for them, and re-layouts  52.4 us
    ppermute x55, starting transfers between devices, swap(): return lax.ppermute(value, axis, [(i, i ^ bit) for i in range(count)])  43.1 us
    select_n x17, other arithmetic, ordered(): jnp.where(keep, mine, theirs)  32.9 us
    pallas_call x2, Pallas kernels, attention_call(): pl.pallas_call(kernel, grid_spec=pltpu.PrefetchScalarGridSpec(num_scalar_...  32.4 us
  transfers between devices with their start and end apart: 65, of which 25 were waited for; matrix products, arithmetic and copies ran while one was open for 47% of the time, Pallas kernels for 3%

profile of v9, /device:TPU:0, one launch (start us, length us, event | category | flops | bytes accessed | tf_op | source)
XLA Modules:
  0.0 1005.2 jit_solution(14127148497084652460)
XLA Ops:
  24.7 37.0 %collective-permute-done = bf16[512,2048]{1,0:T(8,128)(2,1)} collective-permute-done((bf16[512,2048]{1,0:T(8,128)(2,1)}, bf16[512,2048]{1,0:T(8,128)(2,1)}, u32[]{:S(2)}, u32[]{:S(2)}) %collective-permute-start) | collective-permute-done | bytes 2097184 | tf_op jit(solution)/shard_map/ppermute | solution.py:175
  73.4 14.7 %fusion.73.q_ref.k_ref.v_ref = f32[1024,2048]{1,0:T(8,128)} fusion(bf16[1024,2048]{1,0:T(8,128)(2,1)} %pad_maximum_fusion.2, bf16[2048,512]{1,0:T(8,128)(2,1)} %get-tuple-element.215, bf16[2048,512]{1,0:T(8,128)(2,1)} %get-tuple-element.216, bf16[2048,1024]{1,0:T(8,128)(2,1)} %param.18), kind=kOutput, calls=%fused_computation.220 | convolution fusion | flops 8615100416 | bytes 20971520 | tf_op jit(solution)/shard_map/dot_general | solution.py:195
  88.1 12.1 %attend.1 = (bf16[1024,1024]{1,0:T(8,128)(2,1)}, bf16[1024,1024]{1,0:T(8,128)(2,1)}, bf16[1024,512]{1,0:T(8,128)(2,1)}, bf16[1024,512]{1,0:T(8,128)(2,1)}) custom-call(s32[1]{0:T(128)} %bitcast.first_ref, f32[1024,2048]{1,0:T(8,128)} %fusion.73.q_ref.k_ref.v_ref, f32[1024,2048]{1,0:T(8,128)} %fusion.73.q_ref.k_ref.v_ref, ...), custom_call_target="tpu_custom_call" | custom-call | flops 3221225472 | bytes 16106127 | tf_op jit(solution)/shard_map/attend/pallas_call | solution.py:153
  100.2 13.5 %collective-permute-done.4 = bf16[512,2048]{1,0:T(8,128)(2,1)} collective-permute-done((bf16[512,2048]{1,0:T(8,128)(2,1)}, bf16[512,2048]{1,0:T(8,128)(2,1)}, u32[]{:S(2)}, u32[]{:S(2)}) %collective-permute-start.4) | collective-permute-done | bytes 2097184 | tf_op jit(solution)/shard_map/ppermute | solution.py:175
  133.9 32.9 %collective-permute-done.10 = bf16[512,2048]{1,0:T(8,128)(2,1)} collective-permute-done((bf16[512,2048]{1,0:T(8,128)(2,1)}, bf16[512,2048]{1,0:T(8,128)(2,1)}, u32[]{:S(2)}, u32[]{:S(2)}) %collective-permute-start.10) | collective-permute-done | bytes 2097184 | tf_op jit(solution)/shard_map/ppermute | solution.py:175
  186.0 13.7 %convolution_convert_fusion.3 = bf16[2048,1024]{1,0:T(8,128)(2,1)} fusion(bf16[2048,2048]{1,0:T(8,128)(2,1)S(1)} %constant_dynamic-update-slice_fusion, bf16[1024,2048]{1,0:T(8,128)(2,1)} %all-gather.6.cloned.1.call-done), kind=kOutput, calls=%fused_computation.85 | convolution fusion | flops 8592031744 | bytes 16777216 | tf_op jit(solution)/shard_map/td,fd->tf/dot_general | solution.py:199
  199.7 28.6 %collective-permute-done.2 = bf16[512,2048]{1,0:T(8,128)(2,1)S(1)} collective-permute-done((bf16[512,2048]{1,0:T(8,128)(2,1)S(1)}, bf16[512,2048]{1,0:T(8,128)(2,1)S(1)}, u32[]{:S(2)}, u32[]{:S(2)}) %collective-permute-start.2) | collective-permute-done | bytes 2097184 | tf_op jit(solution)/shard_map/ppermute | solution.py:175
  242.0 12.6 %convolution_convert_fusion.1 = bf16[2048,1024]{1,0:T(8,128)(2,1)} fusion(bf16[2048,2048]{1,0:T(8,128)(2,1)} %constant_dynamic-update-slice_fusion.3, bf16[1024,2048]{1,0:T(8,128)(2,1)S(1)} %copy-done.79), kind=kOutput, calls=%fused_computation.83 | convolution fusion | flops 8592031744 | bytes 16777216 | tf_op jit(solution)/shard_map/td,fd->tf/dot_general | solution.py:199
  268.7 14.7 %convolution_convert_fusion.2 = bf16[2048,1024]{1,0:T(8,128)(2,1)} fusion(bf16[1024,2048]{0,1:T(8,128)(2,1)} %all-gather.8.cloned.1.call-done, bf16[1024,2048]{1,0:T(8,128)(2,1)} %collective-permute-done.6, bf16[512,2048]{1,0:T(8,128)(2,1)} %copy-done.34, bf16[512,2048]{1,0:T(8,128)(2,1)S(1)} %multiply_convert_fusion), kind=kOutput, calls=%fused_computation.84 | convolution fusion | flops 8617197568 | bytes 16777216 | tf_op jit(solution)/shard_map/td,fd->tf/dot_general | solution.py:199
  283.4 20.8 %fusion.5 = (bf16[2048,1024]{1,0:T(8,128)(2,1)}, bf16[2048,1024]{1,0:T(8,128)(2,1)}, bf16[2048,1024]{1,0:T(8,128)(2,1)}) fusion(bf16[2048,1024]{1,0:T(8,128)(2,1)} %convolution_convert_fusion.3, bf16[2048,1024]{1,0:T(8,128)(2,1)} %convolution_convert_fusion.2, bf16[1024,2048]{0,1:T(8,128)(2,1)} %all-gather.10.cloned.1.call-done, ...), kind=kOutput, calls=%fused_computation.15 | convolution fusion | flops 8652849152 | bytes 33554432 | tf_op jit(solution)/shard_map/td,fd->tf/dot_general | solution.py:199
  309.2 13.0 %convolution_convert_fusion = bf16[2048,1024]{1,0:T(8,128)(2,1)} fusion(bf16[2048,2048]{1,0:T(8,128)(2,1)} %constant_dynamic-update-slice_fusion.6, bf16[1024,2048]{0,1:T(8,128)(2,1)S(1)} %copy-done.84), kind=kOutput, calls=%fused_computation.82 | convolution fusion | flops 8592031744 | bytes 16777216 | tf_op jit(solution)/shard_map/td,fd->tf/dot_general | solution.py:199
  322.2 20.8 %fusion.2 = (bf16[2048,1024]{1,0:T(8,128)(2,1)}, bf16[2048,1024]{1,0:T(8,128)(2,1)}, bf16[2048,1024]{1,0:T(8,128)(2,1)}) fusion(bf16[2048,1024]{1,0:T(8,128)(2,1)} %convolution_convert_fusion.1, bf16[2048,1024]{1,0:T(8,128)(2,1)} %convolution_convert_fusion, bf16[2048,2048]{1,0:T(8,128)(2,1)} %constant_dynamic-update-slice_fusion.6, ...), kind=kOutput, calls=%fused_computation.12 | convolution fusion | flops 8627683328 | bytes 33554432 | tf_op jit(solution)/shard_map/td,fd->tf/dot_general | solution.py:199
  343.0 13.2 %fusion.75 = f32[1024,2048]{1,0:T(8,128)S(1)} fusion(bf16[2048,1024]{1,0:T(8,128)(2,1)} %get-tuple-element.121, bf16[2048,2048]{1,0:T(8,128)(2,1)} %constant_dynamic-update-slice_fusion.3), kind=kOutput, calls=%fused_computation.222 | convolution fusion | flops 8589934592 | bytes 20971520 | tf_op jit(solution)/shard_map/td,tf->df/dot_general | solution.py:203
  356.3 11.1 %add_convert_fusion.6 = bf16[1024,2048]{1,0:T(8,128)(2,1)} fusion(f32[1024,2048]{1,0:T(8,128)S(1)} %fusion.75, bf16[2048,1024]{1,0:T(8,128)(2,1)S(1)} %copy-done.95, bf16[2048,2048]{1,0:T(8,128)(2,1)S(1)} %bitcast.66), kind=kOutput, calls=%fused_computation.40 | convolution fusion | flops 8594128896 | bytes 25165824 | tf_op jit(solution)/shard_map/td,tf->df/dot_general | solution.py:203
  367.4 10.9 %fusion.43 = f32[1024,2048]{1,0:T(8,128)} fusion(bf16[1024,2048]{0,1:T(8,128)(2,1)} %all-gather.8.cloned.1.call-done, bf16[2048,1024]{1,0:T(8,128)(2,1)} %get-tuple-element.98), kind=kOutput, calls=%fused_computation.121 | convolution fusion | flops 4294967296 | bytes 14680064 | tf_op jit(solution)/shard_map/dot_general | solution.py:195
  402.8 10.9 %fusion.46 = f32[1024,2048]{1,0:T(8,128)} fusion(bf16[1024,2048]{0,1:T(8,128)(2,1)} %all-gather.8.cloned.1.call-done, bf16[2048,1024]{1,0:T(8,128)(2,1)} %get-tuple-element.98), kind=kOutput, calls=%fused_computation.124 | convolution fusion | flops 4294967296 | bytes 14680064 | tf_op jit(solution)/shard_map/dot_general | solution.py:195
  427.6 19.7 %collective-permute-done.15 = bf16[256,2048]{1,0:T(8,128)(2,1)S(1)} collective-permute-done((bf16[256,2048]{1,0:T(8,128)(2,1)S(1)}, bf16[256,2048]{1,0:T(8,128)(2,1)S(1)}, u32[]{:S(2)}, u32[]{:S(2)}) %collective-permute-start.15) | collective-permute-done | bytes 1048608 | tf_op jit(solution)/shard_map/ppermute | solution.py:175
  457.3 14.0 %fusion.76 = f32[1024,2048]{1,0:T(8,128)} fusion(bf16[2048,1024]{1,0:T(8,128)(2,1)S(1)} %copy-done.100, bf16[2048,2048]{1,0:T(8,128)(2,1)} %constant_dynamic-update-slice_fusion.6), kind=kOutput, calls=%fused_computation.223 | convolution fusion | flops 8589934592 | bytes 20971520 | tf_op jit(solution)/shard_map/td,tf->df/dot_general | solution.py:203
  471.3 14.2 %add_convert_fusion.2 = bf16[1024,2048]{1,0:T(8,128)(2,1)} fusion(f32[1024,2048]{1,0:T(8,128)} %fusion.76, bf16[2048,1024]{1,0:T(8,128)(2,1)S(1)} %copy-done.94, bf16[1024,2048]{1,0:T(8,128)(2,1)} %collective-permute-done.6, bf16[512,2048]{1,0:T(8,128)(2,1)S(1)} %copy-done.35, bf16[512,2048]{1,0:T(8,128)(2,1)S(1)} %copy-done.28), kind=kOutput, calls=%fused_computation.36 | convolution fusion | flops 8619294720 | bytes 25165824 | tf_op jit(solution)/shard_map/td,tf->df/dot_general | solution.py:203
  521.8 15.1 %fusion.77 = f32[1024,2048]{1,0:T(8,128)} fusion(bf16[2048,1024]{1,0:T(8,128)(2,1)} %get-tuple-element.114, bf16[2048,2048]{1,0:T(8,128)(2,1)} %constant_dynamic-update-slice_fusion.6), kind=kOutput, calls=%fused_computation.224 | convolution fusion | flops 8589934592 | bytes 20971520 | tf_op jit(solution)/shard_map/td,tf->df/dot_general | solution.py:203
  539.3 13.7 %add_convert_fusion.1 = bf16[1024,2048]{1,0:T(8,128)(2,1)} fusion(f32[1024,2048]{1,0:T(8,128)} %fusion.77, bf16[2048,1024]{1,0:T(8,128)(2,1)S(1)} %copy-done.92, bf16[1024,2048]{1,0:T(8,128)(2,1)} %collective-permute-done.6, bf16[512,2048]{1,0:T(8,128)(2,1)S(1)} %copy-done.36, bf16[512,2048]{1,0:T(8,128)(2,1)S(1)} %copy-done.28), kind=kOutput, calls=%fused_computation.35 | convolution fusion | flops 8619294720 | bytes 25165824 | tf_op jit(solution)/shard_map/td,tf->df/dot_general | solution.py:203
  553.3 11.5 %collective-permute-done.19 = bf16[512,2048]{1,0:T(8,128)(2,1)} collective-permute-done((bf16[512,2048]{1,0:T(8,128)(2,1)}, bf16[512,2048]{1,0:T(8,128)(2,1)}, u32[]{:S(2)}, u32[]{:S(2)}) %collective-permute-start.19) | collective-permute-done | bytes 2097184 | tf_op jit(solution)/shard_map/ppermute | solution.py:175
  579.2 9.5 convolution_convert_fusion.11.m_ref
  592.8 20.3 %attend_back.1 = (bf16[1024,1024]{1,0:T(8,128)(2,1)}, bf16[1024,512]{1,0:T(8,128)(2,1)}, bf16[1024,512]{1,0:T(8,128)(2,1)}) custom-call(s32[1]{0:T(128)} %bitcast.first_ref, bf16[1024,1024]{1,0:T(8,128)(2,1)} %get-tuple-element.78.q_ref, bf16[1024,512]{1,0:T(8,128)(2,1)} %get-tuple-element.79.k_ref, bf16[1024,512]{1,0:T(8,128)(2,1)} %get-tuple-element.80.v_ref, ...), custom_call_target="tpu_custom_call" | custom-call | flops 7516192768 | bytes 37580964 | tf_op jit(solution)/shard_map/attend_back/pallas_call | solution.py:153
  686.5 37.0 %collective-permute-done.33 = bf16[512,2048]{1,0:T(8,128)(2,1)} collective-permute-done((bf16[512,2048]{1,0:T(8,128)(2,1)}, bf16[512,2048]{1,0:T(8,128)(2,1)}, u32[]{:S(2)}, u32[]{:S(2)}) %collective-permute-start.33) | collective-permute-done | bytes 2097184 | tf_op jit(solution)/shard_map/ppermute | solution.py:175
  723.5 9.3 convert_add_fusion.1
  764.7 31.3 %collective-permute-done.37 = bf16[512,2048]{1,0:T(8,128)(2,1)S(1)} collective-permute-done((bf16[512,2048]{1,0:T(8,128)(2,1)S(1)}, bf16[512,2048]{1,0:T(8,128)(2,1)S(1)}, u32[]{:S(2)}, u32[]{:S(2)}) %collective-permute-start.37) | collective-permute-done | bytes 2097184 | tf_op jit(solution)/shard_map/ppermute | solution.py:175
  844.0 29.4 %collective-permute-done.38 = bf16[512,2048]{1,0:T(8,128)(2,1)} collective-permute-done((bf16[512,2048]{1,0:T(8,128)(2,1)S(1)}, bf16[512,2048]{1,0:T(8,128)(2,1)}, u32[]{:S(2)}, u32[]{:S(2)}) %collective-permute-start.38) | collective-permute-done | bytes 2097184 | tf_op jit(solution)/shard_map/ppermute | solution.py:175
  885.1 14.8 %collective-permute-done.48 = bf16[512,1024]{1,0:T(8,128)(2,1)S(1)} collective-permute-done((bf16[512,1024]{1,0:T(8,128)(2,1)S(1)}, bf16[512,1024]{1,0:T(8,128)(2,1)S(1)}, u32[]{:S(2)}, u32[]{:S(2)}) %collective-permute-start.48) | collective-permute-done | bytes 1048608 | tf_op jit(solution)/shard_map/ppermute | solution.py:175
  915.6 18.3 %collective-permute-done.43 = f32[8,64]{1,0:T(8,128)S(1)} collective-permute-done((f32[8,64]{1,0:T(8,128)S(1)}, f32[8,64]{1,0:T(8,128)S(1)}, u32[]{:S(2)}, u32[]{:S(2)}) %collective-permute-start.43) | collective-permute-done | bytes 2080 | tf_op jit(solution)/shard_map/ppermute | solution.py:175
  947.5 9.3 fusion.23
  966.1 9.6 copy.31
  (459 shorter events, 431.7 us)
Async XLA Ops:
  7.2 112.8 %all-gather.6.cloned.1.call-start = ((), (), s32[]{:S(2)}) async-start(), calls=%async_computation.5 | async-start | bytes 5242880 | tf_op jit(solution)/shard_map/all_gather | solution.py:284
  9.7 258.9 %all-gather.8.cloned.1.call-start = ((), (), s32[]{:S(2)}) async-start(), calls=%async_computation.6 | async-start | bytes 5242880 | tf_op jit(solution)/shard_map/all_gather | solution.py:284
  12.8 48.9 %collective-permute-start = (bf16[512,2048]{1,0:T(8,128)(2,1)}, bf16[512,2048]{1,0:T(8,128)(2,1)}, u32[]{:S(2)}, u32[]{:S(2)}) collective-permute-start(bf16[512,2048]{1,0:T(8,128)(2,1)} %fusion.26), channel_id=1, source_target_pairs={{0,1},{1,0},{2,3},{3,2},{4,5},{5,4},{6,7},{7,6},{8,9},{9,8},{10,11... | collective-permute-start | bytes 6291464 | tf_op jit(solution)/shard_map/ppermute | solution.py:175
  18.0 265.4 %all-gather.10.cloned.1.call-start = ((), (), s32[]{:S(2)}) async-start(), calls=%async_computation.7 | async-start | bytes 5242880 | tf_op jit(solution)/shard_map/all_gather | solution.py:284
  18.1 115.8 %collective-permute-start.9 = (bf16[512,2048]{1,0:T(8,128)(2,1)}, bf16[512,2048]{1,0:T(8,128)(2,1)}, u32[]{:S(2)}, u32[]{:S(2)}) collective-permute-start(bf16[512,2048]{1,0:T(8,128)(2,1)} %param.14), channel_id=1, source_target_pairs={{0,16},{8,24},{16,0},{24,8},{1,17},{9,25},{17,1},{25,9},{2,18},{10... | collective-permute-start | bytes 6291464 | tf_op jit(solution)/shard_map/ppermute | solution.py:175
  66.5 47.1 %collective-permute-start.4 = (bf16[512,2048]{1,0:T(8,128)(2,1)}, bf16[512,2048]{1,0:T(8,128)(2,1)}, u32[]{:S(2)}, u32[]{:S(2)}) collective-permute-start(bf16[512,2048]{1,0:T(8,128)(2,1)} %param.14), channel_id=1, source_target_pairs={{0,1},{1,0},{2,3},{3,2},{4,5},{5,4},{6,7},{7,6},{8,9},{9,8},{10,11... | collective-permute-start | bytes 6291464 | tf_op jit(solution)/shard_map/ppermute | solution.py:175
  118.5 64.9 %collective-permute-start.5 = (bf16[1024,2048]{1,0:T(8,128)(2,1)}, bf16[1024,2048]{1,0:T(8,128)(2,1)}, u32[]{:S(2)}, u32[]{:S(2)}) collective-permute-start(bf16[1024,2048]{1,0:T(8,128)(2,1)} %pad_maximum_fusion.3), channel_id=1, source_target_pairs={{0,8},{8,0},{16,24},{24,16},{1,9},{9,1},{17,25},{25,17},{2,10},{10... | collective-permute-start | bytes 12582920 | tf_op jit(solution)/shard_map/ppermute | solution.py:175
  118.5 48.4 %collective-permute-start.10 = (bf16[512,2048]{1,0:T(8,128)(2,1)}, bf16[512,2048]{1,0:T(8,128)(2,1)}, u32[]{:S(2)}, u32[]{:S(2)}) collective-permute-start(bf16[512,2048]{1,0:T(8,128)(2,1)} %collective-permute-done.4), channel_id=1, source_target_pairs={{0,16},{8,24},{16,0},{24,8},{1,17},{9,25},{17,1},{25,9},{2,18},{10... | collective-permute-start | bytes 6291464 | tf_op jit(solution)/shard_map/ppermute | solution.py:175
  126.2 48.1 %collective-permute-start.1 = (bf16[512,2048]{1,0:T(8,128)(2,1)}, bf16[512,2048]{1,0:T(8,128)(2,1)}, u32[]{:S(2)}, u32[]{:S(2)}) collective-permute-start(bf16[512,2048]{1,0:T(8,128)(2,1)} %convolution_convert_fusion.9), channel_id=1, source_target_pairs={{0,1},{1,0},{2,3},{3,2},{4,5},{5,4},{6,7},{7,6},{8,9},{9,8},{10,11... | collective-permute-start | bytes 6291464 | tf_op jit(solution)/shard_map/ppermute | solution.py:175
  130.0 385.4 %reduce-scatter.6.cloned.1.call-start = ((), (), s32[]{:S(2)}) async-start(), calls=%async_computation.8 | async-start | bytes 5242880 | tf_op jit(solution)/shard_map/reduce_scatter | solution.py:288
  169.4 70.3 %collective-permute-start.11 = (bf16[1024,2048]{1,0:T(8,128)(2,1)S(1)}, bf16[1024,2048]{1,0:T(8,128)(2,1)S(1)}, u32[]{:S(2)}, u32[]{:S(2)}) collective-permute-start(bf16[1024,2048]{1,0:T(8,128)(2,1)S(1)} %pad_maximum_fusion.5), channel_id=1, source_target_pairs={{0,8},{8,0},{16,24},{24,16},{1,9},{9,1},{17,25},{25,17},{2,10},{10... | collective-permute-start | bytes 12582920 | tf_op jit(solution)/shard_map/ppermute | solution.py:175
  402.7 166.3 %reduce-scatter.8.cloned.1.call-start = ((), (), s32[]{:S(2)}) async-start(), calls=%async_computation.9 | async-start | bytes 5242880 | tf_op jit(solution)/shard_map/reduce_scatter | solution.py:288
  455.2 47.6 %collective-permute-start.18 = (bf16[512,2048]{1,0:T(8,128)(2,1)}, bf16[512,2048]{1,0:T(8,128)(2,1)}, u32[]{:S(2)}, u32[]{:S(2)}) collective-permute-start(bf16[512,2048]{1,0:T(8,128)(2,1)} %add_convert_fusion.13), channel_id=1, source_target_pairs={{0,16},{8,24},{16,0},{24,8},{1,17},{9,25},{17,1},{25,9},{2,18},{10... | collective-permute-start | bytes 6291464 | tf_op jit(solution)/shard_map/ppermute | solution.py:175
  456.8 47.3 %collective-permute-start.17 = (bf16[512,2048]{1,0:T(8,128)(2,1)}, bf16[512,2048]{1,0:T(8,128)(2,1)}, u32[]{:S(2)}, u32[]{:S(2)}) collective-permute-start(bf16[512,2048]{1,0:T(8,128)(2,1)} %add_convert_fusion.12), channel_id=1, source_target_pairs={{0,1},{1,0},{2,3},{3,2},{4,5},{5,4},{6,7},{7,6},{8,9},{9,8},{10,11... | collective-permute-start | bytes 6291464 | tf_op jit(solution)/shard_map/ppermute | solution.py:175
  485.5 157.7 %reduce-scatter.10.cloned.1.call-start = ((), (), s32[]{:S(2)}) async-start(), calls=%async_computation.10 | async-start | bytes 5242880 | tf_op jit(solution)/shard_map/reduce_scatter | solution.py:288
  517.1 47.7 %collective-permute-start.19 = (bf16[512,2048]{1,0:T(8,128)(2,1)}, bf16[512,2048]{1,0:T(8,128)(2,1)}, u32[]{:S(2)}, u32[]{:S(2)}) collective-permute-start(bf16[512,2048]{1,0:T(8,128)(2,1)} %fusion.71), channel_id=1, source_target_pairs={{0,1},{1,0},{2,3},{3,2},{4,5},{5,4},{6,7},{7,6},{8,9},{9,8},{10,11... | collective-permute-start | bytes 6291464 | tf_op jit(solution)/shard_map/ppermute | solution.py:175
  517.7 51.3 %collective-permute-start.20 = (bf16[256,2048]{1,0:T(8,128)(2,1)}, bf16[256,2048]{1,0:T(8,128)(2,1)S(1)}, u32[]{:S(2)}, u32[]{:S(2)}) collective-permute-start(bf16[256,2048]{1,0:T(8,128)(2,1)} %reduce-scatter.6.cloned.1.call-done), channel_id=1, source_target_pairs={{0,16},{8,24},{16,0},{24,8},{1,17},{9,25},{17,1},{25,9},{2,18},{10... | collective-permute-start | bytes 3145736 | tf_op jit(solution)/shard_map/ppermute | solution.py:175
  553.0 133.4 %reduce-scatter.12.cloned.1.call-start = ((), (), s32[]{:S(2)}) async-start(), calls=%async_computation.11 | async-start | bytes 1310720 | tf_op jit(solution)/shard_map/reduce_scatter | solution.py:288
  643.3 93.8 %all-gather.12.cloned.1.call-start = ((), (), s32[]{:S(2)}) async-start(), calls=%async_computation.12 | async-start | bytes 1310720 | tf_op jit(solution)/shard_map/all_gather | solution.py:284
  669.4 70.5 %collective-permute-start.36 = (bf16[1024,2048]{1,0:T(8,128)(2,1)}, bf16[1024,2048]{1,0:T(8,128)(2,1)}, u32[]{:S(2)}, u32[]{:S(2)}) collective-permute-start(bf16[1024,2048]{1,0:T(8,128)(2,1)} %convolution_convert_fusion.4), channel_id=1, source_target_pairs={{0,8},{8,0},{16,24},{24,16},{1,9},{9,1},{17,25},{25,17},{2,10},{10... | collective-permute-start | bytes 12582920 | tf_op jit(solution)/shard_map/ppermute | solution.py:175
  675.2 48.3 %collective-permute-start.33 = (bf16[512,2048]{1,0:T(8,128)(2,1)}, bf16[512,2048]{1,0:T(8,128)(2,1)}, u32[]{:S(2)}, u32[]{:S(2)}) collective-permute-start(bf16[512,2048]{1,0:T(8,128)(2,1)} %convolution_convert_fusion.10), channel_id=1, source_target_pairs={{0,1},{1,0},{2,3},{3,2},{4,5},{5,4},{6,7},{7,6},{8,9},{9,8},{10,11... | collective-permute-start | bytes 6291464 | tf_op jit(solution)/shard_map/ppermute | solution.py:175
  683.3 49.5 %collective-permute-start.31 = (bf16[512,1024]{1,0:T(8,128)(2,1)S(1)}, bf16[512,1024]{1,0:T(8,128)(2,1)}, u32[]{:S(2)}, u32[]{:S(2)}) collective-permute-start(bf16[512,1024]{1,0:T(8,128)(2,1)S(1)} %constant_dynamic-slice_fusion.1), channel_id=1, source_target_pairs={{0,16},{8,24},{16,0},{24,8},{1,17},{9,25},{17,1},{25,9},{2,18},{10... | collective-permute-start | bytes 3145736 | tf_op jit(solution)/shard_map/ppermute | solution.py:175
  685.1 49.4 %collective-permute-start.32 = (bf16[512,1024]{1,0:T(8,128)(2,1)}, bf16[512,1024]{1,0:T(8,128)(2,1)}, u32[]{:S(2)}, u32[]{:S(2)}) collective-permute-start(bf16[512,1024]{1,0:T(8,128)(2,1)} %constant_dynamic-slice_fusion), channel_id=1, source_target_pairs={{0,16},{8,24},{16,0},{24,8},{1,17},{9,25},{17,1},{25,9},{2,18},{10... | collective-permute-start | bytes 3145736 | tf_op jit(solution)/shard_map/ppermute | solution.py:175
  686.5 122.2 %reduce-scatter.14.cloned.1.call-start = ((), (), s32[]{:S(2)}) async-start(), calls=%async_computation.13 | async-start | bytes 2621440 | tf_op jit(solution)/shard_map/reduce_scatter | solution.py:288
  739.9 133.6 %all-gather.14.cloned.1.call-start = ((), (), s32[]{:S(2)}) async-start(), calls=%async_computation.14 | async-start | bytes 2621440 | tf_op jit(solution)/shard_map/all_gather | solution.py:284
  748.8 47.2 %collective-permute-start.37 = (bf16[512,2048]{1,0:T(8,128)(2,1)S(1)}, bf16[512,2048]{1,0:T(8,128)(2,1)S(1)}, u32[]{:S(2)}, u32[]{:S(2)}) collective-permute-start(bf16[512,2048]{1,0:T(8,128)(2,1)S(1)} %slice.152), channel_id=1, source_target_pairs={{0,1},{1,0},{2,3},{3,2},{4,5},{5,4},{6,7},{7,6},{8,9},{9,8},{10,11... | collective-permute-start | bytes 6291464 | tf_op jit(solution)/shard_map/ppermute | solution.py:175
  757.1 63.5 %collective-permute-start.30 = (bf16[1024,2048]{1,0:T(8,128)(2,1)}, bf16[1024,2048]{1,0:T(8,128)(2,1)}, u32[]{:S(2)}, u32[]{:S(2)}) collective-permute-start(bf16[1024,2048]{1,0:T(8,128)(2,1)} %convolution_convert_fusion.5), channel_id=1, source_target_pairs={{0,8},{8,0},{16,24},{24,16},{1,9},{9,1},{17,25},{25,17},{2,10},{10... | collective-permute-start | bytes 12582920 | tf_op jit(solution)/shard_map/ppermute | solution.py:175
  760.4 52.7 %collective-permute-start.40 = (bf16[2048,512]{0,1:T(8,128)(2,1)}, bf16[2048,512]{0,1:T(8,128)(2,1)}, u32[]{:S(2)}, u32[]{:S(2)}) collective-permute-start(bf16[2048,512]{0,1:T(8,128)(2,1)} %pad_maximum_fusion.9), channel_id=1, source_target_pairs={{0,8},{8,0},{16,24},{24,16},{1,9},{9,1},{17,25},{25,17},{2,10},{10... | collective-permute-start | bytes 6291464 | tf_op jit(solution)/shard_map/ppermute | solution.py:175
  796.0 81.3 %collective-permute-start.53 = (f32[8,256]{1,0:T(8,128)S(1)}, f32[8,256]{1,0:T(8,128)S(1)}, u32[]{:S(2)}, u32[]{:S(2)}) collective-permute-start(f32[8,256]{1,0:T(8,128)S(1)} %add.239), channel_id=1, source_target_pairs={{0,1},{1,0},{2,3},{3,2},{4,5},{5,4},{6,7},{7,6},{8,9},{9,8},{10,11... | collective-permute-start | bytes 24584 | tf_op jit(solution)/shard_map/ppermute | solution.py:175
  825.2 48.2 %collective-permute-start.38 = (bf16[512,2048]{1,0:T(8,128)(2,1)S(1)}, bf16[512,2048]{1,0:T(8,128)(2,1)}, u32[]{:S(2)}, u32[]{:S(2)}) collective-permute-start(bf16[512,2048]{1,0:T(8,128)(2,1)S(1)} %add_convert_fusion.7), channel_id=1, source_target_pairs={{0,1},{1,0},{2,3},{3,2},{4,5},{5,4},{6,7},{7,6},{8,9},{9,8},{10,11... | collective-permute-start | bytes 6291464 | tf_op jit(solution)/shard_map/ppermute | solution.py:175
  826.0 48.1 %collective-permute-start.39 = (bf16[512,2048]{1,0:T(8,128)(2,1)}, bf16[512,2048]{1,0:T(8,128)(2,1)}, u32[]{:S(2)}, u32[]{:S(2)}) collective-permute-start(bf16[512,2048]{1,0:T(8,128)(2,1)} %add_convert_fusion.8), channel_id=1, source_target_pairs={{0,16},{8,24},{16,0},{24,8},{1,17},{9,25},{17,1},{25,9},{2,18},{10... | collective-permute-start | bytes 6291464 | tf_op jit(solution)/shard_map/ppermute | solution.py:175
  831.0 47.0 %collective-permute-start.54 = (bf16[512,2048]{1,0:T(8,128)(2,1)}, bf16[512,2048]{1,0:T(8,128)(2,1)}, u32[]{:S(2)}, u32[]{:S(2)}) collective-permute-start(bf16[512,2048]{1,0:T(8,128)(2,1)} %pad_maximum_fusion.15), channel_id=1, source_target_pairs={{0,8},{8,0},{16,24},{24,16},{1,9},{9,1},{17,25},{25,17},{2,10},{10... | collective-permute-start | bytes 6291464 | tf_op jit(solution)/shard_map/ppermute | solution.py:175
  (136 other events, 1911.4 us)
Sparse Core Ops, SparseCore 0:
  10.2 83.4 all-gather.5
  95.2 79.0 all-gather.7
  175.8 78.7 all-gather.9
  402.8 77.2 reduce-scatter.5
  485.7 77.4 reduce-scatter.7
  565.9 77.2 reduce-scatter.9
  645.5 27.7 reduce-scatter.11
  686.6 28.0 all-gather.11
  740.0 43.1 reduce-scatter.13
  818.0 45.3 all-gather.13

commit v10 on v8

--- a/solution.py
+++ b/solution.py
@@ -524,11 +524,8 @@
     out_wgrad = spread_quarters(out_part, out_over_y, core, ypos, 0)
     query_wgrad = spread_quarters(query_part, swap(query_part, "grp", 2), core, ypos, 0)
     if in_pairs:
-        over_x, over_y = swap(pair_part, "col", 1), swap(pair_part, "grp", 2)
-        half = pair_part.shape[0] // 2
-        across = jnp.concatenate(
-            [swap(over_x[:half], "grp", 2), swap(over_y[half:], "col", 1)], axis=0
-        )
+        over_x, over_y = tie(swap(pair_part, "col", 1), swap(pair_part, "grp", 2))
+        across = swap(over_y, "col", 1)
         pair_part = ordered(ypos, pair_part, over_y, 0)
         theirs = ordered(ypos, over_x, across, 0)
         key_part = ordered(col, pair_part[:, :key_cols], theirs[:, :key_cols], 1)

time: 971 us -> 985 us (1.014)
  waiting for transfers between devices: 265 us -> 286 us
    ppermute x56 -> x55, waiting for transfers between devices: 264 us -> 286 us  [swap(): return lax.ppermute(value, axis, [(i, i ^ bit) for i in range(count)])]
    unnamed x223 -> x224, local copies, waits for them, and re-layouts: 56.8 us -> 53.4 us
    ppermute x56 -> x55, starting transfers between devices: 46.2 us -> 43.8 us  [swap(): return lax.ppermute(value, axis, [(i, i ^ bit) for i in range(count)])]
  transfers between devices with their start and end apart: 66 -> 65, of which waited for: 22 -> 24; matrix products, arithmetic and copies ran while one was open for 51% -> 50% of each run, Pallas kernels for 3% -> 3%
where the time goes in v10:
time: 985 us; the launch traced here: 974 us
  matrix products  346 us (35%)
  waiting for transfers between devices  286 us (29%)
  other arithmetic  161 us (16%)
  local copies, waits for them, and re-layouts  88.1 us (9%)
  starting transfers between devices  45.2 us (5%)
  Pallas kernels  32 us (3%)
  between operations  15.8 us (2%)
    ppermute x55, waiting for transfers between devices, swap(): return lax.ppermute(value, axis, [(i, i ^ bit) for i in range(count)])  286 us
    dot_general x18, matrix products, dot32(): return jnp.dot(left, right, preferred_element_type=jnp.float32)  126 us
    dot_general x9, matrix products, dot_nt(): jnp.einsum('td,fd->tf', left, right, preferred_element_type=jnp.float32)  117 us
    dot_general x9, matrix products, dot_tn(): jnp.einsum('td,tf->df', left, right, preferred_element_type=jnp.float32)  103 us
    unnamed x224, local copies, waits for them, and re-layouts  53.4 us
    ppermute x55, starting transfers between devices, swap(): return lax.ppermute(value, axis, [(i, i ^ bit) for i in range(count)])  43.8 us
    select_n x17, other arithmetic, ordered(): jnp.where(keep, mine, theirs)  35.3 us
    convert_element_type x7, other arithmetic, wide(): return value.astype(jnp.float32)  35.2 us
  transfers between devices with their start and end apart: 65, of which 24 were waited for; matrix products, arithmetic and copies ran while one was open for 50% of the time, Pallas kernels for 3%

profile of v10, /device:TPU:0, one launch (start us, length us, event | category | flops | bytes accessed | tf_op | source)
XLA Modules:
  0.0 974.3 jit_solution(7688460081037966184)
XLA Ops:
  24.6 37.0 %collective-permute-done = bf16[512,2048]{1,0:T(8,128)(2,1)} collective-permute-done((bf16[512,2048]{1,0:T(8,128)(2,1)}, bf16[512,2048]{1,0:T(8,128)(2,1)}, u32[]{:S(2)}, u32[]{:S(2)}) %collective-permute-start) | collective-permute-done | bytes 2097184 | tf_op jit(solution)/shard_map/ppermute | solution.py:175
  73.4 14.7 %fusion.73.q_ref.k_ref.v_ref = f32[1024,2048]{1,0:T(8,128)} fusion(bf16[1024,2048]{1,0:T(8,128)(2,1)} %pad_maximum_fusion.2, bf16[2048,512]{1,0:T(8,128)(2,1)} %get-tuple-element.207, bf16[2048,512]{1,0:T(8,128)(2,1)} %get-tuple-element.208, bf16[2048,1024]{1,0:T(8,128)(2,1)} %param.18), kind=kOutput, calls=%fused_computation.220 | convolution fusion | flops 8615100416 | bytes 20971520 | tf_op jit(solution)/shard_map/dot_general | solution.py:195
  88.1 12.1 %attend.1 = (bf16[1024,1024]{1,0:T(8,128)(2,1)}, bf16[1024,1024]{1,0:T(8,128)(2,1)}, bf16[1024,512]{1,0:T(8,128)(2,1)}, bf16[1024,512]{1,0:T(8,128)(2,1)}) custom-call(s32[1]{0:T(128)} %bitcast.first_ref, f32[1024,2048]{1,0:T(8,128)} %fusion.73.q_ref.k_ref.v_ref, f32[1024,2048]{1,0:T(8,128)} %fusion.73.q_ref.k_ref.v_ref, ...), custom_call_target="tpu_custom_call" | custom-call | flops 3221225472 | bytes 16106127 | tf_op jit(solution)/shard_map/attend/pallas_call | solution.py:153
  100.2 13.5 %collective-permute-done.4 = bf16[512,2048]{1,0:T(8,128)(2,1)} collective-permute-done((bf16[512,2048]{1,0:T(8,128)(2,1)}, bf16[512,2048]{1,0:T(8,128)(2,1)}, u32[]{:S(2)}, u32[]{:S(2)}) %collective-permute-start.4) | collective-permute-done | bytes 2097184 | tf_op jit(solution)/shard_map/ppermute | solution.py:175
  133.7 33.1 %collective-permute-done.10 = bf16[512,2048]{1,0:T(8,128)(2,1)} collective-permute-done((bf16[512,2048]{1,0:T(8,128)(2,1)}, bf16[512,2048]{1,0:T(8,128)(2,1)}, u32[]{:S(2)}, u32[]{:S(2)}) %collective-permute-start.10) | collective-permute-done | bytes 2097184 | tf_op jit(solution)/shard_map/ppermute | solution.py:175
  186.0 13.7 %convolution_convert_fusion.3 = bf16[2048,1024]{1,0:T(8,128)(2,1)} fusion(bf16[2048,2048]{1,0:T(8,128)(2,1)S(1)} %constant_dynamic-update-slice_fusion, bf16[1024,2048]{1,0:T(8,128)(2,1)} %all-gather.6.cloned.1.call-done), kind=kOutput, calls=%fused_computation.85 | convolution fusion | flops 8592031744 | bytes 16777216 | tf_op jit(solution)/shard_map/td,fd->tf/dot_general | solution.py:199
  199.7 28.6 %collective-permute-done.2 = bf16[512,2048]{1,0:T(8,128)(2,1)S(1)} collective-permute-done((bf16[512,2048]{1,0:T(8,128)(2,1)S(1)}, bf16[512,2048]{1,0:T(8,128)(2,1)S(1)}, u32[]{:S(2)}, u32[]{:S(2)}) %collective-permute-start.2) | collective-permute-done | bytes 2097184 | tf_op jit(solution)/shard_map/ppermute | solution.py:175
  242.0 12.6 %convolution_convert_fusion.1 = bf16[2048,1024]{1,0:T(8,128)(2,1)} fusion(bf16[2048,2048]{1,0:T(8,128)(2,1)} %constant_dynamic-update-slice_fusion.3, bf16[1024,2048]{1,0:T(8,128)(2,1)S(1)} %copy-done.82), kind=kOutput, calls=%fused_computation.83 | convolution fusion | flops 8592031744 | bytes 16777216 | tf_op jit(solution)/shard_map/td,fd->tf/dot_general | solution.py:199
  268.7 14.8 %convolution_convert_fusion.2 = bf16[2048,1024]{1,0:T(8,128)(2,1)} fusion(bf16[1024,2048]{0,1:T(8,128)(2,1)} %all-gather.8.cloned.1.call-done, bf16[1024,2048]{1,0:T(8,128)(2,1)} %collective-permute-done.6, bf16[512,2048]{1,0:T(8,128)(2,1)} %copy-done.37, bf16[512,2048]{1,0:T(8,128)(2,1)S(1)} %multiply_convert_fusion), kind=kOutput, calls=%fused_computation.84 | convolution fusion | flops 8617197568 | bytes 16777216 | tf_op jit(solution)/shard_map/td,fd->tf/dot_general | solution.py:199
  283.4 20.8 %fusion.5 = (bf16[2048,1024]{1,0:T(8,128)(2,1)}, bf16[2048,1024]{1,0:T(8,128)(2,1)}, bf16[2048,1024]{1,0:T(8,128)(2,1)}) fusion(bf16[2048,1024]{1,0:T(8,128)(2,1)} %convolution_convert_fusion.3, bf16[2048,1024]{1,0:T(8,128)(2,1)} %convolution_convert_fusion.2, bf16[1024,2048]{0,1:T(8,128)(2,1)} %all-gather.10.cloned.1.call-done, ...), kind=kOutput, calls=%fused_computation.15 | convolution fusion | flops 8652849152 | bytes 33554432 | tf_op jit(solution)/shard_map/td,fd->tf/dot_general | solution.py:199
  309.2 13.2 %convolution_convert_fusion = bf16[2048,1024]{1,0:T(8,128)(2,1)} fusion(bf16[2048,2048]{1,0:T(8,128)(2,1)} %constant_dynamic-update-slice_fusion.6, bf16[1024,2048]{0,1:T(8,128)(2,1)S(1)} %copy-done.85), kind=kOutput, calls=%fused_computation.82 | convolution fusion | flops 8592031744 | bytes 16777216 | tf_op jit(solution)/shard_map/td,fd->tf/dot_general | solution.py:199
  322.4 20.8 %fusion.2 = (bf16[2048,1024]{1,0:T(8,128)(2,1)}, bf16[2048,1024]{1,0:T(8,128)(2,1)}, bf16[2048,1024]{1,0:T(8,128)(2,1)}) fusion(bf16[2048,1024]{1,0:T(8,128)(2,1)} %convolution_convert_fusion.1, bf16[2048,1024]{1,0:T(8,128)(2,1)} %convolution_convert_fusion, bf16[2048,2048]{1,0:T(8,128)(2,1)} %constant_dynamic-update-slice_fusion.6, ...), kind=kOutput, calls=%fused_computation.12 | convolution fusion | flops 8627683328 | bytes 33554432 | tf_op jit(solution)/shard_map/td,fd->tf/dot_general | solution.py:199
  343.3 12.9 %fusion.75 = f32[1024,2048]{1,0:T(8,128)S(1)} fusion(bf16[2048,1024]{1,0:T(8,128)(2,1)} %get-tuple-element.116, bf16[2048,2048]{1,0:T(8,128)(2,1)} %constant_dynamic-update-slice_fusion.3), kind=kOutput, calls=%fused_computation.222 | convolution fusion | flops 8589934592 | bytes 20971520 | tf_op jit(solution)/shard_map/td,tf->df/dot_general | solution.py:203
  356.3 11.1 %add_convert_fusion.6 = bf16[1024,2048]{1,0:T(8,128)(2,1)} fusion(f32[1024,2048]{1,0:T(8,128)S(1)} %fusion.75, bf16[2048,1024]{1,0:T(8,128)(2,1)S(1)} %copy-done.96, bf16[2048,2048]{1,0:T(8,128)(2,1)S(1)} %bitcast.66), kind=kOutput, calls=%fused_computation.40 | convolution fusion | flops 8594128896 | bytes 25165824 | tf_op jit(solution)/shard_map/td,tf->df/dot_general | solution.py:203
  367.3 10.9 %fusion.43 = f32[1024,2048]{1,0:T(8,128)} fusion(bf16[1024,2048]{0,1:T(8,128)(2,1)} %all-gather.8.cloned.1.call-done, bf16[2048,1024]{1,0:T(8,128)(2,1)} %get-tuple-element.94), kind=kOutput, calls=%fused_computation.121 | convolution fusion | flops 4294967296 | bytes 14680064 | tf_op jit(solution)/shard_map/dot_general | solution.py:195
  402.8 10.9 %fusion.46 = f32[1024,2048]{1,0:T(8,128)} fusion(bf16[1024,2048]{0,1:T(8,128)(2,1)} %all-gather.8.cloned.1.call-done, bf16[2048,1024]{1,0:T(8,128)(2,1)} %get-tuple-element.94), kind=kOutput, calls=%fused_computation.124 | convolution fusion | flops 4294967296 | bytes 14680064 | tf_op jit(solution)/shard_map/dot_general | solution.py:195
  427.7 19.7 %collective-permute-done.15 = bf16[256,2048]{1,0:T(8,128)(2,1)S(1)} collective-permute-done((bf16[256,2048]{1,0:T(8,128)(2,1)S(1)}, bf16[256,2048]{1,0:T(8,128)(2,1)S(1)}, u32[]{:S(2)}, u32[]{:S(2)}) %collective-permute-start.15) | collective-permute-done | bytes 1048608 | tf_op jit(solution)/shard_map/ppermute | solution.py:175
  457.6 13.9 %fusion.76 = f32[1024,2048]{1,0:T(8,128)} fusion(bf16[2048,1024]{1,0:T(8,128)(2,1)S(1)} %copy-done.103, bf16[2048,2048]{1,0:T(8,128)(2,1)} %constant_dynamic-update-slice_fusion.6), kind=kOutput, calls=%fused_computation.223 | convolution fusion | flops 8589934592 | bytes 20971520 | tf_op jit(solution)/shard_map/td,tf->df/dot_general | solution.py:203
  471.5 13.9 %add_convert_fusion.2 = bf16[1024,2048]{1,0:T(8,128)(2,1)} fusion(f32[1024,2048]{1,0:T(8,128)} %fusion.76, bf16[2048,1024]{1,0:T(8,128)(2,1)S(1)} %copy-done.95, bf16[1024,2048]{1,0:T(8,128)(2,1)} %collective-permute-done.6, bf16[512,2048]{1,0:T(8,128)(2,1)S(1)} %copy-done.38, bf16[512,2048]{1,0:T(8,128)(2,1)S(1)} %copy-done.30), kind=kOutput, calls=%fused_computation.36 | convolution fusion | flops 8619294720 | bytes 25165824 | tf_op jit(solution)/shard_map/td,tf->df/dot_general | solution.py:203
  522.0 15.0 %fusion.77 = f32[1024,2048]{1,0:T(8,128)} fusion(bf16[2048,1024]{1,0:T(8,128)(2,1)} %get-tuple-element.109, bf16[2048,2048]{1,0:T(8,128)(2,1)} %constant_dynamic-update-slice_fusion.6), kind=kOutput, calls=%fused_computation.224 | convolution fusion | flops 8589934592 | bytes 20971520 | tf_op jit(solution)/shard_map/td,tf->df/dot_general | solution.py:203
  539.4 13.7 %add_convert_fusion.1 = bf16[1024,2048]{1,0:T(8,128)(2,1)} fusion(f32[1024,2048]{1,0:T(8,128)} %fusion.77, bf16[2048,1024]{1,0:T(8,128)(2,1)S(1)} %copy-done.93, bf16[1024,2048]{1,0:T(8,128)(2,1)} %collective-permute-done.6, bf16[512,2048]{1,0:T(8,128)(2,1)S(1)} %copy-done.39, bf16[512,2048]{1,0:T(8,128)(2,1)S(1)} %copy-done.30), kind=kOutput, calls=%fused_computation.35 | convolution fusion | flops 8619294720 | bytes 25165824 | tf_op jit(solution)/shard_map/td,tf->df/dot_general | solution.py:203
  553.7 11.2 %collective-permute-done.19 = bf16[512,2048]{1,0:T(8,128)(2,1)} collective-permute-done((bf16[512,2048]{1,0:T(8,128)(2,1)}, bf16[512,2048]{1,0:T(8,128)(2,1)}, u32[]{:S(2)}, u32[]{:S(2)}) %collective-permute-start.19) | collective-permute-done | bytes 2097184 | tf_op jit(solution)/shard_map/ppermute | solution.py:175
  601.0 19.9 %attend_back.1 = (bf16[1024,1024]{1,0:T(8,128)(2,1)}, bf16[1024,512]{1,0:T(8,128)(2,1)}, bf16[1024,512]{1,0:T(8,128)(2,1)}) custom-call(s32[1]{0:T(128)} %bitcast.first_ref, bf16[1024,1024]{1,0:T(8,128)(2,1)} %get-tuple-element.72.q_ref, bf16[1024,512]{1,0:T(8,128)(2,1)} %get-tuple-element.73.k_ref, bf16[1024,512]{1,0:T(8,128)(2,1)} %get-tuple-element.74.v_ref, ...), custom_call_target="tpu_custom_call" | custom-call | flops 7516192768 | bytes 37580964 | tf_op jit(solution)/shard_map/attend_back/pallas_call | solution.py:153
  686.7 22.6 %collective-permute-done.32 = bf16[512,2048]{1,0:T(8,128)(2,1)} collective-permute-done((bf16[512,2048]{1,0:T(8,128)(2,1)}, bf16[512,2048]{1,0:T(8,128)(2,1)}, u32[]{:S(2)}, u32[]{:S(2)}) %collective-permute-start.32) | collective-permute-done | bytes 2097184 | tf_op jit(solution)/shard_map/ppermute | solution.py:175
  709.3 9.3 convert_add_fusion.1
  759.9 31.3 %collective-permute-done.36 = bf16[512,2048]{1,0:T(8,128)(2,1)S(1)} collective-permute-done((bf16[512,2048]{1,0:T(8,128)(2,1)S(1)}, bf16[512,2048]{1,0:T(8,128)(2,1)S(1)}, u32[]{:S(2)}, u32[]{:S(2)}) %collective-permute-start.36) | collective-permute-done | bytes 2097184 | tf_op jit(solution)/shard_map/ppermute | solution.py:175
  811.1 23.2 %collective-permute-done.38 = bf16[512,2048]{1,0:T(8,128)(2,1)} collective-permute-done((bf16[512,2048]{1,0:T(8,128)(2,1)}, bf16[512,2048]{1,0:T(8,128)(2,1)}, u32[]{:S(2)}, u32[]{:S(2)}) %collective-permute-start.38) | collective-permute-done | bytes 2097184 | tf_op jit(solution)/shard_map/ppermute | solution.py:175
  834.3 12.8 %collective-permute-done.39 = bf16[512,2048]{1,0:T(8,128)(2,1)} collective-permute-done((bf16[512,2048]{1,0:T(8,128)(2,1)}, bf16[512,2048]{1,0:T(8,128)(2,1)}, u32[]{:S(2)}, u32[]{:S(2)}) %collective-permute-start.39) | collective-permute-done | bytes 2097184 | tf_op jit(solution)/shard_map/ppermute | solution.py:175
  847.2 9.5 fusion.23
  875.4 9.4 copy.30
  902.2 8.8 collective-permute-done.43
  935.5 9.4 copy.31
  (465 shorter events, 434.0 us)
Async XLA Ops:
  7.2 112.7 %all-gather.6.cloned.1.call-start = ((), (), s32[]{:S(2)}) async-start(), calls=%async_computation.5 | async-start | bytes 5242880 | tf_op jit(solution)/shard_map/all_gather | solution.py:284
  9.7 258.9 %all-gather.8.cloned.1.call-start = ((), (), s32[]{:S(2)}) async-start(), calls=%async_computation.6 | async-start | bytes 5242880 | tf_op jit(solution)/shard_map/all_gather | solution.py:284
  12.7 48.9 %collective-permute-start = (bf16[512,2048]{1,0:T(8,128)(2,1)}, bf16[512,2048]{1,0:T(8,128)(2,1)}, u32[]{:S(2)}, u32[]{:S(2)}) collective-permute-start(bf16[512,2048]{1,0:T(8,128)(2,1)} %fusion.26), channel_id=1, source_target_pairs={{0,1},{1,0},{2,3},{3,2},{4,5},{5,4},{6,7},{7,6},{8,9},{9,8},{10,11... | collective-permute-start | bytes 6291464 | tf_op jit(solution)/shard_map/ppermute | solution.py:175
  18.0 265.4 %all-gather.10.cloned.1.call-start = ((), (), s32[]{:S(2)}) async-start(), calls=%async_computation.7 | async-start | bytes 5242880 | tf_op jit(solution)/shard_map/all_gather | solution.py:284
  18.1 115.6 %collective-permute-start.9 = (bf16[512,2048]{1,0:T(8,128)(2,1)}, bf16[512,2048]{1,0:T(8,128)(2,1)}, u32[]{:S(2)}, u32[]{:S(2)}) collective-permute-start(bf16[512,2048]{1,0:T(8,128)(2,1)} %param.14), channel_id=1, source_target_pairs={{0,16},{8,24},{16,0},{24,8},{1,17},{9,25},{17,1},{25,9},{2,18},{10... | collective-permute-start | bytes 6291464 | tf_op jit(solution)/shard_map/ppermute | solution.py:175
  66.5 47.1 %collective-permute-start.4 = (bf16[512,2048]{1,0:T(8,128)(2,1)}, bf16[512,2048]{1,0:T(8,128)(2,1)}, u32[]{:S(2)}, u32[]{:S(2)}) collective-permute-start(bf16[512,2048]{1,0:T(8,128)(2,1)} %param.14), channel_id=1, source_target_pairs={{0,1},{1,0},{2,3},{3,2},{4,5},{5,4},{6,7},{7,6},{8,9},{9,8},{10,11... | collective-permute-start | bytes 6291464 | tf_op jit(solution)/shard_map/ppermute | solution.py:175
  118.4 64.9 %collective-permute-start.5 = (bf16[1024,2048]{1,0:T(8,128)(2,1)}, bf16[1024,2048]{1,0:T(8,128)(2,1)}, u32[]{:S(2)}, u32[]{:S(2)}) collective-permute-start(bf16[1024,2048]{1,0:T(8,128)(2,1)} %pad_maximum_fusion.3), channel_id=1, source_target_pairs={{0,8},{8,0},{16,24},{24,16},{1,9},{9,1},{17,25},{25,17},{2,10},{10... | collective-permute-start | bytes 12582920 | tf_op jit(solution)/shard_map/ppermute | solution.py:175
  118.5 48.4 %collective-permute-start.10 = (bf16[512,2048]{1,0:T(8,128)(2,1)}, bf16[512,2048]{1,0:T(8,128)(2,1)}, u32[]{:S(2)}, u32[]{:S(2)}) collective-permute-start(bf16[512,2048]{1,0:T(8,128)(2,1)} %collective-permute-done.4), channel_id=1, source_target_pairs={{0,16},{8,24},{16,0},{24,8},{1,17},{9,25},{17,1},{25,9},{2,18},{10... | collective-permute-start | bytes 6291464 | tf_op jit(solution)/shard_map/ppermute | solution.py:175
  126.2 48.1 %collective-permute-start.1 = (bf16[512,2048]{1,0:T(8,128)(2,1)}, bf16[512,2048]{1,0:T(8,128)(2,1)}, u32[]{:S(2)}, u32[]{:S(2)}) collective-permute-start(bf16[512,2048]{1,0:T(8,128)(2,1)} %convolution_convert_fusion.9), channel_id=1, source_target_pairs={{0,1},{1,0},{2,3},{3,2},{4,5},{5,4},{6,7},{7,6},{8,9},{9,8},{10,11... | collective-permute-start | bytes 6291464 | tf_op jit(solution)/shard_map/ppermute | solution.py:175
  129.9 385.6 %reduce-scatter.6.cloned.1.call-start = ((), (), s32[]{:S(2)}) async-start(), calls=%async_computation.8 | async-start | bytes 5242880 | tf_op jit(solution)/shard_map/reduce_scatter | solution.py:288
  169.4 70.3 %collective-permute-start.11 = (bf16[1024,2048]{1,0:T(8,128)(2,1)S(1)}, bf16[1024,2048]{1,0:T(8,128)(2,1)S(1)}, u32[]{:S(2)}, u32[]{:S(2)}) collective-permute-start(bf16[1024,2048]{1,0:T(8,128)(2,1)S(1)} %pad_maximum_fusion.5), channel_id=1, source_target_pairs={{0,8},{8,0},{16,24},{24,16},{1,9},{9,1},{17,25},{25,17},{2,10},{10... | collective-permute-start | bytes 12582920 | tf_op jit(solution)/shard_map/ppermute | solution.py:175
  402.7 166.4 %reduce-scatter.8.cloned.1.call-start = ((), (), s32[]{:S(2)}) async-start(), calls=%async_computation.9 | async-start | bytes 5242880 | tf_op jit(solution)/shard_map/reduce_scatter | solution.py:288
  455.4 47.6 %collective-permute-start.18 = (bf16[512,2048]{1,0:T(8,128)(2,1)}, bf16[512,2048]{1,0:T(8,128)(2,1)}, u32[]{:S(2)}, u32[]{:S(2)}) collective-permute-start(bf16[512,2048]{1,0:T(8,128)(2,1)} %add_convert_fusion.13), channel_id=1, source_target_pairs={{0,16},{8,24},{16,0},{24,8},{1,17},{9,25},{17,1},{25,9},{2,18},{10... | collective-permute-start | bytes 6291464 | tf_op jit(solution)/shard_map/ppermute | solution.py:175
  456.9 47.3 %collective-permute-start.17 = (bf16[512,2048]{1,0:T(8,128)(2,1)}, bf16[512,2048]{1,0:T(8,128)(2,1)}, u32[]{:S(2)}, u32[]{:S(2)}) collective-permute-start(bf16[512,2048]{1,0:T(8,128)(2,1)} %add_convert_fusion.12), channel_id=1, source_target_pairs={{0,1},{1,0},{2,3},{3,2},{4,5},{5,4},{6,7},{7,6},{8,9},{9,8},{10,11... | collective-permute-start | bytes 6291464 | tf_op jit(solution)/shard_map/ppermute | solution.py:175
  485.5 164.2 %reduce-scatter.10.cloned.1.call-start = ((), (), s32[]{:S(2)}) async-start(), calls=%async_computation.10 | async-start | bytes 5242880 | tf_op jit(solution)/shard_map/reduce_scatter | solution.py:288
  517.2 47.7 %collective-permute-start.19 = (bf16[512,2048]{1,0:T(8,128)(2,1)}, bf16[512,2048]{1,0:T(8,128)(2,1)}, u32[]{:S(2)}, u32[]{:S(2)}) collective-permute-start(bf16[512,2048]{1,0:T(8,128)(2,1)} %fusion.71), channel_id=1, source_target_pairs={{0,1},{1,0},{2,3},{3,2},{4,5},{5,4},{6,7},{7,6},{8,9},{9,8},{10,11... | collective-permute-start | bytes 6291464 | tf_op jit(solution)/shard_map/ppermute | solution.py:175
  517.9 51.2 %collective-permute-start.20 = (bf16[256,2048]{1,0:T(8,128)(2,1)}, bf16[256,2048]{1,0:T(8,128)(2,1)S(1)}, u32[]{:S(2)}, u32[]{:S(2)}) collective-permute-start(bf16[256,2048]{1,0:T(8,128)(2,1)} %reduce-scatter.6.cloned.1.call-done), channel_id=1, source_target_pairs={{0,16},{8,24},{16,0},{24,8},{1,17},{9,25},{17,1},{25,9},{2,18},{10... | collective-permute-start | bytes 3145736 | tf_op jit(solution)/shard_map/ppermute | solution.py:175
  553.2 133.4 %reduce-scatter.12.cloned.1.call-start = ((), (), s32[]{:S(2)}) async-start(), calls=%async_computation.11 | async-start | bytes 1310720 | tf_op jit(solution)/shard_map/reduce_scatter | solution.py:288
  589.1 79.1 %collective-permute-start.29 = (bf16[2048,256]{0,1:T(8,128)(2,1)S(1)}, bf16[2048,256]{0,1:T(8,128)(2,1)}, u32[]{:S(2)}, u32[]{:S(2)}) collective-permute-start(bf16[2048,256]{0,1:T(8,128)(2,1)S(1)} %bitcast.63), channel_id=1, source_target_pairs={{0,16},{8,24},{16,0},{24,8},{1,17},{9,25},{17,1},{25,9},{2,18},{10... | collective-permute-start | bytes 3145736 | tf_op jit(solution)/shard_map/ppermute | solution.py:175
  590.7 86.1 %collective-permute-start.51 = (f32[8,256]{1,0:T(8,128)S(1)}, f32[8,256]{1,0:T(8,128)S(1)}, u32[]{:S(2)}, u32[]{:S(2)}) collective-permute-start(f32[8,256]{1,0:T(8,128)S(1)} %add.239), channel_id=1, source_target_pairs={{0,1},{1,0},{2,3},{3,2},{4,5},{5,4},{6,7},{7,6},{8,9},{9,8},{10,11... | collective-permute-start | bytes 24584 | tf_op jit(solution)/shard_map/ppermute | solution.py:175
  649.7 78.0 %all-gather.12.cloned.1.call-start = ((), (), s32[]{:S(2)}) async-start(), calls=%async_computation.12 | async-start | bytes 1310720 | tf_op jit(solution)/shard_map/all_gather | solution.py:284
  661.2 48.1 %collective-permute-start.32 = (bf16[512,2048]{1,0:T(8,128)(2,1)}, bf16[512,2048]{1,0:T(8,128)(2,1)}, u32[]{:S(2)}, u32[]{:S(2)}) collective-permute-start(bf16[512,2048]{1,0:T(8,128)(2,1)} %convolution_convert_fusion.10), channel_id=1, source_target_pairs={{0,1},{1,0},{2,3},{3,2},{4,5},{5,4},{6,7},{7,6},{8,9},{9,8},{10,11... | collective-permute-start | bytes 6291464 | tf_op jit(solution)/shard_map/ppermute | solution.py:175
  674.8 61.2 %collective-permute-start.35 = (bf16[1024,2048]{1,0:T(8,128)(2,1)}, bf16[1024,2048]{1,0:T(8,128)(2,1)}, u32[]{:S(2)}, u32[]{:S(2)}) collective-permute-start(bf16[1024,2048]{1,0:T(8,128)(2,1)} %convolution_convert_fusion.5), channel_id=1, source_target_pairs={{0,8},{8,0},{16,24},{24,16},{1,9},{9,1},{17,25},{25,17},{2,10},{10... | collective-permute-start | bytes 12582920 | tf_op jit(solution)/shard_map/ppermute | solution.py:175
  676.2 54.8 %collective-permute-start.54 = (bf16[512,2048]{1,0:T(8,128)(2,1)}, bf16[512,2048]{1,0:T(8,128)(2,1)}, u32[]{:S(2)}, u32[]{:S(2)}) collective-permute-start(bf16[512,2048]{1,0:T(8,128)(2,1)} %pad_maximum_fusion.15), channel_id=1, source_target_pairs={{0,8},{8,0},{16,24},{24,16},{1,9},{9,1},{17,25},{25,17},{2,10},{10... | collective-permute-start | bytes 6291464 | tf_op jit(solution)/shard_map/ppermute | solution.py:175
  686.6 113.0 %reduce-scatter.14.cloned.1.call-start = ((), (), s32[]{:S(2)}) async-start(), calls=%async_computation.13 | async-start | bytes 2621440 | tf_op jit(solution)/shard_map/reduce_scatter | solution.py:288
  730.5 126.2 %all-gather.14.cloned.1.call-start = ((), (), s32[]{:S(2)}) async-start(), calls=%async_computation.14 | async-start | bytes 2621440 | tf_op jit(solution)/shard_map/all_gather | solution.py:284
  742.6 48.6 %collective-permute-start.36 = (bf16[512,2048]{1,0:T(8,128)(2,1)S(1)}, bf16[512,2048]{1,0:T(8,128)(2,1)S(1)}, u32[]{:S(2)}, u32[]{:S(2)}) collective-permute-start(bf16[512,2048]{1,0:T(8,128)(2,1)S(1)} %slice.151), channel_id=1, source_target_pairs={{0,1},{1,0},{2,3},{3,2},{4,5},{5,4},{6,7},{7,6},{8,9},{9,8},{10,11... | collective-permute-start | bytes 6291464 | tf_op jit(solution)/shard_map/ppermute | solution.py:175
  747.1 121.1 %collective-permute-start.52 = (bf16[2048,512]{0,1:T(8,128)(2,1)}, bf16[2048,512]{0,1:T(8,128)(2,1)}, u32[]{:S(2)}, u32[]{:S(2)}) collective-permute-start(bf16[2048,512]{0,1:T(8,128)(2,1)} %pad_maximum_fusion.13), channel_id=1, source_target_pairs={{0,8},{8,0},{16,24},{24,16},{1,9},{9,1},{17,25},{25,17},{2,10},{10... | collective-permute-start | bytes 6291464 | tf_op jit(solution)/shard_map/ppermute | solution.py:175
  758.8 75.5 %collective-permute-start.38 = (bf16[512,2048]{1,0:T(8,128)(2,1)}, bf16[512,2048]{1,0:T(8,128)(2,1)}, u32[]{:S(2)}, u32[]{:S(2)}) collective-permute-start(bf16[512,2048]{1,0:T(8,128)(2,1)} %add_convert_fusion.7), channel_id=1, source_target_pairs={{0,1},{1,0},{2,3},{3,2},{4,5},{5,4},{6,7},{7,6},{8,9},{9,8},{10,11... | collective-permute-start | bytes 6291464 | tf_op jit(solution)/shard_map/ppermute | solution.py:175
  799.6 47.5 %collective-permute-start.39 = (bf16[512,2048]{1,0:T(8,128)(2,1)}, bf16[512,2048]{1,0:T(8,128)(2,1)}, u32[]{:S(2)}, u32[]{:S(2)}) collective-permute-start(bf16[512,2048]{1,0:T(8,128)(2,1)} %add_convert_fusion.8), channel_id=1, source_target_pairs={{0,16},{8,24},{16,0},{24,8},{1,17},{9,25},{17,1},{25,9},{2,18},{10... | collective-permute-start | bytes 6291464 | tf_op jit(solution)/shard_map/ppermute | solution.py:175
  808.0 80.3 %collective-permute-start.50 = (bf16[512,2048]{1,0:T(8,128)(2,1)}, bf16[512,2048]{1,0:T(8,128)(2,1)}, u32[]{:S(2)}, u32[]{:S(2)}) collective-permute-start(bf16[512,2048]{1,0:T(8,128)(2,1)} %pad_maximum_fusion.12), channel_id=1, source_target_pairs={{0,8},{8,0},{16,24},{24,16},{1,9},{9,1},{17,25},{25,17},{2,10},{10... | collective-permute-start | bytes 6291464 | tf_op jit(solution)/shard_map/ppermute | solution.py:175
  810.6 83.4 %collective-permute-start.53 = (bf16[2048,512]{0,1:T(8,128)(2,1)}, bf16[2048,512]{0,1:T(8,128)(2,1)}, u32[]{:S(2)}, u32[]{:S(2)}) collective-permute-start(bf16[2048,512]{0,1:T(8,128)(2,1)} %pad_maximum_fusion.14), channel_id=1, source_target_pairs={{0,8},{8,0},{16,24},{24,16},{1,9},{9,1},{17,25},{25,17},{2,10},{10... | collective-permute-start | bytes 6291464 | tf_op jit(solution)/shard_map/ppermute | solution.py:175
  (139 other events, 2241.9 us)
Sparse Core Ops, SparseCore 0:
  10.2 83.4 all-gather.5
  95.2 79.0 all-gather.7
  175.8 78.7 all-gather.9
  402.8 77.2 reduce-scatter.5
  485.6 77.5 reduce-scatter.7
  565.9 77.2 reduce-scatter.9
  649.8 27.6 reduce-scatter.11
  686.8 28.8 all-gather.11
  730.6 44.4 reduce-scatter.13
  804.1 45.5 all-gather.13
